TPU v7x, 128 devices: a whole 4x4x4 slice. The times are simulated.
128 devices in a mesh: au: 8 (over z_hi, y), pa: 8 (over x, z_lo), dev: 2 (over core).
Axes of the slice: x: 4, y: 4, z: 4 (z_hi: 2, z_lo: 2; z = z_hi * 2 + z_lo), core: 2. Of those that a mesh axis runs over, the one named last changes fastest.
Arguments:
- features: bfloat16 [8192, 64, 256], P('au', 'pa'), may hold values from -6 to 6
- item_ids: int32 [8192, 64], P('au', 'pa'), may hold values from 0 to 4095
- item_table: bfloat16 [4096, 256], replicated, may hold values from -4 to 4
- lengths: int32 [8192], P('au'), may hold values from 1 to 64
- routing_seed: int32 [4, 64], replicated, may hold values from 0 to 15
- w_qkv: bfloat16 [3, 256, 256], P(None, None, 'dev'), may hold values from -0.375 to 0.375
- w_out: bfloat16 [256, 256], P('dev'), may hold values from -0.375 to 0.375
- w_bilinear: bfloat16 [256, 256], P(None, 'dev'), may hold values from -0.375 to 0.375
- w_up: bfloat16 [256, 1024], P(None, 'dev'), may hold values from -0.375 to 0.375
- w_down: bfloat16 [1024, 256], P('dev'), may hold values from -0.1875 to 0.1875
Outputs:
- capsules: float32 [8192, 4, 256], P(('au', 'pa'), None, 'dev')
All inputs are finite; a program needn't handle non-finite values.
Results may differ from a plain program's by a relative error of at most 0.012.
The roundings to bfloat16 on the way count: a program that leaves them out, or rounds other values in their place, can miss the bound.
Values may be sent and summed in bfloat16 or wider, within the bound.
No kernel may reach another device: no remote copies, remote signals or barrier semaphores. Data moves between devices by JAX's collectives and lax.ppermute only.
A program may use at most 128 MiB of HBM per device.

v0:
```python
import jax
import jax.numpy as jnp
from jax import lax
from jax.sharding import PartitionSpec as P

D = 256
HEADS = 4
CAPS = 4
ITERS = 3


def laid_out(tiles, dim):
    tiles = jnp.moveaxis(tiles, 0, dim)
    shape = tiles.shape
    return tiles.reshape(*shape[:dim], shape[dim] * shape[dim + 1], *shape[dim + 2 :])


def gather_packed(arrays, axis, dims):
    vector = jnp.concatenate([a.reshape(-1) for a in arrays])
    lines, at, finished = (lax.all_gather(vector, axis), 0, [])
    for a, dim in zip(arrays, dims):
        tiles = lines[:, at : at + a.size].reshape(-1, *a.shape)
        finished.append(laid_out(tiles, dim))
        at += a.size
    return tuple(finished)


def local_routing(vectors, valid, base):
    user_count, history_len, width_here = vectors.shape
    logits = jnp.broadcast_to(base[None], (user_count, CAPS, history_len))
    capsules = jnp.zeros((user_count, CAPS, width_here), jnp.float32)
    for sweep in range(ITERS):
        weights = jax.nn.softmax(logits, axis=1) * valid[:, None, :]
        summed = jnp.einsum("ukl,uld->ukd", weights, vectors, precision=lax.Precision.HIGHEST)
        squares = jnp.sum(summed * summed, axis=-1)
        factor = jnp.sqrt(squares) / (1.0 + squares)
        capsules = summed * factor[..., None]
        if sweep + 1 < ITERS:
            logits = logits + jnp.einsum(
                "ukd,uld->ukl", capsules, vectors, precision=lax.Precision.HIGHEST
            )
    return capsules


def body(
    features, item_ids, item_table, lengths, routing_seed, w_qkv, w_out, w_bilinear, w_up, w_down
):
    pa_count = lax.axis_size("pa")
    dev_count = lax.axis_size("dev")
    owned_users = lengths.shape[0] // pa_count
    head_size = D // HEADS
    share = owned_users // dev_count
    core = lax.axis_index("dev")

    def pick(array):
        shaped = array.reshape((pa_count, dev_count, share) + array.shape[1:])
        chosen = lax.dynamic_index_in_dim(shaped, core, 1, keepdims=False)
        return chosen.reshape((pa_count * share,) + array.shape[1:])

    features = pick(features)
    item_ids = pick(item_ids)
    lengths = pick(lengths)
    w_qkv, w_out, w_bilinear, w_up, w_down = gather_packed(
        (w_qkv, w_out, w_bilinear, w_up, w_down), "dev", (2, 0, 1, 1, 0)
    )
    own_lens = lax.dynamic_slice_in_dim(lengths, lax.axis_index("pa") * share, share)
    features, item_ids = (
        lax.all_to_all(features, "pa", split_axis=0, concat_axis=1, tiled=True),
        lax.all_to_all(item_ids, "pa", split_axis=0, concat_axis=1, tiled=True),
    )
    user_count, span_here, model_width = features.shape
    heads_here = w_qkv.shape[2] // head_size
    inputs = (
        features.astype(jnp.float32) + jnp.take(item_table, item_ids, axis=0).astype(jnp.float32)
    ).astype(jnp.bfloat16)
    flat_rows = inputs.reshape(-1, model_width)

    def project(index):
        shaped = w_qkv[index].reshape(model_width, heads_here, head_size)
        made = jnp.einsum(
            "nd,dhe->hne", flat_rows, shaped, preferred_element_type=jnp.float32
        ).astype(jnp.bfloat16)
        return made.reshape(heads_here, user_count, span_here, head_size)

    queries = project(0)
    key_block = project(1)
    value_block = project(2)
    score_scale = 1.0 / head_size**0.5
    count_here = key_block.shape[2]
    scores = (
        jnp.einsum("huqe,huke->huqk", queries, key_block, preferred_element_type=jnp.float32)
        * score_scale
    )
    positions = jnp.arange(count_here, dtype=jnp.int32)
    valid_keys = positions[None, :] < own_lens[:, None]
    mask_four = valid_keys[None, :, None, :]
    probs = jnp.where(mask_four, jnp.exp(scores), 0.0)
    totals = jnp.sum(probs, axis=-1)
    weighted = jnp.einsum(
        "huqk,huke->huqe",
        probs.astype(jnp.bfloat16),
        value_block,
        preferred_element_type=jnp.float32,
    )
    attended = (weighted / totals[..., None]).astype(jnp.bfloat16)
    out_heads = w_out.reshape(heads_here, head_size, w_out.shape[1])
    attended_term = jnp.einsum(
        "huqe,hef->uqf", attended, out_heads, preferred_element_type=jnp.float32
    )
    hidden = jax.nn.gelu(jnp.dot(flat_rows, w_up, preferred_element_type=jnp.float32)).astype(
        jnp.bfloat16
    )
    partial_terms = attended_term.reshape(-1, w_out.shape[1]) + jnp.dot(
        hidden, w_down, preferred_element_type=jnp.float32
    )
    interest_in = (
        partial_terms + jnp.dot(flat_rows, w_bilinear, preferred_element_type=jnp.float32)
    ).astype(jnp.bfloat16)
    interest_in = interest_in.reshape(user_count, span_here, -1)
    history_len = interest_in.shape[1]
    valid = (jnp.arange(history_len)[None, :] < own_lens[:, None]).astype(jnp.float32)
    base = (routing_seed.astype(jnp.float32) - 7.5) * 0.25
    routed = local_routing(interest_in.astype(jnp.float32), valid, base)
    capsules = lax.all_to_all(routed, "dev", split_axis=2, concat_axis=0, tiled=True)
    return capsules


def solution(mesh):
    in_specs = (
        P("au", "pa", None),
        P("au", "pa"),
        P(),
        P("au"),
        P(),
        P(None, None, "dev"),
        P("dev", None),
        P(None, "dev"),
        P(None, "dev"),
        P("dev", None),
    )
    out_specs = P(("au", "pa"), None, "dev")
    return jax.shard_map(body, mesh=mesh, in_specs=in_specs, out_specs=out_specs, check_vma=False)
```

profile of v0, /device:TPU:1, one launch (start us, length us, event | category | flops | bytes accessed | tf_op | source)
XLA Modules:
  0.0 140.4 jit_solution(1867006073911560895)
XLA Ops:
  6.5 1.1 constant_dynamic-update-slice_fusion.3
  7.6 0.9 copy.136
  8.5 1.1 copy.137
  9.6 1.2 copy.138
  10.8 0.8 bitcast_dynamic-update-slice_fusion
  11.7 1.0 copy-done.7
  12.7 0.9 reshape.215
  13.6 0.7 reshape.245
  14.3 6.2 %all-to-all-start.1 = ((s32[8,1,512]{2,1,0:T(1,128)}), s32[8,1,512]{2,1,0:T(1,128)S(1)}, u32[]{:S(2)}, u32[]{:S(2)}) async-start(s32[8,1,512]{2,1,0:T(1,128)} %reshape.245), calls=%async_computation.1 | async-start | bytes 32768 | tf_op jit(solution)/shard_map/all_to_all | solution.py:69
  20.5 0.8 reshape.205
  21.5 3.0 %constant_dynamic-slice_fusion.1 = bf16[8,1,64,8,256]{4,3,2,1,0:T(8,128)(2,1)} fusion(bf16[8,2,64,8,256]{4,3,2,1,0:T(8,128)(2,1)} %bitcast.141, s32[]{:T(128)S(6)} %select_n.42), kind=kLoop, calls=%fused_computation.91 | loop fusion | bytes 4194308 | tf_op jit(solution)/shard_map/jit(dynamic_index_in_dim)/dynamic_slice | solution.py:57
  24.6 0.9 all-to-all-done.1
  25.6 4.3 %all-to-all-start = ((bf16[512,8,256]{2,1,0:T(8,128)(2,1)}), bf16[512,8,256]{2,1,0:T(8,128)(2,1)}, u32[]{:S(2)}, u32[]{:S(2)}) async-start(bf16[512,8,256]{2,1,0:T(8,128)(2,1)} %bitcast.131), calls=%async_computation | async-start | bytes 4194304 | tf_op jit(solution)/shard_map/all_to_all | solution.py:68
  29.9 0.5 broadcast.110
  30.4 0.7 reduce.7
  31.6 16.9 %gather_fusion = bf16[4096,256]{1,0:T(8,128)(2,1)} fusion(bf16[4096,256]{1,0:T(8,128)(2,1)S(1)} %copy-done, s32[4096]{0:T(1024)S(1)} %broadcast_clamp_fusion), kind=kCustom, calls=%fused_computation | custom fusion | bytes 4210688 | tf_op jit(solution)/shard_map/jit(_take)/gather | solution.py:74
  48.5 1.9 %reshape.233 = bf16[2,425984]{1,0:T(2,128)(2,1)S(1)} reshape(bf16[851968]{0:T(1024)(128)(2,1)} %all-gather.3.cloned.1.call-done) | data formatting | bytes 3407872 | tf_op jit(solution)/shard_map/all_gather | solution.py:20
  50.4 1.2 copy-done.5
  51.6 1.6 %fusion.67 = (bf16[2,131072]{1,0:T(2,128)(2,1)}, bf16[2,131072]{1,0:T(2,128)(2,1)S(1)}) fusion(bf16[2,425984]{1,0:T(2,128)(2,1)S(1)} %reshape.233), kind=kLoop, calls=%fused_computation.100 | loop fusion | bytes 2097152 | tf_op jit(solution)/shard_map/slice | solution.py:22
  53.1 1.4 %slice_bitcast_fusion = bf16[1,2,768,128]{3,1,2,0:T(2,128)(2,1)S(1)} fusion(bf16[2,425984]{1,0:T(2,128)(2,1)} %copy-done.5), kind=kLoop, calls=%fused_computation.44 | loop fusion | bytes 786432
  54.6 0.8 copy.110
  55.4 0.8 copy.103
  56.3 1.8 %slice_bitcast_fusion.1 = (bf16[1,2,256,128]{3,1,2,0:T(2,128)(2,1)}, bf16[2,32768]{1,0:T(2,128)(2,1)S(1)}) fusion(bf16[2,425984]{1,0:T(2,128)(2,1)} %copy-done.5), kind=kLoop, calls=%fused_computation.51 | loop fusion | bytes 524288
  58.2 1.1 copy.150
  59.3 1.0 copy.117
  60.3 1.1 reshape_reshape.3
  61.4 0.9 copy.151
  62.5 3.0 %fusion.27 = bf16[64,8,8,256]{3,2,0,1:T(8,128)(2,1)S(1)} fusion(bf16[8,64,8,256]{3,2,1,0:T(8,128)(2,1)} %bitcast.36, bf16[64,8,8,256]{3,2,1,0:T(8,128)(2,1)S(1)} %bitcast.130, pred[64,8,8]{2,0,1:T(8,128)(4,1)S(1)} %copy.106), kind=kLoop, calls=%fused_computation.32 | loop fusion | flops 5242880 | bytes 6295552 | tf_op jit(solution)/shard_map/convert_element_type | solution.py:75
  65.8 2.1 %fusion.22 = bf16[4,4096,64]{1,2,0:T(8,128)(2,1)} fusion(bf16[256,4,64]{0,2,1:T(8,128)(2,1)S(1)} %bitcast.147, bf16[4096,256,1]{1,0,2:T(8,128)(2,1)S(1)} %bitcast.125), kind=kOutput, calls=%fused_computation.27 | convolution fusion | flops 537919488 | bytes 4325376 | tf_op jit(solution)/shard_map/nd,dhe->hne/dot_general | solution.py:80
  67.9 4.8 %copy.133 = bf16[4,4096,64]{2,1,0:T(8,128)(2,1)} copy(bf16[4,4096,64]{1,2,0:T(8,128)(2,1)} %fusion.22) | data formatting | bytes 4194304 | tf_op jit(solution)/shard_map/reshape | solution.py:83
  72.7 2.1 %fusion.21 = bf16[4,4096,64]{1,2,0:T(8,128)(2,1)} fusion(bf16[256,4,64]{0,2,1:T(8,128)(2,1)S(1)} %bitcast.146, bf16[4096,256,1]{1,0,2:T(8,128)(2,1)S(1)} %bitcast.126), kind=kOutput, calls=%fused_computation.26 | convolution fusion | flops 537919488 | bytes 4325376 | tf_op jit(solution)/shard_map/nd,dhe->hne/dot_general | solution.py:80
  74.9 4.8 %copy.132 = bf16[4,4096,64]{2,1,0:T(8,128)(2,1)} copy(bf16[4,4096,64]{1,2,0:T(8,128)(2,1)} %fusion.21) | data formatting | bytes 4194304 | tf_op jit(solution)/shard_map/reshape | solution.py:83
  79.6 2.1 %fusion.23 = bf16[4,4096,64]{1,2,0:T(8,128)(2,1)} fusion(bf16[256,4,64]{0,2,1:T(8,128)(2,1)S(1)} %bitcast.145, bf16[4096,256,1]{1,0,2:T(8,128)(2,1)S(1)} %bitcast.127), kind=kOutput, calls=%fused_computation.28 | convolution fusion | flops 537919488 | bytes 4325376 | tf_op jit(solution)/shard_map/nd,dhe->hne/dot_general | solution.py:80
  81.7 4.8 %copy.134 = bf16[4,4096,64]{2,1,0:T(8,128)(2,1)} copy(bf16[4,4096,64]{1,2,0:T(8,128)(2,1)} %fusion.23) | data formatting | bytes 4194304 | tf_op jit(solution)/shard_map/reshape | solution.py:83
  86.6 5.0 %fusion.13 = (f32[4,64,64]{2,1,0:T(8,128)S(1)}, f32[4,64,64,64]{2,3,1,0:T(8,128)S(1)}) fusion(pred[64,64]{1,0:T(8,128)(4,1)S(1)} %get-tuple-element.15, bf16[4,64,64,64]{3,2,1,0:T(8,128)(2,1)} %bitcast.134, bf16[4,64,64,64]{3,2,1,0:T(8,128)(2,1)} %bitcast.133), kind=kOutput, calls=%fused_computation.16 | convolution fusion | flops 137347072 | bytes 8458240 | tf_op jit(solution)/shard_map/huqe,huke->huqk/dot_general | solution.py:91
  91.5 5.3 %fusion.10 = bf16[64,64,64,4]{2,1,0,3:T(8,128)(2,1)S(1)} fusion(f32[64,64,4]{1,0,2:T(8,128)S(1)} %bitcast.156, bf16[4,64,64,64]{3,2,1,0:T(8,128)(2,1)S(1)} %bitcast.135, f32[4,64,64,64]{2,3,1,0:T(8,128)S(1)} %get-tuple-element.17, pred[64,64]{1,0:T(8,128)(4,1)S(1)} %get-tuple-element.15), kind=kOutput, calls=%fused_computation.13 | convolution fusion | flops 139460608 | bytes 8458240 | tf_op jit(solution)/shard_map/huqk,huke->huqe/dot_general | solution.py:99
  96.8 2.8 %convolution_bitcast_fusion = f32[4096,256]{1,0:T(8,128)} fusion(bf16[4096,64,4]{1,0,2:T(8,128)(2,1)S(1)} %bitcast.132, bf16[4,64,256]{2,1,0:T(8,128)(2,1)S(1)} %reshape_reshape_reshape.3), kind=kOutput, calls=%fused_computation.19 | convolution fusion | flops 536870912 | bytes 6422528 | tf_op jit(solution)/shard_map/huqe,hef->uqf/dot_general | solution.py:107
  99.7 9.4 %fusion.15 = f32[4096,256]{1,0:T(8,128)} fusion(f32[4096,256]{1,0:T(8,128)} %convolution_bitcast_fusion, bf16[1024,256]{1,0:T(8,128)(2,1)} %reshape_reshape.3, bf16[4096,256]{1,0:T(8,128)(2,1)S(1)} %bitcast.128, bf16[256,1024]{0,1:T(8,128)(2,1)S(1)} %bitcast.148), kind=kOutput, calls=%fused_computation.20 | convolution fusion | flops 4333764608 | bytes 11534336 | tf_op jit(solution)/shard_map/dot_general | solution.py:113
  109.0 3.6 %fusion.20 = bf16[4096,256]{1,0:T(8,128)(2,1)S(1)} fusion(f32[4096,256]{1,0:T(8,128)} %fusion.15, bf16[4096,256]{1,0:T(8,128)(2,1)} %bitcast.129, bf16[256,256]{0,1:T(8,128)(2,1)S(1)} %bitcast.144), kind=kOutput, calls=%fused_computation.22 | convolution fusion | flops 538968064 | bytes 8519680 | tf_op jit(solution)/shard_map/dot_general | solution.py:117
  112.6 1.0 multiply_reduce_fusion.2
  113.9 1.8 %convolution_add_fusion.2 = f32[64,4,64]{2,1,0:T(4,128)S(1)} fusion(bf16[64,64,256]{2,1,0:T(8,128)(2,1)S(1)} %bitcast.121, f32[64,4,256]{2,1,0:T(4,128)S(1)} %get-tuple-element.19, f32[64,4]{1,0:T(8,128)S(1)} %copy.121, f32[4,64]{1,0:T(4,128)S(1)} %get-tuple-element.12), kind=kOutput, calls=%fused_computation.40 | convolution fusion | flops 50413568 | bytes 2426880 | tf_op jit(solution)/shard_map/ukd,uld->ukl/dot_general | solution.py:39
  115.9 1.0 multiply_reduce_fusion.1
  117.1 3.5 %convolution_add_fusion.1 = f32[64,4,64]{2,1,0:T(4,128)S(1)} fusion(f32[64,4,64]{2,1,0:T(4,128)S(1)} %convolution_add_fusion.2, bf16[64,64,256]{2,1,0:T(8,128)(2,1)} %bitcast.123, f32[64,4,256]{2,1,0:T(4,128)S(1)} %get-tuple-element.23, f32[64,4]{1,0:T(8,128)S(1)} %copy.124), kind=kOutput, calls=%fused_computation.39 | convolution fusion | flops 50413568 | bytes 2491392 | tf_op jit(solution)/shard_map/ukd,uld->ukl/dot_general | solution.py:39
  120.8 2.6 %multiply_reduce_fusion = (f32[64,4]{1,0:T(8,128)S(1)}, f32[64,4,256]{2,1,0:T(4,128)S(1)}) fusion(bf16[64,64,256]{2,1,0:T(8,128)(2,1)} %bitcast.124, f32[64,4,64]{2,1,0:T(4,128)S(1)} %get-tuple-element.25, f32[64,64]{1,0:T(8,128)S(1)} %get-tuple-element.24, f32[64,64]{1,0:T(8,128)S(1)} %get-tuple-element.14), kind=kOutput, calls=%fused_computation.45 | convolution fusion | flops 50495232 | bytes 2458624 | tf_op jit(solution)/shard_map/ukl,uld->ukd/dot_general | solution.py:34
  124.6 5.7 %all_to_all.46 = f32[2,1,32768]{2,1,0:T(1,128)S(1)} all-to-all(f32[2,1,32768]{2,1,0:T(1,128)S(1)} %reshape.247), channel_id=1, replica_groups=mesh['au'=8,'pa'=8,'dev'=2] {'dev'}, dimensions={0} | all-to-all | bytes 524288 | tf_op jit(solution)/shard_map/all_to_all | solution.py:124
  130.2 0.5 broadcast.111
  130.8 1.4 %reduce.8 = f32[2,32768]{1,0:T(2,128)S(1)} reduce(f32[2,1,32768]{2,1,0:T(1,128)S(1)} %all_to_all.46, f32[]{:T(128)} %broadcast.111), dimensions={1}, to_apply=%all_to_all.39.reduce_sub_computation | reduce | bytes 524292 | tf_op jit(solution)/shard_map/all_to_all | solution.py:124
  132.6 0.9 copy.129
  (65 shorter events, 3.8 us)
Async XLA Ops:
  6.5 25.0 %copy-start = (bf16[4096,256]{1,0:T(8,128)(2,1)S(1)}, bf16[4096,256]{1,0:T(8,128)(2,1)}, u32[]{:S(2)}) copy-start(bf16[4096,256]{1,0:T(8,128)(2,1)} %param.12) | copy-start | bytes 6291460
  6.5 18.0 %copy-start.11 = (s32[4,64]{1,0:T(4,128)S(1)}, s32[4,64]{1,0:T(4,128)}, u32[]{:S(2)}) copy-start(s32[4,64]{1,0:T(4,128)} %param.14) | copy-start | bytes 3076
  6.5 42.0 %all-gather.3.cloned.1.call-start = ((), (), s32[]{:S(2)}) async-start(), calls=%async_computation.3 | async-start | bytes 2555904 | tf_op jit(solution)/shard_map/all_gather | solution.py:20
  11.7 1.0 copy-start.7
  14.3 11.2 %all-to-all-start.1 = ((s32[8,1,512]{2,1,0:T(1,128)}), s32[8,1,512]{2,1,0:T(1,128)S(1)}, u32[]{:S(2)}, u32[]{:S(2)}) async-start(s32[8,1,512]{2,1,0:T(1,128)} %reshape.245), calls=%async_computation.1 | async-start | bytes 32768 | tf_op jit(solution)/shard_map/all_to_all | solution.py:69
  25.6 36.9 %all-to-all-start = ((bf16[512,8,256]{2,1,0:T(8,128)(2,1)}), bf16[512,8,256]{2,1,0:T(8,128)(2,1)}, u32[]{:S(2)}, u32[]{:S(2)}) async-start(bf16[512,8,256]{2,1,0:T(8,128)(2,1)} %bitcast.131), calls=%async_computation | async-start | bytes 4194304 | tf_op jit(solution)/shard_map/all_to_all | solution.py:68
  50.4 1.2 copy-start.5
  53.1 9.3 %copy-start.4 = (bf16[4096,256]{1,0:T(8,128)(2,1)S(1)}, bf16[4096,256]{1,0:T(8,128)(2,1)}, u32[]{:S(2)}) copy-start(bf16[4096,256]{1,0:T(8,128)(2,1)} %gather_fusion) | copy-start | bytes 6291460
  62.5 3.3 %copy-start.9 = (bf16[1,256,2,128]{1,3,2,0:T(8,128)(2,1)S(1)}, bf16[1,256,2,128]{1,3,2,0:T(8,128)(2,1)}, u32[]{:S(2)}) copy-start(bf16[1,256,2,128]{1,3,2,0:T(8,128)(2,1)} %copy.110) | copy-start | bytes 393220
  65.8 33.8 %copy-start.3 = (bf16[64,8,8,256]{3,2,1,0:T(8,128)(2,1)}, bf16[64,8,8,256]{3,2,1,0:T(8,128)(2,1)S(1)}, u32[]{:S(2)}) copy-start(bf16[64,8,8,256]{3,2,1,0:T(8,128)(2,1)S(1)} %copy.109) | copy-start | bytes 6291460
  67.9 4.8 %copy-start.8 = (bf16[1,256,2,128]{1,3,2,0:T(8,128)(2,1)S(1)}, bf16[1,256,2,128]{1,3,2,0:T(8,128)(2,1)}, u32[]{:S(2)}) copy-start(bf16[1,256,2,128]{1,3,2,0:T(8,128)(2,1)} %copy.103) | copy-start | bytes 393220
  86.6 5.0 %copy-start.6 = (bf16[4,4096,64]{2,1,0:T(8,128)(2,1)S(1)}, bf16[4,4096,64]{2,1,0:T(8,128)(2,1)}, u32[]{:S(2)}) copy-start(bf16[4,4096,64]{2,1,0:T(8,128)(2,1)} %copy.134) | copy-start | bytes 6291460
  96.8 2.9 %copy-start.10 = (bf16[256,2,512]{0,2,1:T(8,128)(2,1)S(1)}, bf16[256,2,512]{0,2,1:T(8,128)(2,1)}, u32[]{:S(2)}) copy-start(bf16[256,2,512]{0,2,1:T(8,128)(2,1)} %copy.117) | copy-start | bytes 1572868
  112.6 3.2 %copy-start.2 = (bf16[4096,256]{1,0:T(8,128)(2,1)}, bf16[4096,256]{1,0:T(8,128)(2,1)S(1)}, u32[]{:S(2)}) copy-start(bf16[4096,256]{1,0:T(8,128)(2,1)S(1)} %fusion.20) | copy-start | bytes 6291460
  117.1 16.5 %copy-start.1 = (bf16[4096,256]{1,0:T(8,128)(2,1)S(1)}, bf16[4096,256]{1,0:T(8,128)(2,1)}, u32[]{:S(2)}) copy-start(bf16[4096,256]{1,0:T(8,128)(2,1)} %param.12) | copy-start | bytes 6291460
Sparse Core Ops, SparseCore 0:
  12.8 16.3 all-gather.2
where the time goes:
time: 141 us; the launch traced here: 140 us
  local copies, waits for them, and re-layouts  61.2 us (43%)
  matrix products  42.4 us (30%)
  between operations  13.8 us (10%)
  starting transfers between devices  10.5 us (7%)
  other arithmetic  5.86 us (4%)
  blocking collectives  5.69 us (4%)
    gather x1, local copies, waits for them, and re-layouts, body(): jnp.take(item_table, item_ids, axis=0).astype(jnp.float32)  16.9 us
    reshape x3, local copies, waits for them, and re-layouts, project(): return made.reshape(heads_here, user_count, span_here, head_size)  14.4 us
    unnamed x40, local copies, waits for them, and re-layouts  14.3 us
    dot_general x1, matrix products, body(): jnp.dot(hidden, w_down, preferred_element_type=jnp.float32)  9.38 us
    dot_general x3, matrix products, project(): jnp.einsum('nd,dhe->hne', flat_rows, shaped, preferred_element_type=jnp.f...  6.29 us
    all_to_all x1, starting transfers between devices, body(): lax.all_to_all(item_ids, 'pa', split_axis=0, concat_axis=1, tiled=True)  6.2 us
    all_to_all x1, blocking collectives, body(): lax.all_to_all(routed, 'dev', split_axis=2, concat_axis=0, tiled=True)  5.69 us
    dot_general x2, matrix products, local_routing(): jnp.einsum('ukd,uld->ukl', capsules, vectors, precision=lax.Precision.HIG...  5.34 us
  transfers between devices with their start and end apart: 3, of which 1 were waited for; matrix products, arithmetic and copies ran while one was open for 26% of the time, Pallas kernels for 0%

commit v1 on v0

v1 whole, which is shorter than its diff:
```python
import functools

import jax
import jax.numpy as jnp
from jax import lax
from jax.experimental import pallas as pl
from jax.experimental.pallas import tpu as pltpu
from jax.sharding import PartitionSpec as P

D = 256
HEADS = 4
CAPS = 4
ITERS = 3
CHUNKS = 2
BLOCK = 8
GROUP = 4
F32 = jnp.float32
BF16 = jnp.bfloat16


def lookup_kernel(core_ref, ids_ref, feat_ref, table_ref, out_ref, wide_ref, *, chunk, per_pair, per_core):
    users, spots, _ = feat_ref.shape
    step = pl.program_id(0)

    @pl.when(step == 0)
    def _():
        rows = 256

        def widen(i, carry):
            at = pl.ds(pl.multiple_of(i * rows, rows), rows)
            wide_ref[at, :] = table_ref[at, :].astype(F32)
            return carry

        lax.fori_loop(0, table_ref.shape[0] // rows, widen, 0)

    first = step * per_pair + core_ref[0] * per_core + chunk * users
    spot = lax.broadcasted_iota(jnp.int32, (spots, D), 0)

    def one(user, carry):
        rows = jnp.broadcast_to(wide_ref[pl.ds(ids_ref[0, first + user], 1), :], (spots, D))
        for p in range(1, spots):
            row = jnp.broadcast_to(wide_ref[pl.ds(ids_ref[p, first + user], 1), :], (spots, D))
            rows = jnp.where(spot == p, row, rows)
        out_ref[user] = (feat_ref[user].astype(F32) + rows).astype(BF16)
        return carry

    lax.fori_loop(0, users, one, 0, unroll=8)


def lookup(core, ids, features, table, chunk, pa_count, dev_count):
    all_users, spots, width = features.shape
    per_pair = all_users // pa_count
    per_core = per_pair // dev_count
    users = per_core // CHUNKS
    return pl.pallas_call(
        functools.partial(lookup_kernel, chunk=chunk, per_pair=per_pair, per_core=per_core),
        out_shape=jax.ShapeDtypeStruct((pa_count * users, spots, width), BF16),
        grid_spec=pltpu.PrefetchScalarGridSpec(
            num_scalar_prefetch=2,
            grid=(pa_count,),
            in_specs=[
                pl.BlockSpec(
                    (users, spots, width),
                    lambda d, c, i: (d * (per_pair // users) + c[0] * CHUNKS + chunk, 0, 0),
                ),
                pl.BlockSpec(table.shape, lambda d, c, i: (0, 0), pipeline_mode=pl.Buffered(1)),
            ],
            out_specs=pl.BlockSpec((users, spots, width), lambda d, c, i: (d, 0, 0)),
            scratch_shapes=[pltpu.VMEM(table.shape, F32)],
        ),
        compiler_params=pltpu.CompilerParams(vmem_limit_bytes=24 << 20),
        name="lookup",
    )(core, ids, features, table)


def weights_kernel(
    core_ref, qkv_a, qkv_b, out_a, out_b, bil_a, bil_b, up_a, up_b, down_a, down_b, qkv, up, tail
):
    half = D // 2
    for i in range(3):
        qkv[:, i * D : i * D + half] = qkv_a[i]
        qkv[:, i * D + half : (i + 1) * D] = qkv_b[i]
    ff = up_a.shape[1]
    up[:, :ff] = up_a[...]
    up[:, ff:] = up_b[...]

    @pl.when(core_ref[0] == 0)
    def _():
        tail[:D, :half] = bil_a[...]
        tail[:D, half:] = bil_b[...]

    @pl.when(core_ref[0] != 0)
    def _():
        tail[:D, :half] = bil_b[...]
        tail[:D, half:] = bil_a[...]

    tail[D : D + half, :] = out_a[...]
    tail[D + half : 2 * D, :] = out_b[...]
    tail[2 * D : 2 * D + ff, :] = down_a[...]
    tail[2 * D + ff :, :] = down_b[...]


def finish_weights(core, own, other):
    ff = own[3].shape[1]
    operands = [w for pair in zip(own, other) for w in pair]
    return pl.pallas_call(
        weights_kernel,
        out_shape=[
            jax.ShapeDtypeStruct((D, 3 * D), BF16),
            jax.ShapeDtypeStruct((D, 2 * ff), BF16),
            jax.ShapeDtypeStruct((2 * D + 2 * ff, D), BF16),
        ],
        in_specs=[pl.BlockSpec(memory_space=pltpu.SMEM)]
        + [pl.BlockSpec(memory_space=pltpu.VMEM)] * len(operands),
        out_specs=[pl.BlockSpec(memory_space=pltpu.VMEM)] * 3,
        compiler_params=pltpu.CompilerParams(vmem_limit_bytes=16 << 20),
        name="weights",
    )(core, *operands)


def split(x):
    high = x.astype(BF16)
    return jnp.concatenate([high, (x - high.astype(F32)).astype(BF16)], axis=0)


def joined(x):
    half = x.shape[0] // 2
    return x[:half] + x[half:]


def encode_kernel(core_ref, x_ref, lens_ref, seed_ref, qkv_ref, up_ref, tail_ref, own_ref, other_ref, interest_ref):
    step = pl.program_id(0)
    history = x_ref.shape[0] * x_ref.shape[2]
    rows = BLOCK * history
    head = D // HEADS
    lanes = HEADS * history
    x = x_ref[...].astype(F32)
    x = jnp.swapaxes(x, 0, 1).reshape(rows, D).astype(BF16)
    qkv = jnp.dot(x, qkv_ref[...], preferred_element_type=F32)
    queries = (qkv[:, :D] * (1.0 / head**0.5)).astype(BF16)
    keys = qkv[:, D : 2 * D].astype(BF16)
    values = qkv[:, 2 * D :].astype(BF16)

    lane_head = lax.broadcasted_iota(jnp.int32, (history, D), 1) // head
    own_head = [(lane_head == h).astype(F32).astype(BF16) for h in range(HEADS)]
    row_head = lax.broadcasted_iota(jnp.int32, (lanes, D), 0) // history
    col_head = lax.broadcasted_iota(jnp.int32, (lanes, D), 1) // head
    ones = (row_head == col_head).astype(F32).astype(BF16)
    position = lax.broadcasted_iota(jnp.int32, (BLOCK, lanes), 1) % history
    lens = lens_ref[pl.ds(pl.multiple_of(step * BLOCK, BLOCK), BLOCK), :]
    key_valid = (position < lens).astype(F32)
    attended = []
    for u in range(BLOCK):
        at = slice(u * history, (u + 1) * history)
        key_wide = jnp.concatenate([keys[at] * m for m in own_head], axis=0)
        value_wide = jnp.concatenate([values[at] * m for m in own_head], axis=0)
        scores = lax.dot_general(
            queries[at], key_wide, (((1,), (1,)), ((), ())), preferred_element_type=F32
        )
        probs = jnp.where(key_valid[u : u + 1] > 0.0, jnp.exp(scores), 0.0)
        rounded = probs.astype(BF16)
        rest = (probs - rounded.astype(F32)).astype(BF16)
        totals = jnp.dot(rounded, ones, preferred_element_type=F32) + jnp.dot(
            rest, ones, preferred_element_type=F32
        )
        weighted = jnp.dot(rounded, value_wide, preferred_element_type=F32)
        attended.append((weighted / totals).astype(BF16))
    attended = jnp.concatenate(attended, axis=0)
    hidden = jax.nn.gelu(jnp.dot(x, up_ref[...], preferred_element_type=F32)).astype(BF16)
    everything = jnp.concatenate([x, attended, hidden], axis=1)
    interest = jnp.dot(everything, tail_ref[...], preferred_element_type=F32).astype(BF16)
    interest_ref[step] = interest

    @pl.when(step == pl.num_programs(0) - 1)
    def _():
        route(core_ref, lens_ref, seed_ref, own_ref, other_ref, interest_ref, history)


def route(core_ref, lens_ref, seed_ref, own_ref, other_ref, interest_ref, history):
    blocks = interest_ref.shape[0]
    lanes = GROUP * history
    groups = BLOCK // GROUP
    lane = lax.broadcasted_iota(jnp.int32, (BLOCK, lanes), 1)
    user = lax.broadcasted_iota(jnp.int32, (BLOCK, lanes), 0)
    mine = (lane // history) == (user % GROUP)
    base = (seed_ref[...].astype(F32) - 7.5) * 0.25
    base = jnp.concatenate([base] * GROUP, axis=1)
    base = jnp.broadcast_to(base[:, None, :], (CAPS, BLOCK, lanes))
    logits = [base] * blocks
    valid = []
    for b in range(blocks):
        real = mine & ((lane % history) < lens_ref[b * BLOCK : (b + 1) * BLOCK, :])
        valid.append([(real & ((user // GROUP) == g)).astype(F32) for g in range(groups)])
    capsules = [None] * blocks
    for sweep in range(ITERS):
        for b in range(blocks):
            top = jnp.max(logits[b], axis=0, keepdims=True)
            weights = jnp.exp(logits[b] - top)
            weights = weights / jnp.sum(weights, axis=0, keepdims=True)
            summed = 0.0
            for g in range(groups):
                part = (weights * valid[b][g][None]).reshape(CAPS * BLOCK, lanes)
                vectors = interest_ref[b, g * lanes : (g + 1) * lanes, :]
                summed = summed + jnp.dot(split(part), vectors, preferred_element_type=F32)
            summed = joined(summed)
            squares = jnp.sum(summed * summed, axis=1, keepdims=True)
            capsules[b] = summed * (jnp.sqrt(squares) / (1.0 + squares))
            if sweep + 1 < ITERS:
                caps = split(capsules[b])
                near = []
                for g in range(groups):
                    vectors = interest_ref[b, g * lanes : (g + 1) * lanes, :]
                    near.append(
                        joined(
                            lax.dot_general(
                                caps, vectors, (((1,), (1,)), ((), ())), preferred_element_type=F32
                            )
                        ).reshape(CAPS, BLOCK, lanes)
                    )
                added = near[-1]
                for g in range(groups - 1):
                    added = jnp.where(((user // GROUP) == g)[None], near[g], added)
                logits[b] = logits[b] + added
    half = D // 2
    low_own = core_ref[0] == 0
    for b in range(blocks):
        made = capsules[b].reshape(CAPS, BLOCK, D)
        low, high = made[:, :, :half], made[:, :, half:]
        own_ref[:, b * BLOCK : (b + 1) * BLOCK, :] = jnp.where(low_own, low, high)
        other_ref[:, b * BLOCK : (b + 1) * BLOCK, :] = jnp.where(low_own, high, low)


def encode(core, gathered, lens, seed, qkv, up, tail):
    pa_count, users, spots, _ = gathered.shape
    history = pa_count * spots
    half = D // 2
    fixed = lambda a: pl.BlockSpec(a.shape, lambda s, c: (0,) * a.ndim, pipeline_mode=pl.Buffered(1))
    made = jax.ShapeDtypeStruct((CAPS, users, half), F32)
    return pl.pallas_call(
        encode_kernel,
        out_shape=[made, made],
        grid_spec=pltpu.PrefetchScalarGridSpec(
            num_scalar_prefetch=1,
            grid=(users // BLOCK,),
            in_specs=[
                pl.BlockSpec((pa_count, BLOCK, spots, D), lambda s, c: (0, s, 0, 0)),
                fixed(lens),
                fixed(seed),
                fixed(qkv),
                fixed(up),
                fixed(tail),
            ],
            out_specs=[pl.BlockSpec(made.shape, lambda s, c: (0, 0, 0))] * 2,
            scratch_shapes=[pltpu.VMEM((users // BLOCK, BLOCK * history, D), BF16)],
        ),
        compiler_params=pltpu.CompilerParams(vmem_limit_bytes=40 << 20),
        name="encode",
    )(core, gathered, lens, seed, qkv, up, tail)


def body(
    features, item_ids, item_table, lengths, routing_seed, w_qkv, w_out, w_bilinear, w_up, w_down
):
    pa_count = lax.axis_size("pa")
    dev_count = lax.axis_size("dev")
    spots = features.shape[1]
    per_core = lengths.shape[0] // (pa_count * dev_count)
    users = per_core // CHUNKS
    core_index = lax.axis_index("dev").astype(jnp.int32)
    core = core_index.reshape(1)
    swap = [(i, dev_count - 1 - i) for i in range(dev_count)]
    own = (w_qkv, w_out, w_bilinear, w_up, w_down)
    other = tuple(lax.ppermute(w, "dev", swap) for w in own)
    qkv, up, tail = finish_weights(core, own, other)
    first = (lax.axis_index("pa") * dev_count + core_index) * per_core
    lens = lax.dynamic_slice_in_dim(lengths, first, per_core).reshape(per_core, 1)
    ids = item_ids.T
    halves = []
    for chunk in range(CHUNKS):
        sent = lookup(core, ids, features, item_table, chunk, pa_count, dev_count)
        got = lax.all_to_all(sent, "pa", split_axis=0, concat_axis=0, tiled=True)
        got = got.reshape(pa_count, users, spots, D)
        kept, passed = encode(
            core, got, lens[chunk * users : (chunk + 1) * users], routing_seed, qkv, up, tail
        )
        halves.append((kept, lax.ppermute(passed, "dev", swap)))
    kept = jnp.concatenate([h[0] for h in halves], axis=1)
    came = jnp.concatenate([h[1] for h in halves], axis=1)
    made = jnp.where(
        core_index == 0,
        jnp.concatenate([kept, came], axis=1),
        jnp.concatenate([came, kept], axis=1),
    )
    return jnp.swapaxes(made, 0, 1)


def solution(mesh):
    in_specs = (
        P("au", "pa", None),
        P("au", "pa"),
        P(),
        P("au"),
        P(),
        P(None, None, "dev"),
        P("dev", None),
        P(None, "dev"),
        P(None, "dev"),
        P("dev", None),
    )
    out_specs = P(("au", "pa"), None, "dev")
    return jax.shard_map(body, mesh=mesh, in_specs=in_specs, out_specs=out_specs, check_vma=False)
```

time: 141 us -> 88.9 us (0.63)
  Pallas kernels: 0 us -> 43.2 us
  matrix products: 42.4 us -> 0 us
  local copies, waits for them, and re-layouts: 61.2 us -> 25 us
  between operations: 13.8 us -> 0.16 us
  other arithmetic: 5.86 us -> 0.02 us
  blocking collectives: 5.69 us -> 0 us
  waiting for transfers between devices: 0.95 us -> 6.51 us
  starting transfers between devices: 10.5 us -> 13.1 us
    pallas_call x0 -> x5, Pallas kernels: none -> 43.2 us  [the longest x2 30.2 us: encode(): pl.pallas_call(encode_kernel, out_shape=[made, made], grid_spec=pltpu.Pre...]
    dot_general x13 -> x0, matrix products: 42.4 us -> none  [the longest x1 9.38 us: body(): jnp.dot(hidden, w_down, preferred_element_type=jnp.float32)]
    gather x1 -> x0, local copies, waits for them, and re-layouts: 16.9 us -> none  [body(): jnp.take(item_table, item_ids, axis=0).astype(jnp.float32)]
    reshape x6 -> x0, local copies, waits for them, and re-layouts: 16.1 us -> none  [the longest x3 14.4 us: project(): return made.reshape(heads_here, user_count, span_here, head_size)]
    unnamed x40 -> x56, local copies, waits for them, and re-layouts: 14.3 us -> 22.5 us
    all_to_all x1 -> x0, blocking collectives: 5.69 us -> none  [body(): lax.all_to_all(routed, 'dev', split_axis=2, concat_axis=0, tiled=True)]
    all_to_all x2, waiting for transfers between devices: 0.94 us -> 5.59 us  [body(): got = lax.all_to_all(sent, 'pa', split_axis=0, concat_axis=0, tiled=True)]
    ppermute x0 -> x7, starting transfers between devices: none -> 3.39 us  [the longest x5 2.72 us: body(): other = tuple((lax.ppermute(w, 'dev', swap) for w in own))]
  transfers between devices with their start and end apart: 3 -> 9, of which waited for: 1 -> 2; matrix products, arithmetic and copies ran while one was open for 26% -> 2% of each run, Pallas kernels for 0% -> 42%
where the time goes in v1:
time: 88.9 us; the launch traced here: 88 us
  Pallas kernels  43.2 us (49%)
  local copies, waits for them, and re-layouts  25 us (28%)
  starting transfers between devices  13.1 us (15%)
  waiting for transfers between devices  6.51 us (7%)
    pallas_call x2, Pallas kernels, encode(): pl.pallas_call(encode_kernel, out_shape=[made, made], grid_spec=pltpu.Pre...  30.2 us
    unnamed x56, local copies, waits for them, and re-layouts  22.5 us
    pallas_call x2, Pallas kernels, lookup(): pl.pallas_call(functools.partial(lookup_kernel, chunk=chunk, per_pair=per...  12.8 us
    all_to_all x2, starting transfers between devices, body(): got = lax.all_to_all(sent, 'pa', split_axis=0, concat_axis=0, tiled=True)  9.76 us
    all_to_all x2, waiting for transfers between devices, body(): got = lax.all_to_all(sent, 'pa', split_axis=0, concat_axis=0, tiled=True)  5.59 us
    ppermute x5, starting transfers between devices, body(): other = tuple((lax.ppermute(w, 'dev', swap) for w in own))  2.72 us
  transfers between devices with their start and end apart: 9, of which 2 were waited for; matrix products, arithmetic and copies ran while one was open for 2% of the time, Pallas kernels for 42%

profile of v1, /device:TPU:1, one launch (start us, length us, event | category | flops | bytes accessed | tf_op | source)
XLA Modules:
  0.0 88.0 jit_solution(15792815722215357868)
XLA Ops:
  0.0 2.2 %copy-done = bf16[1024,8,256]{2,1,0:T(8,128)(2,1)S(1)} copy-done((bf16[1024,8,256]{2,1,0:T(8,128)(2,1)S(1)}, bf16[1024,8,256]{2,1,0:T(8,128)(2,1)}, u32[]{:S(2)}) %copy-start) | copy-done | bytes 4194328
  2.2 1.6 %copy-done.2 = bf16[4096,256]{1,0:T(8,128)(2,1)S(1)} copy-done((bf16[4096,256]{1,0:T(8,128)(2,1)S(1)}, bf16[4096,256]{1,0:T(8,128)(2,1)}, u32[]{:S(2)}) %copy-start.2) | copy-done | bytes 2097176
  3.8 0.8 copy-done.16
  4.5 6.4 %lookup.3 = bf16[256,8,256]{2,1,0:T(8,128)(2,1)S(1)} custom-call(s32[1]{0:T(128)} %bitcast.core_ref, s32[8,1024]{1,0:T(8,128)S(1)} %bitcast.12, bf16[1024,8,256]{2,1,0:T(8,128)(2,1)S(1)} %copy-done, bf16[4096,256]{1,0:T(8,128)(2,1)S(1)} %copy-done.2), custom_call_target="tpu_custom_call" | custom-call | tf_op jit(solution)/shard_map/lookup/pallas_call | solution.py:55
  10.9 1.0 %copy-done.5 = bf16[256,8,256]{2,1,0:T(8,128)(2,1)} copy-done((bf16[256,8,256]{2,1,0:T(8,128)(2,1)}, bf16[256,8,256]{2,1,0:T(8,128)(2,1)S(1)}, u32[]{:S(2)}) %copy-start.5) | copy-done | bytes 1048600
  11.9 6.2 %all-to-all-start.1 = ((bf16[256,8,256]{2,1,0:T(8,128)(2,1)}), bf16[256,8,256]{2,1,0:T(8,128)(2,1)S(1)}, u32[]{:S(2)}, u32[]{:S(2)}) async-start(bf16[256,8,256]{2,1,0:T(8,128)(2,1)} %copy-done.5), calls=%async_computation.1 | async-start | bytes 2097152 | tf_op jit(solution)/shard_map/all_to_all | solution.py:281
  18.1 0.0 copy-start.1
  18.1 2.2 %copy-done.1 = bf16[1024,8,256]{2,1,0:T(8,128)(2,1)S(1)} copy-done((bf16[1024,8,256]{2,1,0:T(8,128)(2,1)S(1)}, bf16[1024,8,256]{2,1,0:T(8,128)(2,1)}, u32[]{:S(2)}) %copy-start.1) | copy-done | bytes 4194328
  20.3 6.4 %lookup.2 = bf16[256,8,256]{2,1,0:T(8,128)(2,1)S(1)} custom-call(s32[1]{0:T(128)} %bitcast.core_ref, s32[8,1024]{1,0:T(8,128)S(1)} %bitcast.13, bf16[1024,8,256]{2,1,0:T(8,128)(2,1)S(1)} %copy-done.1, bf16[4096,256]{1,0:T(8,128)(2,1)S(1)} %copy-done.3), custom_call_target="tpu_custom_call" | custom-call | tf_op jit(solution)/shard_map/lookup/pallas_call | solution.py:55
  26.7 1.0 %copy-done.4 = bf16[256,8,256]{2,1,0:T(8,128)(2,1)} copy-done((bf16[256,8,256]{2,1,0:T(8,128)(2,1)}, bf16[256,8,256]{2,1,0:T(8,128)(2,1)S(1)}, u32[]{:S(2)}) %copy-start.4) | copy-done | bytes 1048600
  27.7 5.6 %all-to-all-done.1 = bf16[256,8,256]{2,1,0:T(8,128)(2,1)S(1)} async-done(((bf16[256,8,256]{2,1,0:T(8,128)(2,1)}), bf16[256,8,256]{2,1,0:T(8,128)(2,1)S(1)}, u32[]{:S(2)}, u32[]{:S(2)}) %all-to-all-start.1) | async-done | bytes 1048608 | tf_op jit(solution)/shard_map/all_to_all | solution.py:281
  33.3 3.6 %all-to-all-start = ((bf16[256,8,256]{2,1,0:T(8,128)(2,1)}), bf16[256,8,256]{2,1,0:T(8,128)(2,1)S(1)}, u32[]{:S(2)}, u32[]{:S(2)}) async-start(bf16[256,8,256]{2,1,0:T(8,128)(2,1)} %copy-done.4), calls=%async_computation | async-start | bytes 2097152 | tf_op jit(solution)/shard_map/all_to_all | solution.py:281
  36.9 1.7 %collective-permute-start.3 = (bf16[256,512]{1,0:T(8,128)(2,1)S(1)}, bf16[256,512]{1,0:T(8,128)(2,1)S(1)}, u32[]{:S(2)}, u32[]{:S(2)}) collective-permute-start(bf16[256,512]{1,0:T(8,128)(2,1)S(1)} %copy-done.8), channel_id=1, source_target_pairs={{0,1},{1,0},{2,3},{3,2},{4,5},{5,4},{6,7},{7,6},{8,9},{9,8},{10,11... | collective-permute-start | bytes 786440 | tf_op jit(solution)/shard_map/ppermute | solution.py:273
  38.6 0.1 collective-permute-start.4
  38.7 0.4 collective-permute-start
  39.1 0.1 collective-permute-start.1
  39.2 0.4 collective-permute-start.2
  39.6 0.8 dynamic_slice.3
  40.4 0.1 slice_bitcast_fusion.1
  40.4 0.7 copy.12.lens_ref
  41.1 0.1 copy.11.lens_ref
  41.2 0.0 collective-permute-done.1.out_b
  41.2 0.6 copy-done.22
  41.9 0.0 collective-permute-done.2.bil_b
  41.9 0.6 copy-done.24
  42.5 0.0 collective-permute-done.qkv_b
  42.5 0.7 copy-done.14
  43.2 0.7 copy-done.11
  43.9 0.9 %copy-done.9 = bf16[256,512]{1,0:T(8,128)(2,1)S(1)} copy-done((bf16[256,512]{1,0:T(8,128)(2,1)S(1)}, bf16[256,512]{1,0:T(8,128)(2,1)}, u32[]{:S(2)}) %copy-start.9) | copy-done | bytes 262168
  44.8 0.9 %copy-done.10 = bf16[512,256]{1,0:T(8,128)(2,1)S(1)} copy-done((bf16[512,256]{1,0:T(8,128)(2,1)S(1)}, bf16[512,256]{1,0:T(8,128)(2,1)}, u32[]{:S(2)}) %copy-start.10) | copy-done | bytes 262168
  45.8 0.9 %copy-done.12 = bf16[512,256]{1,0:T(8,128)(2,1)S(1)} copy-done((bf16[512,256]{1,0:T(8,128)(2,1)S(1)}, bf16[512,256]{1,0:T(8,128)(2,1)}, u32[]{:S(2)}) %copy-start.12) | copy-done | bytes 262168
  46.7 0.9 %copy-done.13 = bf16[3,256,128]{2,1,0:T(8,128)(2,1)S(1)} copy-done((bf16[3,256,128]{2,1,0:T(8,128)(2,1)S(1)}, bf16[3,256,128]{2,1,0:T(8,128)(2,1)}, u32[]{:S(2)}) %copy-start.13) | copy-done | bytes 196632
  47.7 0.9 %copy-done.15 = bf16[3,256,128]{2,1,0:T(8,128)(2,1)S(1)} copy-done((bf16[3,256,128]{2,1,0:T(8,128)(2,1)S(1)}, bf16[3,256,128]{2,1,0:T(8,128)(2,1)}, u32[]{:S(2)}) %copy-start.15) | copy-done | bytes 196632
  48.6 0.8 copy-done.20
  49.4 0.8 copy-done.21
  50.3 0.8 copy-done.23
  51.1 0.8 copy-done.25
  51.9 0.2 weights.1
  52.1 0.7 copy-done.18
  52.9 0.7 copy-done.26
  53.6 15.1 %encode.3 = (f32[4,32,128]{2,1,0:T(8,128)S(1)}, f32[4,32,128]{2,1,0:T(8,128)S(1)}) custom-call(s32[1]{0:T(128)} %bitcast.core_ref, bf16[8,32,8,256]{3,2,1,0:T(8,128)(2,1)S(1)} %bitcast.11, s32[32,1]{1,0:T(8,128)S(1)} %copy-done.18, s32[4,64]{1,0:T(4,128)S(1)} %copy-done.26, bf16[256,768]{1,0:T(8,128)(2,1)S(1)} %get-tuple-element.12.qkv_ref, ...), custom_call_target="tpu_custom_call" | custom-call | tf_op jit(solution)/shard_map/encode/pallas_call | solution.py:239
  68.7 0.2 collective-permute-start.6
  68.9 1.0 %copy-done.7 = bf16[256,1024]{1,0:T(8,128)(2,1)S(1)} copy-done((bf16[256,1024]{1,0:T(8,128)(2,1)S(1)}, bf16[256,1024]{1,0:T(8,128)(2,1)}, u32[]{:S(2)}) %copy-start.7) | copy-done | bytes 524312
  69.9 0.7 copy-done.27
  70.6 15.1 %encode.2 = (f32[4,32,128]{2,1,0:T(8,128)S(1)}, f32[4,32,128]{2,1,0:T(8,128)S(1)}) custom-call(s32[1]{0:T(128)} %bitcast.core_ref, bf16[8,32,8,256]{3,2,1,0:T(8,128)(2,1)S(1)} %bitcast.10, s32[32,1]{1,0:T(8,128)S(1)} %copy.11.lens_ref, s32[4,64]{1,0:T(4,128)S(1)} %copy-done.27, bf16[256,768]{1,0:T(8,128)(2,1)S(1)} %get-tuple-element.12.qkv_ref, ...), custom_call_target="tpu_custom_call" | custom-call | tf_op jit(solution)/shard_map/encode/pallas_call | solution.py:239
  85.7 0.5 collective-permute-start.5
  86.2 0.9 %collective-permute-done.5 = f32[4,32,128]{2,1,0:T(8,128)S(1)} collective-permute-done((f32[4,32,128]{2,1,0:T(8,128)S(1)}, f32[4,32,128]{2,1,0:T(8,128)S(1)}, u32[]{:S(2)}, u32[]{:S(2)}) %collective-permute-start.5) | collective-permute-done | bytes 65568 | tf_op jit(solution)/shard_map/ppermute | solution.py:286
  87.1 0.9 copy.13
  (37 shorter events, 0.1 us)
Async XLA Ops:
  0.0 2.2 %copy-start = (bf16[1024,8,256]{2,1,0:T(8,128)(2,1)S(1)}, bf16[1024,8,256]{2,1,0:T(8,128)(2,1)}, u32[]{:S(2)}) copy-start(bf16[1024,8,256]{2,1,0:T(8,128)(2,1)} %feat_ref.3) | copy-start | bytes 12582916
  2.2 1.6 %copy-start.2 = (bf16[4096,256]{1,0:T(8,128)(2,1)S(1)}, bf16[4096,256]{1,0:T(8,128)(2,1)}, u32[]{:S(2)}) copy-start(bf16[4096,256]{1,0:T(8,128)(2,1)} %table_ref.3) | copy-start | bytes 6291460
  3.8 0.8 copy-start.16
  4.5 13.6 %copy-start.3 = (bf16[4096,256]{1,0:T(8,128)(2,1)S(1)}, bf16[4096,256]{1,0:T(8,128)(2,1)}, u32[]{:S(2)}) copy-start(bf16[4096,256]{1,0:T(8,128)(2,1)} %table_ref.3) | copy-start | bytes 6291460
  4.5 13.6 %copy-start.17 = (s32[1024,8]{0,1:T(8,128)S(1)}, s32[1024,8]{0,1:T(8,128)}, u32[]{:S(2)}) copy-start(s32[1024,8]{0,1:T(8,128)} %param.11) | copy-start | bytes 98308
  10.9 1.0 %copy-start.5 = (bf16[256,8,256]{2,1,0:T(8,128)(2,1)}, bf16[256,8,256]{2,1,0:T(8,128)(2,1)S(1)}, u32[]{:S(2)}) copy-start(bf16[256,8,256]{2,1,0:T(8,128)(2,1)S(1)} %lookup.3) | copy-start | bytes 3145732
  11.9 21.4 %all-to-all-start.1 = ((bf16[256,8,256]{2,1,0:T(8,128)(2,1)}), bf16[256,8,256]{2,1,0:T(8,128)(2,1)S(1)}, u32[]{:S(2)}, u32[]{:S(2)}) async-start(bf16[256,8,256]{2,1,0:T(8,128)(2,1)} %copy-done.5), calls=%async_computation.1 | async-start | bytes 2097152 | tf_op jit(solution)/shard_map/all_to_all | solution.py:281
  18.1 2.2 %copy-start.1 = (bf16[1024,8,256]{2,1,0:T(8,128)(2,1)S(1)}, bf16[1024,8,256]{2,1,0:T(8,128)(2,1)}, u32[]{:S(2)}) copy-start(bf16[1024,8,256]{2,1,0:T(8,128)(2,1)} %feat_ref.3) | copy-start | bytes 12582916
  20.3 16.5 %copy-start.8 = (bf16[256,512]{1,0:T(8,128)(2,1)S(1)}, bf16[256,512]{1,0:T(8,128)(2,1)}, u32[]{:S(2)}) copy-start(bf16[256,512]{1,0:T(8,128)(2,1)} %up_a.1) | copy-start | bytes 786436
  20.3 18.8 %copy-start.19 = (bf16[128,256]{1,0:T(8,128)(2,1)S(1)}, bf16[128,256]{1,0:T(8,128)(2,1)}, u32[]{:S(2)}) copy-start(bf16[128,256]{1,0:T(8,128)(2,1)} %out_a.1) | copy-start | bytes 196612
  26.7 1.0 %copy-start.4 = (bf16[256,8,256]{2,1,0:T(8,128)(2,1)}, bf16[256,8,256]{2,1,0:T(8,128)(2,1)S(1)}, u32[]{:S(2)}) copy-start(bf16[256,8,256]{2,1,0:T(8,128)(2,1)S(1)} %lookup.2) | copy-start | bytes 3145732
  33.3 35.6 %all-to-all-start = ((bf16[256,8,256]{2,1,0:T(8,128)(2,1)}), bf16[256,8,256]{2,1,0:T(8,128)(2,1)S(1)}, u32[]{:S(2)}, u32[]{:S(2)}) async-start(bf16[256,8,256]{2,1,0:T(8,128)(2,1)} %copy-done.4), calls=%async_computation | async-start | bytes 2097152 | tf_op jit(solution)/shard_map/all_to_all | solution.py:281
  36.9 6.3 %collective-permute-start.3 = (bf16[256,512]{1,0:T(8,128)(2,1)S(1)}, bf16[256,512]{1,0:T(8,128)(2,1)S(1)}, u32[]{:S(2)}, u32[]{:S(2)}) collective-permute-start(bf16[256,512]{1,0:T(8,128)(2,1)S(1)} %copy-done.8), channel_id=1, source_target_pairs={{0,1},{1,0},{2,3},{3,2},{4,5},{5,4},{6,7},{7,6},{8,9},{9,8},{10,11... | collective-permute-start | bytes 786440 | tf_op jit(solution)/shard_map/ppermute | solution.py:273
  38.6 4.6 %collective-permute-start.4 = (bf16[512,256]{1,0:T(8,128)(2,1)}, bf16[512,256]{1,0:T(8,128)(2,1)S(1)}, u32[]{:S(2)}, u32[]{:S(2)}) collective-permute-start(bf16[512,256]{1,0:T(8,128)(2,1)} %down_a.1), channel_id=1, source_target_pairs={{0,1},{1,0},{2,3},{3,2},{4,5},{5,4},{6,7},{7,6},{8,9},{9,8},{10,11... | collective-permute-start | bytes 786440 | tf_op jit(solution)/shard_map/ppermute | solution.py:273
  38.7 3.8 %collective-permute-start = (bf16[3,256,128]{2,1,0:T(8,128)(2,1)}, bf16[3,256,128]{2,1,0:T(8,128)(2,1)S(1)}, u32[]{:S(2)}, u32[]{:S(2)}) collective-permute-start(bf16[3,256,128]{2,1,0:T(8,128)(2,1)} %qkv_a.1), channel_id=1, source_target_pairs={{0,1},{1,0},{2,3},{3,2},{4,5},{5,4},{6,7},{7,6},{8,9},{9,8},{10,11... | collective-permute-start | bytes 589832 | tf_op jit(solution)/shard_map/ppermute | solution.py:273
  39.1 2.1 %collective-permute-start.1 = (bf16[128,256]{1,0:T(8,128)(2,1)S(1)}, bf16[128,256]{1,0:T(8,128)(2,1)S(1)}, u32[]{:S(2)}, u32[]{:S(2)}) collective-permute-start(bf16[128,256]{1,0:T(8,128)(2,1)S(1)} %copy-done.19), channel_id=1, source_target_pairs={{0,1},{1,0},{2,3},{3,2},{4,5},{5,4},{6,7},{7,6},{8,9},{9,8},{10,11... | collective-permute-start | bytes 196616 | tf_op jit(solution)/shard_map/ppermute | solution.py:273
  39.2 2.7 %collective-permute-start.2 = (bf16[256,128]{1,0:T(8,128)(2,1)}, bf16[256,128]{1,0:T(8,128)(2,1)S(1)}, u32[]{:S(2)}, u32[]{:S(2)}) collective-permute-start(bf16[256,128]{1,0:T(8,128)(2,1)} %bil_a.1), channel_id=1, source_target_pairs={{0,1},{1,0},{2,3},{3,2},{4,5},{5,4},{6,7},{7,6},{8,9},{9,8},{10,11... | collective-permute-start | bytes 196616 | tf_op jit(solution)/shard_map/ppermute | solution.py:273
  41.2 0.6 copy-start.22
  41.9 0.6 copy-start.24
  42.5 0.7 copy-start.14
  43.2 0.7 copy-start.11
  43.9 0.9 %copy-start.9 = (bf16[256,512]{1,0:T(8,128)(2,1)S(1)}, bf16[256,512]{1,0:T(8,128)(2,1)}, u32[]{:S(2)}) copy-start(bf16[256,512]{1,0:T(8,128)(2,1)} %up_a.1) | copy-start | bytes 786436
  44.8 0.9 %copy-start.10 = (bf16[512,256]{1,0:T(8,128)(2,1)S(1)}, bf16[512,256]{1,0:T(8,128)(2,1)}, u32[]{:S(2)}) copy-start(bf16[512,256]{1,0:T(8,128)(2,1)} %down_a.1) | copy-start | bytes 786436
  45.8 0.9 %copy-start.12 = (bf16[512,256]{1,0:T(8,128)(2,1)S(1)}, bf16[512,256]{1,0:T(8,128)(2,1)}, u32[]{:S(2)}) copy-start(bf16[512,256]{1,0:T(8,128)(2,1)} %copy-done.11) | copy-start | bytes 786436
  46.7 0.9 %copy-start.13 = (bf16[3,256,128]{2,1,0:T(8,128)(2,1)S(1)}, bf16[3,256,128]{2,1,0:T(8,128)(2,1)}, u32[]{:S(2)}) copy-start(bf16[3,256,128]{2,1,0:T(8,128)(2,1)} %qkv_a.1) | copy-start | bytes 589828
  47.7 0.9 %copy-start.15 = (bf16[3,256,128]{2,1,0:T(8,128)(2,1)S(1)}, bf16[3,256,128]{2,1,0:T(8,128)(2,1)}, u32[]{:S(2)}) copy-start(bf16[3,256,128]{2,1,0:T(8,128)(2,1)} %copy-done.14) | copy-start | bytes 589828
  48.6 0.8 copy-start.20
  49.4 0.8 copy-start.21
  50.3 0.8 copy-start.23
  51.1 0.8 copy-start.25
  52.1 16.6 %copy-start.6 = (bf16[256,1024]{1,0:T(8,128)(2,1)}, bf16[256,1024]{1,0:T(8,128)(2,1)S(1)}, u32[]{:S(2)}) copy-start(bf16[256,1024]{1,0:T(8,128)(2,1)S(1)} %get-tuple-element.13.up_ref) | copy-start | bytes 1572868
  52.1 0.7 copy-start.18
  52.9 0.7 copy-start.26
  68.7 17.5 %collective-permute-start.6 = (f32[4,32,128]{2,1,0:T(8,128)S(1)}, f32[4,32,128]{2,1,0:T(8,128)S(1)}, u32[]{:S(2)}, u32[]{:S(2)}) collective-permute-start(f32[4,32,128]{2,1,0:T(8,128)S(1)} %get-tuple-element.18), channel_id=1, source_target_pairs={{0,1},{1,0},{2,3},{3,2},{4,5},{5,4},{6,7},{7,6},{8,9},{9,8},{10,11... | collective-permute-start | bytes 196616 | tf_op jit(solution)/shard_map/ppermute | solution.py:286
  68.9 1.0 %copy-start.7 = (bf16[256,1024]{1,0:T(8,128)(2,1)S(1)}, bf16[256,1024]{1,0:T(8,128)(2,1)}, u32[]{:S(2)}) copy-start(bf16[256,1024]{1,0:T(8,128)(2,1)} %copy-done.6) | copy-start | bytes 1572868
  69.9 0.7 copy-start.27
  85.7 1.4 %collective-permute-start.5 = (f32[4,32,128]{2,1,0:T(8,128)S(1)}, f32[4,32,128]{2,1,0:T(8,128)S(1)}, u32[]{:S(2)}, u32[]{:S(2)}) collective-permute-start(f32[4,32,128]{2,1,0:T(8,128)S(1)} %get-tuple-element.17), channel_id=1, source_target_pairs={{0,1},{1,0},{2,3},{3,2},{4,5},{5,4},{6,7},{7,6},{8,9},{9,8},{10,11... | collective-permute-start | bytes 196616 | tf_op jit(solution)/shard_map/ppermute | solution.py:286

commit v2 on v1

--- a/solution.py
+++ b/solution.py
@@ -18,6 +18,10 @@
 BF16 = jnp.bfloat16
 
 
+def in_hbm(*arrays):
+    return tuple(pltpu.with_memory_space_constraint(a, pltpu.HBM) for a in arrays)
+
+
 def lookup_kernel(core_ref, ids_ref, feat_ref, table_ref, out_ref, wide_ref, *, chunk, per_pair, per_core):
     users, spots, _ = feat_ref.shape
     step = pl.program_id(0)
@@ -54,7 +58,7 @@
     users = per_core // CHUNKS
     return pl.pallas_call(
         functools.partial(lookup_kernel, chunk=chunk, per_pair=per_pair, per_core=per_core),
-        out_shape=jax.ShapeDtypeStruct((pa_count * users, spots, width), BF16),
+        out_shape=pltpu.HBM((pa_count * users, spots, width), BF16),
         grid_spec=pltpu.PrefetchScalarGridSpec(
             num_scalar_prefetch=2,
             grid=(pa_count,),
@@ -70,7 +74,7 @@
         ),
         compiler_params=pltpu.CompilerParams(vmem_limit_bytes=24 << 20),
         name="lookup",
-    )(core, ids, features, table)
+    )(core, ids, *in_hbm(features, table))
 
 
 def weights_kernel(
@@ -106,16 +110,16 @@
     return pl.pallas_call(
         weights_kernel,
         out_shape=[
-            jax.ShapeDtypeStruct((D, 3 * D), BF16),
-            jax.ShapeDtypeStruct((D, 2 * ff), BF16),
-            jax.ShapeDtypeStruct((2 * D + 2 * ff, D), BF16),
+            pltpu.HBM((D, 3 * D), BF16),
+            pltpu.HBM((D, 2 * ff), BF16),
+            pltpu.HBM((2 * D + 2 * ff, D), BF16),
         ],
         in_specs=[pl.BlockSpec(memory_space=pltpu.SMEM)]
         + [pl.BlockSpec(memory_space=pltpu.VMEM)] * len(operands),
         out_specs=[pl.BlockSpec(memory_space=pltpu.VMEM)] * 3,
         compiler_params=pltpu.CompilerParams(vmem_limit_bytes=16 << 20),
         name="weights",
-    )(core, *operands)
+    )(core, *in_hbm(*operands))
 
 
 def split(x):
@@ -255,7 +259,7 @@
         ),
         compiler_params=pltpu.CompilerParams(vmem_limit_bytes=40 << 20),
         name="encode",
-    )(core, gathered, lens, seed, qkv, up, tail)
+    )(core, *in_hbm(gathered, lens, seed, qkv, up, tail))
 
 
 def body(

time: 88.9 us -> 81.9 us (0.921)
  local copies, waits for them, and re-layouts: 25 us -> 6.27 us
  Pallas kernels: 43.2 us -> 55.3 us
    unnamed x56 -> x20, local copies, waits for them, and re-layouts: 22.5 us -> 3.19 us
    pallas_call x2, Pallas kernels: 12.8 us -> 19.4 us  [lookup(): pl.pallas_call(functools.partial(lookup_kernel, chunk=chunk, per_pair=per...]
    pallas_call x2, Pallas kernels: 30.2 us -> 33.2 us  [encode(): pl.pallas_call(encode_kernel, out_shape=[made, made], grid_spec=pltpu.Pre...]
    pallas_call x1, Pallas kernels: 0.17 us -> 2.75 us  [finish_weights(): pl.pallas_call(weights_kernel, out_shape=[pltpu.HBM((D, 3 * D), BF16), pl...]
  transfers between devices with their start and end apart: 9 -> 9, of which waited for: 2 -> 2; matrix products, arithmetic and copies ran while one was open for 2% -> 3% of each run, Pallas kernels for 42% -> 56%
where the time goes in v2:
time: 81.9 us; the launch traced here: 81.2 us
  Pallas kernels  55.3 us (68%)
  starting transfers between devices  13.2 us (16%)
  waiting for transfers between devices  6.36 us (8%)
  local copies, waits for them, and re-layouts  6.27 us (8%)
    pallas_call x2, Pallas kernels, encode(): pl.pallas_call(encode_kernel, out_shape=[made, made], grid_spec=pltpu.Pre...  33.2 us
    pallas_call x2, Pallas kernels, lookup(): pl.pallas_call(functools.partial(lookup_kernel, chunk=chunk, per_pair=per...  19.4 us
    all_to_all x2, starting transfers between devices, body(): got = lax.all_to_all(sent, 'pa', split_axis=0, concat_axis=0, tiled=True)  9.76 us
    all_to_all x2, waiting for transfers between devices, body(): got = lax.all_to_all(sent, 'pa', split_axis=0, concat_axis=0, tiled=True)  5.45 us
    unnamed x20, local copies, waits for them, and re-layouts  3.19 us
    pallas_call x1, Pallas kernels, finish_weights(): pl.pallas_call(weights_kernel, out_shape=[pltpu.HBM((D, 3 * D), BF16), pl...  2.75 us
    ppermute x5, starting transfers between devices, body(): other = tuple((lax.ppermute(w, 'dev', swap) for w in own))  2.72 us
  transfers between devices with their start and end apart: 9, of which 2 were waited for; matrix products, arithmetic and copies ran while one was open for 3% of the time, Pallas kernels for 56%

profile of v2, /device:TPU:1, one launch (start us, length us, event | category | flops | bytes accessed | tf_op | source)
XLA Modules:
  0.0 81.2 jit_solution(203823228716883960)
XLA Ops:
  0.0 0.0 copy-start
  0.0 0.8 copy-done
  0.8 0.0 copy-start.1
  0.8 9.7 %lookup.3 = bf16[256,8,256]{2,1,0:T(8,128)(2,1)} custom-call(s32[1]{0:T(128)} %bitcast.core_ref, s32[8,1024]{1,0:T(8,128)S(1)} %bitcast.10, bf16[1024,8,256]{2,1,0:T(8,128)(2,1)} %feat_ref.3, bf16[4096,256]{1,0:T(8,128)(2,1)} %table_ref.3), custom_call_target="tpu_custom_call" | custom-call | tf_op jit(solution)/shard_map/lookup/pallas_call | solution.py:59
  10.4 6.2 %all-to-all-start.1 = ((bf16[256,8,256]{2,1,0:T(8,128)(2,1)}), bf16[256,8,256]{2,1,0:T(8,128)(2,1)S(1)}, u32[]{:S(2)}, u32[]{:S(2)}) async-start(bf16[256,8,256]{2,1,0:T(8,128)(2,1)} %lookup.3), calls=%async_computation.1 | async-start | bytes 2097152 | tf_op jit(solution)/shard_map/all_to_all | solution.py:285
  16.6 0.0 copy-done.1
  16.7 0.0 copy-start.4
  16.7 0.0 copy-start.5
  16.7 0.0 copy-start.8
  16.7 9.7 %lookup.2 = bf16[256,8,256]{2,1,0:T(8,128)(2,1)} custom-call(s32[1]{0:T(128)} %bitcast.core_ref, s32[8,1024]{1,0:T(8,128)S(1)} %bitcast.11, bf16[1024,8,256]{2,1,0:T(8,128)(2,1)} %feat_ref.3, bf16[4096,256]{1,0:T(8,128)(2,1)} %table_ref.3), custom_call_target="tpu_custom_call" | custom-call | tf_op jit(solution)/shard_map/lookup/pallas_call | solution.py:59
  26.4 5.4 %all-to-all-done.1 = bf16[256,8,256]{2,1,0:T(8,128)(2,1)S(1)} async-done(((bf16[256,8,256]{2,1,0:T(8,128)(2,1)}), bf16[256,8,256]{2,1,0:T(8,128)(2,1)S(1)}, u32[]{:S(2)}, u32[]{:S(2)}) %all-to-all-start.1) | async-done | bytes 1048608 | tf_op jit(solution)/shard_map/all_to_all | solution.py:285
  31.8 0.0 copy-start.3
  31.8 3.6 %all-to-all-start = ((bf16[256,8,256]{2,1,0:T(8,128)(2,1)}), bf16[256,8,256]{2,1,0:T(8,128)(2,1)S(1)}, u32[]{:S(2)}, u32[]{:S(2)}) async-start(bf16[256,8,256]{2,1,0:T(8,128)(2,1)} %lookup.2), calls=%async_computation | async-start | bytes 2097152 | tf_op jit(solution)/shard_map/all_to_all | solution.py:285
  35.4 0.0 copy-done.4
  35.4 1.7 %collective-permute-start.3 = (bf16[256,512]{1,0:T(8,128)(2,1)S(1)}, bf16[256,512]{1,0:T(8,128)(2,1)S(1)}, u32[]{:S(2)}, u32[]{:S(2)}) collective-permute-start(bf16[256,512]{1,0:T(8,128)(2,1)S(1)} %copy-done.4), channel_id=1, source_target_pairs={{0,1},{1,0},{2,3},{3,2},{4,5},{5,4},{6,7},{7,6},{8,9},{9,8},{10,11... | collective-permute-start | bytes 786440 | tf_op jit(solution)/shard_map/ppermute | solution.py:277
  37.1 0.0 copy-done.5
  37.1 0.1 collective-permute-start.4
  37.2 0.0 copy-done.8
  37.2 0.4 collective-permute-start
  37.6 0.1 collective-permute-start.1
  37.7 0.4 collective-permute-start.2
  38.1 0.8 dynamic_slice.3
  38.9 0.1 slice_bitcast_fusion.1
  39.0 0.7 copy.12.lens_ref
  39.7 0.7 copy.11.lens_ref
  40.3 0.0 collective-permute-done.1.out_b
  40.3 0.0 collective-permute-done.2.bil_b
  40.4 0.0 collective-permute-done.qkv_b
  40.4 0.0 copy-start.9
  40.4 0.0 collective-permute-done.3.up_b
  40.4 0.0 copy-start.6
  40.4 0.0 collective-permute-done.4.down_b
  40.4 0.6 copy-done.9
  41.0 0.1 copy-done.6
  41.1 0.0 copy-start.7
  41.1 0.7 copy-done.7
  41.8 2.8 %weights.1 = (bf16[256,768]{1,0:T(8,128)(2,1)}, bf16[256,1024]{1,0:T(8,128)(2,1)}, bf16[1536,256]{1,0:T(8,128)(2,1)}) custom-call(s32[1]{0:T(128)} %bitcast.core_ref, bf16[3,256,128]{2,1,0:T(8,128)(2,1)} %qkv_a.1, bf16[3,256,128]{2,1,0:T(8,128)(2,1)} %copy-done.9, bf16[128,256]{1,0:T(8,128)(2,1)} %out_a.1, bf16[128,256]{1,0:T(8,128)(2,1)} %collective-permute-done.1.out_b, ...), custom_call_target="tpu_custom_call" | custom-call | tf_op jit(solution)/shard_map/weights/pallas_call | solution.py:110
  44.6 0.0 copy-done.3
  44.6 16.6 %encode.3 = (f32[4,32,128]{2,1,0:T(8,128)S(1)}, f32[4,32,128]{2,1,0:T(8,128)S(1)}) custom-call(s32[1]{0:T(128)} %bitcast.core_ref, bf16[8,32,8,256]{3,2,1,0:T(8,128)(2,1)} %bitcast.13, s32[32,1]{1,0:T(8,128)} %copy.12.lens_ref, s32[4,64]{1,0:T(4,128)} %seed_ref.3, bf16[256,768]{1,0:T(8,128)(2,1)} %get-tuple-element.12.qkv_ref, ...), custom_call_target="tpu_custom_call" | custom-call | tf_op jit(solution)/shard_map/encode/pallas_call | solution.py:243
  61.2 0.2 collective-permute-start.6
  61.4 0.0 all-to-all-done
  61.4 0.0 copy-start.2
  61.4 1.0 %copy-done.2 = bf16[256,8,256]{2,1,0:T(8,128)(2,1)} copy-done((bf16[256,8,256]{2,1,0:T(8,128)(2,1)}, bf16[256,8,256]{2,1,0:T(8,128)(2,1)S(1)}, u32[]{:S(2)}) %copy-start.2) | copy-done | bytes 1048600
  62.4 16.6 %encode.2 = (f32[4,32,128]{2,1,0:T(8,128)S(1)}, f32[4,32,128]{2,1,0:T(8,128)S(1)}) custom-call(s32[1]{0:T(128)} %bitcast.core_ref, bf16[8,32,8,256]{3,2,1,0:T(8,128)(2,1)} %bitcast.12, s32[32,1]{1,0:T(8,128)} %copy.11.lens_ref, s32[4,64]{1,0:T(4,128)} %seed_ref.3, bf16[256,768]{1,0:T(8,128)(2,1)} %get-tuple-element.12.qkv_ref, ...), custom_call_target="tpu_custom_call" | custom-call | tf_op jit(solution)/shard_map/encode/pallas_call | solution.py:243
  78.9 0.5 collective-permute-start.5
  79.4 0.0 collective-permute-done.6
  79.4 0.9 %collective-permute-done.5 = f32[4,32,128]{2,1,0:T(8,128)S(1)} collective-permute-done((f32[4,32,128]{2,1,0:T(8,128)S(1)}, f32[4,32,128]{2,1,0:T(8,128)S(1)}, u32[]{:S(2)}, u32[]{:S(2)}) %collective-permute-start.5) | collective-permute-done | bytes 65568 | tf_op jit(solution)/shard_map/ppermute | solution.py:290
  80.4 0.9 %copy.13 = f32[128,4,128]{2,1,0:T(4,128)} copy(f32[128,4,128]{2,0,1:T(8,128)S(1)} %fusion) | data formatting | bytes 524288 | tf_op jit(solution)/shard_map/transpose | solution.py:298
  (1 shorter events, 0.0 us)
Async XLA Ops:
  0.0 0.8 copy-start
  0.8 15.9 %copy-start.1 = (s32[1024,8]{0,1:T(8,128)S(1)}, s32[1024,8]{0,1:T(8,128)}, u32[]{:S(2)}) copy-start(s32[1024,8]{0,1:T(8,128)} %param.11) | copy-start | bytes 98308
  10.4 21.4 %all-to-all-start.1 = ((bf16[256,8,256]{2,1,0:T(8,128)(2,1)}), bf16[256,8,256]{2,1,0:T(8,128)(2,1)S(1)}, u32[]{:S(2)}, u32[]{:S(2)}) async-start(bf16[256,8,256]{2,1,0:T(8,128)(2,1)} %lookup.3), calls=%async_computation.1 | async-start | bytes 2097152 | tf_op jit(solution)/shard_map/all_to_all | solution.py:285
  16.7 18.7 %copy-start.4 = (bf16[256,512]{1,0:T(8,128)(2,1)S(1)}, bf16[256,512]{1,0:T(8,128)(2,1)}, u32[]{:S(2)}) copy-start(bf16[256,512]{1,0:T(8,128)(2,1)} %up_a.1) | copy-start | bytes 786436
  16.7 20.4 %copy-start.5 = (bf16[512,256]{1,0:T(8,128)(2,1)S(1)}, bf16[512,256]{1,0:T(8,128)(2,1)}, u32[]{:S(2)}) copy-start(bf16[512,256]{1,0:T(8,128)(2,1)} %down_a.1) | copy-start | bytes 786436
  16.7 20.5 %copy-start.8 = (bf16[3,256,128]{2,1,0:T(8,128)(2,1)S(1)}, bf16[3,256,128]{2,1,0:T(8,128)(2,1)}, u32[]{:S(2)}) copy-start(bf16[3,256,128]{2,1,0:T(8,128)(2,1)} %qkv_a.1) | copy-start | bytes 589828
  31.8 12.7 %copy-start.3 = (bf16[256,8,256]{2,1,0:T(8,128)(2,1)}, bf16[256,8,256]{2,1,0:T(8,128)(2,1)S(1)}, u32[]{:S(2)}) copy-start(bf16[256,8,256]{2,1,0:T(8,128)(2,1)S(1)} %all-to-all-done.1) | copy-start | bytes 3145732
  31.8 29.5 %all-to-all-start = ((bf16[256,8,256]{2,1,0:T(8,128)(2,1)}), bf16[256,8,256]{2,1,0:T(8,128)(2,1)S(1)}, u32[]{:S(2)}, u32[]{:S(2)}) async-start(bf16[256,8,256]{2,1,0:T(8,128)(2,1)} %lookup.2), calls=%async_computation | async-start | bytes 2097152 | tf_op jit(solution)/shard_map/all_to_all | solution.py:285
  35.4 5.0 %collective-permute-start.3 = (bf16[256,512]{1,0:T(8,128)(2,1)S(1)}, bf16[256,512]{1,0:T(8,128)(2,1)S(1)}, u32[]{:S(2)}, u32[]{:S(2)}) collective-permute-start(bf16[256,512]{1,0:T(8,128)(2,1)S(1)} %copy-done.4), channel_id=1, source_target_pairs={{0,1},{1,0},{2,3},{3,2},{4,5},{5,4},{6,7},{7,6},{8,9},{9,8},{10,11... | collective-permute-start | bytes 786440 | tf_op jit(solution)/shard_map/ppermute | solution.py:277
  37.1 3.3 %collective-permute-start.4 = (bf16[512,256]{1,0:T(8,128)(2,1)S(1)}, bf16[512,256]{1,0:T(8,128)(2,1)S(1)}, u32[]{:S(2)}, u32[]{:S(2)}) collective-permute-start(bf16[512,256]{1,0:T(8,128)(2,1)S(1)} %copy-done.5), channel_id=1, source_target_pairs={{0,1},{1,0},{2,3},{3,2},{4,5},{5,4},{6,7},{7,6},{8,9},{9,8},{10,11... | collective-permute-start | bytes 786440 | tf_op jit(solution)/shard_map/ppermute | solution.py:277
  37.2 3.1 %collective-permute-start = (bf16[3,256,128]{2,1,0:T(8,128)(2,1)S(1)}, bf16[3,256,128]{2,1,0:T(8,128)(2,1)S(1)}, u32[]{:S(2)}, u32[]{:S(2)}) collective-permute-start(bf16[3,256,128]{2,1,0:T(8,128)(2,1)S(1)} %copy-done.8), channel_id=1, source_target_pairs={{0,1},{1,0},{2,3},{3,2},{4,5},{5,4},{6,7},{7,6},{8,9},{9,8},{10,11... | collective-permute-start | bytes 589832 | tf_op jit(solution)/shard_map/ppermute | solution.py:277
  37.6 2.7 %collective-permute-start.1 = (bf16[128,256]{1,0:T(8,128)(2,1)}, bf16[128,256]{1,0:T(8,128)(2,1)}, u32[]{:S(2)}, u32[]{:S(2)}) collective-permute-start(bf16[128,256]{1,0:T(8,128)(2,1)} %out_a.1), channel_id=1, source_target_pairs={{0,1},{1,0},{2,3},{3,2},{4,5},{5,4},{6,7},{7,6},{8,9},{9,8},{10,11... | collective-permute-start | bytes 196616 | tf_op jit(solution)/shard_map/ppermute | solution.py:277
  37.7 2.6 %collective-permute-start.2 = (bf16[256,128]{1,0:T(8,128)(2,1)}, bf16[256,128]{1,0:T(8,128)(2,1)}, u32[]{:S(2)}, u32[]{:S(2)}) collective-permute-start(bf16[256,128]{1,0:T(8,128)(2,1)} %bil_a.1), channel_id=1, source_target_pairs={{0,1},{1,0},{2,3},{3,2},{4,5},{5,4},{6,7},{7,6},{8,9},{9,8},{10,11... | collective-permute-start | bytes 196616 | tf_op jit(solution)/shard_map/ppermute | solution.py:277
  40.4 0.7 copy-start.9
  40.4 0.7 copy-start.6
  41.1 0.7 copy-start.7
  61.2 18.3 %collective-permute-start.6 = (f32[4,32,128]{2,1,0:T(8,128)S(1)}, f32[4,32,128]{2,1,0:T(8,128)S(1)}, u32[]{:S(2)}, u32[]{:S(2)}) collective-permute-start(f32[4,32,128]{2,1,0:T(8,128)S(1)} %get-tuple-element.18), channel_id=1, source_target_pairs={{0,1},{1,0},{2,3},{3,2},{4,5},{5,4},{6,7},{7,6},{8,9},{9,8},{10,11... | collective-permute-start | bytes 196616 | tf_op jit(solution)/shard_map/ppermute | solution.py:290
  61.4 1.0 %copy-start.2 = (bf16[256,8,256]{2,1,0:T(8,128)(2,1)}, bf16[256,8,256]{2,1,0:T(8,128)(2,1)S(1)}, u32[]{:S(2)}) copy-start(bf16[256,8,256]{2,1,0:T(8,128)(2,1)S(1)} %all-to-all-done) | copy-start | bytes 3145732
  78.9 1.4 %collective-permute-start.5 = (f32[4,32,128]{2,1,0:T(8,128)S(1)}, f32[4,32,128]{2,1,0:T(8,128)S(1)}, u32[]{:S(2)}, u32[]{:S(2)}) collective-permute-start(f32[4,32,128]{2,1,0:T(8,128)S(1)} %get-tuple-element.17), channel_id=1, source_target_pairs={{0,1},{1,0},{2,3},{3,2},{4,5},{5,4},{6,7},{7,6},{8,9},{9,8},{10,11... | collective-permute-start | bytes 196616 | tf_op jit(solution)/shard_map/ppermute | solution.py:290

commit v3 on v2

v3 whole, which is shorter than its diff:
```python
import functools

import jax
import jax.numpy as jnp
from jax import lax
from jax.experimental import pallas as pl
from jax.experimental.pallas import tpu as pltpu
from jax.sharding import PartitionSpec as P

D = 256
HEADS = 4
CAPS = 4
ITERS = 3
FIRST = (5, 8)
BLOCK = 8
STEPS = (5, 3)
TABLE_PARTS = 4
GROUP = 4
F32 = jnp.float32
BF16 = jnp.bfloat16


def in_hbm(*arrays):
    return tuple(pltpu.with_memory_space_constraint(a, pltpu.HBM) for a in arrays)


def lookup_kernel(
    core_ref, ids_hbm, feat_hbm, table_hbm, out_hbm, ids, feat, table, wide, out, id_sem, feat_sem, table_sem, out_sem,
    *, start, per_pair, per_core,
):
    pairs, users, spots, _ = feat.shape
    offset = core_ref[0] * per_core + start
    rows = table.shape[0] // TABLE_PARTS
    fetch_ids = pltpu.make_async_copy(ids_hbm, ids, id_sem)
    fetch_ids.start()
    fetch_table = []
    for i in range(TABLE_PARTS):
        at = pl.ds(i * rows, rows)
        fetch_table.append(pltpu.make_async_copy(table_hbm.at[at], table.at[at], table_sem.at[i]))
        fetch_table[-1].start()
    fetch_feat = []
    for d in range(pairs):
        at = pl.ds(d * per_pair + offset, users)
        fetch_feat.append(pltpu.make_async_copy(feat_hbm.at[at], feat.at[d], feat_sem.at[d]))
        fetch_feat[-1].start()
    for i in range(TABLE_PARTS):
        fetch_table[i].wait()

        def widen(j, carry, i=i):
            at = pl.ds(pl.multiple_of(i * rows + j * 128, 128), 128)
            wide[at, :] = table[at, :].astype(F32)
            return carry

        lax.fori_loop(0, rows // 128, widen, 0)
    fetch_ids.wait()
    spot = lax.broadcasted_iota(jnp.int32, (spots, D), 0)
    send = []
    for d in range(pairs):
        fetch_feat[d].wait()
        first = d * per_pair + offset

        def one(user, carry, d=d, first=first):
            rows = jnp.broadcast_to(wide[pl.ds(ids[0, first + user], 1), :], (spots, D))
            for p in range(1, spots):
                row = jnp.broadcast_to(wide[pl.ds(ids[p, first + user], 1), :], (spots, D))
                rows = jnp.where(spot == p, row, rows)
            out[d, user] = (feat[d, user].astype(F32) + rows).astype(BF16)
            return carry

        lax.fori_loop(0, users, one, 0, unroll=8)
        send.append(
            pltpu.make_async_copy(out.at[d], out_hbm.at[pl.ds(d * users, users)], out_sem.at[d])
        )
        send[-1].start()
    for copy in send:
        copy.wait()


def lookup(core, ids, features, table, start, users, pa_count, dev_count):
    all_users, spots, width = features.shape
    per_pair = all_users // pa_count
    per_core = per_pair // dev_count
    block = (pa_count, users, spots, width)
    hbm = pl.BlockSpec(memory_space=pltpu.HBM)
    return pl.pallas_call(
        functools.partial(lookup_kernel, start=start, per_pair=per_pair, per_core=per_core),
        out_shape=pltpu.HBM((pa_count * users, spots, width), BF16),
        in_specs=[pl.BlockSpec(memory_space=pltpu.SMEM), hbm, hbm, hbm],
        out_specs=hbm,
        scratch_shapes=[
            pltpu.SMEM(ids.shape, jnp.int32),
            pltpu.VMEM(block, BF16),
            pltpu.VMEM(table.shape, BF16),
            pltpu.VMEM(table.shape, F32),
            pltpu.VMEM(block, BF16),
            pltpu.SemaphoreType.DMA,
            pltpu.SemaphoreType.DMA((pa_count,)),
            pltpu.SemaphoreType.DMA((TABLE_PARTS,)),
            pltpu.SemaphoreType.DMA((pa_count,)),
        ],
        compiler_params=pltpu.CompilerParams(vmem_limit_bytes=24 << 20),
        name="lookup",
    )(core, *in_hbm(ids, features, table))


def weights_kernel(
    core_ref, qkv_a, qkv_b, out_a, out_b, bil_a, bil_b, up_a, up_b, down_a, down_b, qkv, up, tail
):
    half = D // 2
    for i in range(3):
        qkv[:, i * D : i * D + half] = qkv_a[i]
        qkv[:, i * D + half : (i + 1) * D] = qkv_b[i]
    ff = up_a.shape[1]
    up[:, :ff] = up_a[...]
    up[:, ff:] = up_b[...]

    @pl.when(core_ref[0] == 0)
    def _():
        tail[:D, :half] = bil_a[...]
        tail[:D, half:] = bil_b[...]

    @pl.when(core_ref[0] != 0)
    def _():
        tail[:D, :half] = bil_b[...]
        tail[:D, half:] = bil_a[...]

    tail[D : D + half, :] = out_a[...]
    tail[D + half : 2 * D, :] = out_b[...]
    tail[2 * D : 2 * D + ff, :] = down_a[...]
    tail[2 * D + ff :, :] = down_b[...]


def finish_weights(core, own, other):
    ff = own[3].shape[1]
    operands = [w for pair in zip(own, other) for w in pair]
    return pl.pallas_call(
        weights_kernel,
        out_shape=[
            pltpu.VMEM((D, 3 * D), BF16),
            pltpu.VMEM((D, 2 * ff), BF16),
            pltpu.VMEM((2 * D + 2 * ff, D), BF16),
        ],
        in_specs=[pl.BlockSpec(memory_space=pltpu.SMEM)]
        + [pl.BlockSpec(memory_space=pltpu.VMEM)] * len(operands),
        out_specs=[pl.BlockSpec(memory_space=pltpu.VMEM)] * 3,
        compiler_params=pltpu.CompilerParams(vmem_limit_bytes=16 << 20),
        name="weights",
    )(core, *in_hbm(*operands))


def split(x):
    high = x.astype(BF16)
    return jnp.concatenate([high, (x - high.astype(F32)).astype(BF16)], axis=0)


def joined(x):
    half = x.shape[0] // 2
    return x[:half] + x[half:]


def encode_kernel(core_ref, x_ref, lens_ref, seed_ref, qkv_ref, up_ref, tail_ref, own_ref, other_ref, interest_ref, *, steps):
    step = pl.program_id(0)
    pairs, all_users, spots, _ = x_ref.shape
    block = all_users // steps
    history = pairs * spots
    rows = block * history
    head = D // HEADS
    lanes = HEADS * history
    x = x_ref[:, pl.ds(step * block, block)].astype(F32)
    x = jnp.swapaxes(x, 0, 1).reshape(rows, D).astype(BF16)
    qkv = jnp.dot(x, qkv_ref[...], preferred_element_type=F32)
    queries = (qkv[:, :D] * (1.0 / head**0.5)).astype(BF16)
    keys = qkv[:, D : 2 * D].astype(BF16)
    values = qkv[:, 2 * D :].astype(BF16)

    lane_head = lax.broadcasted_iota(jnp.int32, (history, D), 1) // head
    own_head = [(lane_head == h).astype(F32).astype(BF16) for h in range(HEADS)]
    row_head = lax.broadcasted_iota(jnp.int32, (lanes, D), 0) // history
    col_head = lax.broadcasted_iota(jnp.int32, (lanes, D), 1) // head
    ones = (row_head == col_head).astype(F32).astype(BF16)
    position = lax.broadcasted_iota(jnp.int32, (block, lanes), 1) % history
    lens = lens_ref[pl.ds(pl.multiple_of(step * block, BLOCK), block), :]
    key_valid = (position < lens).astype(F32)
    users = [slice(u * history, (u + 1) * history) for u in range(block)]
    scores = []
    for at in users:
        key_wide = jnp.concatenate([keys[at] * m for m in own_head], axis=0)
        scores.append(
            lax.dot_general(
                queries[at], key_wide, (((1,), (1,)), ((), ())), preferred_element_type=F32
            )
        )
    rounded = [
        jnp.where(key_valid[u : u + 1] > 0.0, jnp.exp(s), 0.0).astype(BF16)
        for u, s in enumerate(scores)
    ]
    totals = jnp.dot(jnp.concatenate(rounded, axis=0), ones, preferred_element_type=F32)
    weighted = []
    for at, r in zip(users, rounded):
        value_wide = jnp.concatenate([values[at] * m for m in own_head], axis=0)
        weighted.append(jnp.dot(r, value_wide, preferred_element_type=F32))
    attended = (jnp.concatenate(weighted, axis=0) / totals).astype(BF16)
    hidden = jax.nn.gelu(jnp.dot(x, up_ref[...], preferred_element_type=F32)).astype(BF16)
    everything = jnp.concatenate([x, attended, hidden], axis=1)
    interest = jnp.dot(everything, tail_ref[...], preferred_element_type=F32).astype(BF16)
    interest_ref[pl.ds(pl.multiple_of(step * rows, rows), rows), :] = interest

    @pl.when(step == steps - 1)
    def _():
        route(core_ref, lens_ref, seed_ref, own_ref, other_ref, interest_ref, history)


def route(core_ref, lens_ref, seed_ref, own_ref, other_ref, interest_ref, history):
    lanes = GROUP * history
    groups = BLOCK // GROUP
    blocks = range(interest_ref.shape[0] // (BLOCK * history))
    lane = lax.broadcasted_iota(jnp.int32, (BLOCK, lanes), 1)
    user = lax.broadcasted_iota(jnp.int32, (BLOCK, lanes), 0)
    mine = (lane // history) == (user % GROUP)
    in_group = [(user // GROUP) == g for g in range(groups)]
    base = (seed_ref[...].astype(F32) - 7.5) * 0.25
    base = jnp.concatenate([base] * GROUP, axis=1)
    base = jnp.broadcast_to(base[:, None, :], (CAPS, BLOCK, lanes))
    logits = [base for _ in blocks]
    valid = []
    for b in blocks:
        real = mine & ((lane % history) < lens_ref[b * BLOCK : (b + 1) * BLOCK, :])
        valid.append([(real & here).astype(F32)[None] for here in in_group])

    def vectors(b, g):
        return interest_ref[(b * groups + g) * lanes : (b * groups + g + 1) * lanes, :]

    def softmax(x):
        weights = jnp.exp(x - jnp.max(x, axis=0, keepdims=True))
        return weights / jnp.sum(weights, axis=0, keepdims=True)

    def parts(weights, b):
        return [split((weights * v).reshape(CAPS * BLOCK, lanes)) for v in valid[b]]

    def squash(summed):
        squares = jnp.sum(summed * summed, axis=1, keepdims=True)
        return summed * (jnp.sqrt(squares) / (1.0 + squares))

    for sweep in range(ITERS):
        if sweep == 0:
            weights = [softmax(base)] * len(logits)
        else:
            weights = [softmax(x) for x in logits]
        weighted = [parts(weights[b], b) for b in blocks]
        summed = [
            joined(
                sum(
                    jnp.dot(weighted[b][g], vectors(b, g), preferred_element_type=F32)
                    for g in range(groups)
                )
            )
            for b in blocks
        ]
        capsules = [squash(x) for x in summed]
        if sweep + 1 < ITERS:
            caps = [split(x) for x in capsules]
            near = [
                [
                    lax.dot_general(
                        caps[b], vectors(b, g), (((1,), (1,)), ((), ())), preferred_element_type=F32
                    )
                    for g in range(groups)
                ]
                for b in blocks
            ]
            for b in blocks:
                added = [joined(x).reshape(CAPS, BLOCK, lanes) for x in near[b]]
                chosen = added[-1]
                for g in range(groups - 1):
                    chosen = jnp.where(in_group[g][None], added[g], chosen)
                logits[b] = logits[b] + chosen
    half = D // 2
    low_own = core_ref[0] == 0
    for b in blocks:
        made = capsules[b].reshape(CAPS, BLOCK, D)
        low, high = made[:, :, :half], made[:, :, half:]
        kept, passed = jnp.where(low_own, low, high), jnp.where(low_own, high, low)
        for j in range(CAPS):
            own_ref[b * BLOCK : (b + 1) * BLOCK, j, :] = kept[j]
            other_ref[b * BLOCK : (b + 1) * BLOCK, j, :] = passed[j]


def encode(core, gathered, lens, seed, qkv, up, tail, steps):
    pa_count, users, spots, _ = gathered.shape
    vmem = pl.BlockSpec(memory_space=pltpu.VMEM)
    made = jax.ShapeDtypeStruct((users, CAPS, D // 2), F32)
    return pl.pallas_call(
        functools.partial(encode_kernel, steps=steps),
        out_shape=[made, made],
        grid=(steps,),
        in_specs=[pl.BlockSpec(memory_space=pltpu.SMEM)] + [vmem] * 6,
        out_specs=[vmem] * 2,
        scratch_shapes=[pltpu.VMEM((users * pa_count * spots, D), BF16)],
        compiler_params=pltpu.CompilerParams(vmem_limit_bytes=40 << 20),
        name="encode",
    )(core, gathered, lens, seed, qkv, up, tail)


def body(
    features, item_ids, item_table, lengths, routing_seed, w_qkv, w_out, w_bilinear, w_up, w_down
):
    pa_count = lax.axis_size("pa")
    dev_count = lax.axis_size("dev")
    spots = features.shape[1]
    per_core = lengths.shape[0] // (pa_count * dev_count)
    core_index = lax.axis_index("dev").astype(jnp.int32)
    core = core_index.reshape(1)
    swap = [(i, dev_count - 1 - i) for i in range(dev_count)]
    own = (w_qkv, w_out, w_bilinear, w_up, w_down)
    other = tuple(lax.ppermute(w, "dev", swap) for w in own)
    qkv, up, tail = finish_weights(core, own, other)
    first = (lax.axis_index("pa") * dev_count + core_index) * per_core
    lens = lax.dynamic_slice_in_dim(lengths, first, per_core).reshape(per_core, 1)
    ids = item_ids.T
    cut = per_core * FIRST[0] // FIRST[1]
    halves = []
    for start, users, steps in ((0, cut, STEPS[0]), (cut, per_core - cut, STEPS[1])):
        if start:
            ids, qkv, up, tail = lax.optimization_barrier((ids, qkv, up, tail))
        sent = lookup(core, ids, features, item_table, start, users, pa_count, dev_count)
        got = lax.all_to_all(sent, "pa", split_axis=0, concat_axis=0, tiled=True)
        got = got.reshape(pa_count, users, spots, D)
        kept, passed = encode(
            core, got, lens[start : start + users], routing_seed, qkv, up, tail, steps
        )
        halves.append((kept, lax.ppermute(passed, "dev", swap)))
    kept = jnp.concatenate([h[0] for h in halves], axis=0)
    came = jnp.concatenate([h[1] for h in halves], axis=0)
    return jnp.where(
        core_index == 0,
        jnp.concatenate([kept, came], axis=0),
        jnp.concatenate([came, kept], axis=0),
    )


def solution(mesh):
    in_specs = (
        P("au", "pa", None),
        P("au", "pa"),
        P(),
        P("au"),
        P(),
        P(None, None, "dev"),
        P("dev", None),
        P(None, "dev"),
        P(None, "dev"),
        P("dev", None),
    )
    out_specs = P(("au", "pa"), None, "dev")
    return jax.shard_map(body, mesh=mesh, in_specs=in_specs, out_specs=out_specs, check_vma=False)
```

time: 81.9 us -> 65.1 us (0.79)
  Pallas kernels: 55.3 us -> 36.8 us
  waiting for transfers between devices: 6.36 us -> 8.75 us
  local copies, waits for them, and re-layouts: 6.27 us -> 4.51 us
    pallas_call x5, Pallas kernels: 55.3 us -> 36.8 us  [the longest x2 19.7 us: encode(): pl.pallas_call(functools.partial(encode_kernel, steps=steps), out_shape=[...]
    slice x3 -> x4, local copies, waits for them, and re-layouts: 1.45 us -> 0.26 us  [body(): lens[start:start + users]]
    all_to_all x2, waiting for transfers between devices: 5.45 us -> 6.56 us  [body(): got = lax.all_to_all(sent, 'pa', split_axis=0, concat_axis=0, tiled=True)]
    ppermute x2, starting transfers between devices: 0.67 us -> 1.71 us  [body(): halves.append((kept, lax.ppermute(passed, 'dev', swap)))]
    ppermute x5, waiting for transfers between devices: 0.01 us -> 0.98 us  [body(): other = tuple((lax.ppermute(w, 'dev', swap) for w in own))]
    transpose x1 -> x0, local copies, waits for them, and re-layouts: 0.87 us -> none  [body(): return jnp.swapaxes(made, 0, 1)]
    unnamed x20 -> x28, local copies, waits for them, and re-layouts: 3.19 us -> 3.49 us
  transfers between devices with their start and end apart: 9 -> 9, of which waited for: 2 -> 4; matrix products, arithmetic and copies ran while one was open for 3% -> 2% of each run, Pallas kernels for 56% -> 43%
where the time goes in v3:
time: 65.1 us; the launch traced here: 64.6 us
  Pallas kernels  36.8 us (57%)
  starting transfers between devices  13.7 us (21%)
  waiting for transfers between devices  8.75 us (13%)
  local copies, waits for them, and re-layouts  4.51 us (7%)
  other arithmetic  0.76 us (1%)
    pallas_call x2, Pallas kernels, encode(): pl.pallas_call(functools.partial(encode_kernel, steps=steps), out_shape=[...  19.7 us
    pallas_call x2, Pallas kernels, lookup(): pl.pallas_call(functools.partial(lookup_kernel, start=start, per_pair=per...  15.5 us
    all_to_all x2, starting transfers between devices, body(): got = lax.all_to_all(sent, 'pa', split_axis=0, concat_axis=0, tiled=True)  9.89 us
    all_to_all x2, waiting for transfers between devices, body(): got = lax.all_to_all(sent, 'pa', split_axis=0, concat_axis=0, tiled=True)  6.56 us
    unnamed x28, local copies, waits for them, and re-layouts  3.49 us
    ppermute x5, starting transfers between devices, body(): other = tuple((lax.ppermute(w, 'dev', swap) for w in own))  2.05 us
    ppermute x2, starting transfers between devices, body(): halves.append((kept, lax.ppermute(passed, 'dev', swap)))  1.71 us
    pallas_call x1, Pallas kernels, finish_weights(): pl.pallas_call(weights_kernel, out_shape=[pltpu.VMEM((D, 3 * D), BF16), p...  1.62 us
  transfers between devices with their start and end apart: 9, of which 4 were waited for; matrix products, arithmetic and copies ran while one was open for 2% of the time, Pallas kernels for 43%

profile of v3, /device:TPU:1, one launch (start us, length us, event | category | flops | bytes accessed | tf_op | source)
XLA Modules:
  0.0 64.6 jit_solution(17507546797955742042)
XLA Ops:
  0.0 9.0 %lookup.2 = bf16[320,8,256]{2,1,0:T(8,128)(2,1)} custom-call(s32[1]{0:T(128)} %bitcast.core_ref, s32[8,1024]{1,0:T(8,128)} %bitcast.10, bf16[1024,8,256]{2,1,0:T(8,128)(2,1)} %feat_hbm.3, bf16[4096,256]{1,0:T(8,128)(2,1)} %table_hbm.3), custom_call_target="tpu_custom_call" | custom-call | tf_op jit(solution)/shard_map/lookup/pallas_call | solution.py:85
  9.0 0.0 copy-start.4
  9.0 0.0 copy-start.5
  9.0 0.0 copy-start.8
  9.0 0.0 copy-start.10
  9.0 0.0 copy-start.11
  9.1 6.3 %all-to-all-start = ((bf16[320,8,256]{2,1,0:T(8,128)(2,1)}), bf16[320,8,256]{2,1,0:T(8,128)(2,1)S(1)}, u32[]{:S(2)}, u32[]{:S(2)}) async-start(bf16[320,8,256]{2,1,0:T(8,128)(2,1)} %lookup.2), calls=%async_computation | async-start | bytes 2621440 | tf_op jit(solution)/shard_map/all_to_all | solution.py:326
  15.4 0.0 copy-done.4
  15.4 1.0 %collective-permute-start.3 = (bf16[256,512]{1,0:T(8,128)(2,1)S(1)}, bf16[256,512]{1,0:T(8,128)(2,1)S(1)}, u32[]{:S(2)}, u32[]{:S(2)}) collective-permute-start(bf16[256,512]{1,0:T(8,128)(2,1)S(1)} %copy-done.4), channel_id=1, source_target_pairs={{0,1},{1,0},{2,3},{3,2},{4,5},{5,4},{6,7},{7,6},{8,9},{9,8},{10,11... | collective-permute-start | bytes 786440 | tf_op jit(solution)/shard_map/ppermute | solution.py:315
  16.4 0.0 copy-done.5
  16.4 0.1 collective-permute-start.4
  16.5 0.0 copy-done.8
  16.5 0.4 collective-permute-start
  17.0 0.0 copy-done.10
  17.0 0.1 collective-permute-start.1
  17.1 0.0 copy-done.11
  17.1 0.4 collective-permute-start.2
  17.5 0.9 %collective-permute-done.1.out_b = bf16[128,256]{1,0:T(8,128)(2,1)S(1)} collective-permute-done((bf16[128,256]{1,0:T(8,128)(2,1)S(1)}, bf16[128,256]{1,0:T(8,128)(2,1)S(1)}, u32[]{:S(2)}, u32[]{:S(2)}) %collective-permute-start.1) | collective-permute-done | bytes 65568 | tf_op jit(solution)/shard_map/ppermute | solution.py:315
  18.4 0.1 collective-permute-done.2.bil_b
  18.5 0.0 collective-permute-done.qkv_b
  18.5 0.0 collective-permute-done.3.up_b
  18.5 0.0 copy-start.6
  18.5 0.0 collective-permute-done.4.down_b
  18.5 0.5 copy-done.12
  19.0 0.1 copy-done.13
  19.1 0.1 copy-done.9
  19.2 0.1 copy-done.6
  19.2 0.7 %copy-done.7 = bf16[512,256]{1,0:T(8,128)(2,1)} copy-done((bf16[512,256]{1,0:T(8,128)(2,1)}, bf16[512,256]{1,0:T(8,128)(2,1)S(1)}, u32[]{:S(2)}) %copy-start.7) | copy-done | bytes 262168
  19.9 1.6 %weights.1 = (bf16[256,768]{1,0:T(8,128)(2,1)S(1)}, bf16[256,1024]{1,0:T(8,128)(2,1)S(1)}, bf16[1536,256]{1,0:T(8,128)(2,1)S(1)}) custom-call(s32[1]{0:T(128)} %bitcast.core_ref, bf16[3,256,128]{2,1,0:T(8,128)(2,1)} %qkv_a.1, bf16[3,256,128]{2,1,0:T(8,128)(2,1)} %copy-done.9, bf16[128,256]{1,0:T(8,128)(2,1)} %out_a.1, bf16[128,256]{1,0:T(8,128)(2,1)} %copy-done.12, ...), custom_call_target="tpu_custom_call" | custom-call | tf_op jit(solution)/shard_map/weights/pallas_call | solution.py:136
  21.6 0.0 copy-start
  21.6 0.0 copy-start.3
  21.6 6.5 %lookup.3 = bf16[192,8,256]{2,1,0:T(8,128)(2,1)} custom-call(s32[1]{0:T(128)} %bitcast.core_ref, s32[8,1024]{1,0:T(8,128)} %bitcast.11, bf16[1024,8,256]{2,1,0:T(8,128)(2,1)} %feat_hbm.3, bf16[4096,256]{1,0:T(8,128)(2,1)} %table_hbm.3), custom_call_target="tpu_custom_call" | custom-call | tf_op jit(solution)/shard_map/lookup/pallas_call | solution.py:85
  28.1 6.6 %all-to-all-done = bf16[320,8,256]{2,1,0:T(8,128)(2,1)S(1)} async-done(((bf16[320,8,256]{2,1,0:T(8,128)(2,1)}), bf16[320,8,256]{2,1,0:T(8,128)(2,1)S(1)}, u32[]{:S(2)}, u32[]{:S(2)}) %all-to-all-start) | async-done | bytes 1310752 | tf_op jit(solution)/shard_map/all_to_all | solution.py:326
  34.7 3.5 %all-to-all-start.1 = ((bf16[192,8,256]{2,1,0:T(8,128)(2,1)}), bf16[192,8,256]{2,1,0:T(8,128)(2,1)S(1)}, u32[]{:S(2)}, u32[]{:S(2)}) async-start(bf16[192,8,256]{2,1,0:T(8,128)(2,1)} %lookup.3), calls=%async_computation.1 | async-start | bytes 1572864 | tf_op jit(solution)/shard_map/all_to_all | solution.py:326
  38.2 0.8 %dynamic_slice.3 = s32[64]{0:T(128)S(1)} dynamic-slice(s32[1024]{0:T(1024)} %param.13, s32[]{:T(128)S(6)} %select_n.12), dynamic_slice_sizes={64} | dynamic-slice | bytes 516 | tf_op jit(solution)/shard_map/dynamic_slice | solution.py:318
  39.0 0.1 copy.11.lens_ref
  39.1 1.0 %copy-done.1 = bf16[256,768]{1,0:T(8,128)(2,1)S(1)} copy-done((bf16[256,768]{1,0:T(8,128)(2,1)S(1)}, bf16[256,768]{1,0:T(8,128)(2,1)}, u32[]{:S(2)}) %copy-start.1) | copy-done | bytes 393240
  40.1 12.3 %encode.2 = (f32[40,4,128]{2,1,0:T(4,128)S(1)}, f32[40,4,128]{2,1,0:T(4,128)}) custom-call(s32[1]{0:T(128)} %bitcast.core_ref, bf16[8,40,8,256]{3,2,1,0:T(8,128)(2,1)S(1)} %bitcast.8, s32[40,1]{1,0:T(8,128)S(1)} %copy.11.lens_ref, s32[4,64]{1,0:T(4,128)S(1)} %copy-done.3, bf16[256,768]{1,0:T(8,128)(2,1)S(1)} %copy-done.1, ...), custom_call_target="tpu_custom_call" | custom-call | tf_op jit(solution)/shard_map/encode/pallas_call | solution.py:292
  52.4 1.6 %collective-permute-start.5 = (f32[40,4,128]{2,1,0:T(4,128)}, f32[40,4,128]{2,1,0:T(4,128)S(1)}, u32[]{:S(2)}, u32[]{:S(2)}) collective-permute-start(f32[40,4,128]{2,1,0:T(4,128)} %get-tuple-element.25), channel_id=1, source_target_pairs={{0,1},{1,0},{2,3},{3,2},{4,5},{5,4},{6,7},{7,6},{8,9},{9,8},{10,11... | collective-permute-start | bytes 245768 | tf_op jit(solution)/shard_map/ppermute | solution.py:331
  54.0 0.1 slice_bitcast_fusion
  54.1 0.1 copy.12.lens_ref
  54.2 0.0 all-to-all-done.1
  54.2 1.0 %copy-done.2 = bf16[256,768]{1,0:T(8,128)(2,1)S(1)} copy-done((bf16[256,768]{1,0:T(8,128)(2,1)S(1)}, bf16[256,768]{1,0:T(8,128)(2,1)}, u32[]{:S(2)}) %copy-start.2) | copy-done | bytes 393240
  55.2 7.3 %encode.3 = (f32[24,4,128]{2,1,0:T(4,128)S(1)}, f32[24,4,128]{2,1,0:T(4,128)S(1)}) custom-call(s32[1]{0:T(128)} %bitcast.core_ref, bf16[8,24,8,256]{3,2,1,0:T(8,128)(2,1)S(1)} %bitcast.9, s32[24,1]{1,0:T(8,128)S(1)} %copy.12.lens_ref, s32[4,64]{1,0:T(4,128)S(1)} %copy-done.3, bf16[256,768]{1,0:T(8,128)(2,1)S(1)} %copy-done.2, ...), custom_call_target="tpu_custom_call" | custom-call | tf_op jit(solution)/shard_map/encode/pallas_call | solution.py:292
  62.6 0.1 collective-permute-start.6
  62.7 1.2 %collective-permute-done.6 = f32[24,4,128]{2,1,0:T(4,128)S(1)} collective-permute-done((f32[24,4,128]{2,1,0:T(4,128)S(1)}, f32[24,4,128]{2,1,0:T(4,128)S(1)}, u32[]{:S(2)}, u32[]{:S(2)}) %collective-permute-start.6) | collective-permute-done | bytes 49184 | tf_op jit(solution)/shard_map/ppermute | solution.py:331
  63.9 0.0 collective-permute-done.5
  63.9 0.8 %maximum_select_fusion = f32[128,4,128]{2,1,0:T(4,128)} fusion(f32[24,4,128]{2,1,0:T(4,128)S(1)} %collective-permute-done.6, f32[40,4,128]{2,1,0:T(4,128)S(1)} %collective-permute-done.5, f32[24,4,128]{2,1,0:T(4,128)S(1)} %get-tuple-element.24, f32[40,4,128]{2,1,0:T(4,128)S(1)} %get-tuple-element.19, pred[]{:T(512)S(6)} %eq.3), kind=kLoop, calls=%fused_computation | loop fusion | flops 458752 | bytes 524289 | tf_op jit(solution)/shard_map/jit(_where)/select_n | solution.py:334
  (9 shorter events, 0.0 us)
Async XLA Ops:
  9.0 6.4 %copy-start.4 = (bf16[256,512]{1,0:T(8,128)(2,1)S(1)}, bf16[256,512]{1,0:T(8,128)(2,1)}, u32[]{:S(2)}) copy-start(bf16[256,512]{1,0:T(8,128)(2,1)} %up_a.1) | copy-start | bytes 786436
  9.0 7.4 %copy-start.5 = (bf16[512,256]{1,0:T(8,128)(2,1)S(1)}, bf16[512,256]{1,0:T(8,128)(2,1)}, u32[]{:S(2)}) copy-start(bf16[512,256]{1,0:T(8,128)(2,1)} %down_a.1) | copy-start | bytes 786436
  9.0 7.5 %copy-start.8 = (bf16[3,256,128]{2,1,0:T(8,128)(2,1)S(1)}, bf16[3,256,128]{2,1,0:T(8,128)(2,1)}, u32[]{:S(2)}) copy-start(bf16[3,256,128]{2,1,0:T(8,128)(2,1)} %qkv_a.1) | copy-start | bytes 589828
  9.0 7.9 %copy-start.10 = (bf16[128,256]{1,0:T(8,128)(2,1)S(1)}, bf16[128,256]{1,0:T(8,128)(2,1)}, u32[]{:S(2)}) copy-start(bf16[128,256]{1,0:T(8,128)(2,1)} %out_a.1) | copy-start | bytes 196612
  9.0 8.0 %copy-start.11 = (bf16[256,128]{1,0:T(8,128)(2,1)S(1)}, bf16[256,128]{1,0:T(8,128)(2,1)}, u32[]{:S(2)}) copy-start(bf16[256,128]{1,0:T(8,128)(2,1)} %bil_a.1) | copy-start | bytes 196612
  9.1 25.6 %all-to-all-start = ((bf16[320,8,256]{2,1,0:T(8,128)(2,1)}), bf16[320,8,256]{2,1,0:T(8,128)(2,1)S(1)}, u32[]{:S(2)}, u32[]{:S(2)}) async-start(bf16[320,8,256]{2,1,0:T(8,128)(2,1)} %lookup.2), calls=%async_computation | async-start | bytes 2621440 | tf_op jit(solution)/shard_map/all_to_all | solution.py:326
  15.4 3.1 %collective-permute-start.3 = (bf16[256,512]{1,0:T(8,128)(2,1)S(1)}, bf16[256,512]{1,0:T(8,128)(2,1)S(1)}, u32[]{:S(2)}, u32[]{:S(2)}) collective-permute-start(bf16[256,512]{1,0:T(8,128)(2,1)S(1)} %copy-done.4), channel_id=1, source_target_pairs={{0,1},{1,0},{2,3},{3,2},{4,5},{5,4},{6,7},{7,6},{8,9},{9,8},{10,11... | collective-permute-start | bytes 786440 | tf_op jit(solution)/shard_map/ppermute | solution.py:315
  16.4 2.0 %collective-permute-start.4 = (bf16[512,256]{1,0:T(8,128)(2,1)S(1)}, bf16[512,256]{1,0:T(8,128)(2,1)S(1)}, u32[]{:S(2)}, u32[]{:S(2)}) collective-permute-start(bf16[512,256]{1,0:T(8,128)(2,1)S(1)} %copy-done.5), channel_id=1, source_target_pairs={{0,1},{1,0},{2,3},{3,2},{4,5},{5,4},{6,7},{7,6},{8,9},{9,8},{10,11... | collective-permute-start | bytes 786440 | tf_op jit(solution)/shard_map/ppermute | solution.py:315
  16.5 1.9 %collective-permute-start = (bf16[3,256,128]{2,1,0:T(8,128)(2,1)S(1)}, bf16[3,256,128]{2,1,0:T(8,128)(2,1)S(1)}, u32[]{:S(2)}, u32[]{:S(2)}) collective-permute-start(bf16[3,256,128]{2,1,0:T(8,128)(2,1)S(1)} %copy-done.8), channel_id=1, source_target_pairs={{0,1},{1,0},{2,3},{3,2},{4,5},{5,4},{6,7},{7,6},{8,9},{9,8},{10,11... | collective-permute-start | bytes 589832 | tf_op jit(solution)/shard_map/ppermute | solution.py:315
  17.0 1.4 %collective-permute-start.1 = (bf16[128,256]{1,0:T(8,128)(2,1)S(1)}, bf16[128,256]{1,0:T(8,128)(2,1)S(1)}, u32[]{:S(2)}, u32[]{:S(2)}) collective-permute-start(bf16[128,256]{1,0:T(8,128)(2,1)S(1)} %copy-done.10), channel_id=1, source_target_pairs={{0,1},{1,0},{2,3},{3,2},{4,5},{5,4},{6,7},{7,6},{8,9},{9,8},{10,11... | collective-permute-start | bytes 196616 | tf_op jit(solution)/shard_map/ppermute | solution.py:315
  17.1 1.4 %collective-permute-start.2 = (bf16[256,128]{1,0:T(8,128)(2,1)S(1)}, bf16[256,128]{1,0:T(8,128)(2,1)S(1)}, u32[]{:S(2)}, u32[]{:S(2)}) collective-permute-start(bf16[256,128]{1,0:T(8,128)(2,1)S(1)} %copy-done.11), channel_id=1, source_target_pairs={{0,1},{1,0},{2,3},{3,2},{4,5},{5,4},{6,7},{7,6},{8,9},{9,8},{10,11... | collective-permute-start | bytes 196616 | tf_op jit(solution)/shard_map/ppermute | solution.py:315
  18.4 0.6 copy-start.12
  18.4 0.6 copy-start.13
  18.5 0.7 %copy-start.9 = (bf16[3,256,128]{2,1,0:T(8,128)(2,1)}, bf16[3,256,128]{2,1,0:T(8,128)(2,1)S(1)}, u32[]{:S(2)}) copy-start(bf16[3,256,128]{2,1,0:T(8,128)(2,1)S(1)} %collective-permute-done.qkv_b) | copy-start | bytes 589828
  18.5 0.8 %copy-start.6 = (bf16[256,512]{1,0:T(8,128)(2,1)}, bf16[256,512]{1,0:T(8,128)(2,1)S(1)}, u32[]{:S(2)}) copy-start(bf16[256,512]{1,0:T(8,128)(2,1)S(1)} %collective-permute-done.3.up_b) | copy-start | bytes 786436
  19.2 0.7 %copy-start.7 = (bf16[512,256]{1,0:T(8,128)(2,1)}, bf16[512,256]{1,0:T(8,128)(2,1)S(1)}, u32[]{:S(2)}) copy-start(bf16[512,256]{1,0:T(8,128)(2,1)S(1)} %collective-permute-done.4.down_b) | copy-start | bytes 786436
  21.6 6.5 %copy-start = (bf16[256,768]{1,0:T(8,128)(2,1)}, bf16[256,768]{1,0:T(8,128)(2,1)S(1)}, u32[]{:S(2)}) copy-start(bf16[256,768]{1,0:T(8,128)(2,1)S(1)} %get-tuple-element.21.qkv_ref) | copy-start | bytes 1179652
  21.6 17.5 %copy-start.3 = (s32[4,64]{1,0:T(4,128)S(1)}, s32[4,64]{1,0:T(4,128)}, u32[]{:S(2)}) copy-start(s32[4,64]{1,0:T(4,128)} %seed_ref.3) | copy-start | bytes 3076
  34.7 19.5 %all-to-all-start.1 = ((bf16[192,8,256]{2,1,0:T(8,128)(2,1)}), bf16[192,8,256]{2,1,0:T(8,128)(2,1)S(1)}, u32[]{:S(2)}, u32[]{:S(2)}) async-start(bf16[192,8,256]{2,1,0:T(8,128)(2,1)} %lookup.3), calls=%async_computation.1 | async-start | bytes 1572864 | tf_op jit(solution)/shard_map/all_to_all | solution.py:326
  39.1 1.0 %copy-start.1 = (bf16[256,768]{1,0:T(8,128)(2,1)S(1)}, bf16[256,768]{1,0:T(8,128)(2,1)}, u32[]{:S(2)}) copy-start(bf16[256,768]{1,0:T(8,128)(2,1)} %copy-done) | copy-start | bytes 1179652
  52.4 11.5 %collective-permute-start.5 = (f32[40,4,128]{2,1,0:T(4,128)}, f32[40,4,128]{2,1,0:T(4,128)S(1)}, u32[]{:S(2)}, u32[]{:S(2)}) collective-permute-start(f32[40,4,128]{2,1,0:T(4,128)} %get-tuple-element.25), channel_id=1, source_target_pairs={{0,1},{1,0},{2,3},{3,2},{4,5},{5,4},{6,7},{7,6},{8,9},{9,8},{10,11... | collective-permute-start | bytes 245768 | tf_op jit(solution)/shard_map/ppermute | solution.py:331
  54.2 1.0 %copy-start.2 = (bf16[256,768]{1,0:T(8,128)(2,1)S(1)}, bf16[256,768]{1,0:T(8,128)(2,1)}, u32[]{:S(2)}) copy-start(bf16[256,768]{1,0:T(8,128)(2,1)} %copy-done) | copy-start | bytes 1179652
  62.6 1.3 %collective-permute-start.6 = (f32[24,4,128]{2,1,0:T(4,128)S(1)}, f32[24,4,128]{2,1,0:T(4,128)S(1)}, u32[]{:S(2)}, u32[]{:S(2)}) collective-permute-start(f32[24,4,128]{2,1,0:T(4,128)S(1)} %get-tuple-element.26), channel_id=1, source_target_pairs={{0,1},{1,0},{2,3},{3,2},{4,5},{5,4},{6,7},{7,6},{8,9},{9,8},{10,11... | collective-permute-start | bytes 147464 | tf_op jit(solution)/shard_map/ppermute | solution.py:331

commit v4 on v3

--- a/solution.py
+++ b/solution.py
@@ -9,11 +9,12 @@
 
 D = 256
 HEADS = 4
+FF = 1024
 CAPS = 4
 ITERS = 3
 FIRST = (5, 8)
 BLOCK = 8
-STEPS = (5, 3)
+STEPS = (2, 2)
 TABLE_PARTS = 4
 GROUP = 4
 F32 = jnp.float32
@@ -48,22 +49,26 @@
 
         def widen(j, carry, i=i):
             at = pl.ds(pl.multiple_of(i * rows + j * 128, 128), 128)
-            wide[at, :] = table[at, :].astype(F32)
+            for h in range(2):
+                wide[h, at, :] = table[at, h * (D // 2) : (h + 1) * (D // 2)].astype(F32)
             return carry
 
         lax.fori_loop(0, rows // 128, widen, 0)
     fetch_ids.wait()
-    spot = lax.broadcasted_iota(jnp.int32, (spots, D), 0)
+    spot = lax.broadcasted_iota(jnp.int32, (spots, D // 2), 0)
     send = []
     for d in range(pairs):
         fetch_feat[d].wait()
         first = d * per_pair + offset
 
         def one(user, carry, d=d, first=first):
-            rows = jnp.broadcast_to(wide[pl.ds(ids[0, first + user], 1), :], (spots, D))
-            for p in range(1, spots):
-                row = jnp.broadcast_to(wide[pl.ds(ids[p, first + user], 1), :], (spots, D))
-                rows = jnp.where(spot == p, row, rows)
+            halves = [None, None]
+            for p in range(spots):
+                at = pl.ds(ids[p, first + user], 1)
+                for h in range(2):
+                    row = jnp.broadcast_to(wide[h, at, :], (spots, D // 2))
+                    halves[h] = row if p == 0 else jnp.where(spot == p, row, halves[h])
+            rows = jnp.concatenate(halves, axis=1)
             out[d, user] = (feat[d, user].astype(F32) + rows).astype(BF16)
             return carry
 
@@ -91,43 +96,46 @@
             pltpu.SMEM(ids.shape, jnp.int32),
             pltpu.VMEM(block, BF16),
             pltpu.VMEM(table.shape, BF16),
-            pltpu.VMEM(table.shape, F32),
+            pltpu.VMEM((2, table.shape[0], D // 2), F32),
             pltpu.VMEM(block, BF16),
             pltpu.SemaphoreType.DMA,
             pltpu.SemaphoreType.DMA((pa_count,)),
             pltpu.SemaphoreType.DMA((TABLE_PARTS,)),
             pltpu.SemaphoreType.DMA((pa_count,)),
         ],
-        compiler_params=pltpu.CompilerParams(vmem_limit_bytes=24 << 20),
+        compiler_params=pltpu.CompilerParams(vmem_limit_bytes=12 << 20),
         name="lookup",
     )(core, *in_hbm(ids, features, table))
 
 
 def weights_kernel(
-    core_ref, qkv_a, qkv_b, out_a, out_b, bil_a, bil_b, up_a, up_b, down_a, down_b, qkv, up, tail
+    core_ref, qkv_a, qkv_b, out_a, out_b, bil_a, bil_b, up_a, up_b, down_a, down_b, all_ref
 ):
     half = D // 2
+    at = 0
     for i in range(3):
-        qkv[:, i * D : i * D + half] = qkv_a[i]
-        qkv[:, i * D + half : (i + 1) * D] = qkv_b[i]
-    ff = up_a.shape[1]
-    up[:, :ff] = up_a[...]
-    up[:, ff:] = up_b[...]
+        all_ref[at : at + D, :half] = qkv_a[i]
+        all_ref[at : at + D, half:] = qkv_b[i]
+        at += D
+    for up in (up_a, up_b):
+        for i in range(up.shape[1] // D):
+            all_ref[at : at + D, :] = up[:, i * D : (i + 1) * D]
+            at += D
 
     @pl.when(core_ref[0] == 0)
     def _():
-        tail[:D, :half] = bil_a[...]
-        tail[:D, half:] = bil_b[...]
+        all_ref[at : at + D, :half] = bil_a[...]
+        all_ref[at : at + D, half:] = bil_b[...]
 
     @pl.when(core_ref[0] != 0)
     def _():
-        tail[:D, :half] = bil_b[...]
-        tail[:D, half:] = bil_a[...]
-
-    tail[D : D + half, :] = out_a[...]
-    tail[D + half : 2 * D, :] = out_b[...]
-    tail[2 * D : 2 * D + ff, :] = down_a[...]
-    tail[2 * D + ff :, :] = down_b[...]
+        all_ref[at : at + D, :half] = bil_b[...]
+        all_ref[at : at + D, half:] = bil_a[...]
+
+    after = at + D
+    for rows in (out_a, out_b, down_a, down_b):
+        all_ref[after : after + rows.shape[0], :] = rows[...]
+        after += rows.shape[0]
 
 
 def finish_weights(core, own, other):
@@ -135,15 +143,11 @@
     operands = [w for pair in zip(own, other) for w in pair]
     return pl.pallas_call(
         weights_kernel,
-        out_shape=[
-            pltpu.VMEM((D, 3 * D), BF16),
-            pltpu.VMEM((D, 2 * ff), BF16),
-            pltpu.VMEM((2 * D + 2 * ff, D), BF16),
-        ],
+        out_shape=pltpu.VMEM((5 * D + 4 * ff, D), BF16),
         in_specs=[pl.BlockSpec(memory_space=pltpu.SMEM)]
         + [pl.BlockSpec(memory_space=pltpu.VMEM)] * len(operands),
-        out_specs=[pl.BlockSpec(memory_space=pltpu.VMEM)] * 3,
-        compiler_params=pltpu.CompilerParams(vmem_limit_bytes=16 << 20),
+        out_specs=pl.BlockSpec(memory_space=pltpu.VMEM),
+        compiler_params=pltpu.CompilerParams(vmem_limit_bytes=8 << 20),
         name="weights",
     )(core, *in_hbm(*operands))
 
@@ -158,7 +162,7 @@
     return x[:half] + x[half:]
 
 
-def encode_kernel(core_ref, x_ref, lens_ref, seed_ref, qkv_ref, up_ref, tail_ref, own_ref, other_ref, interest_ref, *, steps):
+def encode_kernel(core_ref, x_ref, lens_ref, seed_ref, w_ref, own_ref, other_ref, interest_ref, *, steps):
     step = pl.program_id(0)
     pairs, all_users, spots, _ = x_ref.shape
     block = all_users // steps
@@ -168,41 +172,71 @@
     lanes = HEADS * history
     x = x_ref[:, pl.ds(step * block, block)].astype(F32)
     x = jnp.swapaxes(x, 0, 1).reshape(rows, D).astype(BF16)
-    qkv = jnp.dot(x, qkv_ref[...], preferred_element_type=F32)
-    queries = (qkv[:, :D] * (1.0 / head**0.5)).astype(BF16)
-    keys = qkv[:, D : 2 * D].astype(BF16)
-    values = qkv[:, 2 * D :].astype(BF16)
+
+    def through(i):
+        return jnp.dot(x, w_ref[i * D : (i + 1) * D, :], preferred_element_type=F32)
+
+    queries = (through(0) * (1.0 / head**0.5)).astype(BF16)
+    keys = through(1).astype(BF16)
+    values = through(2).astype(BF16)
 
     lane_head = lax.broadcasted_iota(jnp.int32, (history, D), 1) // head
     own_head = [(lane_head == h).astype(F32).astype(BF16) for h in range(HEADS)]
+    odd_even = [own_head[0] + own_head[2], own_head[1] + own_head[3]]
     row_head = lax.broadcasted_iota(jnp.int32, (lanes, D), 0) // history
     col_head = lax.broadcasted_iota(jnp.int32, (lanes, D), 1) // head
     ones = (row_head == col_head).astype(F32).astype(BF16)
     position = lax.broadcasted_iota(jnp.int32, (block, lanes), 1) % history
-    lens = lens_ref[pl.ds(pl.multiple_of(step * block, BLOCK), block), :]
+    lens = lens_ref[pl.ds(step * block, block), :]
     key_valid = (position < lens).astype(F32)
     users = [slice(u * history, (u + 1) * history) for u in range(block)]
     scores = []
-    for at in users:
-        key_wide = jnp.concatenate([keys[at] * m for m in own_head], axis=0)
-        scores.append(
-            lax.dot_general(
-                queries[at], key_wide, (((1,), (1,)), ((), ())), preferred_element_type=F32
-            )
+    none = jnp.zeros((history, D // 2), BF16)
+    for first in range(0, block, 2):
+        pair = users[first : first + 2]
+        key_wide = jnp.concatenate([keys[at] * m for at in pair for m in odd_even], axis=0)
+        query_wide = jnp.concatenate(
+            [
+                part
+                for at in pair
+                for part in (
+                    jnp.concatenate([queries[at, : D // 2], none], axis=1),
+                    jnp.concatenate([none, queries[at, D // 2 :]], axis=1),
+                )
+            ],
+            axis=0,
         )
+        both = lax.dot_general(
+            query_wide, key_wide, (((1,), (1,)), ((), ())), preferred_element_type=F32
+        )
+        for u in range(2):
+            rows_u = both[u * D // 2 : (u + 1) * D // 2, u * D // 2 : (u + 1) * D // 2]
+            scores.append(jnp.concatenate([rows_u[:history], rows_u[history:]], axis=1))
     rounded = [
         jnp.where(key_valid[u : u + 1] > 0.0, jnp.exp(s), 0.0).astype(BF16)
         for u, s in enumerate(scores)
     ]
     totals = jnp.dot(jnp.concatenate(rounded, axis=0), ones, preferred_element_type=F32)
     weighted = []
-    for at, r in zip(users, rounded):
-        value_wide = jnp.concatenate([values[at] * m for m in own_head], axis=0)
-        weighted.append(jnp.dot(r, value_wide, preferred_element_type=F32))
+    for first in range(0, block, 2):
+        pair = users[first : first + 2]
+        value_wide = jnp.concatenate([values[at] * m for at in pair for m in odd_even], axis=0)
+        prob_wide = []
+        for u in range(2):
+            for g in range(2):
+                part = rounded[first + u][:, g * D // 2 : (g + 1) * D // 2]
+                prob_wide.append(jnp.concatenate([part, none] if u == 0 else [none, part], axis=1))
+        both = jnp.dot(jnp.concatenate(prob_wide, axis=0), value_wide, preferred_element_type=F32)
+        for u in range(2):
+            rows_u = both[u * D // 2 : (u + 1) * D // 2]
+            weighted.append(
+                jnp.concatenate([rows_u[:history, : D // 2], rows_u[history:, D // 2 :]], axis=1)
+            )
     attended = (jnp.concatenate(weighted, axis=0) / totals).astype(BF16)
-    hidden = jax.nn.gelu(jnp.dot(x, up_ref[...], preferred_element_type=F32)).astype(BF16)
-    everything = jnp.concatenate([x, attended, hidden], axis=1)
-    interest = jnp.dot(everything, tail_ref[...], preferred_element_type=F32).astype(BF16)
+    tail = 3 + FF // D
+    hidden = [jax.nn.gelu(through(i)).astype(BF16) for i in range(3, tail)]
+    everything = jnp.concatenate([x, attended] + hidden, axis=1)
+    interest = jnp.dot(everything, w_ref[tail * D :, :], preferred_element_type=F32).astype(BF16)
     interest_ref[pl.ds(pl.multiple_of(step * rows, rows), rows), :] = interest
 
     @pl.when(step == steps - 1)
@@ -285,7 +319,7 @@
             other_ref[b * BLOCK : (b + 1) * BLOCK, j, :] = passed[j]
 
 
-def encode(core, gathered, lens, seed, qkv, up, tail, steps):
+def encode(core, gathered, lens, seed, weights, steps):
     pa_count, users, spots, _ = gathered.shape
     vmem = pl.BlockSpec(memory_space=pltpu.VMEM)
     made = jax.ShapeDtypeStruct((users, CAPS, D // 2), F32)
@@ -293,12 +327,12 @@
         functools.partial(encode_kernel, steps=steps),
         out_shape=[made, made],
         grid=(steps,),
-        in_specs=[pl.BlockSpec(memory_space=pltpu.SMEM)] + [vmem] * 6,
+        in_specs=[pl.BlockSpec(memory_space=pltpu.SMEM)] + [vmem] * 4,
         out_specs=[vmem] * 2,
         scratch_shapes=[pltpu.VMEM((users * pa_count * spots, D), BF16)],
-        compiler_params=pltpu.CompilerParams(vmem_limit_bytes=40 << 20),
+        compiler_params=pltpu.CompilerParams(vmem_limit_bytes=24 << 20),
         name="encode",
-    )(core, gathered, lens, seed, qkv, up, tail)
+    )(core, gathered, lens, seed, weights)
 
 
 def body(
@@ -313,20 +347,21 @@
     swap = [(i, dev_count - 1 - i) for i in range(dev_count)]
     own = (w_qkv, w_out, w_bilinear, w_up, w_down)
     other = tuple(lax.ppermute(w, "dev", swap) for w in own)
-    qkv, up, tail = finish_weights(core, own, other)
+    weights = finish_weights(core, own, other)
     first = (lax.axis_index("pa") * dev_count + core_index) * per_core
     lens = lax.dynamic_slice_in_dim(lengths, first, per_core).reshape(per_core, 1)
+    cut = per_core * FIRST[0] // FIRST[1]
+    lens = [lens[:cut], lens[cut:]]
     ids = item_ids.T
-    cut = per_core * FIRST[0] // FIRST[1]
     halves = []
     for start, users, steps in ((0, cut, STEPS[0]), (cut, per_core - cut, STEPS[1])):
         if start:
-            ids, qkv, up, tail = lax.optimization_barrier((ids, qkv, up, tail))
+            ids, weights, lens = lax.optimization_barrier((ids, weights, lens))
         sent = lookup(core, ids, features, item_table, start, users, pa_count, dev_count)
         got = lax.all_to_all(sent, "pa", split_axis=0, concat_axis=0, tiled=True)
         got = got.reshape(pa_count, users, spots, D)
         kept, passed = encode(
-            core, got, lens[start : start + users], routing_seed, qkv, up, tail, steps
+            core, got, lens[int(start > 0)], routing_seed, weights, steps
         )
         halves.append((kept, lax.ppermute(passed, "dev", swap)))
     kept = jnp.concatenate([h[0] for h in halves], axis=0)

time: 65.1 us -> 59 us (0.906)
  Pallas kernels: 36.8 us -> 29.6 us
  starting transfers between devices: 13.7 us -> 16.3 us
  local copies, waits for them, and re-layouts: 4.51 us -> 2.29 us
  waiting for transfers between devices: 8.75 us -> 9.55 us
    pallas_call x2, Pallas kernels: 15.5 us -> 11.1 us  [lookup(): pl.pallas_call(functools.partial(lookup_kernel, start=start, per_pair=per...]
    pallas_call x2, Pallas kernels: 19.7 us -> 16.9 us  [encode(): pl.pallas_call(functools.partial(encode_kernel, steps=steps), out_shape=[...]
    unnamed x28 -> x20, local copies, waits for them, and re-layouts: 3.49 us -> 1.28 us
    ppermute x2, starting transfers between devices: 1.71 us -> 3.67 us  [body(): halves.append((kept, lax.ppermute(passed, 'dev', swap)))]
    all_to_all x2, waiting for transfers between devices: 6.56 us -> 8.5 us  [body(): got = lax.all_to_all(sent, 'pa', split_axis=0, concat_axis=0, tiled=True)]
    ppermute x5, waiting for transfers between devices: 0.98 us -> 0.16 us  [body(): other = tuple((lax.ppermute(w, 'dev', swap) for w in own))]
    all_to_all x2, starting transfers between devices: 9.89 us -> 10.6 us  [body(): got = lax.all_to_all(sent, 'pa', split_axis=0, concat_axis=0, tiled=True)]
  transfers between devices with their start and end apart: 9 -> 9, of which waited for: 4 -> 3; matrix products, arithmetic and copies ran while one was open for 2% -> 2% of each run, Pallas kernels for 43% -> 40%
where the time goes in v4:
time: 59 us; the launch traced here: 58.6 us
  Pallas kernels  29.6 us (50%)
  starting transfers between devices  16.3 us (28%)
  waiting for transfers between devices  9.55 us (16%)
  local copies, waits for them, and re-layouts  2.29 us (4%)
  other arithmetic  0.76 us (1%)
    pallas_call x2, Pallas kernels, encode(): pl.pallas_call(functools.partial(encode_kernel, steps=steps), out_shape=[...  16.9 us
    pallas_call x2, Pallas kernels, lookup(): pl.pallas_call(functools.partial(lookup_kernel, start=start, per_pair=per...  11.1 us
    all_to_all x2, starting transfers between devices, body(): got = lax.all_to_all(sent, 'pa', split_axis=0, concat_axis=0, tiled=True)  10.6 us
    all_to_all x2, waiting for transfers between devices, body(): got = lax.all_to_all(sent, 'pa', split_axis=0, concat_axis=0, tiled=True)  8.5 us
    ppermute x2, starting transfers between devices, body(): halves.append((kept, lax.ppermute(passed, 'dev', swap)))  3.67 us
    ppermute x5, starting transfers between devices, body(): other = tuple((lax.ppermute(w, 'dev', swap) for w in own))  2.05 us
    pallas_call x1, Pallas kernels, finish_weights(): pl.pallas_call(weights_kernel, out_shape=pltpu.VMEM((5 * D + 4 * ff, D),...  1.62 us
    unnamed x20, local copies, waits for them, and re-layouts  1.28 us
  transfers between devices with their start and end apart: 9, of which 3 were waited for; matrix products, arithmetic and copies ran while one was open for 2% of the time, Pallas kernels for 40%

profile of v4, /device:TPU:1, one launch (start us, length us, event | category | flops | bytes accessed | tf_op | source)
XLA Modules:
  0.0 58.6 jit_solution(5472628723437363189)
XLA Ops:
  0.0 6.3 %lookup.2 = bf16[320,8,256]{2,1,0:T(8,128)(2,1)} custom-call(s32[1]{0:T(128)} %bitcast.core_ref, s32[8,1024]{1,0:T(8,128)} %bitcast.9, bf16[1024,8,256]{2,1,0:T(8,128)(2,1)} %feat_hbm.3, bf16[4096,256]{1,0:T(8,128)(2,1)} %table_hbm.3), custom_call_target="tpu_custom_call" | custom-call | tf_op jit(solution)/shard_map/lookup/pallas_call | solution.py:90
  6.3 0.0 copy-start.4
  6.3 0.0 copy-start.6
  6.4 0.0 copy-start.7
  6.4 0.0 copy-start.1
  6.4 0.0 copy-start.2
  6.4 6.3 %all-to-all-start = ((bf16[320,8,256]{2,1,0:T(8,128)(2,1)}), bf16[320,8,256]{2,1,0:T(8,128)(2,1)S(1)}, u32[]{:S(2)}, u32[]{:S(2)}) async-start(bf16[320,8,256]{2,1,0:T(8,128)(2,1)} %lookup.2), calls=%async_computation | async-start | bytes 2621440 | tf_op jit(solution)/shard_map/all_to_all | solution.py:361
  12.7 0.0 copy-done.4
  12.7 1.0 %collective-permute-start = (bf16[3,256,128]{2,1,0:T(8,128)(2,1)S(1)}, bf16[3,256,128]{2,1,0:T(8,128)(2,1)S(1)}, u32[]{:S(2)}, u32[]{:S(2)}) collective-permute-start(bf16[3,256,128]{2,1,0:T(8,128)(2,1)S(1)} %copy-done.4), channel_id=1, source_target_pairs={{0,1},{1,0},{2,3},{3,2},{4,5},{5,4},{6,7},{7,6},{8,9},{9,8},{10,11... | collective-permute-start | bytes 589832 | tf_op jit(solution)/shard_map/ppermute | solution.py:349
  13.8 0.0 copy-done.6
  13.8 0.1 collective-permute-start.1
  13.9 0.0 copy-done.7
  13.9 0.4 collective-permute-start.2
  14.3 0.0 copy-done.1
  14.3 0.1 collective-permute-start.3
  14.4 0.0 copy-done.2
  14.4 0.4 collective-permute-start.4
  14.8 0.8 %dynamic_slice.3 = s32[64]{0:T(128)S(1)} dynamic-slice(s32[1024]{0:T(1024)} %param.13, s32[]{:T(128)S(6)} %select_n.12), dynamic_slice_sizes={64} | dynamic-slice | bytes 516 | tf_op jit(solution)/shard_map/dynamic_slice | solution.py:352
  15.6 0.1 slice_bitcast_fusion
  15.6 0.0 collective-permute-done.1.out_b
  15.6 0.0 copy-start.8
  15.7 0.0 collective-permute-done.2.bil_b
  15.7 0.0 copy-start.9
  15.7 0.0 collective-permute-done.qkv_b
  15.7 0.0 copy-start.5
  15.7 0.2 collective-permute-done.3.up_b
  15.8 0.4 copy-done.8
  16.3 0.0 copy-done.9
  16.3 0.0 copy-done.5
  16.4 0.0 copy-start.3
  16.4 0.7 %copy-done.3 = bf16[256,512]{1,0:T(8,128)(2,1)} copy-done((bf16[256,512]{1,0:T(8,128)(2,1)}, bf16[256,512]{1,0:T(8,128)(2,1)S(1)}, u32[]{:S(2)}) %copy-start.3) | copy-done | bytes 262168
  17.1 0.0 collective-permute-done.4.down_b
  17.1 1.6 %weights.1.w_ref = bf16[3328,256]{1,0:T(8,128)(2,1)S(1)} custom-call(s32[1]{0:T(128)} %bitcast.core_ref, bf16[3,256,128]{2,1,0:T(8,128)(2,1)} %qkv_a.1, bf16[3,256,128]{2,1,0:T(8,128)(2,1)} %copy-done.5, bf16[128,256]{1,0:T(8,128)(2,1)} %out_a.1, bf16[128,256]{1,0:T(8,128)(2,1)} %copy-done.8, bf16[256,128]{1,0:T(8,128)(2,1)} %bil_a.1, ...), custom_call_target="tpu_custom_call" | custom-call | tf_op jit(solution)/shard_map/weights/pallas_call | solution.py:144
  18.7 0.0 copy-start
  18.7 4.8 %lookup.3 = bf16[192,8,256]{2,1,0:T(8,128)(2,1)} custom-call(s32[1]{0:T(128)} %bitcast.core_ref, s32[8,1024]{1,0:T(8,128)} %bitcast.10, bf16[1024,8,256]{2,1,0:T(8,128)(2,1)} %feat_hbm.3, bf16[4096,256]{1,0:T(8,128)(2,1)} %table_hbm.3), custom_call_target="tpu_custom_call" | custom-call | tf_op jit(solution)/shard_map/lookup/pallas_call | solution.py:90
  23.5 8.5 %all-to-all-done = bf16[320,8,256]{2,1,0:T(8,128)(2,1)S(1)} async-done(((bf16[320,8,256]{2,1,0:T(8,128)(2,1)}), bf16[320,8,256]{2,1,0:T(8,128)(2,1)S(1)}, u32[]{:S(2)}, u32[]{:S(2)}) %all-to-all-start) | async-done | bytes 1310752 | tf_op jit(solution)/shard_map/all_to_all | solution.py:361
  32.0 4.2 %all-to-all-start.1 = ((bf16[192,8,256]{2,1,0:T(8,128)(2,1)}), bf16[192,8,256]{2,1,0:T(8,128)(2,1)}, u32[]{:S(2)}, u32[]{:S(2)}) async-start(bf16[192,8,256]{2,1,0:T(8,128)(2,1)} %lookup.3), calls=%async_computation.1 | async-start | bytes 1572864 | tf_op jit(solution)/shard_map/all_to_all | solution.py:361
  36.2 0.1 copy.11.lens_ref
  36.3 0.0 copy-done
  36.3 9.5 %encode.2 = (f32[40,4,128]{2,1,0:T(4,128)S(1)}, f32[40,4,128]{2,1,0:T(4,128)S(1)}) custom-call(s32[1]{0:T(128)} %bitcast.core_ref, bf16[8,40,8,256]{3,2,1,0:T(8,128)(2,1)S(1)} %bitcast.8, s32[40,1]{1,0:T(8,128)S(1)} %copy.11.lens_ref, s32[4,64]{1,0:T(4,128)S(1)} %copy-done, bf16[3328,256]{1,0:T(8,128)(2,1)S(1)} %weights.1.w_ref), custom_call_target="tpu_custom_call" | custom-call | tf_op jit(solution)/shard_map/encode/pallas_call | solution.py:326
  45.9 1.9 %collective-permute-start.5 = (f32[40,4,128]{2,1,0:T(4,128)S(1)}, f32[40,4,128]{2,1,0:T(4,128)S(1)}, u32[]{:S(2)}, u32[]{:S(2)}) collective-permute-start(f32[40,4,128]{2,1,0:T(4,128)S(1)} %get-tuple-element.17), channel_id=1, source_target_pairs={{0,1},{1,0},{2,3},{3,2},{4,5},{5,4},{6,7},{7,6},{8,9},{9,8},{10,11... | collective-permute-start | bytes 245768 | tf_op jit(solution)/shard_map/ppermute | solution.py:366
  47.7 0.1 copy.12.lens_ref
  47.8 0.0 all-to-all-done.1
  47.8 7.3 %encode.3 = (f32[24,4,128]{2,1,0:T(4,128)S(1)}, f32[24,4,128]{2,1,0:T(4,128)S(1)}) custom-call(s32[1]{0:T(128)} %bitcast.core_ref, bf16[8,24,8,256]{3,2,1,0:T(8,128)(2,1)} %bitcast.5.x_ref, s32[24,1]{1,0:T(8,128)S(1)} %copy.12.lens_ref, s32[4,64]{1,0:T(4,128)S(1)} %copy-done, bf16[3328,256]{1,0:T(8,128)(2,1)S(1)} %weights.1.w_ref), custom_call_target="tpu_custom_call" | custom-call | tf_op jit(solution)/shard_map/encode/pallas_call | solution.py:326
  55.2 1.8 %collective-permute-start.6 = (f32[24,4,128]{2,1,0:T(4,128)S(1)}, f32[24,4,128]{2,1,0:T(4,128)S(1)}, u32[]{:S(2)}, u32[]{:S(2)}) collective-permute-start(f32[24,4,128]{2,1,0:T(4,128)S(1)} %get-tuple-element.18), channel_id=1, source_target_pairs={{0,1},{1,0},{2,3},{3,2},{4,5},{5,4},{6,7},{7,6},{8,9},{9,8},{10,11... | collective-permute-start | bytes 147464 | tf_op jit(solution)/shard_map/ppermute | solution.py:366
  57.0 0.9 %collective-permute-done.6 = f32[24,4,128]{2,1,0:T(4,128)S(1)} collective-permute-done((f32[24,4,128]{2,1,0:T(4,128)S(1)}, f32[24,4,128]{2,1,0:T(4,128)S(1)}, u32[]{:S(2)}, u32[]{:S(2)}) %collective-permute-start.6) | collective-permute-done | bytes 49184 | tf_op jit(solution)/shard_map/ppermute | solution.py:366
  57.8 0.0 collective-permute-done.5
  57.8 0.8 %maximum_select_fusion = f32[128,4,128]{2,1,0:T(4,128)} fusion(f32[24,4,128]{2,1,0:T(4,128)S(1)} %collective-permute-done.6, f32[40,4,128]{2,1,0:T(4,128)S(1)} %collective-permute-done.5, f32[24,4,128]{2,1,0:T(4,128)S(1)} %get-tuple-element.16, f32[40,4,128]{2,1,0:T(4,128)S(1)} %get-tuple-element.12, pred[]{:T(512)S(6)} %eq.3), kind=kLoop, calls=%fused_computation | loop fusion | flops 458752 | bytes 524289 | tf_op jit(solution)/shard_map/jit(_where)/select_n | solution.py:369
  (1 shorter events, 0.0 us)
Async XLA Ops:
  6.3 6.4 %copy-start.4 = (bf16[3,256,128]{2,1,0:T(8,128)(2,1)S(1)}, bf16[3,256,128]{2,1,0:T(8,128)(2,1)}, u32[]{:S(2)}) copy-start(bf16[3,256,128]{2,1,0:T(8,128)(2,1)} %qkv_a.1) | copy-start | bytes 589828
  6.3 7.4 %copy-start.6 = (bf16[128,256]{1,0:T(8,128)(2,1)S(1)}, bf16[128,256]{1,0:T(8,128)(2,1)}, u32[]{:S(2)}) copy-start(bf16[128,256]{1,0:T(8,128)(2,1)} %out_a.1) | copy-start | bytes 196612
  6.4 7.5 %copy-start.7 = (bf16[256,128]{1,0:T(8,128)(2,1)S(1)}, bf16[256,128]{1,0:T(8,128)(2,1)}, u32[]{:S(2)}) copy-start(bf16[256,128]{1,0:T(8,128)(2,1)} %bil_a.1) | copy-start | bytes 196612
  6.4 7.9 %copy-start.1 = (bf16[256,512]{1,0:T(8,128)(2,1)S(1)}, bf16[256,512]{1,0:T(8,128)(2,1)}, u32[]{:S(2)}) copy-start(bf16[256,512]{1,0:T(8,128)(2,1)} %up_a.1) | copy-start | bytes 786436
  6.4 8.0 %copy-start.2 = (bf16[512,256]{1,0:T(8,128)(2,1)S(1)}, bf16[512,256]{1,0:T(8,128)(2,1)}, u32[]{:S(2)}) copy-start(bf16[512,256]{1,0:T(8,128)(2,1)} %down_a.1) | copy-start | bytes 786436
  6.4 25.6 %all-to-all-start = ((bf16[320,8,256]{2,1,0:T(8,128)(2,1)}), bf16[320,8,256]{2,1,0:T(8,128)(2,1)S(1)}, u32[]{:S(2)}, u32[]{:S(2)}) async-start(bf16[320,8,256]{2,1,0:T(8,128)(2,1)} %lookup.2), calls=%async_computation | async-start | bytes 2621440 | tf_op jit(solution)/shard_map/all_to_all | solution.py:361
  12.7 2.9 %collective-permute-start = (bf16[3,256,128]{2,1,0:T(8,128)(2,1)S(1)}, bf16[3,256,128]{2,1,0:T(8,128)(2,1)S(1)}, u32[]{:S(2)}, u32[]{:S(2)}) collective-permute-start(bf16[3,256,128]{2,1,0:T(8,128)(2,1)S(1)} %copy-done.4), channel_id=1, source_target_pairs={{0,1},{1,0},{2,3},{3,2},{4,5},{5,4},{6,7},{7,6},{8,9},{9,8},{10,11... | collective-permute-start | bytes 589832 | tf_op jit(solution)/shard_map/ppermute | solution.py:349
  13.8 1.9 %collective-permute-start.1 = (bf16[128,256]{1,0:T(8,128)(2,1)S(1)}, bf16[128,256]{1,0:T(8,128)(2,1)S(1)}, u32[]{:S(2)}, u32[]{:S(2)}) collective-permute-start(bf16[128,256]{1,0:T(8,128)(2,1)S(1)} %copy-done.6), channel_id=1, source_target_pairs={{0,1},{1,0},{2,3},{3,2},{4,5},{5,4},{6,7},{7,6},{8,9},{9,8},{10,11... | collective-permute-start | bytes 196616 | tf_op jit(solution)/shard_map/ppermute | solution.py:349
  13.9 1.8 %collective-permute-start.2 = (bf16[256,128]{1,0:T(8,128)(2,1)S(1)}, bf16[256,128]{1,0:T(8,128)(2,1)S(1)}, u32[]{:S(2)}, u32[]{:S(2)}) collective-permute-start(bf16[256,128]{1,0:T(8,128)(2,1)S(1)} %copy-done.7), channel_id=1, source_target_pairs={{0,1},{1,0},{2,3},{3,2},{4,5},{5,4},{6,7},{7,6},{8,9},{9,8},{10,11... | collective-permute-start | bytes 196616 | tf_op jit(solution)/shard_map/ppermute | solution.py:349
  14.3 1.5 %collective-permute-start.3 = (bf16[256,512]{1,0:T(8,128)(2,1)S(1)}, bf16[256,512]{1,0:T(8,128)(2,1)S(1)}, u32[]{:S(2)}, u32[]{:S(2)}) collective-permute-start(bf16[256,512]{1,0:T(8,128)(2,1)S(1)} %copy-done.1), channel_id=1, source_target_pairs={{0,1},{1,0},{2,3},{3,2},{4,5},{5,4},{6,7},{7,6},{8,9},{9,8},{10,11... | collective-permute-start | bytes 786440 | tf_op jit(solution)/shard_map/ppermute | solution.py:349
  14.4 2.7 %collective-permute-start.4 = (bf16[512,256]{1,0:T(8,128)(2,1)S(1)}, bf16[512,256]{1,0:T(8,128)(2,1)}, u32[]{:S(2)}, u32[]{:S(2)}) collective-permute-start(bf16[512,256]{1,0:T(8,128)(2,1)S(1)} %copy-done.2), channel_id=1, source_target_pairs={{0,1},{1,0},{2,3},{3,2},{4,5},{5,4},{6,7},{7,6},{8,9},{9,8},{10,11... | collective-permute-start | bytes 786440 | tf_op jit(solution)/shard_map/ppermute | solution.py:349
  15.6 0.6 %copy-start.8 = (bf16[128,256]{1,0:T(8,128)(2,1)}, bf16[128,256]{1,0:T(8,128)(2,1)S(1)}, u32[]{:S(2)}) copy-start(bf16[128,256]{1,0:T(8,128)(2,1)S(1)} %collective-permute-done.1.out_b) | copy-start | bytes 196612
  15.7 0.7 %copy-start.9 = (bf16[256,128]{1,0:T(8,128)(2,1)}, bf16[256,128]{1,0:T(8,128)(2,1)S(1)}, u32[]{:S(2)}) copy-start(bf16[256,128]{1,0:T(8,128)(2,1)S(1)} %collective-permute-done.2.bil_b) | copy-start | bytes 196612
  15.7 0.7 %copy-start.5 = (bf16[3,256,128]{2,1,0:T(8,128)(2,1)}, bf16[3,256,128]{2,1,0:T(8,128)(2,1)S(1)}, u32[]{:S(2)}) copy-start(bf16[3,256,128]{2,1,0:T(8,128)(2,1)S(1)} %collective-permute-done.qkv_b) | copy-start | bytes 589828
  16.4 0.7 %copy-start.3 = (bf16[256,512]{1,0:T(8,128)(2,1)}, bf16[256,512]{1,0:T(8,128)(2,1)S(1)}, u32[]{:S(2)}) copy-start(bf16[256,512]{1,0:T(8,128)(2,1)S(1)} %collective-permute-done.3.up_b) | copy-start | bytes 786436
  18.7 17.6 %copy-start = (s32[4,64]{1,0:T(4,128)S(1)}, s32[4,64]{1,0:T(4,128)}, u32[]{:S(2)}) copy-start(s32[4,64]{1,0:T(4,128)} %seed_ref.3) | copy-start | bytes 3076
  32.0 15.8 %all-to-all-start.1 = ((bf16[192,8,256]{2,1,0:T(8,128)(2,1)}), bf16[192,8,256]{2,1,0:T(8,128)(2,1)}, u32[]{:S(2)}, u32[]{:S(2)}) async-start(bf16[192,8,256]{2,1,0:T(8,128)(2,1)} %lookup.3), calls=%async_computation.1 | async-start | bytes 1572864 | tf_op jit(solution)/shard_map/all_to_all | solution.py:361
  45.9 12.0 %collective-permute-start.5 = (f32[40,4,128]{2,1,0:T(4,128)S(1)}, f32[40,4,128]{2,1,0:T(4,128)S(1)}, u32[]{:S(2)}, u32[]{:S(2)}) collective-permute-start(f32[40,4,128]{2,1,0:T(4,128)S(1)} %get-tuple-element.17), channel_id=1, source_target_pairs={{0,1},{1,0},{2,3},{3,2},{4,5},{5,4},{6,7},{7,6},{8,9},{9,8},{10,11... | collective-permute-start | bytes 245768 | tf_op jit(solution)/shard_map/ppermute | solution.py:366
  55.2 2.7 %collective-permute-start.6 = (f32[24,4,128]{2,1,0:T(4,128)S(1)}, f32[24,4,128]{2,1,0:T(4,128)S(1)}, u32[]{:S(2)}, u32[]{:S(2)}) collective-permute-start(f32[24,4,128]{2,1,0:T(4,128)S(1)} %get-tuple-element.18), channel_id=1, source_target_pairs={{0,1},{1,0},{2,3},{3,2},{4,5},{5,4},{6,7},{7,6},{8,9},{9,8},{10,11... | collective-permute-start | bytes 147464 | tf_op jit(solution)/shard_map/ppermute | solution.py:366

commit v5 on v4

--- a/solution.py
+++ b/solution.py
@@ -16,6 +16,8 @@
 BLOCK = 8
 STEPS = (2, 2)
 TABLE_PARTS = 4
+AHEAD = 5
+Z_LO = 2
 GROUP = 4
 F32 = jnp.float32
 BF16 = jnp.bfloat16
@@ -26,9 +28,10 @@
 
 
 def lookup_kernel(
-    core_ref, ids_hbm, feat_hbm, table_hbm, out_hbm, ids, feat, table, wide, out, id_sem, feat_sem, table_sem, out_sem,
-    *, start, per_pair, per_core,
+    core_ref, to_ref, ids_hbm, feat_hbm, table_hbm, *refs, start, per_pair, per_core
 ):
+    out_hbm, scratch = refs[:-9], refs[-9:]
+    ids, feat, table, wide, out, id_sem, feat_sem, table_sem, out_sem = scratch
     pairs, users, spots, _ = feat.shape
     offset = core_ref[0] * per_core + start
     rows = table.shape[0] // TABLE_PARTS
@@ -41,7 +44,7 @@
         fetch_table[-1].start()
     fetch_feat = []
     for d in range(pairs):
-        at = pl.ds(d * per_pair + offset, users)
+        at = pl.ds(to_ref[d] * per_pair + offset, users)
         fetch_feat.append(pltpu.make_async_copy(feat_hbm.at[at], feat.at[d], feat_sem.at[d]))
         fetch_feat[-1].start()
     for i in range(TABLE_PARTS):
@@ -59,7 +62,7 @@
     send = []
     for d in range(pairs):
         fetch_feat[d].wait()
-        first = d * per_pair + offset
+        first = to_ref[d] * per_pair + offset
 
         def one(user, carry, d=d, first=first):
             halves = [None, None]
@@ -73,25 +76,28 @@
             return carry
 
         lax.fori_loop(0, users, one, 0, unroll=8)
-        send.append(
-            pltpu.make_async_copy(out.at[d], out_hbm.at[pl.ds(d * users, users)], out_sem.at[d])
-        )
+        if len(out_hbm) == pairs:
+            target = out_hbm[d]
+        else:
+            target = out_hbm[0].at[pl.ds(d * users, users)]
+        send.append(pltpu.make_async_copy(out.at[d], target, out_sem.at[d]))
         send[-1].start()
     for copy in send:
         copy.wait()
 
 
-def lookup(core, ids, features, table, start, users, pa_count, dev_count):
+def lookup(core, to, ids, features, table, start, users, pa_count, dev_count, apart):
     all_users, spots, width = features.shape
     per_pair = all_users // pa_count
     per_core = per_pair // dev_count
     block = (pa_count, users, spots, width)
     hbm = pl.BlockSpec(memory_space=pltpu.HBM)
+    outs = pa_count if apart else 1
     return pl.pallas_call(
         functools.partial(lookup_kernel, start=start, per_pair=per_pair, per_core=per_core),
-        out_shape=pltpu.HBM((pa_count * users, spots, width), BF16),
-        in_specs=[pl.BlockSpec(memory_space=pltpu.SMEM), hbm, hbm, hbm],
-        out_specs=hbm,
+        out_shape=[pltpu.HBM((users * (1 if apart else pa_count), spots, width), BF16)] * outs,
+        in_specs=[pl.BlockSpec(memory_space=pltpu.SMEM)] * 2 + [hbm, hbm, hbm],
+        out_specs=[hbm] * outs,
         scratch_shapes=[
             pltpu.SMEM(ids.shape, jnp.int32),
             pltpu.VMEM(block, BF16),
@@ -105,7 +111,7 @@
         ],
         compiler_params=pltpu.CompilerParams(vmem_limit_bytes=12 << 20),
         name="lookup",
-    )(core, *in_hbm(ids, features, table))
+    )(core, to, *in_hbm(ids, features, table))
 
 
 def weights_kernel(
@@ -162,8 +168,19 @@
     return x[:half] + x[half:]
 
 
-def encode_kernel(core_ref, x_ref, lens_ref, seed_ref, w_ref, own_ref, other_ref, interest_ref, *, steps):
+def encode_kernel(core_ref, from_ref, *refs, steps):
+    parts = refs[:-7]
+    lens_ref, seed_ref, w_ref, own_ref, other_ref, interest_ref, x_ref = refs[-7:]
     step = pl.program_id(0)
+    if len(parts) == 1:
+        x_ref = parts[0]
+    else:
+
+        @pl.when(step == 0)
+        def _():
+            for i, part in enumerate(parts):
+                x_ref[from_ref[i]] = part[...]
+
     pairs, all_users, spots, _ = x_ref.shape
     block = all_users // steps
     history = pairs * spots
@@ -319,20 +336,31 @@
             other_ref[b * BLOCK : (b + 1) * BLOCK, j, :] = passed[j]
 
 
-def encode(core, gathered, lens, seed, weights, steps):
-    pa_count, users, spots, _ = gathered.shape
+def encode(core, origin, parts, lens, seed, weights, steps):
+    users = lens.shape[0]
+    spots = parts[0].shape[-2]
+    pa_count = origin.shape[0]
+    whole = (pa_count, users, spots, D)
     vmem = pl.BlockSpec(memory_space=pltpu.VMEM)
     made = jax.ShapeDtypeStruct((users, CAPS, D // 2), F32)
     return pl.pallas_call(
         functools.partial(encode_kernel, steps=steps),
         out_shape=[made, made],
         grid=(steps,),
-        in_specs=[pl.BlockSpec(memory_space=pltpu.SMEM)] + [vmem] * 4,
+        in_specs=[pl.BlockSpec(memory_space=pltpu.SMEM)] * 2 + [vmem] * (3 + len(parts)),
         out_specs=[vmem] * 2,
-        scratch_shapes=[pltpu.VMEM((users * pa_count * spots, D), BF16)],
+        scratch_shapes=[
+            pltpu.VMEM((users * pa_count * spots, D), BF16),
+            pltpu.VMEM(whole if len(parts) > 1 else (1, 1, spots, D), BF16),
+        ],
         compiler_params=pltpu.CompilerParams(vmem_limit_bytes=24 << 20),
         name="encode",
-    )(core, gathered, lens, seed, weights)
+    )(core, origin, *parts, lens, seed, weights)
+
+
+def moved_to(place, along, across, count):
+    rest = count // Z_LO
+    return (place // Z_LO + along + rest) % rest * Z_LO + (place % Z_LO + across) % Z_LO
 
 
 def body(
@@ -353,16 +381,33 @@
     cut = per_core * FIRST[0] // FIRST[1]
     lens = [lens[:cut], lens[cut:]]
     ids = item_ids.T
+    place = lax.axis_index("pa").astype(jnp.int32)
+    moves = [(i // Z_LO, i % Z_LO) for i in range(pa_count)]
+    index = jnp.arange(pa_count, dtype=jnp.int32)
+    along, across = index // Z_LO, index % Z_LO
+    moved = [moved_to(place, along, across, pa_count), moved_to(place, -along, across, pa_count)]
+    sent = lookup(
+        core, index, ids, features, item_table, 0, cut, pa_count, dev_count, False
+    )[0]
+    got = lax.all_to_all(sent, "pa", split_axis=0, concat_axis=0, tiled=True)
+    ids, weights, lens = lax.optimization_barrier((ids, weights, lens))
+    late = lookup(
+        core, moved[0], ids, features, item_table, cut, per_core - cut, pa_count, dev_count, True
+    )
+    parts = [late[0]]
+    for i in range(1, pa_count):
+        pairs = [(p, moved_to(p, *moves[i], pa_count)) for p in range(pa_count)]
+        block = late[i]
+        if i > AHEAD:
+            block, parts[i - AHEAD] = lax.optimization_barrier((block, parts[i - AHEAD]))
+        parts.append(lax.ppermute(block, "pa", pairs))
+    got = [got.reshape(pa_count, cut, spots, D)]
     halves = []
-    for start, users, steps in ((0, cut, STEPS[0]), (cut, per_core - cut, STEPS[1])):
-        if start:
-            ids, weights, lens = lax.optimization_barrier((ids, weights, lens))
-        sent = lookup(core, ids, features, item_table, start, users, pa_count, dev_count)
-        got = lax.all_to_all(sent, "pa", split_axis=0, concat_axis=0, tiled=True)
-        got = got.reshape(pa_count, users, spots, D)
-        kept, passed = encode(
-            core, got, lens[int(start > 0)], routing_seed, weights, steps
-        )
+    for origin, given, lengths_here, steps in (
+        (index, got, lens[0], STEPS[0]),
+        (moved[1], parts, lens[1], STEPS[1]),
+    ):
+        kept, passed = encode(core, origin, given, lengths_here, routing_seed, weights, steps)
         halves.append((kept, lax.ppermute(passed, "dev", swap)))
     kept = jnp.concatenate([h[0] for h in halves], axis=0)
     came = jnp.concatenate([h[1] for h in halves], axis=0)

time: 59 us -> 59.3 us (level)
  waiting for transfers between devices: 9.55 us -> 4.36 us
  starting transfers between devices: 16.3 us -> 18.7 us
  Pallas kernels: 29.6 us -> 31.9 us
  local copies, waits for them, and re-layouts: 2.29 us -> 3.1 us
    all_to_all x2 -> x1, waiting for transfers between devices: 8.5 us -> 0.01 us  [body(): got = lax.all_to_all(sent, 'pa', split_axis=0, concat_axis=0, tiled=True)]
    ppermute x0 -> x7, starting transfers between devices: none -> 7.97 us  [body(): parts.append(lax.ppermute(block, 'pa', pairs))]
    all_to_all x2 -> x1, starting transfers between devices: 10.6 us -> 6.35 us  [body(): got = lax.all_to_all(sent, 'pa', split_axis=0, concat_axis=0, tiled=True)]
    ppermute x0 -> x7, waiting for transfers between devices: none -> 3.01 us  [body(): parts.append(lax.ppermute(block, 'pa', pairs))]
    ppermute x2, starting transfers between devices: 3.67 us -> 2.34 us  [body(): halves.append((kept, lax.ppermute(passed, 'dev', swap)))]
    pallas_call x2, Pallas kernels: 16.9 us -> 18 us  [encode(): pl.pallas_call(functools.partial(encode_kernel, steps=steps), out_shape=[...]
    pallas_call x2, Pallas kernels: 11.1 us -> 12.2 us  [lookup(): pl.pallas_call(functools.partial(lookup_kernel, start=start, per_pair=per...]
    unnamed x20 -> x26, local copies, waits for them, and re-layouts: 1.28 us -> 2.09 us
  transfers between devices with their start and end apart: 9 -> 15, of which waited for: 3 -> 3; matrix products, arithmetic and copies ran while one was open for 2% -> 2% of each run, Pallas kernels for 40% -> 42%
where the time goes in v5:
time: 59.3 us; the launch traced here: 59 us
  Pallas kernels  31.9 us (54%)
  starting transfers between devices  18.7 us (32%)
  waiting for transfers between devices  4.36 us (7%)
  local copies, waits for them, and re-layouts  3.1 us (5%)
  other arithmetic  0.79 us (1%)
    pallas_call x2, Pallas kernels, encode(): pl.pallas_call(functools.partial(encode_kernel, steps=steps), out_shape=[...  18 us
    pallas_call x2, Pallas kernels, lookup(): pl.pallas_call(functools.partial(lookup_kernel, start=start, per_pair=per...  12.2 us
    ppermute x7, starting transfers between devices, body(): parts.append(lax.ppermute(block, 'pa', pairs))  7.97 us
    all_to_all x1, starting transfers between devices, body(): got = lax.all_to_all(sent, 'pa', split_axis=0, concat_axis=0, tiled=True)  6.35 us
    ppermute x7, waiting for transfers between devices, body(): parts.append(lax.ppermute(block, 'pa', pairs))  3.01 us
    ppermute x2, starting transfers between devices, body(): halves.append((kept, lax.ppermute(passed, 'dev', swap)))  2.34 us
    unnamed x26, local copies, waits for them, and re-layouts  2.09 us
    ppermute x5, starting transfers between devices, body(): other = tuple((lax.ppermute(w, 'dev', swap) for w in own))  2.05 us
  transfers between devices with their start and end apart: 15, of which 3 were waited for; matrix products, arithmetic and copies ran while one was open for 2% of the time, Pallas kernels for 42%

profile of v5, /device:TPU:1, one launch (start us, length us, event | category | flops | bytes accessed | tf_op | source)
XLA Modules:
  0.0 59.0 jit_solution(10028209032931400607)
XLA Ops:
  0.0 6.9 %lookup.2 = bf16[320,8,256]{2,1,0:T(8,128)(2,1)} custom-call(s32[1]{0:T(128)} %bitcast.core_ref, s32[8]{0:T(128)S(1)} %iota.12.to_ref, s32[8,1024]{1,0:T(8,128)} %bitcast.8, bf16[1024,8,256]{2,1,0:T(8,128)(2,1)} %feat_hbm.3, bf16[4096,256]{1,0:T(8,128)(2,1)} %table_hbm.3), custom_call_target="tpu_custom_call" | custom-call | tf_op jit(solution)/shard_map/lookup/pallas_call | solution.py:96
  6.9 0.0 copy-start.4
  6.9 0.0 copy-start.5
  6.9 0.0 copy-start.7
  6.9 0.0 copy-start.9
  7.0 0.0 copy-start.10
  7.0 6.3 %all-to-all-start = ((bf16[320,8,256]{2,1,0:T(8,128)(2,1)}), bf16[320,8,256]{2,1,0:T(8,128)(2,1)S(1)}, u32[]{:S(2)}, u32[]{:S(2)}) async-start(bf16[320,8,256]{2,1,0:T(8,128)(2,1)} %lookup.2), calls=%async_computation | async-start | bytes 2621440 | tf_op jit(solution)/shard_map/all_to_all | solution.py:392
  13.3 1.0 %collective-permute-start.3 = (bf16[256,512]{1,0:T(8,128)(2,1)S(1)}, bf16[256,512]{1,0:T(8,128)(2,1)S(1)}, u32[]{:S(2)}, u32[]{:S(2)}) collective-permute-start(bf16[256,512]{1,0:T(8,128)(2,1)S(1)} %copy-done.4), channel_id=1, source_target_pairs={{0,1},{1,0},{2,3},{3,2},{4,5},{5,4},{6,7},{7,6},{8,9},{9,8},{10,11... | collective-permute-start | bytes 786440 | tf_op jit(solution)/shard_map/ppermute | solution.py:377
  14.4 0.1 collective-permute-start.4
  14.5 0.4 collective-permute-start
  14.9 0.1 collective-permute-start.1
  15.0 0.4 collective-permute-start.2
  15.4 0.8 %dynamic_slice.3 = s32[64]{0:T(128)S(1)} dynamic-slice(s32[1024]{0:T(1024)} %param.13, s32[]{:T(128)S(6)} %select_n.53), dynamic_slice_sizes={64} | dynamic-slice | bytes 516 | tf_op jit(solution)/shard_map/dynamic_slice | solution.py:380
  16.1 0.1 slice_bitcast_fusion
  16.2 0.0 collective-permute-done.1.out_b
  16.3 0.1 collective-permute-done.2.bil_b
  16.4 0.0 collective-permute-done.qkv_b
  16.4 0.0 collective-permute-done.3.up_b
  16.4 0.5 copy-done.11
  16.9 0.1 copy-done.12
  17.0 0.1 copy-done.8
  17.1 0.7 %copy-done.6 = bf16[256,512]{1,0:T(8,128)(2,1)} copy-done((bf16[256,512]{1,0:T(8,128)(2,1)}, bf16[256,512]{1,0:T(8,128)(2,1)S(1)}, u32[]{:S(2)}) %copy-start.6) | copy-done | bytes 262168
  17.8 0.0 collective-permute-done.4.down_b
  17.8 1.6 %weights.1.refs_3_.refs_10_ = bf16[3328,256]{1,0:T(8,128)(2,1)S(1)} custom-call(s32[1]{0:T(128)} %bitcast.core_ref, bf16[3,256,128]{2,1,0:T(8,128)(2,1)} %qkv_a.1, bf16[3,256,128]{2,1,0:T(8,128)(2,1)} %copy-done.8, bf16[128,256]{1,0:T(8,128)(2,1)} %out_a.1, bf16[128,256]{1,0:T(8,128)(2,1)} %copy-done.11, bf16[256,128]{1,0:T(8,128)(2,1)} %bil_a.1, ...), custom_call_target="tpu_custom_call" | custom-call | tf_op jit(solution)/shard_map/weights/pallas_call | solution.py:150
  19.4 0.0 copy-start.3
  19.4 5.3 %lookup.3 = (bf16[24,8,256]{2,1,0:T(8,128)(2,1)}, bf16[24,8,256]{2,1,0:T(8,128)(2,1)}, bf16[24,8,256]{2,1,0:T(8,128)(2,1)}, bf16[24,8,256]{2,1,0:T(8,128)(2,1)},...) custom-call(s32[1]{0:T(128)} %bitcast.core_ref, ...), custom_call_target="tpu_custom_call" | custom-call | tf_op jit(solution)/shard_map/lookup/pallas_call | solution.py:96
  24.8 0.0 copy-start
  24.8 1.7 %collective-permute-start.6 = (bf16[24,8,256]{2,1,0:T(8,128)(2,1)}, bf16[24,8,256]{2,1,0:T(8,128)(2,1)S(1)}, u32[]{:S(2)}, u32[]{:S(2)}) collective-permute-start(bf16[24,8,256]{2,1,0:T(8,128)(2,1)} %get-tuple-element.34), channel_id=1, source_target_pairs={{0,4},{2,6},{4,8},{6,10},{8,12},{10,14},{12,0},{14,2},{1,5},{3,7},... | collective-permute-start | bytes 294920 | tf_op jit(solution)/shard_map/ppermute | solution.py:403
  26.5 1.2 %collective-permute-start.5 = (bf16[24,8,256]{2,1,0:T(8,128)(2,1)}, bf16[24,8,256]{2,1,0:T(8,128)(2,1)S(1)}, u32[]{:S(2)}, u32[]{:S(2)}) collective-permute-start(bf16[24,8,256]{2,1,0:T(8,128)(2,1)} %get-tuple-element.31), channel_id=1, source_target_pairs={{0,2},{2,0},{4,6},{6,4},{8,10},{10,8},{12,14},{14,12},{1,3},{3,1},... | collective-permute-start | bytes 294920 | tf_op jit(solution)/shard_map/ppermute | solution.py:403
  27.7 1.2 %collective-permute-start.7 = (bf16[24,8,256]{2,1,0:T(8,128)(2,1)}, bf16[24,8,256]{2,1,0:T(8,128)(2,1)S(1)}, u32[]{:S(2)}, u32[]{:S(2)}) collective-permute-start(bf16[24,8,256]{2,1,0:T(8,128)(2,1)} %get-tuple-element.36), channel_id=1, source_target_pairs={{0,6},{2,4},{4,10},{6,8},{8,14},{10,12},{12,2},{14,0},{1,7},{3,5},... | collective-permute-start | bytes 294920 | tf_op jit(solution)/shard_map/ppermute | solution.py:403
  28.9 0.1 copy.11.refs_1_
  29.0 1.3 %collective-permute-start.8 = (bf16[24,8,256]{2,1,0:T(8,128)(2,1)}, bf16[24,8,256]{2,1,0:T(8,128)(2,1)S(1)}, u32[]{:S(2)}, u32[]{:S(2)}) collective-permute-start(bf16[24,8,256]{2,1,0:T(8,128)(2,1)} %get-tuple-element.37), channel_id=1, source_target_pairs={{0,8},{2,10},{4,12},{6,14},{8,0},{10,2},{12,4},{14,6},{1,9},{3,11}... | collective-permute-start | bytes 294920 | tf_op jit(solution)/shard_map/ppermute | solution.py:403
  30.3 2.6 %collective-permute-start.9 = (bf16[24,8,256]{2,1,0:T(8,128)(2,1)}, bf16[24,8,256]{2,1,0:T(8,128)(2,1)}, u32[]{:S(2)}, u32[]{:S(2)}) collective-permute-start(bf16[24,8,256]{2,1,0:T(8,128)(2,1)} %get-tuple-element.38), channel_id=1, source_target_pairs={{0,10},{2,8},{4,14},{6,12},{8,2},{10,0},{12,6},{14,4},{1,11},{3,9}... | collective-permute-start | bytes 294920 | tf_op jit(solution)/shard_map/ppermute | solution.py:403
  32.8 3.0 %collective-permute-done.6.refs_2_ = bf16[24,8,256]{2,1,0:T(8,128)(2,1)S(1)} collective-permute-done((bf16[24,8,256]{2,1,0:T(8,128)(2,1)}, bf16[24,8,256]{2,1,0:T(8,128)(2,1)S(1)}, u32[]{:S(2)}, u32[]{:S(2)}) %collective-permute-start.6) | collective-permute-done | bytes 98336 | tf_op jit(solution)/shard_map/ppermute | solution.py:403
  35.8 0.0 collective-permute-start.11
  35.8 0.0 collective-permute-done.5.refs_1_
  35.8 0.0 collective-permute-start.10
  35.9 0.0 all-to-all-done
  35.9 10.7 %encode.2 = (f32[40,4,128]{2,1,0:T(4,128)S(1)}, f32[40,4,128]{2,1,0:T(4,128)}) custom-call(s32[1]{0:T(128)} %bitcast.core_ref, s32[8]{0:T(128)S(1)} %iota.11.from_ref, bf16[8,40,8,256]{3,2,1,0:T(8,128)(2,1)S(1)} %bitcast.7, s32[40,1]{1,0:T(8,128)S(1)} %copy.11.refs_1_, s32[4,64]{1,0:T(4,128)S(1)} %copy-done.3, bf16[3328,256]{1,0:T(8,128)(2,1)S(1)} %weights.1.refs_3_.refs_10_), custom_call_target="tpu_custom_call" | custom-call | tf_op jit(solution)/shard_map/encode/pallas_call | solution.py:346
  46.6 0.6 %copy-done.1 = f32[40,4,128]{2,1,0:T(4,128)} copy-done((f32[40,4,128]{2,1,0:T(4,128)}, f32[40,4,128]{2,1,0:T(4,128)S(1)}, u32[]{:S(2)}) %copy-start.1) | copy-done | bytes 81944
  47.3 0.0 collective-permute-done.7.refs_3_
  47.3 2.2 %collective-permute-start.12 = (f32[40,4,128]{2,1,0:T(4,128)}, f32[40,4,128]{2,1,0:T(4,128)S(1)}, u32[]{:S(2)}, u32[]{:S(2)}) collective-permute-start(f32[40,4,128]{2,1,0:T(4,128)} %get-tuple-element.43), channel_id=1, source_target_pairs={{0,1},{1,0},{2,3},{3,2},{4,5},{5,4},{6,7},{7,6},{8,9},{9,8},{10,11... | collective-permute-start | bytes 245768 | tf_op jit(solution)/shard_map/ppermute | solution.py:411
  49.5 0.1 copy.12.refs_8_
  49.6 0.0 collective-permute-done.10.refs_6_
  49.7 7.3 %encode.3 = (f32[24,4,128]{2,1,0:T(4,128)S(1)}, f32[24,4,128]{2,1,0:T(4,128)S(1)}) custom-call(s32[1]{0:T(128)} %bitcast.core_ref, s32[8]{0:T(128)S(1)} %fusion.2.from_ref, bf16[24,8,256]{2,1,0:T(8,128)(2,1)S(1)} %copy-done, bf16[24,8,256]{2,1,0:T(8,128)(2,1)S(1)} %collective-permute-done.5.refs_1_, bf16[24,8,256]{2,1,0:T(8,128)(2,1)S(1)} %collective-permute-done.6.refs_2_, ...), custom_call_target="tpu_custom_call" | custom-call | tf_op jit(solution)/shard_map/encode/pallas_call | solution.py:346
  57.0 0.1 collective-permute-start.13
  57.1 1.2 %collective-permute-done.13 = f32[24,4,128]{2,1,0:T(4,128)S(1)} collective-permute-done((f32[24,4,128]{2,1,0:T(4,128)S(1)}, f32[24,4,128]{2,1,0:T(4,128)S(1)}, u32[]{:S(2)}, u32[]{:S(2)}) %collective-permute-start.13) | collective-permute-done | bytes 49184 | tf_op jit(solution)/shard_map/ppermute | solution.py:411
  58.3 0.8 %maximum_select_fusion = f32[128,4,128]{2,1,0:T(4,128)} fusion(f32[24,4,128]{2,1,0:T(4,128)S(1)} %collective-permute-done.13, f32[40,4,128]{2,1,0:T(4,128)S(1)} %collective-permute-done.12, f32[24,4,128]{2,1,0:T(4,128)S(1)} %get-tuple-element.42, f32[40,4,128]{2,1,0:T(4,128)S(1)} %copy-done.2, pred[]{:T(512)S(6)} %eq.12), kind=kLoop, calls=%fused_computation | loop fusion | flops 458752 | bytes 524289 | tf_op jit(solution)/shard_map/jit(_where)/select_n | solution.py:414
  (23 shorter events, 0.1 us)
Async XLA Ops:
  6.9 6.4 %copy-start.4 = (bf16[256,512]{1,0:T(8,128)(2,1)S(1)}, bf16[256,512]{1,0:T(8,128)(2,1)}, u32[]{:S(2)}) copy-start(bf16[256,512]{1,0:T(8,128)(2,1)} %up_a.1) | copy-start | bytes 786436
  6.9 7.4 %copy-start.5 = (bf16[512,256]{1,0:T(8,128)(2,1)S(1)}, bf16[512,256]{1,0:T(8,128)(2,1)}, u32[]{:S(2)}) copy-start(bf16[512,256]{1,0:T(8,128)(2,1)} %down_a.1) | copy-start | bytes 786436
  6.9 7.5 %copy-start.7 = (bf16[3,256,128]{2,1,0:T(8,128)(2,1)S(1)}, bf16[3,256,128]{2,1,0:T(8,128)(2,1)}, u32[]{:S(2)}) copy-start(bf16[3,256,128]{2,1,0:T(8,128)(2,1)} %qkv_a.1) | copy-start | bytes 589828
  6.9 7.9 %copy-start.9 = (bf16[128,256]{1,0:T(8,128)(2,1)S(1)}, bf16[128,256]{1,0:T(8,128)(2,1)}, u32[]{:S(2)}) copy-start(bf16[128,256]{1,0:T(8,128)(2,1)} %out_a.1) | copy-start | bytes 196612
  7.0 8.0 %copy-start.10 = (bf16[256,128]{1,0:T(8,128)(2,1)S(1)}, bf16[256,128]{1,0:T(8,128)(2,1)}, u32[]{:S(2)}) copy-start(bf16[256,128]{1,0:T(8,128)(2,1)} %bil_a.1) | copy-start | bytes 196612
  7.0 28.9 %all-to-all-start = ((bf16[320,8,256]{2,1,0:T(8,128)(2,1)}), bf16[320,8,256]{2,1,0:T(8,128)(2,1)S(1)}, u32[]{:S(2)}, u32[]{:S(2)}) async-start(bf16[320,8,256]{2,1,0:T(8,128)(2,1)} %lookup.2), calls=%async_computation | async-start | bytes 2621440 | tf_op jit(solution)/shard_map/all_to_all | solution.py:392
  13.3 3.1 %collective-permute-start.3 = (bf16[256,512]{1,0:T(8,128)(2,1)S(1)}, bf16[256,512]{1,0:T(8,128)(2,1)S(1)}, u32[]{:S(2)}, u32[]{:S(2)}) collective-permute-start(bf16[256,512]{1,0:T(8,128)(2,1)S(1)} %copy-done.4), channel_id=1, source_target_pairs={{0,1},{1,0},{2,3},{3,2},{4,5},{5,4},{6,7},{7,6},{8,9},{9,8},{10,11... | collective-permute-start | bytes 786440 | tf_op jit(solution)/shard_map/ppermute | solution.py:377
  14.4 3.4 %collective-permute-start.4 = (bf16[512,256]{1,0:T(8,128)(2,1)S(1)}, bf16[512,256]{1,0:T(8,128)(2,1)}, u32[]{:S(2)}, u32[]{:S(2)}) collective-permute-start(bf16[512,256]{1,0:T(8,128)(2,1)S(1)} %copy-done.5), channel_id=1, source_target_pairs={{0,1},{1,0},{2,3},{3,2},{4,5},{5,4},{6,7},{7,6},{8,9},{9,8},{10,11... | collective-permute-start | bytes 786440 | tf_op jit(solution)/shard_map/ppermute | solution.py:377
  14.5 1.9 %collective-permute-start = (bf16[3,256,128]{2,1,0:T(8,128)(2,1)S(1)}, bf16[3,256,128]{2,1,0:T(8,128)(2,1)S(1)}, u32[]{:S(2)}, u32[]{:S(2)}) collective-permute-start(bf16[3,256,128]{2,1,0:T(8,128)(2,1)S(1)} %copy-done.7), channel_id=1, source_target_pairs={{0,1},{1,0},{2,3},{3,2},{4,5},{5,4},{6,7},{7,6},{8,9},{9,8},{10,11... | collective-permute-start | bytes 589832 | tf_op jit(solution)/shard_map/ppermute | solution.py:377
  14.9 1.4 %collective-permute-start.1 = (bf16[128,256]{1,0:T(8,128)(2,1)S(1)}, bf16[128,256]{1,0:T(8,128)(2,1)S(1)}, u32[]{:S(2)}, u32[]{:S(2)}) collective-permute-start(bf16[128,256]{1,0:T(8,128)(2,1)S(1)} %copy-done.9), channel_id=1, source_target_pairs={{0,1},{1,0},{2,3},{3,2},{4,5},{5,4},{6,7},{7,6},{8,9},{9,8},{10,11... | collective-permute-start | bytes 196616 | tf_op jit(solution)/shard_map/ppermute | solution.py:377
  15.0 1.4 %collective-permute-start.2 = (bf16[256,128]{1,0:T(8,128)(2,1)S(1)}, bf16[256,128]{1,0:T(8,128)(2,1)S(1)}, u32[]{:S(2)}, u32[]{:S(2)}) collective-permute-start(bf16[256,128]{1,0:T(8,128)(2,1)S(1)} %copy-done.10), channel_id=1, source_target_pairs={{0,1},{1,0},{2,3},{3,2},{4,5},{5,4},{6,7},{7,6},{8,9},{9,8},{10,11... | collective-permute-start | bytes 196616 | tf_op jit(solution)/shard_map/ppermute | solution.py:377
  16.3 0.6 %copy-start.11 = (bf16[128,256]{1,0:T(8,128)(2,1)}, bf16[128,256]{1,0:T(8,128)(2,1)S(1)}, u32[]{:S(2)}) copy-start(bf16[128,256]{1,0:T(8,128)(2,1)S(1)} %collective-permute-done.1.out_b) | copy-start | bytes 196612
  16.4 0.6 %copy-start.12 = (bf16[256,128]{1,0:T(8,128)(2,1)}, bf16[256,128]{1,0:T(8,128)(2,1)S(1)}, u32[]{:S(2)}) copy-start(bf16[256,128]{1,0:T(8,128)(2,1)S(1)} %collective-permute-done.2.bil_b) | copy-start | bytes 196612
  16.4 0.7 %copy-start.8 = (bf16[3,256,128]{2,1,0:T(8,128)(2,1)}, bf16[3,256,128]{2,1,0:T(8,128)(2,1)S(1)}, u32[]{:S(2)}) copy-start(bf16[3,256,128]{2,1,0:T(8,128)(2,1)S(1)} %collective-permute-done.qkv_b) | copy-start | bytes 589828
  17.1 0.7 %copy-start.6 = (bf16[256,512]{1,0:T(8,128)(2,1)}, bf16[256,512]{1,0:T(8,128)(2,1)S(1)}, u32[]{:S(2)}) copy-start(bf16[256,512]{1,0:T(8,128)(2,1)S(1)} %collective-permute-done.3.up_b) | copy-start | bytes 786436
  19.4 16.5 %copy-start.3 = (s32[4,64]{1,0:T(4,128)S(1)}, s32[4,64]{1,0:T(4,128)}, u32[]{:S(2)}) copy-start(s32[4,64]{1,0:T(4,128)} %refs_9_.1) | copy-start | bytes 3076
  24.8 24.9 %copy-start = (bf16[24,8,256]{2,1,0:T(8,128)(2,1)S(1)}, bf16[24,8,256]{2,1,0:T(8,128)(2,1)}, u32[]{:S(2)}) copy-start(bf16[24,8,256]{2,1,0:T(8,128)(2,1)} %get-tuple-element.29.refs_0_) | copy-start | bytes 294916
  24.8 11.1 %collective-permute-start.6 = (bf16[24,8,256]{2,1,0:T(8,128)(2,1)}, bf16[24,8,256]{2,1,0:T(8,128)(2,1)S(1)}, u32[]{:S(2)}, u32[]{:S(2)}) collective-permute-start(bf16[24,8,256]{2,1,0:T(8,128)(2,1)} %get-tuple-element.34), channel_id=1, source_target_pairs={{0,4},{2,6},{4,8},{6,10},{8,12},{10,14},{12,0},{14,2},{1,5},{3,7},... | collective-permute-start | bytes 294920 | tf_op jit(solution)/shard_map/ppermute | solution.py:403
  26.5 9.3 %collective-permute-start.5 = (bf16[24,8,256]{2,1,0:T(8,128)(2,1)}, bf16[24,8,256]{2,1,0:T(8,128)(2,1)S(1)}, u32[]{:S(2)}, u32[]{:S(2)}) collective-permute-start(bf16[24,8,256]{2,1,0:T(8,128)(2,1)} %get-tuple-element.31), channel_id=1, source_target_pairs={{0,2},{2,0},{4,6},{6,4},{8,10},{10,8},{12,14},{14,12},{1,3},{3,1},... | collective-permute-start | bytes 294920 | tf_op jit(solution)/shard_map/ppermute | solution.py:403
  27.7 19.6 %collective-permute-start.7 = (bf16[24,8,256]{2,1,0:T(8,128)(2,1)}, bf16[24,8,256]{2,1,0:T(8,128)(2,1)S(1)}, u32[]{:S(2)}, u32[]{:S(2)}) collective-permute-start(bf16[24,8,256]{2,1,0:T(8,128)(2,1)} %get-tuple-element.36), channel_id=1, source_target_pairs={{0,6},{2,4},{4,10},{6,8},{8,14},{10,12},{12,2},{14,0},{1,7},{3,5},... | collective-permute-start | bytes 294920 | tf_op jit(solution)/shard_map/ppermute | solution.py:403
  29.0 20.7 %collective-permute-start.8 = (bf16[24,8,256]{2,1,0:T(8,128)(2,1)}, bf16[24,8,256]{2,1,0:T(8,128)(2,1)S(1)}, u32[]{:S(2)}, u32[]{:S(2)}) collective-permute-start(bf16[24,8,256]{2,1,0:T(8,128)(2,1)} %get-tuple-element.37), channel_id=1, source_target_pairs={{0,8},{2,10},{4,12},{6,14},{8,0},{10,2},{12,4},{14,6},{1,9},{3,11}... | collective-permute-start | bytes 294920 | tf_op jit(solution)/shard_map/ppermute | solution.py:403
  30.3 19.4 %collective-permute-start.9 = (bf16[24,8,256]{2,1,0:T(8,128)(2,1)}, bf16[24,8,256]{2,1,0:T(8,128)(2,1)}, u32[]{:S(2)}, u32[]{:S(2)}) collective-permute-start(bf16[24,8,256]{2,1,0:T(8,128)(2,1)} %get-tuple-element.38), channel_id=1, source_target_pairs={{0,10},{2,8},{4,14},{6,12},{8,2},{10,0},{12,6},{14,4},{1,11},{3,9}... | collective-permute-start | bytes 294920 | tf_op jit(solution)/shard_map/ppermute | solution.py:403
  35.8 13.8 %collective-permute-start.11 = (bf16[24,8,256]{2,1,0:T(8,128)(2,1)}, bf16[24,8,256]{2,1,0:T(8,128)(2,1)}, u32[]{:S(2)}, u32[]{:S(2)}) collective-permute-start(bf16[24,8,256]{2,1,0:T(8,128)(2,1)} %get-tuple-element.40), channel_id=1, source_target_pairs={{0,14},{2,12},{4,2},{6,0},{8,6},{10,4},{12,10},{14,8},{1,15},{3,13... | collective-permute-start | bytes 294920 | tf_op jit(solution)/shard_map/ppermute | solution.py:403
  35.8 13.8 %collective-permute-start.10 = (bf16[24,8,256]{2,1,0:T(8,128)(2,1)}, bf16[24,8,256]{2,1,0:T(8,128)(2,1)}, u32[]{:S(2)}, u32[]{:S(2)}) collective-permute-start(bf16[24,8,256]{2,1,0:T(8,128)(2,1)} %get-tuple-element.39), channel_id=1, source_target_pairs={{0,12},{2,14},{4,0},{6,2},{8,4},{10,6},{12,8},{14,10},{1,13},{3,15... | collective-permute-start | bytes 294920 | tf_op jit(solution)/shard_map/ppermute | solution.py:403
  46.6 0.6 %copy-start.1 = (f32[40,4,128]{2,1,0:T(4,128)}, f32[40,4,128]{2,1,0:T(4,128)S(1)}, u32[]{:S(2)}) copy-start(f32[40,4,128]{2,1,0:T(4,128)S(1)} %get-tuple-element.27) | copy-start | bytes 245764
  47.3 11.0 %copy-start.2 = (f32[40,4,128]{2,1,0:T(4,128)S(1)}, f32[40,4,128]{2,1,0:T(4,128)}, u32[]{:S(2)}) copy-start(f32[40,4,128]{2,1,0:T(4,128)} %copy-done.1) | copy-start | bytes 245764
  47.3 11.0 %collective-permute-start.12 = (f32[40,4,128]{2,1,0:T(4,128)}, f32[40,4,128]{2,1,0:T(4,128)S(1)}, u32[]{:S(2)}, u32[]{:S(2)}) collective-permute-start(f32[40,4,128]{2,1,0:T(4,128)} %get-tuple-element.43), channel_id=1, source_target_pairs={{0,1},{1,0},{2,3},{3,2},{4,5},{5,4},{6,7},{7,6},{8,9},{9,8},{10,11... | collective-permute-start | bytes 245768 | tf_op jit(solution)/shard_map/ppermute | solution.py:411
  57.0 1.3 %collective-permute-start.13 = (f32[24,4,128]{2,1,0:T(4,128)S(1)}, f32[24,4,128]{2,1,0:T(4,128)S(1)}, u32[]{:S(2)}, u32[]{:S(2)}) collective-permute-start(f32[24,4,128]{2,1,0:T(4,128)S(1)} %get-tuple-element.44), channel_id=1, source_target_pairs={{0,1},{1,0},{2,3},{3,2},{4,5},{5,4},{6,7},{7,6},{8,9},{9,8},{10,11... | collective-permute-start | bytes 147464 | tf_op jit(solution)/shard_map/ppermute | solution.py:411

commit v6 on v5

--- a/solution.py
+++ b/solution.py
@@ -12,7 +12,7 @@
 FF = 1024
 CAPS = 4
 ITERS = 3
-FIRST = (5, 8)
+FIRST = (3, 8)
 BLOCK = 8
 STEPS = (2, 2)
 TABLE_PARTS = 4
@@ -27,28 +27,38 @@
     return tuple(pltpu.with_memory_space_constraint(a, pltpu.HBM) for a in arrays)
 
 
-def lookup_kernel(
-    core_ref, to_ref, ids_hbm, feat_hbm, table_hbm, *refs, start, per_pair, per_core
-):
-    out_hbm, scratch = refs[:-9], refs[-9:]
-    ids, feat, table, wide, out, id_sem, feat_sem, table_sem, out_sem = scratch
+def moved_to(place, along, across, count):
+    rest = count // Z_LO
+    return (place // Z_LO + along + rest) % rest * Z_LO + (place % Z_LO + across) % Z_LO
+
+
+def lookup_kernel(*refs, start, per_pair, per_core, outs):
+    later = outs > 1
+    ids_hbm, feat_hbm, table_hbm = refs[:3]
+    out_hbm, refs = refs[3 : 3 + outs], refs[3 + outs :]
+    wide, table, table_sem, ids, feat, out, id_sem, feat_sem, out_sem = refs
     pairs, users, spots, _ = feat.shape
-    offset = core_ref[0] * per_core + start
-    rows = table.shape[0] // TABLE_PARTS
+    place = lax.axis_index("pa")
+    offset = lax.axis_index("dev") * per_core + start
+    if later:
+        owners = [moved_to(place, i // Z_LO, i % Z_LO, pairs) for i in range(pairs)]
+    else:
+        owners = list(range(pairs))
     fetch_ids = pltpu.make_async_copy(ids_hbm, ids, id_sem)
     fetch_ids.start()
     fetch_table = []
+    rows = table.shape[0] // TABLE_PARTS
     for i in range(TABLE_PARTS):
         at = pl.ds(i * rows, rows)
         fetch_table.append(pltpu.make_async_copy(table_hbm.at[at], table.at[at], table_sem.at[i]))
         fetch_table[-1].start()
     fetch_feat = []
     for d in range(pairs):
-        at = pl.ds(to_ref[d] * per_pair + offset, users)
+        at = pl.ds(owners[d] * per_pair + offset, users)
         fetch_feat.append(pltpu.make_async_copy(feat_hbm.at[at], feat.at[d], feat_sem.at[d]))
         fetch_feat[-1].start()
-    for i in range(TABLE_PARTS):
-        fetch_table[i].wait()
+    for i, fetch in enumerate(fetch_table):
+        fetch.wait()
 
         def widen(j, carry, i=i):
             at = pl.ds(pl.multiple_of(i * rows + j * 128, 128), 128)
@@ -62,7 +72,7 @@
     send = []
     for d in range(pairs):
         fetch_feat[d].wait()
-        first = to_ref[d] * per_pair + offset
+        first = owners[d] * per_pair + offset
 
         def one(user, carry, d=d, first=first):
             halves = [None, None]
@@ -76,7 +86,7 @@
             return carry
 
         lax.fori_loop(0, users, one, 0, unroll=8)
-        if len(out_hbm) == pairs:
+        if later:
             target = out_hbm[d]
         else:
             target = out_hbm[0].at[pl.ds(d * users, users)]
@@ -86,38 +96,43 @@
         copy.wait()
 
 
-def lookup(core, to, ids, features, table, start, users, pa_count, dev_count, apart):
+def lookup(ids, features, table, start, users, pa_count, dev_count, later):
     all_users, spots, width = features.shape
     per_pair = all_users // pa_count
     per_core = per_pair // dev_count
     block = (pa_count, users, spots, width)
     hbm = pl.BlockSpec(memory_space=pltpu.HBM)
-    outs = pa_count if apart else 1
+    outs = pa_count if later else 1
+    made = [pltpu.HBM((users * (1 if later else pa_count), spots, width), BF16)] * outs
+    scratch = [
+        pltpu.VMEM((2, table.shape[0], D // 2), F32),
+        pltpu.VMEM(table.shape, BF16),
+        pltpu.SemaphoreType.DMA((TABLE_PARTS,)),
+        pltpu.SMEM(ids.shape, jnp.int32),
+        pltpu.VMEM(block, BF16),
+        pltpu.VMEM(block, BF16),
+        pltpu.SemaphoreType.DMA,
+        pltpu.SemaphoreType.DMA((pa_count,)),
+        pltpu.SemaphoreType.DMA((pa_count,)),
+    ]
     return pl.pallas_call(
-        functools.partial(lookup_kernel, start=start, per_pair=per_pair, per_core=per_core),
-        out_shape=[pltpu.HBM((users * (1 if apart else pa_count), spots, width), BF16)] * outs,
-        in_specs=[pl.BlockSpec(memory_space=pltpu.SMEM)] * 2 + [hbm, hbm, hbm],
+        functools.partial(
+            lookup_kernel, start=start, per_pair=per_pair, per_core=per_core, outs=outs
+        ),
+        out_shape=made,
+        in_specs=[hbm, hbm, hbm],
         out_specs=[hbm] * outs,
-        scratch_shapes=[
-            pltpu.SMEM(ids.shape, jnp.int32),
-            pltpu.VMEM(block, BF16),
-            pltpu.VMEM(table.shape, BF16),
-            pltpu.VMEM((2, table.shape[0], D // 2), F32),
-            pltpu.VMEM(block, BF16),
-            pltpu.SemaphoreType.DMA,
-            pltpu.SemaphoreType.DMA((pa_count,)),
-            pltpu.SemaphoreType.DMA((TABLE_PARTS,)),
-            pltpu.SemaphoreType.DMA((pa_count,)),
-        ],
+        scratch_shapes=scratch,
         compiler_params=pltpu.CompilerParams(vmem_limit_bytes=12 << 20),
         name="lookup",
-    )(core, to, *in_hbm(ids, features, table))
+    )(*in_hbm(ids, features, table))
 
 
 def weights_kernel(
-    core_ref, qkv_a, qkv_b, out_a, out_b, bil_a, bil_b, up_a, up_b, down_a, down_b, all_ref
+    qkv_a, qkv_b, out_a, out_b, bil_a, bil_b, up_a, up_b, down_a, down_b, all_ref
 ):
     half = D // 2
+    low = lax.axis_index("dev") == 0
     at = 0
     for i in range(3):
         all_ref[at : at + D, :half] = qkv_a[i]
@@ -128,12 +143,12 @@
             all_ref[at : at + D, :] = up[:, i * D : (i + 1) * D]
             at += D
 
-    @pl.when(core_ref[0] == 0)
+    @pl.when(low)
     def _():
         all_ref[at : at + D, :half] = bil_a[...]
         all_ref[at : at + D, half:] = bil_b[...]
 
-    @pl.when(core_ref[0] != 0)
+    @pl.when(jnp.logical_not(low))
     def _():
         all_ref[at : at + D, :half] = bil_b[...]
         all_ref[at : at + D, half:] = bil_a[...]
@@ -144,18 +159,17 @@
         after += rows.shape[0]
 
 
-def finish_weights(core, own, other):
+def finish_weights(own, other):
     ff = own[3].shape[1]
-    operands = [w for pair in zip(own, other) for w in pair]
+    operands = [w for pair in zip(in_hbm(*own), other) for w in pair]
     return pl.pallas_call(
         weights_kernel,
         out_shape=pltpu.VMEM((5 * D + 4 * ff, D), BF16),
-        in_specs=[pl.BlockSpec(memory_space=pltpu.SMEM)]
-        + [pl.BlockSpec(memory_space=pltpu.VMEM)] * len(operands),
+        in_specs=[pl.BlockSpec(memory_space=pltpu.VMEM)] * len(operands),
         out_specs=pl.BlockSpec(memory_space=pltpu.VMEM),
         compiler_params=pltpu.CompilerParams(vmem_limit_bytes=8 << 20),
         name="weights",
-    )(core, *in_hbm(*operands))
+    )(*operands)
 
 
 def split(x):
@@ -168,19 +182,25 @@
     return x[:half] + x[half:]
 
 
-def encode_kernel(core_ref, from_ref, *refs, steps):
-    parts = refs[:-7]
-    lens_ref, seed_ref, w_ref, own_ref, other_ref, interest_ref, x_ref = refs[-7:]
+def encode_kernel(*refs, steps, start, later):
+    count = 2 if later else 0
+    lens_ref, seed_ref, w_ref = refs[:3]
+    parts = refs[3 + count : -4]
+    own_ref, other_ref, interest_ref, x_ref = refs[-4:]
     step = pl.program_id(0)
-    if len(parts) == 1:
-        x_ref = parts[0]
-    else:
+    if later:
+        place = lax.axis_index("pa")
 
         @pl.when(step == 0)
         def _():
             for i, part in enumerate(parts):
-                x_ref[from_ref[i]] = part[...]
-
+                origin = moved_to(place, -(i // Z_LO), i % Z_LO, len(parts))
+                x_ref[origin] = part[...]
+            own_ref[:start] = refs[3][:start]
+            other_ref[:start] = refs[4][:start]
+
+    else:
+        x_ref = parts[0]
     pairs, all_users, spots, _ = x_ref.shape
     block = all_users // steps
     history = pairs * spots
@@ -258,10 +278,10 @@
 
     @pl.when(step == steps - 1)
     def _():
-        route(core_ref, lens_ref, seed_ref, own_ref, other_ref, interest_ref, history)
-
-
-def route(core_ref, lens_ref, seed_ref, own_ref, other_ref, interest_ref, history):
+        route(lens_ref, seed_ref, own_ref, other_ref, interest_ref, history, start)
+
+
+def route(lens_ref, seed_ref, own_ref, other_ref, interest_ref, history, start):
     lanes = GROUP * history
     groups = BLOCK // GROUP
     blocks = range(interest_ref.shape[0] // (BLOCK * history))
@@ -326,41 +346,39 @@
                     chosen = jnp.where(in_group[g][None], added[g], chosen)
                 logits[b] = logits[b] + chosen
     half = D // 2
-    low_own = core_ref[0] == 0
+    low_own = lax.axis_index("dev") == 0
     for b in blocks:
         made = capsules[b].reshape(CAPS, BLOCK, D)
         low, high = made[:, :, :half], made[:, :, half:]
         kept, passed = jnp.where(low_own, low, high), jnp.where(low_own, high, low)
         for j in range(CAPS):
-            own_ref[b * BLOCK : (b + 1) * BLOCK, j, :] = kept[j]
-            other_ref[b * BLOCK : (b + 1) * BLOCK, j, :] = passed[j]
-
-
-def encode(core, origin, parts, lens, seed, weights, steps):
+            at = slice(start + b * BLOCK, start + (b + 1) * BLOCK)
+            own_ref[at, j, :] = kept[j]
+            other_ref[at, j, :] = passed[j]
+
+
+def encode(parts, lens, seed, weights, steps, start, all_users, before):
     users = lens.shape[0]
+    later = len(before) > 0
     spots = parts[0].shape[-2]
-    pa_count = origin.shape[0]
-    whole = (pa_count, users, spots, D)
+    pa_count = len(parts) if later else parts[0].shape[0]
+    whole = (pa_count, users, spots, D) if later else (1, 1, spots, D)
     vmem = pl.BlockSpec(memory_space=pltpu.VMEM)
-    made = jax.ShapeDtypeStruct((users, CAPS, D // 2), F32)
+    operands = [lens, seed, weights, *before, *parts]
+    made = pltpu.VMEM((all_users, CAPS, D // 2), F32)
     return pl.pallas_call(
-        functools.partial(encode_kernel, steps=steps),
+        functools.partial(encode_kernel, steps=steps, start=start, later=later),
         out_shape=[made, made],
         grid=(steps,),
-        in_specs=[pl.BlockSpec(memory_space=pltpu.SMEM)] * 2 + [vmem] * (3 + len(parts)),
+        in_specs=[vmem] * len(operands),
         out_specs=[vmem] * 2,
         scratch_shapes=[
             pltpu.VMEM((users * pa_count * spots, D), BF16),
-            pltpu.VMEM(whole if len(parts) > 1 else (1, 1, spots, D), BF16),
+            pltpu.VMEM(whole, BF16),
         ],
         compiler_params=pltpu.CompilerParams(vmem_limit_bytes=24 << 20),
         name="encode",
-    )(core, origin, *parts, lens, seed, weights)
-
-
-def moved_to(place, along, across, count):
-    rest = count // Z_LO
-    return (place // Z_LO + along + rest) % rest * Z_LO + (place % Z_LO + across) % Z_LO
+    )(*operands)
 
 
 def body(
@@ -370,49 +388,37 @@
     dev_count = lax.axis_size("dev")
     spots = features.shape[1]
     per_core = lengths.shape[0] // (pa_count * dev_count)
-    core_index = lax.axis_index("dev").astype(jnp.int32)
-    core = core_index.reshape(1)
+    core = lax.axis_index("dev").astype(jnp.int32)
     swap = [(i, dev_count - 1 - i) for i in range(dev_count)]
     own = (w_qkv, w_out, w_bilinear, w_up, w_down)
-    other = tuple(lax.ppermute(w, "dev", swap) for w in own)
-    weights = finish_weights(core, own, other)
-    first = (lax.axis_index("pa") * dev_count + core_index) * per_core
+    weights = finish_weights(own, tuple(lax.ppermute(w, "dev", swap) for w in own))
+    first = (lax.axis_index("pa") * dev_count + core) * per_core
     lens = lax.dynamic_slice_in_dim(lengths, first, per_core).reshape(per_core, 1)
     cut = per_core * FIRST[0] // FIRST[1]
     lens = [lens[:cut], lens[cut:]]
     ids = item_ids.T
-    place = lax.axis_index("pa").astype(jnp.int32)
-    moves = [(i // Z_LO, i % Z_LO) for i in range(pa_count)]
-    index = jnp.arange(pa_count, dtype=jnp.int32)
-    along, across = index // Z_LO, index % Z_LO
-    moved = [moved_to(place, along, across, pa_count), moved_to(place, -along, across, pa_count)]
-    sent = lookup(
-        core, index, ids, features, item_table, 0, cut, pa_count, dev_count, False
-    )[0]
+    counts = (pa_count, dev_count)
+    sent = lookup(ids, features, item_table, 0, cut, *counts, False)[0]
     got = lax.all_to_all(sent, "pa", split_axis=0, concat_axis=0, tiled=True)
+    got = got.reshape(pa_count, cut, spots, D)
     ids, weights, lens = lax.optimization_barrier((ids, weights, lens))
-    late = lookup(
-        core, moved[0], ids, features, item_table, cut, per_core - cut, pa_count, dev_count, True
-    )
+    late = lookup(ids, features, item_table, cut, per_core - cut, *counts, True)
     parts = [late[0]]
     for i in range(1, pa_count):
-        pairs = [(p, moved_to(p, *moves[i], pa_count)) for p in range(pa_count)]
+        pairs = [
+            (p, moved_to(p, i // Z_LO, i % Z_LO, pa_count)) for p in range(pa_count)
+        ]
         block = late[i]
         if i > AHEAD:
             block, parts[i - AHEAD] = lax.optimization_barrier((block, parts[i - AHEAD]))
         parts.append(lax.ppermute(block, "pa", pairs))
-    got = [got.reshape(pa_count, cut, spots, D)]
-    halves = []
-    for origin, given, lengths_here, steps in (
-        (index, got, lens[0], STEPS[0]),
-        (moved[1], parts, lens[1], STEPS[1]),
-    ):
-        kept, passed = encode(core, origin, given, lengths_here, routing_seed, weights, steps)
-        halves.append((kept, lax.ppermute(passed, "dev", swap)))
-    kept = jnp.concatenate([h[0] for h in halves], axis=0)
-    came = jnp.concatenate([h[1] for h in halves], axis=0)
+    made = encode([got], lens[0], routing_seed, weights, STEPS[0], 0, per_core, ())
+    kept, passed = encode(
+        parts, lens[1], routing_seed, weights, STEPS[1], cut, per_core, tuple(made)
+    )
+    came = lax.ppermute(passed, "dev", swap)
     return jnp.where(
-        core_index == 0,
+        core == 0,
         jnp.concatenate([kept, came], axis=0),
         jnp.concatenate([came, kept], axis=0),
     )

time: 59.3 us -> 58 us (0.978)
  Pallas kernels: 31.9 us -> 29.3 us
  waiting for transfers between devices: 4.36 us -> 6.46 us
  local copies, waits for them, and re-layouts: 3.1 us -> 1.02 us
  starting transfers between devices: 18.7 us -> 20.1 us
    ppermute x7, waiting for transfers between devices: 3.01 us -> 5.46 us  [body(): parts.append(lax.ppermute(block, 'pa', pairs))]
    unnamed x26 -> x4, local copies, waits for them, and re-layouts: 2.09 us -> 0.01 us
    ppermute x7, starting transfers between devices: 7.97 us -> 9.62 us  [body(): parts.append(lax.ppermute(block, 'pa', pairs))]
    pallas_call x2, Pallas kernels: 12.2 us -> 11 us  [lookup(): pl.pallas_call(functools.partial(lookup_kernel, start=start, per_pair=per...]
    pallas_call x2, Pallas kernels: 18 us -> 16.9 us  [encode(): pl.pallas_call(functools.partial(encode_kernel, steps=steps, start=start,...]
    all_to_all x1, starting transfers between devices: 6.35 us -> 5.47 us  [body(): got = lax.all_to_all(sent, 'pa', split_axis=0, concat_axis=0, tiled=True)]
    ppermute x7 -> x6, starting transfers between devices: 4.39 us -> 4.97 us  [the longest x1 2.53 us: body(): came = lax.ppermute(passed, 'dev', swap)]
    ppermute x7 -> x6, waiting for transfers between devices: 1.34 us -> 1 us  [the longest x1 0.99 us: body(): came = lax.ppermute(passed, 'dev', swap)]
  transfers between devices with their start and end apart: 15 -> 14, of which waited for: 3 -> 3; matrix products, arithmetic and copies ran while one was open for 2% -> 2% of each run, Pallas kernels for 42% -> 32%
where the time goes in v6:
time: 58 us; the launch traced here: 57.7 us
  Pallas kernels  29.3 us (51%)
  starting transfers between devices  20.1 us (35%)
  waiting for transfers between devices  6.46 us (11%)
  local copies, waits for them, and re-layouts  1.02 us (2%)
  other arithmetic  0.76 us (1%)
    pallas_call x2, Pallas kernels, encode(): pl.pallas_call(functools.partial(encode_kernel, steps=steps, start=start,...  16.9 us
    pallas_call x2, Pallas kernels, lookup(): pl.pallas_call(functools.partial(lookup_kernel, start=start, per_pair=per...  11 us
    ppermute x7, starting transfers between devices, body(): parts.append(lax.ppermute(block, 'pa', pairs))  9.62 us
    all_to_all x1, starting transfers between devices, body(): got = lax.all_to_all(sent, 'pa', split_axis=0, concat_axis=0, tiled=True)  5.47 us
    ppermute x7, waiting for transfers between devices, body(): parts.append(lax.ppermute(block, 'pa', pairs))  5.46 us
    ppermute x1, starting transfers between devices, body(): came = lax.ppermute(passed, 'dev', swap)  2.53 us
    ppermute x5, starting transfers between devices, body(): lax.ppermute(w, 'dev', swap)  2.44 us
    pallas_call x1, Pallas kernels, finish_weights(): pl.pallas_call(weights_kernel, out_shape=pltpu.VMEM((5 * D + 4 * ff, D),...  1.35 us
  transfers between devices with their start and end apart: 14, of which 3 were waited for; matrix products, arithmetic and copies ran while one was open for 2% of the time, Pallas kernels for 32%

profile of v6, /device:TPU:1, one launch (start us, length us, event | category | flops | bytes accessed | tf_op | source)
XLA Modules:
  0.0 57.7 jit_solution(14170586977606373634)
XLA Ops:
  0.0 1.4 %collective-permute-start.1 = (bf16[128,256]{1,0:T(8,128)(2,1)}, bf16[128,256]{1,0:T(8,128)(2,1)S(1)}, u32[]{:S(2)}, u32[]{:S(2)}) collective-permute-start(bf16[128,256]{1,0:T(8,128)(2,1)} %out_a.1), channel_id=1, source_target_pairs={{0,1},{1,0},{2,3},{3,2},{4,5},{5,4},{6,7},{7,6},{8,9},{9,8},{10,11... | collective-permute-start | bytes 196616 | tf_op jit(solution)/shard_map/ppermute | solution.py:394
  1.4 0.0 collective-permute-start.2
  1.4 0.5 collective-permute-start
  1.9 0.0 collective-permute-start.3
  1.9 0.5 collective-permute-start.4
  2.4 4.7 %lookup.2 = bf16[192,8,256]{2,1,0:T(8,128)(2,1)} custom-call(s32[8,1024]{1,0:T(8,128)} %bitcast.7, bf16[1024,8,256]{2,1,0:T(8,128)(2,1)} %refs_1_.6, bf16[4096,256]{1,0:T(8,128)(2,1)} %refs_2_.3), custom_call_target="tpu_custom_call" | custom-call | tf_op jit(solution)/shard_map/lookup/pallas_call | solution.py:118
  7.1 5.5 %all-to-all-start = ((bf16[192,8,256]{2,1,0:T(8,128)(2,1)}), bf16[192,8,256]{2,1,0:T(8,128)(2,1)S(1)}, u32[]{:S(2)}, u32[]{:S(2)}) async-start(bf16[192,8,256]{2,1,0:T(8,128)(2,1)} %lookup.2), calls=%async_computation | async-start | bytes 1572864 | tf_op jit(solution)/shard_map/all_to_all | solution.py:402
  12.6 0.8 %dynamic_slice.3 = s32[64]{0:T(128)S(1)} dynamic-slice(s32[1024]{0:T(1024)} %param.13, s32[]{:T(128)S(6)} %select_n.12), dynamic_slice_sizes={64} | dynamic-slice | bytes 516 | tf_op jit(solution)/shard_map/dynamic_slice | solution.py:396
  13.4 0.1 slice_bitcast_fusion
  13.4 0.0 collective-permute-done.1.out_b
  13.4 0.0 collective-permute-done.2.bil_b
  13.4 0.0 collective-permute-done.qkv_b
  13.4 0.0 collective-permute-done.3.up_b
  13.5 0.0 collective-permute-done.4.down_b
  13.5 1.4 %weights.1.refs_2_ = bf16[3328,256]{1,0:T(8,128)(2,1)S(1)} custom-call(bf16[3,256,128]{2,1,0:T(8,128)(2,1)} %qkv_a.1, bf16[3,256,128]{2,1,0:T(8,128)(2,1)S(1)} %collective-permute-done.qkv_b, bf16[128,256]{1,0:T(8,128)(2,1)} %out_a.1, bf16[128,256]{1,0:T(8,128)(2,1)S(1)} %collective-permute-done.1.out_b, bf16[256,128]{1,0:T(8,128)(2,1)} %bil_a.1, ...), custom_call_target="tpu_custom_call" | custom-call | tf_op jit(solution)/shard_map/weights/pallas_call | solution.py:165
  14.8 0.0 copy-start.1
  14.8 6.3 %lookup.3 = (bf16[40,8,256]{2,1,0:T(8,128)(2,1)}, bf16[40,8,256]{2,1,0:T(8,128)(2,1)}, bf16[40,8,256]{2,1,0:T(8,128)(2,1)}, bf16[40,8,256]{2,1,0:T(8,128)(2,1)},...) custom-call(s32[8,1024]{1,0:T(8,128)} %bitcast.8, ...), custom_call_target="tpu_custom_call" | custom-call | tf_op jit(solution)/shard_map/lookup/pallas_call | solution.py:118
  21.2 0.0 copy-start
  21.2 1.5 %collective-permute-start.5 = (bf16[40,8,256]{2,1,0:T(8,128)(2,1)}, bf16[40,8,256]{2,1,0:T(8,128)(2,1)S(1)}, u32[]{:S(2)}, u32[]{:S(2)}) collective-permute-start(bf16[40,8,256]{2,1,0:T(8,128)(2,1)} %get-tuple-element.33), channel_id=1, source_target_pairs={{0,2},{2,0},{4,6},{6,4},{8,10},{10,8},{12,14},{14,12},{1,3},{3,1},... | collective-permute-start | bytes 491528 | tf_op jit(solution)/shard_map/ppermute | solution.py:414
  22.7 1.2 %collective-permute-start.6 = (bf16[40,8,256]{2,1,0:T(8,128)(2,1)}, bf16[40,8,256]{2,1,0:T(8,128)(2,1)S(1)}, u32[]{:S(2)}, u32[]{:S(2)}) collective-permute-start(bf16[40,8,256]{2,1,0:T(8,128)(2,1)} %get-tuple-element.36), channel_id=1, source_target_pairs={{0,4},{2,6},{4,8},{6,10},{8,12},{10,14},{12,0},{14,2},{1,5},{3,7},... | collective-permute-start | bytes 491528 | tf_op jit(solution)/shard_map/ppermute | solution.py:414
  23.9 1.2 %collective-permute-start.7 = (bf16[40,8,256]{2,1,0:T(8,128)(2,1)}, bf16[40,8,256]{2,1,0:T(8,128)(2,1)S(1)}, u32[]{:S(2)}, u32[]{:S(2)}) collective-permute-start(bf16[40,8,256]{2,1,0:T(8,128)(2,1)} %get-tuple-element.38), channel_id=1, source_target_pairs={{0,6},{2,4},{4,10},{6,8},{8,14},{10,12},{12,2},{14,0},{1,7},{3,5},... | collective-permute-start | bytes 491528 | tf_op jit(solution)/shard_map/ppermute | solution.py:414
  25.1 1.3 %collective-permute-start.8 = (bf16[40,8,256]{2,1,0:T(8,128)(2,1)}, bf16[40,8,256]{2,1,0:T(8,128)(2,1)S(1)}, u32[]{:S(2)}, u32[]{:S(2)}) collective-permute-start(bf16[40,8,256]{2,1,0:T(8,128)(2,1)} %get-tuple-element.39), channel_id=1, source_target_pairs={{0,8},{2,10},{4,12},{6,14},{8,0},{10,2},{12,4},{14,6},{1,9},{3,11}... | collective-permute-start | bytes 491528 | tf_op jit(solution)/shard_map/ppermute | solution.py:414
  26.4 2.6 %collective-permute-start.9 = (bf16[40,8,256]{2,1,0:T(8,128)(2,1)}, bf16[40,8,256]{2,1,0:T(8,128)(2,1)S(1)}, u32[]{:S(2)}, u32[]{:S(2)}) collective-permute-start(bf16[40,8,256]{2,1,0:T(8,128)(2,1)} %get-tuple-element.40), channel_id=1, source_target_pairs={{0,10},{2,8},{4,14},{6,12},{8,2},{10,0},{12,6},{14,4},{1,11},{3,9}... | collective-permute-start | bytes 491528 | tf_op jit(solution)/shard_map/ppermute | solution.py:414
  29.0 0.0 collective-permute-done.5.refs_6_
  29.0 1.5 %collective-permute-start.10 = (bf16[40,8,256]{2,1,0:T(8,128)(2,1)}, bf16[40,8,256]{2,1,0:T(8,128)(2,1)}, u32[]{:S(2)}, u32[]{:S(2)}) collective-permute-start(bf16[40,8,256]{2,1,0:T(8,128)(2,1)} %get-tuple-element.41), channel_id=1, source_target_pairs={{0,12},{2,14},{4,0},{6,2},{8,4},{10,6},{12,8},{14,10},{1,13},{3,15... | collective-permute-start | bytes 491528 | tf_op jit(solution)/shard_map/ppermute | solution.py:414
  30.5 0.0 collective-permute-done.6.refs_7_
  30.5 0.4 collective-permute-start.11
  30.8 0.1 copy.11.refs_0_
  30.9 0.1 copy.12.refs_0_
  31.0 0.0 all-to-all-done
  31.0 0.0 copy-done.1
  31.0 6.2 %encode.2 = (f32[64,4,128]{2,1,0:T(4,128)S(1)}, f32[64,4,128]{2,1,0:T(4,128)S(1)}) custom-call(s32[24,1]{1,0:T(8,128)S(1)} %copy.11.refs_0_, s32[4,64]{1,0:T(4,128)S(1)} %copy-done.1, bf16[3328,256]{1,0:T(8,128)(2,1)S(1)} %weights.1.refs_2_, bf16[8,24,8,256]{3,2,1,0:T(8,128)(2,1)S(1)} %bitcast.6), custom_call_target="tpu_custom_call" | custom-call | tf_op jit(solution)/shard_map/encode/pallas_call | solution.py:369
  37.2 0.0 collective-permute-done.7.refs_8_
  37.2 0.0 collective-permute-done.8.refs_9_
  37.3 3.3 %collective-permute-done.9.refs_10_ = bf16[40,8,256]{2,1,0:T(8,128)(2,1)S(1)} collective-permute-done((bf16[40,8,256]{2,1,0:T(8,128)(2,1)}, bf16[40,8,256]{2,1,0:T(8,128)(2,1)S(1)}, u32[]{:S(2)}, u32[]{:S(2)}) %collective-permute-start.9) | collective-permute-done | bytes 163872 | tf_op jit(solution)/shard_map/ppermute | solution.py:414
  40.6 0.0 collective-permute-done.10.refs_11_
  40.6 2.1 %collective-permute-done.11.refs_12_ = bf16[40,8,256]{2,1,0:T(8,128)(2,1)} collective-permute-done((bf16[40,8,256]{2,1,0:T(8,128)(2,1)}, bf16[40,8,256]{2,1,0:T(8,128)(2,1)}, u32[]{:S(2)}, u32[]{:S(2)}) %collective-permute-start.11) | collective-permute-done | bytes 163872 | tf_op jit(solution)/shard_map/ppermute | solution.py:414
  42.7 0.0 copy-done
  42.7 10.7 %encode.3 = (f32[64,4,128]{2,1,0:T(4,128)S(1)}, f32[64,4,128]{2,1,0:T(4,128)S(1)}) custom-call(s32[40,1]{1,0:T(8,128)S(1)} %copy.12.refs_0_, s32[4,64]{1,0:T(4,128)S(1)} %copy-done.1, bf16[3328,256]{1,0:T(8,128)(2,1)S(1)} %weights.1.refs_2_, f32[64,4,128]{2,1,0:T(4,128)S(1)} %get-tuple-element.28.refs_3_, f32[64,4,128]{2,1,0:T(4,128)S(1)} %get-tuple-element.29.refs_4_, ...), custom_call_target="tpu_custom_call" | custom-call | tf_op jit(solution)/shard_map/encode/pallas_call | solution.py:369
  53.4 2.5 %collective-permute-start.12 = (f32[64,4,128]{2,1,0:T(4,128)S(1)}, f32[64,4,128]{2,1,0:T(4,128)S(1)}, u32[]{:S(2)}, u32[]{:S(2)}) collective-permute-start(f32[64,4,128]{2,1,0:T(4,128)S(1)} %get-tuple-element.44), channel_id=1, source_target_pairs={{0,1},{1,0},{2,3},{3,2},{4,5},{5,4},{6,7},{7,6},{8,9},{9,8},{10,11... | collective-permute-start | bytes 393224 | tf_op jit(solution)/shard_map/ppermute | solution.py:419
  55.9 1.0 %collective-permute-done.12 = f32[64,4,128]{2,1,0:T(4,128)S(1)} collective-permute-done((f32[64,4,128]{2,1,0:T(4,128)S(1)}, f32[64,4,128]{2,1,0:T(4,128)S(1)}, u32[]{:S(2)}, u32[]{:S(2)}) %collective-permute-start.12) | collective-permute-done | bytes 131104 | tf_op jit(solution)/shard_map/ppermute | solution.py:419
  56.9 0.8 %maximum_select_fusion = f32[128,4,128]{2,1,0:T(4,128)} fusion(f32[64,4,128]{2,1,0:T(4,128)S(1)} %collective-permute-done.12, f32[64,4,128]{2,1,0:T(4,128)S(1)} %get-tuple-element.43, pred[]{:T(512)S(6)} %eq.3), kind=kLoop, calls=%fused_computation | loop fusion | flops 196608 | bytes 524289 | tf_op jit(solution)/shard_map/jit(_where)/select_n | solution.py:420
  (1 shorter events, 0.0 us)
Async XLA Ops:
  0.0 13.4 %collective-permute-start.1 = (bf16[128,256]{1,0:T(8,128)(2,1)}, bf16[128,256]{1,0:T(8,128)(2,1)S(1)}, u32[]{:S(2)}, u32[]{:S(2)}) collective-permute-start(bf16[128,256]{1,0:T(8,128)(2,1)} %out_a.1), channel_id=1, source_target_pairs={{0,1},{1,0},{2,3},{3,2},{4,5},{5,4},{6,7},{7,6},{8,9},{9,8},{10,11... | collective-permute-start | bytes 196616 | tf_op jit(solution)/shard_map/ppermute | solution.py:394
  1.4 12.0 %collective-permute-start.2 = (bf16[256,128]{1,0:T(8,128)(2,1)}, bf16[256,128]{1,0:T(8,128)(2,1)S(1)}, u32[]{:S(2)}, u32[]{:S(2)}) collective-permute-start(bf16[256,128]{1,0:T(8,128)(2,1)} %bil_a.1), channel_id=1, source_target_pairs={{0,1},{1,0},{2,3},{3,2},{4,5},{5,4},{6,7},{7,6},{8,9},{9,8},{10,11... | collective-permute-start | bytes 196616 | tf_op jit(solution)/shard_map/ppermute | solution.py:394
  1.4 12.0 %collective-permute-start = (bf16[3,256,128]{2,1,0:T(8,128)(2,1)}, bf16[3,256,128]{2,1,0:T(8,128)(2,1)S(1)}, u32[]{:S(2)}, u32[]{:S(2)}) collective-permute-start(bf16[3,256,128]{2,1,0:T(8,128)(2,1)} %qkv_a.1), channel_id=1, source_target_pairs={{0,1},{1,0},{2,3},{3,2},{4,5},{5,4},{6,7},{7,6},{8,9},{9,8},{10,11... | collective-permute-start | bytes 589832 | tf_op jit(solution)/shard_map/ppermute | solution.py:394
  1.9 11.5 %collective-permute-start.3 = (bf16[256,512]{1,0:T(8,128)(2,1)}, bf16[256,512]{1,0:T(8,128)(2,1)S(1)}, u32[]{:S(2)}, u32[]{:S(2)}) collective-permute-start(bf16[256,512]{1,0:T(8,128)(2,1)} %up_a.1), channel_id=1, source_target_pairs={{0,1},{1,0},{2,3},{3,2},{4,5},{5,4},{6,7},{7,6},{8,9},{9,8},{10,11... | collective-permute-start | bytes 786440 | tf_op jit(solution)/shard_map/ppermute | solution.py:394
  1.9 11.5 %collective-permute-start.4 = (bf16[512,256]{1,0:T(8,128)(2,1)}, bf16[512,256]{1,0:T(8,128)(2,1)S(1)}, u32[]{:S(2)}, u32[]{:S(2)}) collective-permute-start(bf16[512,256]{1,0:T(8,128)(2,1)} %down_a.1), channel_id=1, source_target_pairs={{0,1},{1,0},{2,3},{3,2},{4,5},{5,4},{6,7},{7,6},{8,9},{9,8},{10,11... | collective-permute-start | bytes 786440 | tf_op jit(solution)/shard_map/ppermute | solution.py:394
  7.1 23.9 %all-to-all-start = ((bf16[192,8,256]{2,1,0:T(8,128)(2,1)}), bf16[192,8,256]{2,1,0:T(8,128)(2,1)S(1)}, u32[]{:S(2)}, u32[]{:S(2)}) async-start(bf16[192,8,256]{2,1,0:T(8,128)(2,1)} %lookup.2), calls=%async_computation | async-start | bytes 1572864 | tf_op jit(solution)/shard_map/all_to_all | solution.py:402
  14.8 16.2 %copy-start.1 = (s32[4,64]{1,0:T(4,128)S(1)}, s32[4,64]{1,0:T(4,128)}, u32[]{:S(2)}) copy-start(s32[4,64]{1,0:T(4,128)} %refs_1_.7) | copy-start | bytes 3076
  21.2 21.5 %copy-start = (bf16[40,8,256]{2,1,0:T(8,128)(2,1)S(1)}, bf16[40,8,256]{2,1,0:T(8,128)(2,1)}, u32[]{:S(2)}) copy-start(bf16[40,8,256]{2,1,0:T(8,128)(2,1)} %get-tuple-element.31.refs_5_) | copy-start | bytes 491524
  21.2 7.8 %collective-permute-start.5 = (bf16[40,8,256]{2,1,0:T(8,128)(2,1)}, bf16[40,8,256]{2,1,0:T(8,128)(2,1)S(1)}, u32[]{:S(2)}, u32[]{:S(2)}) collective-permute-start(bf16[40,8,256]{2,1,0:T(8,128)(2,1)} %get-tuple-element.33), channel_id=1, source_target_pairs={{0,2},{2,0},{4,6},{6,4},{8,10},{10,8},{12,14},{14,12},{1,3},{3,1},... | collective-permute-start | bytes 491528 | tf_op jit(solution)/shard_map/ppermute | solution.py:414
  22.7 7.7 %collective-permute-start.6 = (bf16[40,8,256]{2,1,0:T(8,128)(2,1)}, bf16[40,8,256]{2,1,0:T(8,128)(2,1)S(1)}, u32[]{:S(2)}, u32[]{:S(2)}) collective-permute-start(bf16[40,8,256]{2,1,0:T(8,128)(2,1)} %get-tuple-element.36), channel_id=1, source_target_pairs={{0,4},{2,6},{4,8},{6,10},{8,12},{10,14},{12,0},{14,2},{1,5},{3,7},... | collective-permute-start | bytes 491528 | tf_op jit(solution)/shard_map/ppermute | solution.py:414
  23.9 13.3 %collective-permute-start.7 = (bf16[40,8,256]{2,1,0:T(8,128)(2,1)}, bf16[40,8,256]{2,1,0:T(8,128)(2,1)S(1)}, u32[]{:S(2)}, u32[]{:S(2)}) collective-permute-start(bf16[40,8,256]{2,1,0:T(8,128)(2,1)} %get-tuple-element.38), channel_id=1, source_target_pairs={{0,6},{2,4},{4,10},{6,8},{8,14},{10,12},{12,2},{14,0},{1,7},{3,5},... | collective-permute-start | bytes 491528 | tf_op jit(solution)/shard_map/ppermute | solution.py:414
  25.1 12.1 %collective-permute-start.8 = (bf16[40,8,256]{2,1,0:T(8,128)(2,1)}, bf16[40,8,256]{2,1,0:T(8,128)(2,1)S(1)}, u32[]{:S(2)}, u32[]{:S(2)}) collective-permute-start(bf16[40,8,256]{2,1,0:T(8,128)(2,1)} %get-tuple-element.39), channel_id=1, source_target_pairs={{0,8},{2,10},{4,12},{6,14},{8,0},{10,2},{12,4},{14,6},{1,9},{3,11}... | collective-permute-start | bytes 491528 | tf_op jit(solution)/shard_map/ppermute | solution.py:414
  26.4 14.2 %collective-permute-start.9 = (bf16[40,8,256]{2,1,0:T(8,128)(2,1)}, bf16[40,8,256]{2,1,0:T(8,128)(2,1)S(1)}, u32[]{:S(2)}, u32[]{:S(2)}) collective-permute-start(bf16[40,8,256]{2,1,0:T(8,128)(2,1)} %get-tuple-element.40), channel_id=1, source_target_pairs={{0,10},{2,8},{4,14},{6,12},{8,2},{10,0},{12,6},{14,4},{1,11},{3,9}... | collective-permute-start | bytes 491528 | tf_op jit(solution)/shard_map/ppermute | solution.py:414
  29.0 11.6 %collective-permute-start.10 = (bf16[40,8,256]{2,1,0:T(8,128)(2,1)}, bf16[40,8,256]{2,1,0:T(8,128)(2,1)}, u32[]{:S(2)}, u32[]{:S(2)}) collective-permute-start(bf16[40,8,256]{2,1,0:T(8,128)(2,1)} %get-tuple-element.41), channel_id=1, source_target_pairs={{0,12},{2,14},{4,0},{6,2},{8,4},{10,6},{12,8},{14,10},{1,13},{3,15... | collective-permute-start | bytes 491528 | tf_op jit(solution)/shard_map/ppermute | solution.py:414
  30.5 12.2 %collective-permute-start.11 = (bf16[40,8,256]{2,1,0:T(8,128)(2,1)}, bf16[40,8,256]{2,1,0:T(8,128)(2,1)}, u32[]{:S(2)}, u32[]{:S(2)}) collective-permute-start(bf16[40,8,256]{2,1,0:T(8,128)(2,1)} %get-tuple-element.42), channel_id=1, source_target_pairs={{0,14},{2,12},{4,2},{6,0},{8,6},{10,4},{12,10},{14,8},{1,15},{3,13... | collective-permute-start | bytes 491528 | tf_op jit(solution)/shard_map/ppermute | solution.py:414
  53.4 3.5 %collective-permute-start.12 = (f32[64,4,128]{2,1,0:T(4,128)S(1)}, f32[64,4,128]{2,1,0:T(4,128)S(1)}, u32[]{:S(2)}, u32[]{:S(2)}) collective-permute-start(f32[64,4,128]{2,1,0:T(4,128)S(1)} %get-tuple-element.44), channel_id=1, source_target_pairs={{0,1},{1,0},{2,3},{3,2},{4,5},{5,4},{6,7},{7,6},{8,9},{9,8},{10,11... | collective-permute-start | bytes 393224 | tf_op jit(solution)/shard_map/ppermute | solution.py:419

commit v7 on v6

--- a/solution.py
+++ b/solution.py
@@ -12,7 +12,7 @@
 FF = 1024
 CAPS = 4
 ITERS = 3
-FIRST = (3, 8)
+FIRST = (4, 8)
 BLOCK = 8
 STEPS = (2, 2)
 TABLE_PARTS = 4
@@ -391,7 +391,6 @@
     core = lax.axis_index("dev").astype(jnp.int32)
     swap = [(i, dev_count - 1 - i) for i in range(dev_count)]
     own = (w_qkv, w_out, w_bilinear, w_up, w_down)
-    weights = finish_weights(own, tuple(lax.ppermute(w, "dev", swap) for w in own))
     first = (lax.axis_index("pa") * dev_count + core) * per_core
     lens = lax.dynamic_slice_in_dim(lengths, first, per_core).reshape(per_core, 1)
     cut = per_core * FIRST[0] // FIRST[1]
@@ -399,8 +398,10 @@
     ids = item_ids.T
     counts = (pa_count, dev_count)
     sent = lookup(ids, features, item_table, 0, cut, *counts, False)[0]
+    own, sent = lax.optimization_barrier((own, sent))
     got = lax.all_to_all(sent, "pa", split_axis=0, concat_axis=0, tiled=True)
     got = got.reshape(pa_count, cut, spots, D)
+    weights = finish_weights(own, tuple(lax.ppermute(w, "dev", swap) for w in own))
     ids, weights, lens = lax.optimization_barrier((ids, weights, lens))
     late = lookup(ids, features, item_table, cut, per_core - cut, *counts, True)
     parts = [late[0]]

time: 58 us -> 56.7 us (0.978)
  waiting for transfers between devices: 6.46 us -> 1.02 us
  local copies, waits for them, and re-layouts: 1.02 us -> 4.95 us
    ppermute x7, waiting for transfers between devices: 5.46 us -> 0.02 us  [body(): parts.append(lax.ppermute(block, 'pa', pairs))]
    unnamed x4 -> x20, local copies, waits for them, and re-layouts: 0.01 us -> 2.18 us
    optimization_barrier x2, local copies, waits for them, and re-layouts: 0.17 us -> 1.43 us  [body(): ids, weights, lens = lax.optimization_barrier((ids, weights, lens))]
    all_to_all x1, starting transfers between devices: 5.47 us -> 6.22 us  [body(): got = lax.all_to_all(sent, 'pa', split_axis=0, concat_axis=0, tiled=True)]
    ppermute x1, starting transfers between devices: 2.53 us -> 1.84 us  [body(): came = lax.ppermute(passed, 'dev', swap)]
  transfers between devices with their start and end apart: 14 -> 14, of which waited for: 3 -> 1; matrix products, arithmetic and copies ran while one was open for 2% -> 5% of each run, Pallas kernels for 32% -> 27%
where the time goes in v7:
time: 56.7 us; the launch traced here: 56.3 us
  Pallas kernels  29.6 us (52%)
  starting transfers between devices  19.8 us (35%)
  local copies, waits for them, and re-layouts  4.95 us (9%)
  waiting for transfers between devices  1.02 us (2%)
  other arithmetic  0.76 us (1%)
    pallas_call x2, Pallas kernels, encode(): pl.pallas_call(functools.partial(encode_kernel, steps=steps, start=start,...  17.2 us
    pallas_call x2, Pallas kernels, lookup(): pl.pallas_call(functools.partial(lookup_kernel, start=start, per_pair=per...  11.1 us
    ppermute x7, starting transfers between devices, body(): parts.append(lax.ppermute(block, 'pa', pairs))  9.74 us
    all_to_all x1, starting transfers between devices, body(): got = lax.all_to_all(sent, 'pa', split_axis=0, concat_axis=0, tiled=True)  6.22 us
    unnamed x20, local copies, waits for them, and re-layouts  2.18 us
    ppermute x5, starting transfers between devices, body(): lax.ppermute(w, 'dev', swap)  2.05 us
    ppermute x1, starting transfers between devices, body(): came = lax.ppermute(passed, 'dev', swap)  1.84 us
    optimization_barrier x2, local copies, waits for them, and re-layouts, body(): ids, weights, lens = lax.optimization_barrier((ids, weights, lens))  1.43 us
  transfers between devices with their start and end apart: 14, of which 1 were waited for; matrix products, arithmetic and copies ran while one was open for 5% of the time, Pallas kernels for 27%

profile of v7, /device:TPU:1, one launch (start us, length us, event | category | flops | bytes accessed | tf_op | source)
XLA Modules:
  0.0 56.3 jit_solution(7548710938215741147)
XLA Ops:
  0.0 0.0 copy-start.9
  0.0 0.0 copy-start.7
  0.0 5.5 %lookup.2 = bf16[256,8,256]{2,1,0:T(8,128)(2,1)} custom-call(s32[8,1024]{1,0:T(8,128)} %bitcast.7, bf16[1024,8,256]{2,1,0:T(8,128)(2,1)} %refs_1_.6, bf16[4096,256]{1,0:T(8,128)(2,1)} %refs_2_.3), custom_call_target="tpu_custom_call" | custom-call | tf_op jit(solution)/shard_map/lookup/pallas_call | solution.py:118
  5.6 6.2 %all-to-all-start = ((bf16[256,8,256]{2,1,0:T(8,128)(2,1)}), bf16[256,8,256]{2,1,0:T(8,128)(2,1)S(1)}, u32[]{:S(2)}, u32[]{:S(2)}) async-start(bf16[256,8,256]{2,1,0:T(8,128)(2,1)} %lookup.2), calls=%async_computation | async-start | bytes 2097152 | tf_op jit(solution)/shard_map/all_to_all | solution.py:402
  11.8 0.0 copy-done.5
  11.8 1.0 %collective-permute-start.3 = (bf16[256,512]{1,0:T(8,128)(2,1)S(1)}, bf16[256,512]{1,0:T(8,128)(2,1)S(1)}, u32[]{:S(2)}, u32[]{:S(2)}) collective-permute-start(bf16[256,512]{1,0:T(8,128)(2,1)S(1)} %copy-done.5), channel_id=1, source_target_pairs={{0,1},{1,0},{2,3},{3,2},{4,5},{5,4},{6,7},{7,6},{8,9},{9,8},{10,11... | collective-permute-start | bytes 786440 | tf_op jit(solution)/shard_map/ppermute | solution.py:404
  12.8 0.0 copy-done.6
  12.8 0.1 collective-permute-start.4
  12.9 0.4 collective-permute-start.1
  13.3 0.1 collective-permute-start.2
  13.4 0.4 collective-permute-start
  13.8 0.8 %dynamic_slice.3 = s32[64]{0:T(128)S(1)} dynamic-slice(s32[1024]{0:T(1024)} %param.13, s32[]{:T(128)S(6)} %select_n.12), dynamic_slice_sizes={64} | dynamic-slice | bytes 516 | tf_op jit(solution)/shard_map/dynamic_slice | solution.py:395
  14.6 0.6 %slice_bitcast_fusion = (s32[32,1]{0,1:T(1,128)S(1)}, s32[32,1]{0,1:T(1,128)}) fusion(s32[64]{0:T(128)S(1)} %dynamic_slice.3), kind=kLoop, calls=%fused_computation.1 | loop fusion | bytes 512 | tf_op jit(solution)/shard_map/slice | solution.py:397
  15.2 0.0 collective-permute-done.1.out_b
  15.2 0.0 collective-permute-done.2.bil_b
  15.2 0.6 %copy-done.1 = bf16[256,128]{1,0:T(8,128)(2,1)} copy-done((bf16[256,128]{1,0:T(8,128)(2,1)}, bf16[256,128]{1,0:T(8,128)(2,1)S(1)}, u32[]{:S(2)}) %copy-start.1) | copy-done | bytes 65560
  15.8 0.0 collective-permute-done.qkv_b
  15.8 0.0 collective-permute-done.3.up_b
  15.8 0.0 collective-permute-done.4.down_b
  15.8 0.0 copy-start.2
  15.9 0.8 %copy-done.2 = bf16[256,128]{1,0:T(8,128)(2,1)S(1)} copy-done((bf16[256,128]{1,0:T(8,128)(2,1)S(1)}, bf16[256,128]{1,0:T(8,128)(2,1)}, u32[]{:S(2)}) %copy-start.2) | copy-done | bytes 65560
  16.7 1.3 %weights.1.refs_2_ = bf16[3328,256]{1,0:T(8,128)(2,1)S(1)} custom-call(bf16[3,256,128]{2,1,0:T(8,128)(2,1)} %qkv_a, bf16[3,256,128]{2,1,0:T(8,128)(2,1)S(1)} %collective-permute-done.qkv_b, bf16[128,256]{1,0:T(8,128)(2,1)} %out_a, bf16[128,256]{1,0:T(8,128)(2,1)S(1)} %collective-permute-done.1.out_b, bf16[256,128]{1,0:T(8,128)(2,1)} %bil_a, ...), custom_call_target="tpu_custom_call" | custom-call | tf_op jit(solution)/shard_map/weights/pallas_call | solution.py:165
  18.0 5.6 %lookup.3 = (bf16[32,8,256]{2,1,0:T(8,128)(2,1)}, bf16[32,8,256]{2,1,0:T(8,128)(2,1)}, bf16[32,8,256]{2,1,0:T(8,128)(2,1)}, bf16[32,8,256]{2,1,0:T(8,128)(2,1)},...) custom-call(s32[8,1024]{1,0:T(8,128)} %bitcast.8, ...), custom_call_target="tpu_custom_call" | custom-call | tf_op jit(solution)/shard_map/lookup/pallas_call | solution.py:118
  23.6 0.0 copy-start
  23.6 1.8 %collective-permute-start.5 = (bf16[32,8,256]{2,1,0:T(8,128)(2,1)}, bf16[32,8,256]{2,1,0:T(8,128)(2,1)S(1)}, u32[]{:S(2)}, u32[]{:S(2)}) collective-permute-start(bf16[32,8,256]{2,1,0:T(8,128)(2,1)} %get-tuple-element.45), channel_id=1, source_target_pairs={{0,2},{2,0},{4,6},{6,4},{8,10},{10,8},{12,14},{14,12},{1,3},{3,1},... | collective-permute-start | bytes 393224 | tf_op jit(solution)/shard_map/ppermute | solution.py:415
  25.4 1.2 %collective-permute-start.6 = (bf16[32,8,256]{2,1,0:T(8,128)(2,1)}, bf16[32,8,256]{2,1,0:T(8,128)(2,1)S(1)}, u32[]{:S(2)}, u32[]{:S(2)}) collective-permute-start(bf16[32,8,256]{2,1,0:T(8,128)(2,1)} %get-tuple-element.48), channel_id=1, source_target_pairs={{0,4},{2,6},{4,8},{6,10},{8,12},{10,14},{12,0},{14,2},{1,5},{3,7},... | collective-permute-start | bytes 393224 | tf_op jit(solution)/shard_map/ppermute | solution.py:415
  26.6 1.2 %collective-permute-start.7 = (bf16[32,8,256]{2,1,0:T(8,128)(2,1)}, bf16[32,8,256]{2,1,0:T(8,128)(2,1)S(1)}, u32[]{:S(2)}, u32[]{:S(2)}) collective-permute-start(bf16[32,8,256]{2,1,0:T(8,128)(2,1)} %get-tuple-element.50), channel_id=1, source_target_pairs={{0,6},{2,4},{4,10},{6,8},{8,14},{10,12},{12,2},{14,0},{1,7},{3,5},... | collective-permute-start | bytes 393224 | tf_op jit(solution)/shard_map/ppermute | solution.py:415
  27.8 1.3 %collective-permute-start.8 = (bf16[32,8,256]{2,1,0:T(8,128)(2,1)}, bf16[32,8,256]{2,1,0:T(8,128)(2,1)S(1)}, u32[]{:S(2)}, u32[]{:S(2)}) collective-permute-start(bf16[32,8,256]{2,1,0:T(8,128)(2,1)} %get-tuple-element.51), channel_id=1, source_target_pairs={{0,8},{2,10},{4,12},{6,14},{8,0},{10,2},{12,4},{14,6},{1,9},{3,11}... | collective-permute-start | bytes 393224 | tf_op jit(solution)/shard_map/ppermute | solution.py:415
  29.1 2.6 %collective-permute-start.9 = (bf16[32,8,256]{2,1,0:T(8,128)(2,1)}, bf16[32,8,256]{2,1,0:T(8,128)(2,1)S(1)}, u32[]{:S(2)}, u32[]{:S(2)}) collective-permute-start(bf16[32,8,256]{2,1,0:T(8,128)(2,1)} %get-tuple-element.52), channel_id=1, source_target_pairs={{0,10},{2,8},{4,14},{6,12},{8,2},{10,0},{12,6},{14,4},{1,11},{3,9}... | collective-permute-start | bytes 393224 | tf_op jit(solution)/shard_map/ppermute | solution.py:415
  31.6 0.0 collective-permute-done.5.refs_6_
  31.6 1.5 %collective-permute-start.10 = (bf16[32,8,256]{2,1,0:T(8,128)(2,1)}, bf16[32,8,256]{2,1,0:T(8,128)(2,1)}, u32[]{:S(2)}, u32[]{:S(2)}) collective-permute-start(bf16[32,8,256]{2,1,0:T(8,128)(2,1)} %get-tuple-element.53), channel_id=1, source_target_pairs={{0,12},{2,14},{4,0},{6,2},{8,4},{10,6},{12,8},{14,10},{1,13},{3,15... | collective-permute-start | bytes 393224 | tf_op jit(solution)/shard_map/ppermute | solution.py:415
  33.1 0.0 collective-permute-done.6.refs_7_
  33.1 0.3 collective-permute-start.11
  33.4 0.7 %copy.12.refs_0_ = s32[32,1]{1,0:T(8,128)} copy(s32[32,1]{0,1:T(1,128)S(1)} %get-tuple-element.36) | data formatting | bytes 256 | tf_op jit(solution)/shard_map/optimization_barrier | solution.py:405
  34.1 0.7 %copy.11.refs_0_ = s32[32,1]{1,0:T(8,128)S(1)} copy(s32[32,1]{0,1:T(1,128)} %get-tuple-element.38) | data formatting | bytes 256 | tf_op jit(solution)/shard_map/optimization_barrier | solution.py:405
  34.8 0.0 all-to-all-done
  34.8 0.0 copy-start.4
  34.8 0.7 %copy-done.4 = s32[4,64]{1,0:T(4,128)S(1)} copy-done((s32[4,64]{1,0:T(4,128)S(1)}, s32[4,64]{1,0:T(4,128)}, u32[]{:S(2)}) %copy-start.4) | copy-done | bytes 1048
  35.5 8.0 %encode.2 = (f32[64,4,128]{2,1,0:T(4,128)S(1)}, f32[64,4,128]{2,1,0:T(4,128)S(1)}) custom-call(s32[32,1]{1,0:T(8,128)S(1)} %copy.11.refs_0_, s32[4,64]{1,0:T(4,128)S(1)} %copy-done.4, bf16[3328,256]{1,0:T(8,128)(2,1)S(1)} %weights.1.refs_2_, bf16[8,32,8,256]{3,2,1,0:T(8,128)(2,1)S(1)} %bitcast.6), custom_call_target="tpu_custom_call" | custom-call | tf_op jit(solution)/shard_map/encode/pallas_call | solution.py:369
  43.5 0.0 collective-permute-done.7.refs_8_
  43.5 0.0 collective-permute-done.8.refs_9_
  43.6 0.0 collective-permute-done.9.refs_10_
  43.6 0.0 collective-permute-done.10.refs_11_
  43.6 0.0 collective-permute-done.11.refs_12_
  43.6 9.1 %encode.3 = (f32[64,4,128]{2,1,0:T(4,128)S(1)}, f32[64,4,128]{2,1,0:T(4,128)S(1)}) custom-call(s32[32,1]{1,0:T(8,128)S(1)} %copy-done.3, s32[4,64]{1,0:T(4,128)S(1)} %copy-done.4, bf16[3328,256]{1,0:T(8,128)(2,1)S(1)} %weights.1.refs_2_, f32[64,4,128]{2,1,0:T(4,128)S(1)} %get-tuple-element.40.refs_3_, f32[64,4,128]{2,1,0:T(4,128)S(1)} %get-tuple-element.41.refs_4_, ...), custom_call_target="tpu_custom_call" | custom-call | tf_op jit(solution)/shard_map/encode/pallas_call | solution.py:369
  52.8 1.8 %collective-permute-start.12 = (f32[64,4,128]{2,1,0:T(4,128)S(1)}, f32[64,4,128]{2,1,0:T(4,128)S(1)}, u32[]{:S(2)}, u32[]{:S(2)}) collective-permute-start(f32[64,4,128]{2,1,0:T(4,128)S(1)} %get-tuple-element.56), channel_id=1, source_target_pairs={{0,1},{1,0},{2,3},{3,2},{4,5},{5,4},{6,7},{7,6},{8,9},{9,8},{10,11... | collective-permute-start | bytes 393224 | tf_op jit(solution)/shard_map/ppermute | solution.py:420
  54.6 1.0 %collective-permute-done.12 = f32[64,4,128]{2,1,0:T(4,128)S(1)} collective-permute-done((f32[64,4,128]{2,1,0:T(4,128)S(1)}, f32[64,4,128]{2,1,0:T(4,128)S(1)}, u32[]{:S(2)}, u32[]{:S(2)}) %collective-permute-start.12) | collective-permute-done | bytes 131104 | tf_op jit(solution)/shard_map/ppermute | solution.py:420
  55.6 0.8 %maximum_select_fusion = f32[128,4,128]{2,1,0:T(4,128)} fusion(f32[64,4,128]{2,1,0:T(4,128)S(1)} %collective-permute-done.12, f32[64,4,128]{2,1,0:T(4,128)S(1)} %get-tuple-element.55, pred[]{:T(512)S(6)} %eq.3), kind=kLoop, calls=%fused_computation | loop fusion | flops 196608 | bytes 524289 | tf_op jit(solution)/shard_map/jit(_where)/select_n | solution.py:421
  (10 shorter events, 0.0 us)
Async XLA Ops:
  0.0 11.8 %copy-start.5 = (bf16[256,512]{1,0:T(8,128)(2,1)S(1)}, bf16[256,512]{1,0:T(8,128)(2,1)}, u32[]{:S(2)}) copy-start(bf16[256,512]{1,0:T(8,128)(2,1)} %up_a) | copy-start | bytes 786436
  0.0 12.8 %copy-start.6 = (bf16[512,256]{1,0:T(8,128)(2,1)S(1)}, bf16[512,256]{1,0:T(8,128)(2,1)}, u32[]{:S(2)}) copy-start(bf16[512,256]{1,0:T(8,128)(2,1)} %down_a) | copy-start | bytes 786436
  0.0 12.9 %copy-start.8 = (bf16[128,256]{1,0:T(8,128)(2,1)S(1)}, bf16[128,256]{1,0:T(8,128)(2,1)}, u32[]{:S(2)}) copy-start(bf16[128,256]{1,0:T(8,128)(2,1)} %out_a) | copy-start | bytes 196612
  0.0 13.3 %copy-start.9 = (bf16[256,128]{1,0:T(8,128)(2,1)S(1)}, bf16[256,128]{1,0:T(8,128)(2,1)}, u32[]{:S(2)}) copy-start(bf16[256,128]{1,0:T(8,128)(2,1)} %bil_a) | copy-start | bytes 196612
  0.0 13.4 %copy-start.7 = (bf16[3,256,128]{2,1,0:T(8,128)(2,1)S(1)}, bf16[3,256,128]{2,1,0:T(8,128)(2,1)}, u32[]{:S(2)}) copy-start(bf16[3,256,128]{2,1,0:T(8,128)(2,1)} %qkv_a) | copy-start | bytes 589828
  5.6 29.2 %all-to-all-start = ((bf16[256,8,256]{2,1,0:T(8,128)(2,1)}), bf16[256,8,256]{2,1,0:T(8,128)(2,1)S(1)}, u32[]{:S(2)}, u32[]{:S(2)}) async-start(bf16[256,8,256]{2,1,0:T(8,128)(2,1)} %lookup.2), calls=%async_computation | async-start | bytes 2097152 | tf_op jit(solution)/shard_map/all_to_all | solution.py:402
  11.8 4.0 %collective-permute-start.3 = (bf16[256,512]{1,0:T(8,128)(2,1)S(1)}, bf16[256,512]{1,0:T(8,128)(2,1)S(1)}, u32[]{:S(2)}, u32[]{:S(2)}) collective-permute-start(bf16[256,512]{1,0:T(8,128)(2,1)S(1)} %copy-done.5), channel_id=1, source_target_pairs={{0,1},{1,0},{2,3},{3,2},{4,5},{5,4},{6,7},{7,6},{8,9},{9,8},{10,11... | collective-permute-start | bytes 786440 | tf_op jit(solution)/shard_map/ppermute | solution.py:404
  12.8 3.0 %collective-permute-start.4 = (bf16[512,256]{1,0:T(8,128)(2,1)S(1)}, bf16[512,256]{1,0:T(8,128)(2,1)S(1)}, u32[]{:S(2)}, u32[]{:S(2)}) collective-permute-start(bf16[512,256]{1,0:T(8,128)(2,1)S(1)} %copy-done.6), channel_id=1, source_target_pairs={{0,1},{1,0},{2,3},{3,2},{4,5},{5,4},{6,7},{7,6},{8,9},{9,8},{10,11... | collective-permute-start | bytes 786440 | tf_op jit(solution)/shard_map/ppermute | solution.py:404
  12.9 2.3 %collective-permute-start.1 = (bf16[128,256]{1,0:T(8,128)(2,1)S(1)}, bf16[128,256]{1,0:T(8,128)(2,1)S(1)}, u32[]{:S(2)}, u32[]{:S(2)}) collective-permute-start(bf16[128,256]{1,0:T(8,128)(2,1)S(1)} %copy-done.8), channel_id=1, source_target_pairs={{0,1},{1,0},{2,3},{3,2},{4,5},{5,4},{6,7},{7,6},{8,9},{9,8},{10,11... | collective-permute-start | bytes 196616 | tf_op jit(solution)/shard_map/ppermute | solution.py:404
  13.3 1.9 %collective-permute-start.2 = (bf16[256,128]{1,0:T(8,128)(2,1)S(1)}, bf16[256,128]{1,0:T(8,128)(2,1)S(1)}, u32[]{:S(2)}, u32[]{:S(2)}) collective-permute-start(bf16[256,128]{1,0:T(8,128)(2,1)S(1)} %copy-done.9), channel_id=1, source_target_pairs={{0,1},{1,0},{2,3},{3,2},{4,5},{5,4},{6,7},{7,6},{8,9},{9,8},{10,11... | collective-permute-start | bytes 196616 | tf_op jit(solution)/shard_map/ppermute | solution.py:404
  13.4 2.4 %collective-permute-start = (bf16[3,256,128]{2,1,0:T(8,128)(2,1)S(1)}, bf16[3,256,128]{2,1,0:T(8,128)(2,1)S(1)}, u32[]{:S(2)}, u32[]{:S(2)}) collective-permute-start(bf16[3,256,128]{2,1,0:T(8,128)(2,1)S(1)} %copy-done.7), channel_id=1, source_target_pairs={{0,1},{1,0},{2,3},{3,2},{4,5},{5,4},{6,7},{7,6},{8,9},{9,8},{10,11... | collective-permute-start | bytes 589832 | tf_op jit(solution)/shard_map/ppermute | solution.py:404
  15.2 0.6 %copy-start.1 = (bf16[256,128]{1,0:T(8,128)(2,1)}, bf16[256,128]{1,0:T(8,128)(2,1)S(1)}, u32[]{:S(2)}) copy-start(bf16[256,128]{1,0:T(8,128)(2,1)S(1)} %collective-permute-done.2.bil_b) | copy-start | bytes 196612
  15.8 0.8 %copy-start.2 = (bf16[256,128]{1,0:T(8,128)(2,1)S(1)}, bf16[256,128]{1,0:T(8,128)(2,1)}, u32[]{:S(2)}) copy-start(bf16[256,128]{1,0:T(8,128)(2,1)} %copy-done.1) | copy-start | bytes 196612
  23.6 20.0 %copy-start = (bf16[32,8,256]{2,1,0:T(8,128)(2,1)S(1)}, bf16[32,8,256]{2,1,0:T(8,128)(2,1)}, u32[]{:S(2)}) copy-start(bf16[32,8,256]{2,1,0:T(8,128)(2,1)} %get-tuple-element.43.refs_5_) | copy-start | bytes 393220
  23.6 8.0 %collective-permute-start.5 = (bf16[32,8,256]{2,1,0:T(8,128)(2,1)}, bf16[32,8,256]{2,1,0:T(8,128)(2,1)S(1)}, u32[]{:S(2)}, u32[]{:S(2)}) collective-permute-start(bf16[32,8,256]{2,1,0:T(8,128)(2,1)} %get-tuple-element.45), channel_id=1, source_target_pairs={{0,2},{2,0},{4,6},{6,4},{8,10},{10,8},{12,14},{14,12},{1,3},{3,1},... | collective-permute-start | bytes 393224 | tf_op jit(solution)/shard_map/ppermute | solution.py:415
  25.4 7.7 %collective-permute-start.6 = (bf16[32,8,256]{2,1,0:T(8,128)(2,1)}, bf16[32,8,256]{2,1,0:T(8,128)(2,1)S(1)}, u32[]{:S(2)}, u32[]{:S(2)}) collective-permute-start(bf16[32,8,256]{2,1,0:T(8,128)(2,1)} %get-tuple-element.48), channel_id=1, source_target_pairs={{0,4},{2,6},{4,8},{6,10},{8,12},{10,14},{12,0},{14,2},{1,5},{3,7},... | collective-permute-start | bytes 393224 | tf_op jit(solution)/shard_map/ppermute | solution.py:415
  26.6 17.0 %collective-permute-start.7 = (bf16[32,8,256]{2,1,0:T(8,128)(2,1)}, bf16[32,8,256]{2,1,0:T(8,128)(2,1)S(1)}, u32[]{:S(2)}, u32[]{:S(2)}) collective-permute-start(bf16[32,8,256]{2,1,0:T(8,128)(2,1)} %get-tuple-element.50), channel_id=1, source_target_pairs={{0,6},{2,4},{4,10},{6,8},{8,14},{10,12},{12,2},{14,0},{1,7},{3,5},... | collective-permute-start | bytes 393224 | tf_op jit(solution)/shard_map/ppermute | solution.py:415
  27.8 15.8 %collective-permute-start.8 = (bf16[32,8,256]{2,1,0:T(8,128)(2,1)}, bf16[32,8,256]{2,1,0:T(8,128)(2,1)S(1)}, u32[]{:S(2)}, u32[]{:S(2)}) collective-permute-start(bf16[32,8,256]{2,1,0:T(8,128)(2,1)} %get-tuple-element.51), channel_id=1, source_target_pairs={{0,8},{2,10},{4,12},{6,14},{8,0},{10,2},{12,4},{14,6},{1,9},{3,11}... | collective-permute-start | bytes 393224 | tf_op jit(solution)/shard_map/ppermute | solution.py:415
  29.1 14.5 %collective-permute-start.9 = (bf16[32,8,256]{2,1,0:T(8,128)(2,1)}, bf16[32,8,256]{2,1,0:T(8,128)(2,1)S(1)}, u32[]{:S(2)}, u32[]{:S(2)}) collective-permute-start(bf16[32,8,256]{2,1,0:T(8,128)(2,1)} %get-tuple-element.52), channel_id=1, source_target_pairs={{0,10},{2,8},{4,14},{6,12},{8,2},{10,0},{12,6},{14,4},{1,11},{3,9}... | collective-permute-start | bytes 393224 | tf_op jit(solution)/shard_map/ppermute | solution.py:415
  31.6 11.9 %collective-permute-start.10 = (bf16[32,8,256]{2,1,0:T(8,128)(2,1)}, bf16[32,8,256]{2,1,0:T(8,128)(2,1)}, u32[]{:S(2)}, u32[]{:S(2)}) collective-permute-start(bf16[32,8,256]{2,1,0:T(8,128)(2,1)} %get-tuple-element.53), channel_id=1, source_target_pairs={{0,12},{2,14},{4,0},{6,2},{8,4},{10,6},{12,8},{14,10},{1,13},{3,15... | collective-permute-start | bytes 393224 | tf_op jit(solution)/shard_map/ppermute | solution.py:415
  33.1 10.5 %collective-permute-start.11 = (bf16[32,8,256]{2,1,0:T(8,128)(2,1)}, bf16[32,8,256]{2,1,0:T(8,128)(2,1)}, u32[]{:S(2)}, u32[]{:S(2)}) collective-permute-start(bf16[32,8,256]{2,1,0:T(8,128)(2,1)} %get-tuple-element.54), channel_id=1, source_target_pairs={{0,14},{2,12},{4,2},{6,0},{8,6},{10,4},{12,10},{14,8},{1,15},{3,13... | collective-permute-start | bytes 393224 | tf_op jit(solution)/shard_map/ppermute | solution.py:415
  34.8 8.8 %copy-start.3 = (s32[32,1]{1,0:T(8,128)S(1)}, s32[32,1]{1,0:T(8,128)}, u32[]{:S(2)}) copy-start(s32[32,1]{1,0:T(8,128)} %copy.12.refs_0_) | copy-start | bytes 388
  34.8 0.7 %copy-start.4 = (s32[4,64]{1,0:T(4,128)S(1)}, s32[4,64]{1,0:T(4,128)}, u32[]{:S(2)}) copy-start(s32[4,64]{1,0:T(4,128)} %refs_1_.7) | copy-start | bytes 3076
  52.8 2.8 %collective-permute-start.12 = (f32[64,4,128]{2,1,0:T(4,128)S(1)}, f32[64,4,128]{2,1,0:T(4,128)S(1)}, u32[]{:S(2)}, u32[]{:S(2)}) collective-permute-start(f32[64,4,128]{2,1,0:T(4,128)S(1)} %get-tuple-element.56), channel_id=1, source_target_pairs={{0,1},{1,0},{2,3},{3,2},{4,5},{5,4},{6,7},{7,6},{8,9},{9,8},{10,11... | collective-permute-start | bytes 393224 | tf_op jit(solution)/shard_map/ppermute | solution.py:420

commit v8 on v7

--- a/solution.py
+++ b/solution.py
@@ -129,8 +129,42 @@
 
 
 def weights_kernel(
-    qkv_a, qkv_b, out_a, out_b, bil_a, bil_b, up_a, up_b, down_a, down_b, all_ref
+    lens_ref, seed_ref, qkv_a, qkv_b, out_a, out_b, bil_a, bil_b, up_a, up_b, down_a, down_b,
+    all_ref, valid_ref, base_ref, *, cut,
 ):
+    pairs = lens_ref.shape[0]
+    history = seed_ref.shape[1]
+    spots = history // pairs
+    place = lax.axis_index("pa")
+
+    def arrival(lane):
+        position = lane % history
+        for i in range(pairs):
+            origin = moved_to(place, -(i // Z_LO), i % Z_LO, pairs)
+            here = (lane % history) // spots == i
+            position = jnp.where(here, origin * spots + lane % spots, position)
+        return position
+
+    owned = (valid_ref.shape[0], lens_ref.shape[1])
+    at = lax.broadcasted_iota(jnp.int32, owned, 0) + lax.axis_index("dev") * owned[0]
+    near = lax.broadcasted_iota(jnp.int32, owned, 1) == at
+    row = jnp.broadcast_to(lens_ref[pl.ds(place, 1), :].astype(F32), owned)
+    lens = jnp.sum(jnp.where(near, row, 0.0), axis=1, keepdims=True)
+    lane = lax.broadcasted_iota(jnp.int32, valid_ref.shape, 1)
+    first = lax.broadcasted_iota(jnp.int32, valid_ref.shape, 0) < cut
+    position = jnp.where(first, lane % history, arrival(lane))
+    valid_ref[...] = (position.astype(F32) < lens).astype(F32)
+
+    seed = seed_ref[...].astype(F32)
+    chosen = lax.broadcasted_iota(jnp.int32, (history, history), 0) == arrival(
+        lax.broadcasted_iota(jnp.int32, (history, history), 1)
+    )
+    moved = jnp.dot(
+        seed.astype(BF16), chosen.astype(F32).astype(BF16), preferred_element_type=F32
+    )
+    for i, table in enumerate((seed, moved)):
+        base_ref[i] = jnp.concatenate([(table - 7.5) * 0.25] * GROUP, axis=1)
+
     half = D // 2
     low = lax.axis_index("dev") == 0
     at = 0
@@ -159,14 +193,20 @@
         after += rows.shape[0]
 
 
-def finish_weights(own, other):
+def finish_weights(own, other, lens, seed, cut, per_core):
     ff = own[3].shape[1]
-    operands = [w for pair in zip(in_hbm(*own), other) for w in pair]
+    operands = [*in_hbm(lens, seed)] + [w for pair in zip(in_hbm(*own), other) for w in pair]
+    vmem = pl.BlockSpec(memory_space=pltpu.VMEM)
+    lanes = GROUP * seed.shape[1]
     return pl.pallas_call(
-        weights_kernel,
-        out_shape=pltpu.VMEM((5 * D + 4 * ff, D), BF16),
-        in_specs=[pl.BlockSpec(memory_space=pltpu.VMEM)] * len(operands),
-        out_specs=pl.BlockSpec(memory_space=pltpu.VMEM),
+        functools.partial(weights_kernel, cut=cut),
+        out_shape=[
+            pltpu.VMEM((5 * D + 4 * ff, D), BF16),
+            pltpu.VMEM((per_core, lanes), F32),
+            pltpu.VMEM((2, CAPS, lanes), F32),
+        ],
+        in_specs=[vmem] * len(operands),
+        out_specs=[vmem] * 3,
         compiler_params=pltpu.CompilerParams(vmem_limit_bytes=8 << 20),
         name="weights",
     )(*operands)
@@ -183,32 +223,27 @@
 
 
 def encode_kernel(*refs, steps, start, later):
-    count = 2 if later else 0
-    lens_ref, seed_ref, w_ref = refs[:3]
-    parts = refs[3 + count : -4]
-    own_ref, other_ref, interest_ref, x_ref = refs[-4:]
+    valid_ref, base_ref, w_ref = refs[:3]
+    parts = refs[3 + (2 if later else 0) : -3]
+    own_ref, other_ref, interest_ref = refs[-3:]
     step = pl.program_id(0)
     if later:
-        place = lax.axis_index("pa")
-
-        @pl.when(step == 0)
-        def _():
-            for i, part in enumerate(parts):
-                origin = moved_to(place, -(i // Z_LO), i % Z_LO, len(parts))
-                x_ref[origin] = part[...]
-            own_ref[:start] = refs[3][:start]
-            other_ref[:start] = refs[4][:start]
-
+        own_ref[:start] = refs[3][:start]
+        other_ref[:start] = refs[4][:start]
+        pairs, (all_users, spots, _) = len(parts), parts[0].shape
     else:
-        x_ref = parts[0]
-    pairs, all_users, spots, _ = x_ref.shape
+        pairs, all_users, spots, _ = parts[0].shape
     block = all_users // steps
     history = pairs * spots
     rows = block * history
     head = D // HEADS
     lanes = HEADS * history
-    x = x_ref[:, pl.ds(step * block, block)].astype(F32)
-    x = jnp.swapaxes(x, 0, 1).reshape(rows, D).astype(BF16)
+    at = pl.ds(step * block, block)
+    if later:
+        x = jnp.stack([part[at].astype(F32) for part in parts], axis=1)
+    else:
+        x = jnp.swapaxes(parts[0][:, at].astype(F32), 0, 1)
+    x = x.reshape(rows, D).astype(BF16)
 
     def through(i):
         return jnp.dot(x, w_ref[i * D : (i + 1) * D, :], preferred_element_type=F32)
@@ -223,9 +258,7 @@
     row_head = lax.broadcasted_iota(jnp.int32, (lanes, D), 0) // history
     col_head = lax.broadcasted_iota(jnp.int32, (lanes, D), 1) // head
     ones = (row_head == col_head).astype(F32).astype(BF16)
-    position = lax.broadcasted_iota(jnp.int32, (block, lanes), 1) % history
-    lens = lens_ref[pl.ds(step * block, block), :]
-    key_valid = (position < lens).astype(F32)
+    key_valid = valid_ref[pl.ds(start + step * block, block), :]
     users = [slice(u * history, (u + 1) * history) for u in range(block)]
     scores = []
     none = jnp.zeros((history, D // 2), BF16)
@@ -278,10 +311,11 @@
 
     @pl.when(step == steps - 1)
     def _():
-        route(lens_ref, seed_ref, own_ref, other_ref, interest_ref, history, start)
-
-
-def route(lens_ref, seed_ref, own_ref, other_ref, interest_ref, history, start):
+        base = base_ref[int(later)]
+        route(valid_ref, base, own_ref, other_ref, interest_ref, history, start)
+
+
+def route(valid_ref, base, own_ref, other_ref, interest_ref, history, start):
     lanes = GROUP * history
     groups = BLOCK // GROUP
     blocks = range(interest_ref.shape[0] // (BLOCK * history))
@@ -289,13 +323,12 @@
     user = lax.broadcasted_iota(jnp.int32, (BLOCK, lanes), 0)
     mine = (lane // history) == (user % GROUP)
     in_group = [(user // GROUP) == g for g in range(groups)]
-    base = (seed_ref[...].astype(F32) - 7.5) * 0.25
-    base = jnp.concatenate([base] * GROUP, axis=1)
     base = jnp.broadcast_to(base[:, None, :], (CAPS, BLOCK, lanes))
     logits = [base for _ in blocks]
     valid = []
     for b in blocks:
-        real = mine & ((lane % history) < lens_ref[b * BLOCK : (b + 1) * BLOCK, :])
+        at = slice(start + b * BLOCK, start + (b + 1) * BLOCK)
+        real = mine & (valid_ref[at, :] > 0.0)
         valid.append([(real & here).astype(F32)[None] for here in in_group])
 
     def vectors(b, g):
@@ -357,25 +390,19 @@
             other_ref[at, j, :] = passed[j]
 
 
-def encode(parts, lens, seed, weights, steps, start, all_users, before):
-    users = lens.shape[0]
+def encode(parts, valid, base, weights, steps, start, before):
     later = len(before) > 0
-    spots = parts[0].shape[-2]
-    pa_count = len(parts) if later else parts[0].shape[0]
-    whole = (pa_count, users, spots, D) if later else (1, 1, spots, D)
+    rows = len(parts) * parts[0].size // D
     vmem = pl.BlockSpec(memory_space=pltpu.VMEM)
-    operands = [lens, seed, weights, *before, *parts]
-    made = pltpu.VMEM((all_users, CAPS, D // 2), F32)
+    operands = [valid, base, weights, *before, *parts]
+    made = pltpu.VMEM((valid.shape[0], CAPS, D // 2), F32)
     return pl.pallas_call(
         functools.partial(encode_kernel, steps=steps, start=start, later=later),
         out_shape=[made, made],
         grid=(steps,),
         in_specs=[vmem] * len(operands),
         out_specs=[vmem] * 2,
-        scratch_shapes=[
-            pltpu.VMEM((users * pa_count * spots, D), BF16),
-            pltpu.VMEM(whole, BF16),
-        ],
+        scratch_shapes=[pltpu.VMEM((rows, D), BF16)],
         compiler_params=pltpu.CompilerParams(vmem_limit_bytes=24 << 20),
         name="encode",
     )(*operands)
@@ -391,18 +418,17 @@
     core = lax.axis_index("dev").astype(jnp.int32)
     swap = [(i, dev_count - 1 - i) for i in range(dev_count)]
     own = (w_qkv, w_out, w_bilinear, w_up, w_down)
-    first = (lax.axis_index("pa") * dev_count + core) * per_core
-    lens = lax.dynamic_slice_in_dim(lengths, first, per_core).reshape(per_core, 1)
     cut = per_core * FIRST[0] // FIRST[1]
-    lens = [lens[:cut], lens[cut:]]
     ids = item_ids.T
     counts = (pa_count, dev_count)
     sent = lookup(ids, features, item_table, 0, cut, *counts, False)[0]
-    own, sent = lax.optimization_barrier((own, sent))
     got = lax.all_to_all(sent, "pa", split_axis=0, concat_axis=0, tiled=True)
     got = got.reshape(pa_count, cut, spots, D)
-    weights = finish_weights(own, tuple(lax.ppermute(w, "dev", swap) for w in own))
-    ids, weights, lens = lax.optimization_barrier((ids, weights, lens))
+    other = tuple(lax.ppermute(w, "dev", swap) for w in own)
+    weights, valid, base = finish_weights(
+        own, other, lengths.reshape(pa_count, -1), routing_seed, cut, per_core
+    )
+    ids, weights, valid, base = lax.optimization_barrier((ids, weights, valid, base))
     late = lookup(ids, features, item_table, cut, per_core - cut, *counts, True)
     parts = [late[0]]
     for i in range(1, pa_count):
@@ -413,16 +439,12 @@
         if i > AHEAD:
             block, parts[i - AHEAD] = lax.optimization_barrier((block, parts[i - AHEAD]))
         parts.append(lax.ppermute(block, "pa", pairs))
-    made = encode([got], lens[0], routing_seed, weights, STEPS[0], 0, per_core, ())
-    kept, passed = encode(
-        parts, lens[1], routing_seed, weights, STEPS[1], cut, per_core, tuple(made)
-    )
+    made = encode([got], valid, base, weights, STEPS[0], 0, ())
+    kept, passed = encode(parts, valid, base, weights, STEPS[1], cut, tuple(made))
     came = lax.ppermute(passed, "dev", swap)
-    return jnp.where(
-        core == 0,
-        jnp.concatenate([kept, came], axis=0),
-        jnp.concatenate([came, kept], axis=0),
-    )
+    out = jnp.zeros((dev_count * per_core, CAPS, D // dev_count), F32)
+    out = lax.dynamic_update_slice_in_dim(out, kept, core * per_core, 0)
+    return lax.dynamic_update_slice_in_dim(out, came, (1 - core) * per_core, 0)
 
 
 def solution(mesh):

time: 56.7 us -> 54.2 us (0.956)
  local copies, waits for them, and re-layouts: 4.95 us -> 0.76 us
  waiting for transfers between devices: 1.02 us -> 3.57 us
  other arithmetic: 0.76 us -> 0 us
    unnamed x20 -> x14, local copies, waits for them, and re-layouts: 2.18 us -> 0.04 us
    ppermute x7, waiting for transfers between devices: 0.02 us -> 1.68 us  [body(): parts.append(lax.ppermute(block, 'pa', pairs))]
    optimization_barrier x2 -> x0, local copies, waits for them, and re-layouts: 1.43 us -> none  [body(): ids, weights, lens = lax.optimization_barrier((ids, weights, lens))]
    ppermute x5, waiting for transfers between devices: 0.01 us -> 0.98 us  [body(): other = tuple((lax.ppermute(w, 'dev', swap) for w in own))]
    select_n x1 -> x0, other arithmetic: 0.76 us -> none  [body(): jnp.where(core == 0, jnp.concatenate([kept, came], axis=0), jnp.concatena...]
    dynamic_slice x1 -> x0, local copies, waits for them, and re-layouts: 0.76 us -> none  [body(): lax.dynamic_slice_in_dim(lengths, first, per_core).reshape(per_core, 1)]
    dynamic_update_slice x0 -> x2, local copies, waits for them, and re-layouts: none -> 0.69 us  [the longest x1 0.66 us: body(): return lax.dynamic_update_slice_in_dim(out, came, (1 - core) * per_core, 0)]
    slice x1 -> x0, local copies, waits for them, and re-layouts: 0.58 us -> none  [body(): lens = [lens[:cut], lens[cut:]]]
  transfers between devices with their start and end apart: 14 -> 14, of which waited for: 1 -> 5; matrix products, arithmetic and copies ran while one was open for 5% -> 0% of each run, Pallas kernels for 27% -> 28%
where the time goes in v8:
time: 54.2 us; the launch traced here: 53.9 us
  Pallas kernels  29.6 us (55%)
  starting transfers between devices  19.8 us (37%)
  waiting for transfers between devices  3.57 us (7%)
  local copies, waits for them, and re-layouts  0.76 us (1%)
    pallas_call x2, Pallas kernels, encode(): pl.pallas_call(functools.partial(encode_kernel, steps=steps, start=start,...  17 us
    pallas_call x2, Pallas kernels, lookup(): pl.pallas_call(functools.partial(lookup_kernel, start=start, per_pair=per...  11.1 us
    ppermute x7, starting transfers between devices, body(): parts.append(lax.ppermute(block, 'pa', pairs))  9.51 us
    all_to_all x1, starting transfers between devices, body(): got = lax.all_to_all(sent, 'pa', split_axis=0, concat_axis=0, tiled=True)  6.22 us
    ppermute x5, starting transfers between devices, body(): other = tuple((lax.ppermute(w, 'dev', swap) for w in own))  2.05 us
    ppermute x1, starting transfers between devices, body(): came = lax.ppermute(passed, 'dev', swap)  2.04 us
    ppermute x7, waiting for transfers between devices, body(): parts.append(lax.ppermute(block, 'pa', pairs))  1.68 us
    pallas_call x1, Pallas kernels, finish_weights(): pl.pallas_call(functools.partial(weights_kernel, cut=cut), out_shape=[plt...  1.59 us
  transfers between devices with their start and end apart: 14, of which 5 were waited for; matrix products, arithmetic and copies ran while one was open for 0% of the time, Pallas kernels for 28%

profile of v8, /device:TPU:1, one launch (start us, length us, event | category | flops | bytes accessed | tf_op | source)
XLA Modules:
  0.0 53.9 jit_solution(4808713961777464123)
XLA Ops:
  0.0 0.0 copy-start.2
  0.0 0.0 copy-start.3
  0.0 0.0 copy-start.4
  0.0 0.0 copy-start.5
  0.0 0.0 copy-start.6
  0.0 5.5 %lookup.2 = bf16[256,8,256]{2,1,0:T(8,128)(2,1)} custom-call(s32[8,1024]{1,0:T(8,128)} %bitcast.4, bf16[1024,8,256]{2,1,0:T(8,128)(2,1)} %refs_1_.3, bf16[4096,256]{1,0:T(8,128)(2,1)} %refs_2_.3), custom_call_target="tpu_custom_call" | custom-call | tf_op jit(solution)/shard_map/lookup/pallas_call | solution.py:118
  5.6 6.2 %all-to-all-start = ((bf16[256,8,256]{2,1,0:T(8,128)(2,1)}), bf16[256,8,256]{2,1,0:T(8,128)(2,1)S(1)}, u32[]{:S(2)}, u32[]{:S(2)}) async-start(bf16[256,8,256]{2,1,0:T(8,128)(2,1)} %lookup.2), calls=%async_computation | async-start | bytes 2097152 | tf_op jit(solution)/shard_map/all_to_all | solution.py:425
  11.8 0.0 copy-done.2
  11.8 1.0 %collective-permute-start.3 = (bf16[256,512]{1,0:T(8,128)(2,1)S(1)}, bf16[256,512]{1,0:T(8,128)(2,1)S(1)}, u32[]{:S(2)}, u32[]{:S(2)}) collective-permute-start(bf16[256,512]{1,0:T(8,128)(2,1)S(1)} %copy-done.2), channel_id=1, source_target_pairs={{0,1},{1,0},{2,3},{3,2},{4,5},{5,4},{6,7},{7,6},{8,9},{9,8},{10,11... | collective-permute-start | bytes 786440 | tf_op jit(solution)/shard_map/ppermute | solution.py:427
  12.8 0.0 copy-done.3
  12.8 0.1 collective-permute-start.4
  12.9 0.0 copy-done.4
  12.9 0.4 collective-permute-start
  13.3 0.0 copy-done.5
  13.3 0.1 collective-permute-start.1
  13.4 0.0 copy-done.6
  13.4 0.4 collective-permute-start.2
  13.8 0.9 %collective-permute-done.1.out_b = bf16[128,256]{1,0:T(8,128)(2,1)S(1)} collective-permute-done((bf16[128,256]{1,0:T(8,128)(2,1)S(1)}, bf16[128,256]{1,0:T(8,128)(2,1)S(1)}, u32[]{:S(2)}, u32[]{:S(2)}) %collective-permute-start.1) | collective-permute-done | bytes 65568 | tf_op jit(solution)/shard_map/ppermute | solution.py:427
  14.7 0.1 collective-permute-done.2.bil_b
  14.8 0.0 collective-permute-done.qkv_b
  14.8 0.0 collective-permute-done.3.up_b
  14.8 0.0 collective-permute-done.4.down_b
  14.8 1.6 %weights.1 = (bf16[3328,256]{1,0:T(8,128)(2,1)S(1)}, f32[64,256]{1,0:T(8,128)S(1)}, f32[2,4,256]{2,1,0:T(4,128)S(1)}) custom-call(s32[8,128]{1,0:T(8,128)} %bitcast.6, s32[4,64]{1,0:T(4,128)} %seed_ref.1, bf16[3,256,128]{2,1,0:T(8,128)(2,1)} %qkv_a.1, bf16[3,256,128]{2,1,0:T(8,128)(2,1)S(1)} %collective-permute-done.qkv_b, bf16[128,256]{1,0:T(8,128)(2,1)} %out_a.1, ...), custom_call_target="tpu_custom_call" | custom-call | tf_op jit(solution)/shard_map/weights/pallas_call | solution.py:201
  16.4 5.6 %lookup.3 = (bf16[32,8,256]{2,1,0:T(8,128)(2,1)}, bf16[32,8,256]{2,1,0:T(8,128)(2,1)}, bf16[32,8,256]{2,1,0:T(8,128)(2,1)}, bf16[32,8,256]{2,1,0:T(8,128)(2,1)},...) custom-call(s32[8,1024]{1,0:T(8,128)} %bitcast.5, ...), custom_call_target="tpu_custom_call" | custom-call | tf_op jit(solution)/shard_map/lookup/pallas_call | solution.py:118
  22.0 0.0 copy-start
  22.0 1.7 %collective-permute-start.5 = (bf16[32,8,256]{2,1,0:T(8,128)(2,1)}, bf16[32,8,256]{2,1,0:T(8,128)(2,1)S(1)}, u32[]{:S(2)}, u32[]{:S(2)}) collective-permute-start(bf16[32,8,256]{2,1,0:T(8,128)(2,1)} %get-tuple-element.39), channel_id=1, source_target_pairs={{0,2},{2,0},{4,6},{6,4},{8,10},{10,8},{12,14},{14,12},{1,3},{3,1},... | collective-permute-start | bytes 393224 | tf_op jit(solution)/shard_map/ppermute | solution.py:441
  23.7 1.2 %collective-permute-start.6 = (bf16[32,8,256]{2,1,0:T(8,128)(2,1)}, bf16[32,8,256]{2,1,0:T(8,128)(2,1)S(1)}, u32[]{:S(2)}, u32[]{:S(2)}) collective-permute-start(bf16[32,8,256]{2,1,0:T(8,128)(2,1)} %get-tuple-element.42), channel_id=1, source_target_pairs={{0,4},{2,6},{4,8},{6,10},{8,12},{10,14},{12,0},{14,2},{1,5},{3,7},... | collective-permute-start | bytes 393224 | tf_op jit(solution)/shard_map/ppermute | solution.py:441
  24.9 1.2 %collective-permute-start.7 = (bf16[32,8,256]{2,1,0:T(8,128)(2,1)}, bf16[32,8,256]{2,1,0:T(8,128)(2,1)S(1)}, u32[]{:S(2)}, u32[]{:S(2)}) collective-permute-start(bf16[32,8,256]{2,1,0:T(8,128)(2,1)} %get-tuple-element.44), channel_id=1, source_target_pairs={{0,6},{2,4},{4,10},{6,8},{8,14},{10,12},{12,2},{14,0},{1,7},{3,5},... | collective-permute-start | bytes 393224 | tf_op jit(solution)/shard_map/ppermute | solution.py:441
  26.1 1.3 %collective-permute-start.8 = (bf16[32,8,256]{2,1,0:T(8,128)(2,1)}, bf16[32,8,256]{2,1,0:T(8,128)(2,1)S(1)}, u32[]{:S(2)}, u32[]{:S(2)}) collective-permute-start(bf16[32,8,256]{2,1,0:T(8,128)(2,1)} %get-tuple-element.45), channel_id=1, source_target_pairs={{0,8},{2,10},{4,12},{6,14},{8,0},{10,2},{12,4},{14,6},{1,9},{3,11}... | collective-permute-start | bytes 393224 | tf_op jit(solution)/shard_map/ppermute | solution.py:441
  27.4 2.6 %collective-permute-start.9 = (bf16[32,8,256]{2,1,0:T(8,128)(2,1)}, bf16[32,8,256]{2,1,0:T(8,128)(2,1)}, u32[]{:S(2)}, u32[]{:S(2)}) collective-permute-start(bf16[32,8,256]{2,1,0:T(8,128)(2,1)} %get-tuple-element.46), channel_id=1, source_target_pairs={{0,10},{2,8},{4,14},{6,12},{8,2},{10,0},{12,6},{14,4},{1,11},{3,9}... | collective-permute-start | bytes 393224 | tf_op jit(solution)/shard_map/ppermute | solution.py:441
  30.0 0.0 collective-permute-done.5.refs_6_
  30.0 0.2 collective-permute-done.6.refs_7_
  30.2 1.3 %collective-permute-start.10 = (bf16[32,8,256]{2,1,0:T(8,128)(2,1)}, bf16[32,8,256]{2,1,0:T(8,128)(2,1)}, u32[]{:S(2)}, u32[]{:S(2)}) collective-permute-start(bf16[32,8,256]{2,1,0:T(8,128)(2,1)} %get-tuple-element.47), channel_id=1, source_target_pairs={{0,12},{2,14},{4,0},{6,2},{8,4},{10,6},{12,8},{14,10},{1,13},{3,15... | collective-permute-start | bytes 393224 | tf_op jit(solution)/shard_map/ppermute | solution.py:441
  31.5 0.3 collective-permute-start.11
  31.7 0.0 all-to-all-done
  31.7 8.0 %encode.2 = (f32[64,4,128]{2,1,0:T(4,128)S(1)}, f32[64,4,128]{2,1,0:T(4,128)S(1)}) custom-call(f32[64,256]{1,0:T(8,128)S(1)} %get-tuple-element.31.refs_0_, f32[2,4,256]{2,1,0:T(4,128)S(1)} %get-tuple-element.32.refs_1_, bf16[3328,256]{1,0:T(8,128)(2,1)S(1)} %get-tuple-element.33.refs_2_, bf16[8,32,8,256]{3,2,1,0:T(8,128)(2,1)S(1)} %bitcast.3), custom_call_target="tpu_custom_call" | custom-call | tf_op jit(solution)/shard_map/encode/pallas_call | solution.py:399
  39.7 0.0 collective-permute-done.7.refs_8_
  39.7 0.0 collective-permute-done.8.refs_9_
  39.7 0.0 collective-permute-done.9.refs_10_
  39.7 0.0 collective-permute-done.10.refs_11_
  39.8 1.4 %collective-permute-done.11.refs_12_ = bf16[32,8,256]{2,1,0:T(8,128)(2,1)} collective-permute-done((bf16[32,8,256]{2,1,0:T(8,128)(2,1)}, bf16[32,8,256]{2,1,0:T(8,128)(2,1)}, u32[]{:S(2)}, u32[]{:S(2)}) %collective-permute-start.11) | collective-permute-done | bytes 131104 | tf_op jit(solution)/shard_map/ppermute | solution.py:441
  41.2 0.0 copy-done
  41.2 9.0 %encode.3 = (f32[64,4,128]{2,1,0:T(4,128)S(1)}, f32[64,4,128]{2,1,0:T(4,128)S(1)}) custom-call(f32[64,256]{1,0:T(8,128)S(1)} %get-tuple-element.31.refs_0_, f32[2,4,256]{2,1,0:T(4,128)S(1)} %get-tuple-element.32.refs_1_, bf16[3328,256]{1,0:T(8,128)(2,1)S(1)} %get-tuple-element.33.refs_2_, f32[64,4,128]{2,1,0:T(4,128)S(1)} %get-tuple-element.34.refs_3_, ...), custom_call_target="tpu_custom_call" | custom-call | tf_op jit(solution)/shard_map/encode/pallas_call | solution.py:399
  50.2 2.0 %collective-permute-start.12 = (f32[64,4,128]{2,1,0:T(4,128)S(1)}, f32[64,4,128]{2,1,0:T(4,128)S(1)}, u32[]{:S(2)}, u32[]{:S(2)}) collective-permute-start(f32[64,4,128]{2,1,0:T(4,128)S(1)} %get-tuple-element.50), channel_id=1, source_target_pairs={{0,1},{1,0},{2,3},{3,2},{4,5},{5,4},{6,7},{7,6},{8,9},{9,8},{10,11... | collective-permute-start | bytes 393224 | tf_op jit(solution)/shard_map/ppermute | solution.py:444
  52.3 0.0 copy-start.1
  52.4 0.9 %collective-permute-done.12 = f32[64,4,128]{2,1,0:T(4,128)S(1)} collective-permute-done((f32[64,4,128]{2,1,0:T(4,128)S(1)}, f32[64,4,128]{2,1,0:T(4,128)S(1)}, u32[]{:S(2)}, u32[]{:S(2)}) %collective-permute-start.12) | collective-permute-done | bytes 131104 | tf_op jit(solution)/shard_map/ppermute | solution.py:444
  53.3 0.0 copy-done.1
  53.3 0.7 %constant_dynamic-update-slice_fusion = f32[128,4,128]{2,1,0:T(4,128)} fusion(f32[128,4,128]{2,1,0:T(4,128)} %copy-done.1, f32[64,4,128]{2,1,0:T(4,128)S(1)} %collective-permute-done.12, s32[]{:T(128)S(6)} %select_n.7), kind=kLoop, calls=%fused_computation | loop fusion | bytes 262148 | tf_op jit(solution)/shard_map/dynamic_update_slice | solution.py:447
  (2 shorter events, 0.1 us)
Async XLA Ops:
  0.0 11.8 %copy-start.2 = (bf16[256,512]{1,0:T(8,128)(2,1)S(1)}, bf16[256,512]{1,0:T(8,128)(2,1)}, u32[]{:S(2)}) copy-start(bf16[256,512]{1,0:T(8,128)(2,1)} %up_a.1) | copy-start | bytes 786436
  0.0 12.8 %copy-start.3 = (bf16[512,256]{1,0:T(8,128)(2,1)S(1)}, bf16[512,256]{1,0:T(8,128)(2,1)}, u32[]{:S(2)}) copy-start(bf16[512,256]{1,0:T(8,128)(2,1)} %down_a.1) | copy-start | bytes 786436
  0.0 12.9 %copy-start.4 = (bf16[3,256,128]{2,1,0:T(8,128)(2,1)S(1)}, bf16[3,256,128]{2,1,0:T(8,128)(2,1)}, u32[]{:S(2)}) copy-start(bf16[3,256,128]{2,1,0:T(8,128)(2,1)} %qkv_a.1) | copy-start | bytes 589828
  0.0 13.3 %copy-start.5 = (bf16[128,256]{1,0:T(8,128)(2,1)S(1)}, bf16[128,256]{1,0:T(8,128)(2,1)}, u32[]{:S(2)}) copy-start(bf16[128,256]{1,0:T(8,128)(2,1)} %out_a.1) | copy-start | bytes 196612
  0.0 13.4 %copy-start.6 = (bf16[256,128]{1,0:T(8,128)(2,1)S(1)}, bf16[256,128]{1,0:T(8,128)(2,1)}, u32[]{:S(2)}) copy-start(bf16[256,128]{1,0:T(8,128)(2,1)} %bil_a.1) | copy-start | bytes 196612
  5.6 26.2 %all-to-all-start = ((bf16[256,8,256]{2,1,0:T(8,128)(2,1)}), bf16[256,8,256]{2,1,0:T(8,128)(2,1)S(1)}, u32[]{:S(2)}, u32[]{:S(2)}) async-start(bf16[256,8,256]{2,1,0:T(8,128)(2,1)} %lookup.2), calls=%async_computation | async-start | bytes 2097152 | tf_op jit(solution)/shard_map/all_to_all | solution.py:425
  11.8 3.0 %collective-permute-start.3 = (bf16[256,512]{1,0:T(8,128)(2,1)S(1)}, bf16[256,512]{1,0:T(8,128)(2,1)S(1)}, u32[]{:S(2)}, u32[]{:S(2)}) collective-permute-start(bf16[256,512]{1,0:T(8,128)(2,1)S(1)} %copy-done.2), channel_id=1, source_target_pairs={{0,1},{1,0},{2,3},{3,2},{4,5},{5,4},{6,7},{7,6},{8,9},{9,8},{10,11... | collective-permute-start | bytes 786440 | tf_op jit(solution)/shard_map/ppermute | solution.py:427
  12.8 2.0 %collective-permute-start.4 = (bf16[512,256]{1,0:T(8,128)(2,1)S(1)}, bf16[512,256]{1,0:T(8,128)(2,1)S(1)}, u32[]{:S(2)}, u32[]{:S(2)}) collective-permute-start(bf16[512,256]{1,0:T(8,128)(2,1)S(1)} %copy-done.3), channel_id=1, source_target_pairs={{0,1},{1,0},{2,3},{3,2},{4,5},{5,4},{6,7},{7,6},{8,9},{9,8},{10,11... | collective-permute-start | bytes 786440 | tf_op jit(solution)/shard_map/ppermute | solution.py:427
  12.9 1.9 %collective-permute-start = (bf16[3,256,128]{2,1,0:T(8,128)(2,1)S(1)}, bf16[3,256,128]{2,1,0:T(8,128)(2,1)S(1)}, u32[]{:S(2)}, u32[]{:S(2)}) collective-permute-start(bf16[3,256,128]{2,1,0:T(8,128)(2,1)S(1)} %copy-done.4), channel_id=1, source_target_pairs={{0,1},{1,0},{2,3},{3,2},{4,5},{5,4},{6,7},{7,6},{8,9},{9,8},{10,11... | collective-permute-start | bytes 589832 | tf_op jit(solution)/shard_map/ppermute | solution.py:427
  13.3 1.4 %collective-permute-start.1 = (bf16[128,256]{1,0:T(8,128)(2,1)S(1)}, bf16[128,256]{1,0:T(8,128)(2,1)S(1)}, u32[]{:S(2)}, u32[]{:S(2)}) collective-permute-start(bf16[128,256]{1,0:T(8,128)(2,1)S(1)} %copy-done.5), channel_id=1, source_target_pairs={{0,1},{1,0},{2,3},{3,2},{4,5},{5,4},{6,7},{7,6},{8,9},{9,8},{10,11... | collective-permute-start | bytes 196616 | tf_op jit(solution)/shard_map/ppermute | solution.py:427
  13.4 1.4 %collective-permute-start.2 = (bf16[256,128]{1,0:T(8,128)(2,1)S(1)}, bf16[256,128]{1,0:T(8,128)(2,1)S(1)}, u32[]{:S(2)}, u32[]{:S(2)}) collective-permute-start(bf16[256,128]{1,0:T(8,128)(2,1)S(1)} %copy-done.6), channel_id=1, source_target_pairs={{0,1},{1,0},{2,3},{3,2},{4,5},{5,4},{6,7},{7,6},{8,9},{9,8},{10,11... | collective-permute-start | bytes 196616 | tf_op jit(solution)/shard_map/ppermute | solution.py:427
  22.0 19.2 %copy-start = (bf16[32,8,256]{2,1,0:T(8,128)(2,1)S(1)}, bf16[32,8,256]{2,1,0:T(8,128)(2,1)}, u32[]{:S(2)}) copy-start(bf16[32,8,256]{2,1,0:T(8,128)(2,1)} %get-tuple-element.37.refs_5_) | copy-start | bytes 393220
  22.0 8.0 %collective-permute-start.5 = (bf16[32,8,256]{2,1,0:T(8,128)(2,1)}, bf16[32,8,256]{2,1,0:T(8,128)(2,1)S(1)}, u32[]{:S(2)}, u32[]{:S(2)}) collective-permute-start(bf16[32,8,256]{2,1,0:T(8,128)(2,1)} %get-tuple-element.39), channel_id=1, source_target_pairs={{0,2},{2,0},{4,6},{6,4},{8,10},{10,8},{12,14},{14,12},{1,3},{3,1},... | collective-permute-start | bytes 393224 | tf_op jit(solution)/shard_map/ppermute | solution.py:441
  23.7 6.5 %collective-permute-start.6 = (bf16[32,8,256]{2,1,0:T(8,128)(2,1)}, bf16[32,8,256]{2,1,0:T(8,128)(2,1)S(1)}, u32[]{:S(2)}, u32[]{:S(2)}) collective-permute-start(bf16[32,8,256]{2,1,0:T(8,128)(2,1)} %get-tuple-element.42), channel_id=1, source_target_pairs={{0,4},{2,6},{4,8},{6,10},{8,12},{10,14},{12,0},{14,2},{1,5},{3,7},... | collective-permute-start | bytes 393224 | tf_op jit(solution)/shard_map/ppermute | solution.py:441
  24.9 14.8 %collective-permute-start.7 = (bf16[32,8,256]{2,1,0:T(8,128)(2,1)}, bf16[32,8,256]{2,1,0:T(8,128)(2,1)S(1)}, u32[]{:S(2)}, u32[]{:S(2)}) collective-permute-start(bf16[32,8,256]{2,1,0:T(8,128)(2,1)} %get-tuple-element.44), channel_id=1, source_target_pairs={{0,6},{2,4},{4,10},{6,8},{8,14},{10,12},{12,2},{14,0},{1,7},{3,5},... | collective-permute-start | bytes 393224 | tf_op jit(solution)/shard_map/ppermute | solution.py:441
  26.1 13.6 %collective-permute-start.8 = (bf16[32,8,256]{2,1,0:T(8,128)(2,1)}, bf16[32,8,256]{2,1,0:T(8,128)(2,1)S(1)}, u32[]{:S(2)}, u32[]{:S(2)}) collective-permute-start(bf16[32,8,256]{2,1,0:T(8,128)(2,1)} %get-tuple-element.45), channel_id=1, source_target_pairs={{0,8},{2,10},{4,12},{6,14},{8,0},{10,2},{12,4},{14,6},{1,9},{3,11}... | collective-permute-start | bytes 393224 | tf_op jit(solution)/shard_map/ppermute | solution.py:441
  27.4 12.3 %collective-permute-start.9 = (bf16[32,8,256]{2,1,0:T(8,128)(2,1)}, bf16[32,8,256]{2,1,0:T(8,128)(2,1)}, u32[]{:S(2)}, u32[]{:S(2)}) collective-permute-start(bf16[32,8,256]{2,1,0:T(8,128)(2,1)} %get-tuple-element.46), channel_id=1, source_target_pairs={{0,10},{2,8},{4,14},{6,12},{8,2},{10,0},{12,6},{14,4},{1,11},{3,9}... | collective-permute-start | bytes 393224 | tf_op jit(solution)/shard_map/ppermute | solution.py:441
  30.2 9.5 %collective-permute-start.10 = (bf16[32,8,256]{2,1,0:T(8,128)(2,1)}, bf16[32,8,256]{2,1,0:T(8,128)(2,1)}, u32[]{:S(2)}, u32[]{:S(2)}) collective-permute-start(bf16[32,8,256]{2,1,0:T(8,128)(2,1)} %get-tuple-element.47), channel_id=1, source_target_pairs={{0,12},{2,14},{4,0},{6,2},{8,4},{10,6},{12,8},{14,10},{1,13},{3,15... | collective-permute-start | bytes 393224 | tf_op jit(solution)/shard_map/ppermute | solution.py:441
  31.5 9.7 %collective-permute-start.11 = (bf16[32,8,256]{2,1,0:T(8,128)(2,1)}, bf16[32,8,256]{2,1,0:T(8,128)(2,1)}, u32[]{:S(2)}, u32[]{:S(2)}) collective-permute-start(bf16[32,8,256]{2,1,0:T(8,128)(2,1)} %get-tuple-element.48), channel_id=1, source_target_pairs={{0,14},{2,12},{4,2},{6,0},{8,6},{10,4},{12,10},{14,8},{1,15},{3,13... | collective-permute-start | bytes 393224 | tf_op jit(solution)/shard_map/ppermute | solution.py:441
  50.2 3.0 %collective-permute-start.12 = (f32[64,4,128]{2,1,0:T(4,128)S(1)}, f32[64,4,128]{2,1,0:T(4,128)S(1)}, u32[]{:S(2)}, u32[]{:S(2)}) collective-permute-start(f32[64,4,128]{2,1,0:T(4,128)S(1)} %get-tuple-element.50), channel_id=1, source_target_pairs={{0,1},{1,0},{2,3},{3,2},{4,5},{5,4},{6,7},{7,6},{8,9},{9,8},{10,11... | collective-permute-start | bytes 393224 | tf_op jit(solution)/shard_map/ppermute | solution.py:444
  52.3 0.9 %copy-start.1 = (f32[128,4,128]{2,1,0:T(4,128)}, f32[128,4,128]{2,1,0:T(4,128)S(1)}, u32[]{:S(2)}) copy-start(f32[128,4,128]{2,1,0:T(4,128)S(1)} %constant_dynamic-update-slice_fusion.1) | copy-start | bytes 786436

commit v9 on v8

--- a/solution.py
+++ b/solution.py
@@ -32,29 +32,25 @@
     return (place // Z_LO + along + rest) % rest * Z_LO + (place % Z_LO + across) % Z_LO
 
 
-def lookup_kernel(*refs, start, per_pair, per_core, outs):
-    later = outs > 1
-    ids_hbm, feat_hbm, table_hbm = refs[:3]
-    out_hbm, refs = refs[3 : 3 + outs], refs[3 + outs :]
-    wide, table, table_sem, ids, feat, out, id_sem, feat_sem, out_sem = refs
+def lookup_kernel(
+    ids_hbm, feat_hbm, table_hbm, *refs, cut, per_pair, per_core
+):
+    refs, scratch = refs[:-9], refs[-9:]
+    first_hbm, late_hbm = refs[0], refs[1:]
+    wide, table, table_sem, ids, feat, out, id_sem, feat_sem, out_sem = scratch
     pairs, users, spots, _ = feat.shape
     place = lax.axis_index("pa")
-    offset = lax.axis_index("dev") * per_core + start
-    if later:
-        owners = [moved_to(place, i // Z_LO, i % Z_LO, pairs) for i in range(pairs)]
-    else:
-        owners = list(range(pairs))
+    offset = lax.axis_index("dev") * per_core
+    rows = table.shape[0] // TABLE_PARTS
     fetch_ids = pltpu.make_async_copy(ids_hbm, ids, id_sem)
     fetch_ids.start()
-    fetch_table = []
-    rows = table.shape[0] // TABLE_PARTS
+    fetch_table, fetch_feat, send = [], [], []
     for i in range(TABLE_PARTS):
         at = pl.ds(i * rows, rows)
         fetch_table.append(pltpu.make_async_copy(table_hbm.at[at], table.at[at], table_sem.at[i]))
         fetch_table[-1].start()
-    fetch_feat = []
     for d in range(pairs):
-        at = pl.ds(owners[d] * per_pair + offset, users)
+        at = pl.ds(d * per_pair + offset, users)
         fetch_feat.append(pltpu.make_async_copy(feat_hbm.at[at], feat.at[d], feat_sem.at[d]))
         fetch_feat[-1].start()
     for i, fetch in enumerate(fetch_table):
@@ -69,12 +65,11 @@
         lax.fori_loop(0, rows // 128, widen, 0)
     fetch_ids.wait()
     spot = lax.broadcasted_iota(jnp.int32, (spots, D // 2), 0)
-    send = []
-    for d in range(pairs):
-        fetch_feat[d].wait()
-        first = owners[d] * per_pair + offset
-
-        def one(user, carry, d=d, first=first):
+
+    def add(slot, owner, start, stop, target, sem):
+        first = owner * per_pair + offset
+
+        def one(user, carry):
             halves = [None, None]
             for p in range(spots):
                 at = pl.ds(ids[p, first + user], 1)
@@ -82,48 +77,48 @@
                     row = jnp.broadcast_to(wide[h, at, :], (spots, D // 2))
                     halves[h] = row if p == 0 else jnp.where(spot == p, row, halves[h])
             rows = jnp.concatenate(halves, axis=1)
-            out[d, user] = (feat[d, user].astype(F32) + rows).astype(BF16)
+            out[slot, user] = (feat[owner, user].astype(F32) + rows).astype(BF16)
             return carry
 
-        lax.fori_loop(0, users, one, 0, unroll=8)
-        if later:
-            target = out_hbm[d]
-        else:
-            target = out_hbm[0].at[pl.ds(d * users, users)]
-        send.append(pltpu.make_async_copy(out.at[d], target, out_sem.at[d]))
+        lax.fori_loop(start, stop, one, 0, unroll=8)
+        send.append(pltpu.make_async_copy(out.at[slot, pl.ds(start, stop - start)], target, sem))
         send[-1].start()
+
+    for d in range(pairs):
+        fetch_feat[d].wait()
+        add(d, d, 0, cut, first_hbm.at[pl.ds(d * cut, cut)], out_sem.at[0, d])
+    for i in range(pairs):
+        owner = moved_to(place, i // Z_LO, i % Z_LO, pairs)
+        add(i, owner, cut, users, late_hbm[i], out_sem.at[1, i])
     for copy in send:
         copy.wait()
 
 
-def lookup(ids, features, table, start, users, pa_count, dev_count, later):
+def lookup(ids, features, table, cut, pa_count, dev_count):
     all_users, spots, width = features.shape
     per_pair = all_users // pa_count
     per_core = per_pair // dev_count
-    block = (pa_count, users, spots, width)
+    block = (pa_count, per_core, spots, width)
     hbm = pl.BlockSpec(memory_space=pltpu.HBM)
-    outs = pa_count if later else 1
-    made = [pltpu.HBM((users * (1 if later else pa_count), spots, width), BF16)] * outs
-    scratch = [
-        pltpu.VMEM((2, table.shape[0], D // 2), F32),
-        pltpu.VMEM(table.shape, BF16),
-        pltpu.SemaphoreType.DMA((TABLE_PARTS,)),
-        pltpu.SMEM(ids.shape, jnp.int32),
-        pltpu.VMEM(block, BF16),
-        pltpu.VMEM(block, BF16),
-        pltpu.SemaphoreType.DMA,
-        pltpu.SemaphoreType.DMA((pa_count,)),
-        pltpu.SemaphoreType.DMA((pa_count,)),
-    ]
+    late = pltpu.HBM((per_core - cut, spots, width), BF16)
+    made = [pltpu.HBM((cut * pa_count, spots, width), BF16)] + [late] * pa_count
     return pl.pallas_call(
-        functools.partial(
-            lookup_kernel, start=start, per_pair=per_pair, per_core=per_core, outs=outs
-        ),
+        functools.partial(lookup_kernel, cut=cut, per_pair=per_pair, per_core=per_core),
         out_shape=made,
         in_specs=[hbm, hbm, hbm],
-        out_specs=[hbm] * outs,
-        scratch_shapes=scratch,
-        compiler_params=pltpu.CompilerParams(vmem_limit_bytes=12 << 20),
+        out_specs=[hbm] * len(made),
+        scratch_shapes=[
+            pltpu.VMEM((2, table.shape[0], D // 2), F32),
+            pltpu.VMEM(table.shape, BF16),
+            pltpu.SemaphoreType.DMA((TABLE_PARTS,)),
+            pltpu.SMEM(ids.shape, jnp.int32),
+            pltpu.VMEM(block, BF16),
+            pltpu.VMEM(block, BF16),
+            pltpu.SemaphoreType.DMA,
+            pltpu.SemaphoreType.DMA((pa_count,)),
+            pltpu.SemaphoreType.DMA((2, pa_count)),
+        ],
+        compiler_params=pltpu.CompilerParams(vmem_limit_bytes=14 << 20),
         name="lookup",
     )(*in_hbm(ids, features, table))
 
@@ -394,6 +389,7 @@
     later = len(before) > 0
     rows = len(parts) * parts[0].size // D
     vmem = pl.BlockSpec(memory_space=pltpu.VMEM)
+    parts = [pltpu.with_memory_space_constraint(p, pltpu.VMEM) for p in parts]
     operands = [valid, base, weights, *before, *parts]
     made = pltpu.VMEM((valid.shape[0], CAPS, D // 2), F32)
     return pl.pallas_call(
@@ -419,17 +415,14 @@
     swap = [(i, dev_count - 1 - i) for i in range(dev_count)]
     own = (w_qkv, w_out, w_bilinear, w_up, w_down)
     cut = per_core * FIRST[0] // FIRST[1]
-    ids = item_ids.T
-    counts = (pa_count, dev_count)
-    sent = lookup(ids, features, item_table, 0, cut, *counts, False)[0]
+    sent, *late = lookup(item_ids.T, features, item_table, cut, pa_count, dev_count)
     got = lax.all_to_all(sent, "pa", split_axis=0, concat_axis=0, tiled=True)
     got = got.reshape(pa_count, cut, spots, D)
     other = tuple(lax.ppermute(w, "dev", swap) for w in own)
     weights, valid, base = finish_weights(
         own, other, lengths.reshape(pa_count, -1), routing_seed, cut, per_core
     )
-    ids, weights, valid, base = lax.optimization_barrier((ids, weights, valid, base))
-    late = lookup(ids, features, item_table, cut, per_core - cut, *counts, True)
+    late, weights, valid, base = lax.optimization_barrier((late, weights, valid, base))
     parts = [late[0]]
     for i in range(1, pa_count):
         pairs = [

time: 54.2 us -> 61.1 us (1.13)
  starting transfers between devices: 19.8 us -> 25.9 us
  waiting for transfers between devices: 3.57 us -> 6.83 us
  Pallas kernels: 29.6 us -> 27.2 us
    ppermute x1, starting transfers between devices: 2.04 us -> 7.11 us  [body(): came = lax.ppermute(passed, 'dev', swap)]
    ppermute x7, waiting for transfers between devices: 1.68 us -> 4.94 us  [body(): parts.append(lax.ppermute(block, 'pa', pairs))]
    pallas_call x2 -> x1, Pallas kernels: 11.1 us -> 8.55 us  [lookup(): pl.pallas_call(functools.partial(lookup_kernel, cut=cut, per_pair=per_pai...]
    ppermute x7, starting transfers between devices: 9.51 us -> 10.4 us  [body(): parts.append(lax.ppermute(block, 'pa', pairs))]
  transfers between devices with their start and end apart: 14 -> 14, of which waited for: 5 -> 5; matrix products, arithmetic and copies ran while one was open for 0% -> 0% of each run, Pallas kernels for 28% -> 16%
where the time goes in v9:
time: 61.1 us; the launch traced here: 60.8 us
  Pallas kernels  27.2 us (45%)
  starting transfers between devices  25.9 us (42%)
  waiting for transfers between devices  6.83 us (11%)
  local copies, waits for them, and re-layouts  0.77 us (1%)
    pallas_call x2, Pallas kernels, encode(): pl.pallas_call(functools.partial(encode_kernel, steps=steps, start=start,...  17 us
    ppermute x7, starting transfers between devices, body(): parts.append(lax.ppermute(block, 'pa', pairs))  10.4 us
    pallas_call x1, Pallas kernels, lookup(): pl.pallas_call(functools.partial(lookup_kernel, cut=cut, per_pair=per_pai...  8.55 us
    ppermute x1, starting transfers between devices, body(): came = lax.ppermute(passed, 'dev', swap)  7.11 us
    all_to_all x1, starting transfers between devices, body(): got = lax.all_to_all(sent, 'pa', split_axis=0, concat_axis=0, tiled=True)  6.35 us
    ppermute x7, waiting for transfers between devices, body(): parts.append(lax.ppermute(block, 'pa', pairs))  4.94 us
    ppermute x5, starting transfers between devices, body(): other = tuple((lax.ppermute(w, 'dev', swap) for w in own))  2.06 us
    pallas_call x1, Pallas kernels, finish_weights(): pl.pallas_call(functools.partial(weights_kernel, cut=cut), out_shape=[plt...  1.62 us
  transfers between devices with their start and end apart: 14, of which 5 were waited for; matrix products, arithmetic and copies ran while one was open for 0% of the time, Pallas kernels for 16%

profile of v9, /device:TPU:1, one launch (start us, length us, event | category | flops | bytes accessed | tf_op | source)
XLA Modules:
  0.0 60.8 jit_solution(2901131055351302300)
XLA Ops:
  0.0 8.5 %lookup.1 = (bf16[256,8,256]{2,1,0:T(8,128)(2,1)}, bf16[32,8,256]{2,1,0:T(8,128)(2,1)}, bf16[32,8,256]{2,1,0:T(8,128)(2,1)}, bf16[32,8,256]{2,1,0:T(8,128)(2,1)}...) custom-call(s32[8,1024]{1,0:T(8,128)} %bitcast.4, ...), custom_call_target="tpu_custom_call" | custom-call | tf_op jit(solution)/shard_map/lookup/pallas_call | solution.py:105
  8.6 0.0 copy-start.2
  8.6 0.0 copy-start.3
  8.6 0.0 copy-start.4
  8.6 0.0 copy-start.5
  8.6 0.0 copy-start.6
  8.6 6.3 %all-to-all-start = ((bf16[256,8,256]{2,1,0:T(8,128)(2,1)}), bf16[256,8,256]{2,1,0:T(8,128)(2,1)S(1)}, u32[]{:S(2)}, u32[]{:S(2)}) async-start(bf16[256,8,256]{2,1,0:T(8,128)(2,1)} %get-tuple-element.50), calls=%async_computation | async-start | bytes 2097152 | tf_op jit(solution)/shard_map/all_to_all | solution.py:419
  15.0 0.0 copy-done.2
  15.0 1.0 %collective-permute-start.3 = (bf16[256,512]{1,0:T(8,128)(2,1)S(1)}, bf16[256,512]{1,0:T(8,128)(2,1)S(1)}, u32[]{:S(2)}, u32[]{:S(2)}) collective-permute-start(bf16[256,512]{1,0:T(8,128)(2,1)S(1)} %copy-done.2), channel_id=1, source_target_pairs={{0,1},{1,0},{2,3},{3,2},{4,5},{5,4},{6,7},{7,6},{8,9},{9,8},{10,11... | collective-permute-start | bytes 786440 | tf_op jit(solution)/shard_map/ppermute | solution.py:421
  16.0 0.0 copy-done.3
  16.0 0.1 collective-permute-start.4
  16.1 0.0 copy-done.4
  16.1 0.4 collective-permute-start
  16.5 0.0 copy-done.5
  16.5 0.1 collective-permute-start.1
  16.6 0.0 copy-done.6
  16.6 0.4 collective-permute-start.2
  17.0 0.9 %collective-permute-done.1.out_b = bf16[128,256]{1,0:T(8,128)(2,1)S(1)} collective-permute-done((bf16[128,256]{1,0:T(8,128)(2,1)S(1)}, bf16[128,256]{1,0:T(8,128)(2,1)S(1)}, u32[]{:S(2)}, u32[]{:S(2)}) %collective-permute-start.1) | collective-permute-done | bytes 65568 | tf_op jit(solution)/shard_map/ppermute | solution.py:421
  17.9 0.1 collective-permute-done.2.bil_b
  18.0 0.0 collective-permute-done.qkv_b
  18.0 0.0 collective-permute-done.3.up_b
  18.0 0.0 collective-permute-done.4.down_b
  18.0 0.0 copy-start
  18.0 1.6 %weights.1 = (bf16[3328,256]{1,0:T(8,128)(2,1)S(1)}, f32[64,256]{1,0:T(8,128)S(1)}, f32[2,4,256]{2,1,0:T(4,128)S(1)}) custom-call(s32[8,128]{1,0:T(8,128)} %bitcast.5, s32[4,64]{1,0:T(4,128)} %seed_ref.1, bf16[3,256,128]{2,1,0:T(8,128)(2,1)} %qkv_a.1, bf16[3,256,128]{2,1,0:T(8,128)(2,1)S(1)} %collective-permute-done.qkv_b, bf16[128,256]{1,0:T(8,128)(2,1)} %out_a.1, ...), custom_call_target="tpu_custom_call" | custom-call | tf_op jit(solution)/shard_map/weights/pallas_call | solution.py:196
  19.7 1.7 %collective-permute-start.6 = (bf16[32,8,256]{2,1,0:T(8,128)(2,1)}, bf16[32,8,256]{2,1,0:T(8,128)(2,1)S(1)}, u32[]{:S(2)}, u32[]{:S(2)}) collective-permute-start(bf16[32,8,256]{2,1,0:T(8,128)(2,1)} %get-tuple-element.58), channel_id=1, source_target_pairs={{0,4},{2,6},{4,8},{6,10},{8,12},{10,14},{12,0},{14,2},{1,5},{3,7},... | collective-permute-start | bytes 393224 | tf_op jit(solution)/shard_map/ppermute | solution.py:434
  21.4 1.2 %collective-permute-start.5 = (bf16[32,8,256]{2,1,0:T(8,128)(2,1)}, bf16[32,8,256]{2,1,0:T(8,128)(2,1)S(1)}, u32[]{:S(2)}, u32[]{:S(2)}) collective-permute-start(bf16[32,8,256]{2,1,0:T(8,128)(2,1)} %get-tuple-element.55), channel_id=1, source_target_pairs={{0,2},{2,0},{4,6},{6,4},{8,10},{10,8},{12,14},{14,12},{1,3},{3,1},... | collective-permute-start | bytes 393224 | tf_op jit(solution)/shard_map/ppermute | solution.py:434
  22.6 1.2 %collective-permute-start.7 = (bf16[32,8,256]{2,1,0:T(8,128)(2,1)}, bf16[32,8,256]{2,1,0:T(8,128)(2,1)S(1)}, u32[]{:S(2)}, u32[]{:S(2)}) collective-permute-start(bf16[32,8,256]{2,1,0:T(8,128)(2,1)} %get-tuple-element.60), channel_id=1, source_target_pairs={{0,6},{2,4},{4,10},{6,8},{8,14},{10,12},{12,2},{14,0},{1,7},{3,5},... | collective-permute-start | bytes 393224 | tf_op jit(solution)/shard_map/ppermute | solution.py:434
  23.8 1.3 %collective-permute-start.8 = (bf16[32,8,256]{2,1,0:T(8,128)(2,1)}, bf16[32,8,256]{2,1,0:T(8,128)(2,1)S(1)}, u32[]{:S(2)}, u32[]{:S(2)}) collective-permute-start(bf16[32,8,256]{2,1,0:T(8,128)(2,1)} %get-tuple-element.61), channel_id=1, source_target_pairs={{0,8},{2,10},{4,12},{6,14},{8,0},{10,2},{12,4},{14,6},{1,9},{3,11}... | collective-permute-start | bytes 393224 | tf_op jit(solution)/shard_map/ppermute | solution.py:434
  25.1 2.6 %collective-permute-start.9 = (bf16[32,8,256]{2,1,0:T(8,128)(2,1)}, bf16[32,8,256]{2,1,0:T(8,128)(2,1)}, u32[]{:S(2)}, u32[]{:S(2)}) collective-permute-start(bf16[32,8,256]{2,1,0:T(8,128)(2,1)} %get-tuple-element.62), channel_id=1, source_target_pairs={{0,10},{2,8},{4,14},{6,12},{8,2},{10,0},{12,6},{14,4},{1,11},{3,9}... | collective-permute-start | bytes 393224 | tf_op jit(solution)/shard_map/ppermute | solution.py:434
  27.6 4.8 %collective-permute-done.6.refs_7_ = bf16[32,8,256]{2,1,0:T(8,128)(2,1)S(1)} collective-permute-done((bf16[32,8,256]{2,1,0:T(8,128)(2,1)}, bf16[32,8,256]{2,1,0:T(8,128)(2,1)S(1)}, u32[]{:S(2)}, u32[]{:S(2)}) %collective-permute-start.6) | collective-permute-done | bytes 131104 | tf_op jit(solution)/shard_map/ppermute | solution.py:434
  32.5 0.8 %collective-permute-start.11 = (bf16[32,8,256]{2,1,0:T(8,128)(2,1)}, bf16[32,8,256]{2,1,0:T(8,128)(2,1)}, u32[]{:S(2)}, u32[]{:S(2)}) collective-permute-start(bf16[32,8,256]{2,1,0:T(8,128)(2,1)} %get-tuple-element.64), channel_id=1, source_target_pairs={{0,14},{2,12},{4,2},{6,0},{8,6},{10,4},{12,10},{14,8},{1,15},{3,13... | collective-permute-start | bytes 393224 | tf_op jit(solution)/shard_map/ppermute | solution.py:434
  33.2 0.0 collective-permute-done.5.refs_6_
  33.2 1.7 %collective-permute-start.10 = (bf16[32,8,256]{2,1,0:T(8,128)(2,1)}, bf16[32,8,256]{2,1,0:T(8,128)(2,1)}, u32[]{:S(2)}, u32[]{:S(2)}) collective-permute-start(bf16[32,8,256]{2,1,0:T(8,128)(2,1)} %get-tuple-element.63), channel_id=1, source_target_pairs={{0,12},{2,14},{4,0},{6,2},{8,4},{10,6},{12,8},{14,10},{1,13},{3,15... | collective-permute-start | bytes 393224 | tf_op jit(solution)/shard_map/ppermute | solution.py:434
  34.9 0.0 all-to-all-done
  34.9 8.0 %encode.2 = (f32[64,4,128]{2,1,0:T(4,128)S(1)}, f32[64,4,128]{2,1,0:T(4,128)S(1)}) custom-call(f32[64,256]{1,0:T(8,128)S(1)} %get-tuple-element.47.refs_0_, f32[2,4,256]{2,1,0:T(4,128)S(1)} %get-tuple-element.48.refs_1_, bf16[3328,256]{1,0:T(8,128)(2,1)S(1)} %get-tuple-element.49.refs_2_, bf16[8,32,8,256]{3,2,1,0:T(8,128)(2,1)S(1)} %bitcast.3), custom_call_target="tpu_custom_call" | custom-call | tf_op jit(solution)/shard_map/encode/pallas_call | solution.py:395
  42.9 0.0 collective-permute-done.7.refs_8_
  42.9 0.0 collective-permute-done.8.refs_9_
  42.9 0.0 collective-permute-done.9.refs_10_
  42.9 0.0 collective-permute-done.11.refs_12_
  43.0 0.1 collective-permute-done.10.refs_11_
  43.0 0.0 copy-done
  43.0 9.0 %encode.3 = (f32[64,4,128]{2,1,0:T(4,128)S(1)}, f32[64,4,128]{2,1,0:T(4,128)S(1)}) custom-call(f32[64,256]{1,0:T(8,128)S(1)} %get-tuple-element.47.refs_0_, f32[2,4,256]{2,1,0:T(4,128)S(1)} %get-tuple-element.48.refs_1_, bf16[3328,256]{1,0:T(8,128)(2,1)S(1)} %get-tuple-element.49.refs_2_, f32[64,4,128]{2,1,0:T(4,128)S(1)} %get-tuple-element.51.refs_3_, ...), custom_call_target="tpu_custom_call" | custom-call | tf_op jit(solution)/shard_map/encode/pallas_call | solution.py:395
  52.1 7.1 %collective-permute-start.12 = (f32[64,4,128]{2,1,0:T(4,128)S(1)}, f32[64,4,128]{2,1,0:T(4,128)S(1)}, u32[]{:S(2)}, u32[]{:S(2)}) collective-permute-start(f32[64,4,128]{2,1,0:T(4,128)S(1)} %get-tuple-element.66), channel_id=1, source_target_pairs={{0,1},{1,0},{2,3},{3,2},{4,5},{5,4},{6,7},{7,6},{8,9},{9,8},{10,11... | collective-permute-start | bytes 393224 | tf_op jit(solution)/shard_map/ppermute | solution.py:437
  59.3 0.0 copy-start.1
  59.3 0.9 %collective-permute-done.12 = f32[64,4,128]{2,1,0:T(4,128)S(1)} collective-permute-done((f32[64,4,128]{2,1,0:T(4,128)S(1)}, f32[64,4,128]{2,1,0:T(4,128)S(1)}, u32[]{:S(2)}, u32[]{:S(2)}) %collective-permute-start.12) | collective-permute-done | bytes 131104 | tf_op jit(solution)/shard_map/ppermute | solution.py:437
  60.2 0.0 copy-done.1
  60.2 0.7 %constant_dynamic-update-slice_fusion = f32[128,4,128]{2,1,0:T(4,128)} fusion(f32[128,4,128]{2,1,0:T(4,128)} %copy-done.1, f32[64,4,128]{2,1,0:T(4,128)S(1)} %collective-permute-done.12, s32[]{:T(128)S(6)} %select_n.7), kind=kLoop, calls=%fused_computation | loop fusion | bytes 262148 | tf_op jit(solution)/shard_map/dynamic_update_slice | solution.py:440
  (2 shorter events, 0.1 us)
Async XLA Ops:
  8.6 6.4 %copy-start.2 = (bf16[256,512]{1,0:T(8,128)(2,1)S(1)}, bf16[256,512]{1,0:T(8,128)(2,1)}, u32[]{:S(2)}) copy-start(bf16[256,512]{1,0:T(8,128)(2,1)} %up_a.1) | copy-start | bytes 786436
  8.6 7.4 %copy-start.3 = (bf16[512,256]{1,0:T(8,128)(2,1)S(1)}, bf16[512,256]{1,0:T(8,128)(2,1)}, u32[]{:S(2)}) copy-start(bf16[512,256]{1,0:T(8,128)(2,1)} %down_a.1) | copy-start | bytes 786436
  8.6 7.5 %copy-start.4 = (bf16[3,256,128]{2,1,0:T(8,128)(2,1)S(1)}, bf16[3,256,128]{2,1,0:T(8,128)(2,1)}, u32[]{:S(2)}) copy-start(bf16[3,256,128]{2,1,0:T(8,128)(2,1)} %qkv_a.1) | copy-start | bytes 589828
  8.6 7.9 %copy-start.5 = (bf16[128,256]{1,0:T(8,128)(2,1)S(1)}, bf16[128,256]{1,0:T(8,128)(2,1)}, u32[]{:S(2)}) copy-start(bf16[128,256]{1,0:T(8,128)(2,1)} %out_a.1) | copy-start | bytes 196612
  8.6 8.0 %copy-start.6 = (bf16[256,128]{1,0:T(8,128)(2,1)S(1)}, bf16[256,128]{1,0:T(8,128)(2,1)}, u32[]{:S(2)}) copy-start(bf16[256,128]{1,0:T(8,128)(2,1)} %bil_a.1) | copy-start | bytes 196612
  8.6 26.3 %all-to-all-start = ((bf16[256,8,256]{2,1,0:T(8,128)(2,1)}), bf16[256,8,256]{2,1,0:T(8,128)(2,1)S(1)}, u32[]{:S(2)}, u32[]{:S(2)}) async-start(bf16[256,8,256]{2,1,0:T(8,128)(2,1)} %get-tuple-element.50), calls=%async_computation | async-start | bytes 2097152 | tf_op jit(solution)/shard_map/all_to_all | solution.py:419
  15.0 3.0 %collective-permute-start.3 = (bf16[256,512]{1,0:T(8,128)(2,1)S(1)}, bf16[256,512]{1,0:T(8,128)(2,1)S(1)}, u32[]{:S(2)}, u32[]{:S(2)}) collective-permute-start(bf16[256,512]{1,0:T(8,128)(2,1)S(1)} %copy-done.2), channel_id=1, source_target_pairs={{0,1},{1,0},{2,3},{3,2},{4,5},{5,4},{6,7},{7,6},{8,9},{9,8},{10,11... | collective-permute-start | bytes 786440 | tf_op jit(solution)/shard_map/ppermute | solution.py:421
  16.0 2.0 %collective-permute-start.4 = (bf16[512,256]{1,0:T(8,128)(2,1)S(1)}, bf16[512,256]{1,0:T(8,128)(2,1)S(1)}, u32[]{:S(2)}, u32[]{:S(2)}) collective-permute-start(bf16[512,256]{1,0:T(8,128)(2,1)S(1)} %copy-done.3), channel_id=1, source_target_pairs={{0,1},{1,0},{2,3},{3,2},{4,5},{5,4},{6,7},{7,6},{8,9},{9,8},{10,11... | collective-permute-start | bytes 786440 | tf_op jit(solution)/shard_map/ppermute | solution.py:421
  16.1 1.9 %collective-permute-start = (bf16[3,256,128]{2,1,0:T(8,128)(2,1)S(1)}, bf16[3,256,128]{2,1,0:T(8,128)(2,1)S(1)}, u32[]{:S(2)}, u32[]{:S(2)}) collective-permute-start(bf16[3,256,128]{2,1,0:T(8,128)(2,1)S(1)} %copy-done.4), channel_id=1, source_target_pairs={{0,1},{1,0},{2,3},{3,2},{4,5},{5,4},{6,7},{7,6},{8,9},{9,8},{10,11... | collective-permute-start | bytes 589832 | tf_op jit(solution)/shard_map/ppermute | solution.py:421
  16.5 1.4 %collective-permute-start.1 = (bf16[128,256]{1,0:T(8,128)(2,1)S(1)}, bf16[128,256]{1,0:T(8,128)(2,1)S(1)}, u32[]{:S(2)}, u32[]{:S(2)}) collective-permute-start(bf16[128,256]{1,0:T(8,128)(2,1)S(1)} %copy-done.5), channel_id=1, source_target_pairs={{0,1},{1,0},{2,3},{3,2},{4,5},{5,4},{6,7},{7,6},{8,9},{9,8},{10,11... | collective-permute-start | bytes 196616 | tf_op jit(solution)/shard_map/ppermute | solution.py:421
  16.6 1.4 %collective-permute-start.2 = (bf16[256,128]{1,0:T(8,128)(2,1)S(1)}, bf16[256,128]{1,0:T(8,128)(2,1)S(1)}, u32[]{:S(2)}, u32[]{:S(2)}) collective-permute-start(bf16[256,128]{1,0:T(8,128)(2,1)S(1)} %copy-done.6), channel_id=1, source_target_pairs={{0,1},{1,0},{2,3},{3,2},{4,5},{5,4},{6,7},{7,6},{8,9},{9,8},{10,11... | collective-permute-start | bytes 196616 | tf_op jit(solution)/shard_map/ppermute | solution.py:421
  18.0 25.0 %copy-start = (bf16[32,8,256]{2,1,0:T(8,128)(2,1)S(1)}, bf16[32,8,256]{2,1,0:T(8,128)(2,1)}, u32[]{:S(2)}) copy-start(bf16[32,8,256]{2,1,0:T(8,128)(2,1)} %get-tuple-element.53.refs_5_) | copy-start | bytes 393220
  19.7 12.8 %collective-permute-start.6 = (bf16[32,8,256]{2,1,0:T(8,128)(2,1)}, bf16[32,8,256]{2,1,0:T(8,128)(2,1)S(1)}, u32[]{:S(2)}, u32[]{:S(2)}) collective-permute-start(bf16[32,8,256]{2,1,0:T(8,128)(2,1)} %get-tuple-element.58), channel_id=1, source_target_pairs={{0,4},{2,6},{4,8},{6,10},{8,12},{10,14},{12,0},{14,2},{1,5},{3,7},... | collective-permute-start | bytes 393224 | tf_op jit(solution)/shard_map/ppermute | solution.py:434
  21.4 11.8 %collective-permute-start.5 = (bf16[32,8,256]{2,1,0:T(8,128)(2,1)}, bf16[32,8,256]{2,1,0:T(8,128)(2,1)S(1)}, u32[]{:S(2)}, u32[]{:S(2)}) collective-permute-start(bf16[32,8,256]{2,1,0:T(8,128)(2,1)} %get-tuple-element.55), channel_id=1, source_target_pairs={{0,2},{2,0},{4,6},{6,4},{8,10},{10,8},{12,14},{14,12},{1,3},{3,1},... | collective-permute-start | bytes 393224 | tf_op jit(solution)/shard_map/ppermute | solution.py:434
  22.6 20.3 %collective-permute-start.7 = (bf16[32,8,256]{2,1,0:T(8,128)(2,1)}, bf16[32,8,256]{2,1,0:T(8,128)(2,1)S(1)}, u32[]{:S(2)}, u32[]{:S(2)}) collective-permute-start(bf16[32,8,256]{2,1,0:T(8,128)(2,1)} %get-tuple-element.60), channel_id=1, source_target_pairs={{0,6},{2,4},{4,10},{6,8},{8,14},{10,12},{12,2},{14,0},{1,7},{3,5},... | collective-permute-start | bytes 393224 | tf_op jit(solution)/shard_map/ppermute | solution.py:434
  23.8 19.2 %collective-permute-start.8 = (bf16[32,8,256]{2,1,0:T(8,128)(2,1)}, bf16[32,8,256]{2,1,0:T(8,128)(2,1)S(1)}, u32[]{:S(2)}, u32[]{:S(2)}) collective-permute-start(bf16[32,8,256]{2,1,0:T(8,128)(2,1)} %get-tuple-element.61), channel_id=1, source_target_pairs={{0,8},{2,10},{4,12},{6,14},{8,0},{10,2},{12,4},{14,6},{1,9},{3,11}... | collective-permute-start | bytes 393224 | tf_op jit(solution)/shard_map/ppermute | solution.py:434
  25.1 17.9 %collective-permute-start.9 = (bf16[32,8,256]{2,1,0:T(8,128)(2,1)}, bf16[32,8,256]{2,1,0:T(8,128)(2,1)}, u32[]{:S(2)}, u32[]{:S(2)}) collective-permute-start(bf16[32,8,256]{2,1,0:T(8,128)(2,1)} %get-tuple-element.62), channel_id=1, source_target_pairs={{0,10},{2,8},{4,14},{6,12},{8,2},{10,0},{12,6},{14,4},{1,11},{3,9}... | collective-permute-start | bytes 393224 | tf_op jit(solution)/shard_map/ppermute | solution.py:434
  32.5 10.5 %collective-permute-start.11 = (bf16[32,8,256]{2,1,0:T(8,128)(2,1)}, bf16[32,8,256]{2,1,0:T(8,128)(2,1)}, u32[]{:S(2)}, u32[]{:S(2)}) collective-permute-start(bf16[32,8,256]{2,1,0:T(8,128)(2,1)} %get-tuple-element.64), channel_id=1, source_target_pairs={{0,14},{2,12},{4,2},{6,0},{8,6},{10,4},{12,10},{14,8},{1,15},{3,13... | collective-permute-start | bytes 393224 | tf_op jit(solution)/shard_map/ppermute | solution.py:434
  33.2 9.8 %collective-permute-start.10 = (bf16[32,8,256]{2,1,0:T(8,128)(2,1)}, bf16[32,8,256]{2,1,0:T(8,128)(2,1)}, u32[]{:S(2)}, u32[]{:S(2)}) collective-permute-start(bf16[32,8,256]{2,1,0:T(8,128)(2,1)} %get-tuple-element.63), channel_id=1, source_target_pairs={{0,12},{2,14},{4,0},{6,2},{8,4},{10,6},{12,8},{14,10},{1,13},{3,15... | collective-permute-start | bytes 393224 | tf_op jit(solution)/shard_map/ppermute | solution.py:434
  52.1 8.1 %collective-permute-start.12 = (f32[64,4,128]{2,1,0:T(4,128)S(1)}, f32[64,4,128]{2,1,0:T(4,128)S(1)}, u32[]{:S(2)}, u32[]{:S(2)}) collective-permute-start(f32[64,4,128]{2,1,0:T(4,128)S(1)} %get-tuple-element.66), channel_id=1, source_target_pairs={{0,1},{1,0},{2,3},{3,2},{4,5},{5,4},{6,7},{7,6},{8,9},{9,8},{10,11... | collective-permute-start | bytes 393224 | tf_op jit(solution)/shard_map/ppermute | solution.py:437
  59.3 0.9 %copy-start.1 = (f32[128,4,128]{2,1,0:T(4,128)}, f32[128,4,128]{2,1,0:T(4,128)S(1)}, u32[]{:S(2)}) copy-start(f32[128,4,128]{2,1,0:T(4,128)S(1)} %constant_dynamic-update-slice_fusion.1) | copy-start | bytes 786436

commit v10 on v8

--- a/solution.py
+++ b/solution.py
@@ -32,10 +32,28 @@
     return (place // Z_LO + along + rest) % rest * Z_LO + (place % Z_LO + across) % Z_LO
 
 
+def packed_pieces(qkv, out, bilinear, up, down):
+    half = D // 2
+    pieces = [qkv.at[i] for i in range(3)] + [bilinear]
+    for w in (up, out, down):
+        pieces += [w.at[:, pl.ds(i, half)] for i in range(0, w.shape[1], half)]
+    return pieces
+
+
 def lookup_kernel(*refs, start, per_pair, per_core, outs):
     later = outs > 1
-    ids_hbm, feat_hbm, table_hbm = refs[:3]
-    out_hbm, refs = refs[3 : 3 + outs], refs[3 + outs :]
+    ids_hbm, feat_hbm, table_hbm, refs = *refs[:3], refs[3:]
+    if not later:
+        own, refs = refs[:5], refs[5:]
+    out_hbm, refs = refs[:outs], refs[outs:]
+    pack = []
+    if not later:
+        packed, pack_sem, refs = refs[0], refs[-1], refs[1:-1]
+        at = 0
+        for piece in packed_pieces(*own):
+            target = packed.at[pl.ds(at, piece.shape[0])]
+            pack.append(pltpu.make_async_copy(piece, target, pack_sem.at[len(pack)]))
+            at += piece.shape[0]
     wide, table, table_sem, ids, feat, out, id_sem, feat_sem, out_sem = refs
     pairs, users, spots, _ = feat.shape
     place = lax.axis_index("pa")
@@ -52,6 +70,8 @@
         at = pl.ds(i * rows, rows)
         fetch_table.append(pltpu.make_async_copy(table_hbm.at[at], table.at[at], table_sem.at[i]))
         fetch_table[-1].start()
+    for copy in pack:
+        copy.start()
     fetch_feat = []
     for d in range(pairs):
         at = pl.ds(owners[d] * per_pair + offset, users)
@@ -92,11 +112,11 @@
             target = out_hbm[0].at[pl.ds(d * users, users)]
         send.append(pltpu.make_async_copy(out.at[d], target, out_sem.at[d]))
         send[-1].start()
-    for copy in send:
+    for copy in send + pack:
         copy.wait()
 
 
-def lookup(ids, features, table, start, users, pa_count, dev_count, later):
+def lookup(ids, features, table, start, users, pa_count, dev_count, later, own=()):
     all_users, spots, width = features.shape
     per_pair = all_users // pa_count
     per_core = per_pair // dev_count
@@ -104,6 +124,8 @@
     hbm = pl.BlockSpec(memory_space=pltpu.HBM)
     outs = pa_count if later else 1
     made = [pltpu.HBM((users * (1 if later else pa_count), spots, width), BF16)] * outs
+    if own:
+        made.append(pltpu.HBM((sum(w.size for w in own) // (D // 2), D // 2), BF16))
     scratch = [
         pltpu.VMEM((2, table.shape[0], D // 2), F32),
         pltpu.VMEM(table.shape, BF16),
@@ -115,22 +137,24 @@
         pltpu.SemaphoreType.DMA((pa_count,)),
         pltpu.SemaphoreType.DMA((pa_count,)),
     ]
+    if own:
+        pieces = 4 + sum(w.shape[1] // (D // 2) for w in (own[1], own[3], own[4]))
+        scratch.append(pltpu.SemaphoreType.DMA((pieces,)))
     return pl.pallas_call(
         functools.partial(
             lookup_kernel, start=start, per_pair=per_pair, per_core=per_core, outs=outs
         ),
         out_shape=made,
-        in_specs=[hbm, hbm, hbm],
-        out_specs=[hbm] * outs,
+        in_specs=[hbm] * (3 + len(own)),
+        out_specs=[hbm] * len(made),
         scratch_shapes=scratch,
         compiler_params=pltpu.CompilerParams(vmem_limit_bytes=12 << 20),
         name="lookup",
-    )(*in_hbm(ids, features, table))
+    )(*in_hbm(ids, features, table, *own))
 
 
 def weights_kernel(
-    lens_ref, seed_ref, qkv_a, qkv_b, out_a, out_b, bil_a, bil_b, up_a, up_b, down_a, down_b,
-    all_ref, valid_ref, base_ref, *, cut,
+    lens_ref, seed_ref, own, other, all_ref, valid_ref, base_ref, *, cut, ff
 ):
     pairs = lens_ref.shape[0]
     history = seed_ref.shape[1]
@@ -169,37 +193,45 @@
     low = lax.axis_index("dev") == 0
     at = 0
     for i in range(3):
-        all_ref[at : at + D, :half] = qkv_a[i]
-        all_ref[at : at + D, half:] = qkv_b[i]
+        all_ref[at : at + D, :half] = own[at : at + D]
+        all_ref[at : at + D, half:] = other[at : at + D]
         at += D
-    for up in (up_a, up_b):
-        for i in range(up.shape[1] // D):
-            all_ref[at : at + D, :] = up[:, i * D : (i + 1) * D]
+    bilinear = slice(at, at + D)
+    source = at + D
+    for part in (own, other):
+        for i in range(ff // D):
+            for h in range(2):
+                rows = slice(source + (2 * i + h) * D, source + (2 * i + h + 1) * D)
+                all_ref[at : at + D, h * half : (h + 1) * half] = part[rows]
             at += D
 
     @pl.when(low)
     def _():
-        all_ref[at : at + D, :half] = bil_a[...]
-        all_ref[at : at + D, half:] = bil_b[...]
+        all_ref[at : at + D, :half] = own[bilinear]
+        all_ref[at : at + D, half:] = other[bilinear]
 
     @pl.when(jnp.logical_not(low))
     def _():
-        all_ref[at : at + D, :half] = bil_b[...]
-        all_ref[at : at + D, half:] = bil_a[...]
+        all_ref[at : at + D, :half] = other[bilinear]
+        all_ref[at : at + D, half:] = own[bilinear]
 
     after = at + D
-    for rows in (out_a, out_b, down_a, down_b):
-        all_ref[after : after + rows.shape[0], :] = rows[...]
-        after += rows.shape[0]
-
-
-def finish_weights(own, other, lens, seed, cut, per_core):
-    ff = own[3].shape[1]
-    operands = [*in_hbm(lens, seed)] + [w for pair in zip(in_hbm(*own), other) for w in pair]
+    source += 2 * ff
+    for count in (half, ff):
+        for part in (own, other):
+            for h in range(2):
+                rows = slice(source + h * count, source + (h + 1) * count)
+                all_ref[after : after + count, h * half : (h + 1) * half] = part[rows]
+            after += count
+        source += 2 * count
+
+
+def finish_weights(own, other, lens, seed, cut, per_core, ff):
+    operands = in_hbm(lens, seed, own, other)
     vmem = pl.BlockSpec(memory_space=pltpu.VMEM)
     lanes = GROUP * seed.shape[1]
     return pl.pallas_call(
-        functools.partial(weights_kernel, cut=cut),
+        functools.partial(weights_kernel, cut=cut, ff=ff),
         out_shape=[
             pltpu.VMEM((5 * D + 4 * ff, D), BF16),
             pltpu.VMEM((per_core, lanes), F32),
@@ -403,7 +435,7 @@
         in_specs=[vmem] * len(operands),
         out_specs=[vmem] * 2,
         scratch_shapes=[pltpu.VMEM((rows, D), BF16)],
-        compiler_params=pltpu.CompilerParams(vmem_limit_bytes=24 << 20),
+        compiler_params=pltpu.CompilerParams(vmem_limit_bytes=10 << 20),
         name="encode",
     )(*operands)
 
@@ -421,15 +453,15 @@
     cut = per_core * FIRST[0] // FIRST[1]
     ids = item_ids.T
     counts = (pa_count, dev_count)
-    sent = lookup(ids, features, item_table, 0, cut, *counts, False)[0]
+    sent, packed = lookup(ids, features, item_table, 0, cut, *counts, False, own)
     got = lax.all_to_all(sent, "pa", split_axis=0, concat_axis=0, tiled=True)
     got = got.reshape(pa_count, cut, spots, D)
-    other = tuple(lax.ppermute(w, "dev", swap) for w in own)
-    weights, valid, base = finish_weights(
-        own, other, lengths.reshape(pa_count, -1), routing_seed, cut, per_core
-    )
-    ids, weights, valid, base = lax.optimization_barrier((ids, weights, valid, base))
+    other = lax.ppermute(packed, "dev", swap)
+    ids, other = lax.optimization_barrier((ids, other))
     late = lookup(ids, features, item_table, cut, per_core - cut, *counts, True)
+    lens, late = lax.optimization_barrier((lengths.reshape(pa_count, -1), late))
+    ff = w_up.shape[1]
+    weights, valid, base = finish_weights(packed, other, lens, routing_seed, cut, per_core, ff)
     parts = [late[0]]
     for i in range(1, pa_count):
         pairs = [
@@ -437,7 +469,9 @@
         ]
         block = late[i]
         if i > AHEAD:
-            block, parts[i - AHEAD] = lax.optimization_barrier((block, parts[i - AHEAD]))
+            block, parts[i - AHEAD], valid = lax.optimization_barrier(
+                (block, parts[i - AHEAD], valid)
+            )
         parts.append(lax.ppermute(block, "pa", pairs))
     made = encode([got], valid, base, weights, STEPS[0], 0, ())
     kept, passed = encode(parts, valid, base, weights, STEPS[1], cut, tuple(made))

time: 54.2 us -> 75.3 us (1.39)
  Pallas kernels: 29.6 us -> 52 us
  starting transfers between devices: 19.8 us -> 17.5 us
  waiting for transfers between devices: 3.57 us -> 4.66 us
    pallas_call x2, Pallas kernels: 11.1 us -> 33 us  [lookup(): pl.pallas_call(functools.partial(lookup_kernel, start=start, per_pair=per...]
    ppermute x7, waiting for transfers between devices: 1.68 us -> 3.75 us  [body(): parts.append(lax.ppermute(block, 'pa', pairs))]
    ppermute x5 -> x1, waiting for transfers between devices: 0.98 us -> 0.01 us  [body(): other = lax.ppermute(packed, 'dev', swap)]
    all_to_all x1, starting transfers between devices: 6.22 us -> 5.46 us  [body(): got = lax.all_to_all(sent, 'pa', split_axis=0, concat_axis=0, tiled=True)]
    ppermute x5 -> x1, starting transfers between devices: 2.05 us -> 1.5 us  [body(): other = lax.ppermute(packed, 'dev', swap)]
  transfers between devices with their start and end apart: 14 -> 10, of which waited for: 5 -> 4; matrix products, arithmetic and copies ran while one was open for 0% -> 0% of each run, Pallas kernels for 28% -> 21%
where the time goes in v10:
time: 75.3 us; the launch traced here: 75 us
  Pallas kernels  52 us (69%)
  starting transfers between devices  17.5 us (23%)
  waiting for transfers between devices  4.66 us (6%)
    pallas_call x2, Pallas kernels, lookup(): pl.pallas_call(functools.partial(lookup_kernel, start=start, per_pair=per...  33 us
    pallas_call x2, Pallas kernels, encode(): pl.pallas_call(functools.partial(encode_kernel, steps=steps, start=start,...  17 us
    ppermute x7, starting transfers between devices, body(): parts.append(lax.ppermute(block, 'pa', pairs))  9.03 us
    all_to_all x1, starting transfers between devices, body(): got = lax.all_to_all(sent, 'pa', split_axis=0, concat_axis=0, tiled=True)  5.46 us
    ppermute x7, waiting for transfers between devices, body(): parts.append(lax.ppermute(block, 'pa', pairs))  3.75 us
    pallas_call x1, Pallas kernels, finish_weights(): pl.pallas_call(functools.partial(weights_kernel, cut=cut, ff=ff), out_sha...  1.96 us
    ppermute x1, starting transfers between devices, body(): came = lax.ppermute(passed, 'dev', swap)  1.54 us
  transfers between devices with their start and end apart: 10, of which 4 were waited for; matrix products, arithmetic and copies ran while one was open for 0% of the time, Pallas kernels for 21%

profile of v10, /device:TPU:1, one launch (start us, length us, event | category | flops | bytes accessed | tf_op | source)
XLA Modules:
  0.0 75.0 jit_solution(6107378713902208503)
XLA Ops:
  0.0 27.2 %lookup.2 = (bf16[256,8,256]{2,1,0:T(8,128)(2,1)}, bf16[3328,128]{1,0:T(8,128)(2,1)}) custom-call(s32[8,1024]{1,0:T(8,128)} %bitcast.4, bf16[1024,8,256]{2,1,0:T(8,128)(2,1)} %refs_1_.3, bf16[4096,256]{1,0:T(8,128)(2,1)} %refs_2_.3, bf16[3,256,128]{2,1,0:T(8,128)(2,1)} %refs_3_.1, bf16[128,256]{1,0:T(8,128)(2,1)} %refs_4_.1, bf16[256,128]{1,0:T(8,128)(2,1)} %refs_5_.1, ...), custom_call_target="tpu_custom_call" | custom-call | tf_op jit(solution)/shard_map/lookup/pallas_call | solution.py:143
  27.2 1.5 %collective-permute-start = (bf16[3328,128]{1,0:T(8,128)(2,1)}, bf16[3328,128]{1,0:T(8,128)(2,1)S(1)}, u32[]{:S(2)}, u32[]{:S(2)}) collective-permute-start(bf16[3328,128]{1,0:T(8,128)(2,1)} %get-tuple-element.39.own), channel_id=1, source_target_pairs={{0,1},{1,0},{2,3},{3,2},{4,5},{5,4},{6,7},{7,6},{8,9},{9,8},{10,11... | collective-permute-start | bytes 2555912 | tf_op jit(solution)/shard_map/ppermute | solution.py:459
  28.7 5.5 %all-to-all-start = ((bf16[256,8,256]{2,1,0:T(8,128)(2,1)}), bf16[256,8,256]{2,1,0:T(8,128)(2,1)S(1)}, u32[]{:S(2)}, u32[]{:S(2)}) async-start(bf16[256,8,256]{2,1,0:T(8,128)(2,1)} %get-tuple-element.60), calls=%async_computation | async-start | bytes 2097152 | tf_op jit(solution)/shard_map/all_to_all | solution.py:457
  34.2 0.0 collective-permute-done.other
  34.2 0.0 copy-start.1
  34.2 5.8 %lookup.3 = (bf16[32,8,256]{2,1,0:T(8,128)(2,1)}, bf16[32,8,256]{2,1,0:T(8,128)(2,1)}, bf16[32,8,256]{2,1,0:T(8,128)(2,1)}, bf16[32,8,256]{2,1,0:T(8,128)(2,1)},...) custom-call(s32[8,1024]{1,0:T(8,128)} %bitcast.5, ...), custom_call_target="tpu_custom_call" | custom-call | tf_op jit(solution)/shard_map/lookup/pallas_call | solution.py:143
  40.0 0.0 copy-done.1
  40.0 0.0 copy-start
  40.1 1.5 %collective-permute-start.2 = (bf16[32,8,256]{2,1,0:T(8,128)(2,1)}, bf16[32,8,256]{2,1,0:T(8,128)(2,1)S(1)}, u32[]{:S(2)}, u32[]{:S(2)}) collective-permute-start(bf16[32,8,256]{2,1,0:T(8,128)(2,1)} %get-tuple-element.52), channel_id=1, source_target_pairs={{0,2},{2,0},{4,6},{6,4},{8,10},{10,8},{12,14},{14,12},{1,3},{3,1},... | collective-permute-start | bytes 393224 | tf_op jit(solution)/shard_map/ppermute | solution.py:475
  41.6 1.2 %collective-permute-start.1 = (bf16[32,8,256]{2,1,0:T(8,128)(2,1)}, bf16[32,8,256]{2,1,0:T(8,128)(2,1)S(1)}, u32[]{:S(2)}, u32[]{:S(2)}) collective-permute-start(bf16[32,8,256]{2,1,0:T(8,128)(2,1)} %get-tuple-element.50), channel_id=1, source_target_pairs={{0,4},{2,6},{4,8},{6,10},{8,12},{10,14},{12,0},{14,2},{1,5},{3,7},... | collective-permute-start | bytes 393224 | tf_op jit(solution)/shard_map/ppermute | solution.py:475
  42.8 1.2 %collective-permute-start.3 = (bf16[32,8,256]{2,1,0:T(8,128)(2,1)}, bf16[32,8,256]{2,1,0:T(8,128)(2,1)S(1)}, u32[]{:S(2)}, u32[]{:S(2)}) collective-permute-start(bf16[32,8,256]{2,1,0:T(8,128)(2,1)} %get-tuple-element.66), channel_id=1, source_target_pairs={{0,6},{2,4},{4,10},{6,8},{8,14},{10,12},{12,2},{14,0},{1,7},{3,5},... | collective-permute-start | bytes 393224 | tf_op jit(solution)/shard_map/ppermute | solution.py:475
  44.0 1.3 %collective-permute-start.4 = (bf16[32,8,256]{2,1,0:T(8,128)(2,1)}, bf16[32,8,256]{2,1,0:T(8,128)(2,1)S(1)}, u32[]{:S(2)}, u32[]{:S(2)}) collective-permute-start(bf16[32,8,256]{2,1,0:T(8,128)(2,1)} %get-tuple-element.67), channel_id=1, source_target_pairs={{0,8},{2,10},{4,12},{6,14},{8,0},{10,2},{12,4},{14,6},{1,9},{3,11}... | collective-permute-start | bytes 393224 | tf_op jit(solution)/shard_map/ppermute | solution.py:475
  45.3 2.6 %collective-permute-start.5 = (bf16[32,8,256]{2,1,0:T(8,128)(2,1)}, bf16[32,8,256]{2,1,0:T(8,128)(2,1)}, u32[]{:S(2)}, u32[]{:S(2)}) collective-permute-start(bf16[32,8,256]{2,1,0:T(8,128)(2,1)} %get-tuple-element.68), channel_id=1, source_target_pairs={{0,10},{2,8},{4,14},{6,12},{8,2},{10,0},{12,6},{14,4},{1,11},{3,9}... | collective-permute-start | bytes 393224 | tf_op jit(solution)/shard_map/ppermute | solution.py:475
  47.8 2.0 %weights.1 = (bf16[3328,256]{1,0:T(8,128)(2,1)S(1)}, f32[64,256]{1,0:T(8,128)S(1)}, f32[2,4,256]{2,1,0:T(4,128)S(1)}) custom-call(s32[8,128]{1,0:T(8,128)} %bitcast.6, s32[4,64]{1,0:T(4,128)} %seed_ref.1, bf16[3328,128]{1,0:T(8,128)(2,1)} %get-tuple-element.39.own, bf16[3328,128]{1,0:T(8,128)(2,1)} %copy-done.1), custom_call_target="tpu_custom_call" | custom-call | tf_op jit(solution)/shard_map/weights/pallas_call | solution.py:233
  49.8 1.3 %collective-permute-done.2.refs_6_ = bf16[32,8,256]{2,1,0:T(8,128)(2,1)S(1)} collective-permute-done((bf16[32,8,256]{2,1,0:T(8,128)(2,1)}, bf16[32,8,256]{2,1,0:T(8,128)(2,1)S(1)}, u32[]{:S(2)}, u32[]{:S(2)}) %collective-permute-start.2) | collective-permute-done | bytes 131104 | tf_op jit(solution)/shard_map/ppermute | solution.py:475
  51.1 2.2 %collective-permute-done.1.refs_7_ = bf16[32,8,256]{2,1,0:T(8,128)(2,1)S(1)} collective-permute-done((bf16[32,8,256]{2,1,0:T(8,128)(2,1)}, bf16[32,8,256]{2,1,0:T(8,128)(2,1)S(1)}, u32[]{:S(2)}, u32[]{:S(2)}) %collective-permute-start.1) | collective-permute-done | bytes 131104 | tf_op jit(solution)/shard_map/ppermute | solution.py:475
  53.3 0.8 %collective-permute-start.7 = (bf16[32,8,256]{2,1,0:T(8,128)(2,1)}, bf16[32,8,256]{2,1,0:T(8,128)(2,1)}, u32[]{:S(2)}, u32[]{:S(2)}) collective-permute-start(bf16[32,8,256]{2,1,0:T(8,128)(2,1)} %get-tuple-element.70), channel_id=1, source_target_pairs={{0,14},{2,12},{4,2},{6,0},{8,6},{10,4},{12,10},{14,8},{1,15},{3,13... | collective-permute-start | bytes 393224 | tf_op jit(solution)/shard_map/ppermute | solution.py:475
  54.1 0.5 collective-permute-start.6
  54.5 0.0 all-to-all-done
  54.5 8.0 %encode.2 = (f32[64,4,128]{2,1,0:T(4,128)S(1)}, f32[64,4,128]{2,1,0:T(4,128)S(1)}) custom-call(f32[64,256]{1,0:T(8,128)S(1)} %get-tuple-element.57.refs_0_, f32[2,4,256]{2,1,0:T(4,128)S(1)} %get-tuple-element.58.refs_1_, bf16[3328,256]{1,0:T(8,128)(2,1)S(1)} %get-tuple-element.59.refs_2_, bf16[8,32,8,256]{3,2,1,0:T(8,128)(2,1)S(1)} %bitcast.3), custom_call_target="tpu_custom_call" | custom-call | tf_op jit(solution)/shard_map/encode/pallas_call | solution.py:431
  62.5 0.0 collective-permute-done.3.refs_8_
  62.5 0.0 collective-permute-done.4.refs_9_
  62.5 0.3 collective-permute-done.5.refs_10_
  62.8 0.0 collective-permute-done.7.refs_12_
  62.8 0.0 collective-permute-done.6.refs_11_
  62.8 0.0 copy-done
  62.8 9.0 %encode.3 = (f32[64,4,128]{2,1,0:T(4,128)S(1)}, f32[64,4,128]{2,1,0:T(4,128)S(1)}) custom-call(f32[64,256]{1,0:T(8,128)S(1)} %get-tuple-element.57.refs_0_, f32[2,4,256]{2,1,0:T(4,128)S(1)} %get-tuple-element.58.refs_1_, bf16[3328,256]{1,0:T(8,128)(2,1)S(1)} %get-tuple-element.59.refs_2_, f32[64,4,128]{2,1,0:T(4,128)S(1)} %get-tuple-element.61.refs_3_, ...), custom_call_target="tpu_custom_call" | custom-call | tf_op jit(solution)/shard_map/encode/pallas_call | solution.py:431
  71.8 1.5 %collective-permute-start.8 = (f32[64,4,128]{2,1,0:T(4,128)S(1)}, f32[64,4,128]{2,1,0:T(4,128)S(1)}, u32[]{:S(2)}, u32[]{:S(2)}) collective-permute-start(f32[64,4,128]{2,1,0:T(4,128)S(1)} %get-tuple-element.72), channel_id=1, source_target_pairs={{0,1},{1,0},{2,3},{3,2},{4,5},{5,4},{6,7},{7,6},{8,9},{9,8},{10,11... | collective-permute-start | bytes 393224 | tf_op jit(solution)/shard_map/ppermute | solution.py:478
  73.5 0.0 copy-start.2
  73.5 0.9 %collective-permute-done.8 = f32[64,4,128]{2,1,0:T(4,128)S(1)} collective-permute-done((f32[64,4,128]{2,1,0:T(4,128)S(1)}, f32[64,4,128]{2,1,0:T(4,128)S(1)}, u32[]{:S(2)}, u32[]{:S(2)}) %collective-permute-start.8) | collective-permute-done | bytes 131104 | tf_op jit(solution)/shard_map/ppermute | solution.py:478
  74.4 0.0 copy-done.2
  74.4 0.7 constant_dynamic-update-slice_fusion
  (2 shorter events, 0.1 us)
Async XLA Ops:
  27.2 7.0 %collective-permute-start = (bf16[3328,128]{1,0:T(8,128)(2,1)}, bf16[3328,128]{1,0:T(8,128)(2,1)S(1)}, u32[]{:S(2)}, u32[]{:S(2)}) collective-permute-start(bf16[3328,128]{1,0:T(8,128)(2,1)} %get-tuple-element.39.own), channel_id=1, source_target_pairs={{0,1},{1,0},{2,3},{3,2},{4,5},{5,4},{6,7},{7,6},{8,9},{9,8},{10,11... | collective-permute-start | bytes 2555912 | tf_op jit(solution)/shard_map/ppermute | solution.py:459
  28.7 25.8 %all-to-all-start = ((bf16[256,8,256]{2,1,0:T(8,128)(2,1)}), bf16[256,8,256]{2,1,0:T(8,128)(2,1)S(1)}, u32[]{:S(2)}, u32[]{:S(2)}) async-start(bf16[256,8,256]{2,1,0:T(8,128)(2,1)} %get-tuple-element.60), calls=%async_computation | async-start | bytes 2097152 | tf_op jit(solution)/shard_map/all_to_all | solution.py:457
  34.2 5.9 %copy-start.1 = (bf16[3328,128]{1,0:T(8,128)(2,1)}, bf16[3328,128]{1,0:T(8,128)(2,1)S(1)}, u32[]{:S(2)}) copy-start(bf16[3328,128]{1,0:T(8,128)(2,1)S(1)} %collective-permute-done.other) | copy-start | bytes 2555908
  40.0 22.8 %copy-start = (bf16[32,8,256]{2,1,0:T(8,128)(2,1)S(1)}, bf16[32,8,256]{2,1,0:T(8,128)(2,1)}, u32[]{:S(2)}) copy-start(bf16[32,8,256]{2,1,0:T(8,128)(2,1)} %get-tuple-element.63.refs_5_) | copy-start | bytes 393220
  40.1 11.0 %collective-permute-start.2 = (bf16[32,8,256]{2,1,0:T(8,128)(2,1)}, bf16[32,8,256]{2,1,0:T(8,128)(2,1)S(1)}, u32[]{:S(2)}, u32[]{:S(2)}) collective-permute-start(bf16[32,8,256]{2,1,0:T(8,128)(2,1)} %get-tuple-element.52), channel_id=1, source_target_pairs={{0,2},{2,0},{4,6},{6,4},{8,10},{10,8},{12,14},{14,12},{1,3},{3,1},... | collective-permute-start | bytes 393224 | tf_op jit(solution)/shard_map/ppermute | solution.py:475
  41.6 11.7 %collective-permute-start.1 = (bf16[32,8,256]{2,1,0:T(8,128)(2,1)}, bf16[32,8,256]{2,1,0:T(8,128)(2,1)S(1)}, u32[]{:S(2)}, u32[]{:S(2)}) collective-permute-start(bf16[32,8,256]{2,1,0:T(8,128)(2,1)} %get-tuple-element.50), channel_id=1, source_target_pairs={{0,4},{2,6},{4,8},{6,10},{8,12},{10,14},{12,0},{14,2},{1,5},{3,7},... | collective-permute-start | bytes 393224 | tf_op jit(solution)/shard_map/ppermute | solution.py:475
  42.8 19.7 %collective-permute-start.3 = (bf16[32,8,256]{2,1,0:T(8,128)(2,1)}, bf16[32,8,256]{2,1,0:T(8,128)(2,1)S(1)}, u32[]{:S(2)}, u32[]{:S(2)}) collective-permute-start(bf16[32,8,256]{2,1,0:T(8,128)(2,1)} %get-tuple-element.66), channel_id=1, source_target_pairs={{0,6},{2,4},{4,10},{6,8},{8,14},{10,12},{12,2},{14,0},{1,7},{3,5},... | collective-permute-start | bytes 393224 | tf_op jit(solution)/shard_map/ppermute | solution.py:475
  44.0 18.6 %collective-permute-start.4 = (bf16[32,8,256]{2,1,0:T(8,128)(2,1)}, bf16[32,8,256]{2,1,0:T(8,128)(2,1)S(1)}, u32[]{:S(2)}, u32[]{:S(2)}) collective-permute-start(bf16[32,8,256]{2,1,0:T(8,128)(2,1)} %get-tuple-element.67), channel_id=1, source_target_pairs={{0,8},{2,10},{4,12},{6,14},{8,0},{10,2},{12,4},{14,6},{1,9},{3,11}... | collective-permute-start | bytes 393224 | tf_op jit(solution)/shard_map/ppermute | solution.py:475
  45.3 17.5 %collective-permute-start.5 = (bf16[32,8,256]{2,1,0:T(8,128)(2,1)}, bf16[32,8,256]{2,1,0:T(8,128)(2,1)}, u32[]{:S(2)}, u32[]{:S(2)}) collective-permute-start(bf16[32,8,256]{2,1,0:T(8,128)(2,1)} %get-tuple-element.68), channel_id=1, source_target_pairs={{0,10},{2,8},{4,14},{6,12},{8,2},{10,0},{12,6},{14,4},{1,11},{3,9}... | collective-permute-start | bytes 393224 | tf_op jit(solution)/shard_map/ppermute | solution.py:475
  53.3 9.5 %collective-permute-start.7 = (bf16[32,8,256]{2,1,0:T(8,128)(2,1)}, bf16[32,8,256]{2,1,0:T(8,128)(2,1)}, u32[]{:S(2)}, u32[]{:S(2)}) collective-permute-start(bf16[32,8,256]{2,1,0:T(8,128)(2,1)} %get-tuple-element.70), channel_id=1, source_target_pairs={{0,14},{2,12},{4,2},{6,0},{8,6},{10,4},{12,10},{14,8},{1,15},{3,13... | collective-permute-start | bytes 393224 | tf_op jit(solution)/shard_map/ppermute | solution.py:475
  54.1 8.7 %collective-permute-start.6 = (bf16[32,8,256]{2,1,0:T(8,128)(2,1)}, bf16[32,8,256]{2,1,0:T(8,128)(2,1)}, u32[]{:S(2)}, u32[]{:S(2)}) collective-permute-start(bf16[32,8,256]{2,1,0:T(8,128)(2,1)} %get-tuple-element.69), channel_id=1, source_target_pairs={{0,12},{2,14},{4,0},{6,2},{8,4},{10,6},{12,8},{14,10},{1,13},{3,15... | collective-permute-start | bytes 393224 | tf_op jit(solution)/shard_map/ppermute | solution.py:475
  71.8 2.5 %collective-permute-start.8 = (f32[64,4,128]{2,1,0:T(4,128)S(1)}, f32[64,4,128]{2,1,0:T(4,128)S(1)}, u32[]{:S(2)}, u32[]{:S(2)}) collective-permute-start(f32[64,4,128]{2,1,0:T(4,128)S(1)} %get-tuple-element.72), channel_id=1, source_target_pairs={{0,1},{1,0},{2,3},{3,2},{4,5},{5,4},{6,7},{7,6},{8,9},{9,8},{10,11... | collective-permute-start | bytes 393224 | tf_op jit(solution)/shard_map/ppermute | solution.py:478
  73.5 0.9 %copy-start.2 = (f32[128,4,128]{2,1,0:T(4,128)}, f32[128,4,128]{2,1,0:T(4,128)S(1)}, u32[]{:S(2)}) copy-start(f32[128,4,128]{2,1,0:T(4,128)S(1)} %constant_dynamic-update-slice_fusion.1) | copy-start | bytes 786436

commit v11 on v10

--- a/solution.py
+++ b/solution.py
@@ -15,7 +15,7 @@
 FIRST = (4, 8)
 BLOCK = 8
 STEPS = (2, 2)
-TABLE_PARTS = 4
+TABLE_PARTS = 2
 AHEAD = 5
 Z_LO = 2
 GROUP = 4
@@ -34,9 +34,9 @@
 
 def packed_pieces(qkv, out, bilinear, up, down):
     half = D // 2
-    pieces = [qkv.at[i] for i in range(3)] + [bilinear]
+    pieces = [(qkv, (i,)) for i in range(3)] + [(bilinear, ())]
     for w in (up, out, down):
-        pieces += [w.at[:, pl.ds(i, half)] for i in range(0, w.shape[1], half)]
+        pieces += [(w, (slice(None), slice(i, i + half))) for i in range(0, w.shape[1], half)]
     return pieces
 
 
@@ -46,14 +46,12 @@
     if not later:
         own, refs = refs[:5], refs[5:]
     out_hbm, refs = refs[:outs], refs[outs:]
-    pack = []
+    fetch_own = []
     if not later:
-        packed, pack_sem, refs = refs[0], refs[-1], refs[1:-1]
-        at = 0
-        for piece in packed_pieces(*own):
-            target = packed.at[pl.ds(at, piece.shape[0])]
-            pack.append(pltpu.make_async_copy(piece, target, pack_sem.at[len(pack)]))
-            at += piece.shape[0]
+        packed_hbm, held, packed, own_sem = refs[0], refs[-7:-2], refs[-2], refs[-1]
+        refs = refs[1:-7]
+        for i, w in enumerate(own):
+            fetch_own.append(pltpu.make_async_copy(w, held[i], own_sem.at[i]))
     wide, table, table_sem, ids, feat, out, id_sem, feat_sem, out_sem = refs
     pairs, users, spots, _ = feat.shape
     place = lax.axis_index("pa")
@@ -70,7 +68,7 @@
         at = pl.ds(i * rows, rows)
         fetch_table.append(pltpu.make_async_copy(table_hbm.at[at], table.at[at], table_sem.at[i]))
         fetch_table[-1].start()
-    for copy in pack:
+    for copy in fetch_own:
         copy.start()
     fetch_feat = []
     for d in range(pairs):
@@ -87,9 +85,19 @@
             return carry
 
         lax.fori_loop(0, rows // 128, widen, 0)
+    send = []
+    if not later:
+        for copy in fetch_own:
+            copy.wait()
+        at = 0
+        for ref, index in packed_pieces(*held):
+            piece = ref[(*index, Ellipsis)]
+            packed[at : at + piece.shape[0], :] = piece
+            at += piece.shape[0]
+        send.append(pltpu.make_async_copy(packed, packed_hbm, own_sem.at[len(own)]))
+        send[-1].start()
     fetch_ids.wait()
     spot = lax.broadcasted_iota(jnp.int32, (spots, D // 2), 0)
-    send = []
     for d in range(pairs):
         fetch_feat[d].wait()
         first = owners[d] * per_pair + offset
@@ -105,14 +113,14 @@
             out[d, user] = (feat[d, user].astype(F32) + rows).astype(BF16)
             return carry
 
-        lax.fori_loop(0, users, one, 0, unroll=8)
+        lax.fori_loop(0, users, one, 0, unroll=16)
         if later:
             target = out_hbm[d]
         else:
             target = out_hbm[0].at[pl.ds(d * users, users)]
         send.append(pltpu.make_async_copy(out.at[d], target, out_sem.at[d]))
         send[-1].start()
-    for copy in send + pack:
+    for copy in send:
         copy.wait()
 
 
@@ -138,8 +146,8 @@
         pltpu.SemaphoreType.DMA((pa_count,)),
     ]
     if own:
-        pieces = 4 + sum(w.shape[1] // (D // 2) for w in (own[1], own[3], own[4]))
-        scratch.append(pltpu.SemaphoreType.DMA((pieces,)))
+        scratch += [pltpu.VMEM(w.shape, BF16) for w in own]
+        scratch += [pltpu.VMEM(made[-1].shape, BF16), pltpu.SemaphoreType.DMA((len(own) + 1,))]
     return pl.pallas_call(
         functools.partial(
             lookup_kernel, start=start, per_pair=per_pair, per_core=per_core, outs=outs
@@ -290,7 +298,7 @@
     row_head = lax.broadcasted_iota(jnp.int32, (lanes, D), 0) // history
     col_head = lax.broadcasted_iota(jnp.int32, (lanes, D), 1) // head
     ones = (row_head == col_head).astype(F32).astype(BF16)
-    key_valid = valid_ref[pl.ds(start + step * block, block), :]
+    key_valid = [valid_ref[pl.ds(start + step * block + u, 1), :] for u in range(block)]
     users = [slice(u * history, (u + 1) * history) for u in range(block)]
     scores = []
     none = jnp.zeros((history, D // 2), BF16)
@@ -315,7 +323,7 @@
             rows_u = both[u * D // 2 : (u + 1) * D // 2, u * D // 2 : (u + 1) * D // 2]
             scores.append(jnp.concatenate([rows_u[:history], rows_u[history:]], axis=1))
     rounded = [
-        jnp.where(key_valid[u : u + 1] > 0.0, jnp.exp(s), 0.0).astype(BF16)
+        jnp.where(key_valid[u] > 0.0, jnp.exp(s), 0.0).astype(BF16)
         for u, s in enumerate(scores)
     ]
     totals = jnp.dot(jnp.concatenate(rounded, axis=0), ones, preferred_element_type=F32)

time: 75.3 us -> 54 us (0.72)
  Pallas kernels: 52 us -> 30.7 us
    pallas_call x2, Pallas kernels: 33 us -> 11.7 us  [lookup(): pl.pallas_call(functools.partial(lookup_kernel, start=start, per_pair=per...]
  transfers between devices with their start and end apart: 10 -> 10, of which waited for: 4 -> 4; matrix products, arithmetic and copies ran while one was open for 0% -> 0% of each run, Pallas kernels for 21% -> 29%
where the time goes in v11:
time: 54 us; the launch traced here: 53.7 us
  Pallas kernels  30.7 us (57%)
  starting transfers between devices  17.5 us (32%)
  waiting for transfers between devices  4.65 us (9%)
  local copies, waits for them, and re-layouts  0.74 us (1%)
    pallas_call x2, Pallas kernels, encode(): pl.pallas_call(functools.partial(encode_kernel, steps=steps, start=start,...  17 us
    pallas_call x2, Pallas kernels, lookup(): pl.pallas_call(functools.partial(lookup_kernel, start=start, per_pair=per...  11.7 us
    ppermute x7, starting transfers between devices, body(): parts.append(lax.ppermute(block, 'pa', pairs))  9.02 us
    all_to_all x1, starting transfers between devices, body(): got = lax.all_to_all(sent, 'pa', split_axis=0, concat_axis=0, tiled=True)  5.46 us
    ppermute x7, waiting for transfers between devices, body(): parts.append(lax.ppermute(block, 'pa', pairs))  3.74 us
    pallas_call x1, Pallas kernels, finish_weights(): pl.pallas_call(functools.partial(weights_kernel, cut=cut, ff=ff), out_sha...  1.96 us
    ppermute x1, starting transfers between devices, body(): came = lax.ppermute(passed, 'dev', swap)  1.55 us
    ppermute x1, starting transfers between devices, body(): other = lax.ppermute(packed, 'dev', swap)  1.5 us
  transfers between devices with their start and end apart: 10, of which 4 were waited for; matrix products, arithmetic and copies ran while one was open for 0% of the time, Pallas kernels for 29%

profile of v11, /device:TPU:1, one launch (start us, length us, event | category | flops | bytes accessed | tf_op | source)
XLA Modules:
  0.0 53.7 jit_solution(6406342868775342166)
XLA Ops:
  0.0 5.9 %lookup.2 = (bf16[256,8,256]{2,1,0:T(8,128)(2,1)}, bf16[3328,128]{1,0:T(8,128)(2,1)}) custom-call(s32[8,1024]{1,0:T(8,128)} %bitcast.4, bf16[1024,8,256]{2,1,0:T(8,128)(2,1)} %refs_1_.3, bf16[4096,256]{1,0:T(8,128)(2,1)} %refs_2_.3, bf16[3,256,128]{2,1,0:T(8,128)(2,1)} %refs_3_.1, bf16[128,256]{1,0:T(8,128)(2,1)} %refs_4_.1, bf16[256,128]{1,0:T(8,128)(2,1)} %refs_5_.1, ...), custom_call_target="tpu_custom_call" | custom-call | tf_op jit(solution)/shard_map/lookup/pallas_call | solution.py:151
  5.9 1.5 %collective-permute-start = (bf16[3328,128]{1,0:T(8,128)(2,1)}, bf16[3328,128]{1,0:T(8,128)(2,1)S(1)}, u32[]{:S(2)}, u32[]{:S(2)}) collective-permute-start(bf16[3328,128]{1,0:T(8,128)(2,1)} %get-tuple-element.39.own), channel_id=1, source_target_pairs={{0,1},{1,0},{2,3},{3,2},{4,5},{5,4},{6,7},{7,6},{8,9},{9,8},{10,11... | collective-permute-start | bytes 2555912 | tf_op jit(solution)/shard_map/ppermute | solution.py:467
  7.4 5.5 %all-to-all-start = ((bf16[256,8,256]{2,1,0:T(8,128)(2,1)}), bf16[256,8,256]{2,1,0:T(8,128)(2,1)S(1)}, u32[]{:S(2)}, u32[]{:S(2)}) async-start(bf16[256,8,256]{2,1,0:T(8,128)(2,1)} %get-tuple-element.60), calls=%async_computation | async-start | bytes 2097152 | tf_op jit(solution)/shard_map/all_to_all | solution.py:465
  12.9 0.0 collective-permute-done.other
  12.9 0.0 copy-start.1
  12.9 5.8 %lookup.3 = (bf16[32,8,256]{2,1,0:T(8,128)(2,1)}, bf16[32,8,256]{2,1,0:T(8,128)(2,1)}, bf16[32,8,256]{2,1,0:T(8,128)(2,1)}, bf16[32,8,256]{2,1,0:T(8,128)(2,1)},...) custom-call(s32[8,1024]{1,0:T(8,128)} %bitcast.5, ...), custom_call_target="tpu_custom_call" | custom-call | tf_op jit(solution)/shard_map/lookup/pallas_call | solution.py:151
  18.7 0.0 copy-done.1
  18.7 0.0 copy-start
  18.8 1.5 %collective-permute-start.2 = (bf16[32,8,256]{2,1,0:T(8,128)(2,1)}, bf16[32,8,256]{2,1,0:T(8,128)(2,1)S(1)}, u32[]{:S(2)}, u32[]{:S(2)}) collective-permute-start(bf16[32,8,256]{2,1,0:T(8,128)(2,1)} %get-tuple-element.52), channel_id=1, source_target_pairs={{0,2},{2,0},{4,6},{6,4},{8,10},{10,8},{12,14},{14,12},{1,3},{3,1},... | collective-permute-start | bytes 393224 | tf_op jit(solution)/shard_map/ppermute | solution.py:483
  20.3 1.2 %collective-permute-start.1 = (bf16[32,8,256]{2,1,0:T(8,128)(2,1)}, bf16[32,8,256]{2,1,0:T(8,128)(2,1)S(1)}, u32[]{:S(2)}, u32[]{:S(2)}) collective-permute-start(bf16[32,8,256]{2,1,0:T(8,128)(2,1)} %get-tuple-element.50), channel_id=1, source_target_pairs={{0,4},{2,6},{4,8},{6,10},{8,12},{10,14},{12,0},{14,2},{1,5},{3,7},... | collective-permute-start | bytes 393224 | tf_op jit(solution)/shard_map/ppermute | solution.py:483
  21.5 1.2 %collective-permute-start.3 = (bf16[32,8,256]{2,1,0:T(8,128)(2,1)}, bf16[32,8,256]{2,1,0:T(8,128)(2,1)S(1)}, u32[]{:S(2)}, u32[]{:S(2)}) collective-permute-start(bf16[32,8,256]{2,1,0:T(8,128)(2,1)} %get-tuple-element.66), channel_id=1, source_target_pairs={{0,6},{2,4},{4,10},{6,8},{8,14},{10,12},{12,2},{14,0},{1,7},{3,5},... | collective-permute-start | bytes 393224 | tf_op jit(solution)/shard_map/ppermute | solution.py:483
  22.7 1.3 %collective-permute-start.4 = (bf16[32,8,256]{2,1,0:T(8,128)(2,1)}, bf16[32,8,256]{2,1,0:T(8,128)(2,1)S(1)}, u32[]{:S(2)}, u32[]{:S(2)}) collective-permute-start(bf16[32,8,256]{2,1,0:T(8,128)(2,1)} %get-tuple-element.67), channel_id=1, source_target_pairs={{0,8},{2,10},{4,12},{6,14},{8,0},{10,2},{12,4},{14,6},{1,9},{3,11}... | collective-permute-start | bytes 393224 | tf_op jit(solution)/shard_map/ppermute | solution.py:483
  24.0 2.6 %collective-permute-start.5 = (bf16[32,8,256]{2,1,0:T(8,128)(2,1)}, bf16[32,8,256]{2,1,0:T(8,128)(2,1)}, u32[]{:S(2)}, u32[]{:S(2)}) collective-permute-start(bf16[32,8,256]{2,1,0:T(8,128)(2,1)} %get-tuple-element.68), channel_id=1, source_target_pairs={{0,10},{2,8},{4,14},{6,12},{8,2},{10,0},{12,6},{14,4},{1,11},{3,9}... | collective-permute-start | bytes 393224 | tf_op jit(solution)/shard_map/ppermute | solution.py:483
  26.5 2.0 %weights.1 = (bf16[3328,256]{1,0:T(8,128)(2,1)S(1)}, f32[64,256]{1,0:T(8,128)S(1)}, f32[2,4,256]{2,1,0:T(4,128)S(1)}) custom-call(s32[8,128]{1,0:T(8,128)} %bitcast.6, s32[4,64]{1,0:T(4,128)} %seed_ref.1, bf16[3328,128]{1,0:T(8,128)(2,1)} %get-tuple-element.39.own, bf16[3328,128]{1,0:T(8,128)(2,1)} %copy-done.1), custom_call_target="tpu_custom_call" | custom-call | tf_op jit(solution)/shard_map/weights/pallas_call | solution.py:241
  28.5 1.3 %collective-permute-done.2.refs_6_ = bf16[32,8,256]{2,1,0:T(8,128)(2,1)S(1)} collective-permute-done((bf16[32,8,256]{2,1,0:T(8,128)(2,1)}, bf16[32,8,256]{2,1,0:T(8,128)(2,1)S(1)}, u32[]{:S(2)}, u32[]{:S(2)}) %collective-permute-start.2) | collective-permute-done | bytes 131104 | tf_op jit(solution)/shard_map/ppermute | solution.py:483
  29.8 2.2 %collective-permute-done.1.refs_7_ = bf16[32,8,256]{2,1,0:T(8,128)(2,1)S(1)} collective-permute-done((bf16[32,8,256]{2,1,0:T(8,128)(2,1)}, bf16[32,8,256]{2,1,0:T(8,128)(2,1)S(1)}, u32[]{:S(2)}, u32[]{:S(2)}) %collective-permute-start.1) | collective-permute-done | bytes 131104 | tf_op jit(solution)/shard_map/ppermute | solution.py:483
  32.0 0.8 %collective-permute-start.7 = (bf16[32,8,256]{2,1,0:T(8,128)(2,1)}, bf16[32,8,256]{2,1,0:T(8,128)(2,1)}, u32[]{:S(2)}, u32[]{:S(2)}) collective-permute-start(bf16[32,8,256]{2,1,0:T(8,128)(2,1)} %get-tuple-element.70), channel_id=1, source_target_pairs={{0,14},{2,12},{4,2},{6,0},{8,6},{10,4},{12,10},{14,8},{1,15},{3,13... | collective-permute-start | bytes 393224 | tf_op jit(solution)/shard_map/ppermute | solution.py:483
  32.8 0.5 collective-permute-start.6
  33.2 0.0 all-to-all-done
  33.2 8.0 %encode.2 = (f32[64,4,128]{2,1,0:T(4,128)S(1)}, f32[64,4,128]{2,1,0:T(4,128)S(1)}) custom-call(f32[64,256]{1,0:T(8,128)S(1)} %get-tuple-element.57.refs_0_, f32[2,4,256]{2,1,0:T(4,128)S(1)} %get-tuple-element.58.refs_1_, bf16[3328,256]{1,0:T(8,128)(2,1)S(1)} %get-tuple-element.59.refs_2_, bf16[8,32,8,256]{3,2,1,0:T(8,128)(2,1)S(1)} %bitcast.3), custom_call_target="tpu_custom_call" | custom-call | tf_op jit(solution)/shard_map/encode/pallas_call | solution.py:439
  41.2 0.0 collective-permute-done.3.refs_8_
  41.2 0.0 collective-permute-done.4.refs_9_
  41.2 0.3 collective-permute-done.5.refs_10_
  41.5 0.0 collective-permute-done.7.refs_12_
  41.5 0.0 collective-permute-done.6.refs_11_
  41.5 0.0 copy-done
  41.5 9.0 %encode.3 = (f32[64,4,128]{2,1,0:T(4,128)S(1)}, f32[64,4,128]{2,1,0:T(4,128)S(1)}) custom-call(f32[64,256]{1,0:T(8,128)S(1)} %get-tuple-element.57.refs_0_, f32[2,4,256]{2,1,0:T(4,128)S(1)} %get-tuple-element.58.refs_1_, bf16[3328,256]{1,0:T(8,128)(2,1)S(1)} %get-tuple-element.59.refs_2_, f32[64,4,128]{2,1,0:T(4,128)S(1)} %get-tuple-element.61.refs_3_, ...), custom_call_target="tpu_custom_call" | custom-call | tf_op jit(solution)/shard_map/encode/pallas_call | solution.py:439
  50.5 1.6 %collective-permute-start.8 = (f32[64,4,128]{2,1,0:T(4,128)S(1)}, f32[64,4,128]{2,1,0:T(4,128)S(1)}, u32[]{:S(2)}, u32[]{:S(2)}) collective-permute-start(f32[64,4,128]{2,1,0:T(4,128)S(1)} %get-tuple-element.72), channel_id=1, source_target_pairs={{0,1},{1,0},{2,3},{3,2},{4,5},{5,4},{6,7},{7,6},{8,9},{9,8},{10,11... | collective-permute-start | bytes 393224 | tf_op jit(solution)/shard_map/ppermute | solution.py:486
  52.2 0.0 copy-start.2
  52.2 0.9 %collective-permute-done.8 = f32[64,4,128]{2,1,0:T(4,128)S(1)} collective-permute-done((f32[64,4,128]{2,1,0:T(4,128)S(1)}, f32[64,4,128]{2,1,0:T(4,128)S(1)}, u32[]{:S(2)}, u32[]{:S(2)}) %collective-permute-start.8) | collective-permute-done | bytes 131104 | tf_op jit(solution)/shard_map/ppermute | solution.py:486
  53.1 0.0 copy-done.2
  53.1 0.7 %constant_dynamic-update-slice_fusion = f32[128,4,128]{2,1,0:T(4,128)} fusion(f32[128,4,128]{2,1,0:T(4,128)} %copy-done.2, f32[64,4,128]{2,1,0:T(4,128)S(1)} %collective-permute-done.8, s32[]{:T(128)S(6)} %select_n.7), kind=kLoop, calls=%fused_computation | loop fusion | bytes 262148 | tf_op jit(solution)/shard_map/dynamic_update_slice | solution.py:489
  (2 shorter events, 0.1 us)
Async XLA Ops:
  5.9 7.0 %collective-permute-start = (bf16[3328,128]{1,0:T(8,128)(2,1)}, bf16[3328,128]{1,0:T(8,128)(2,1)S(1)}, u32[]{:S(2)}, u32[]{:S(2)}) collective-permute-start(bf16[3328,128]{1,0:T(8,128)(2,1)} %get-tuple-element.39.own), channel_id=1, source_target_pairs={{0,1},{1,0},{2,3},{3,2},{4,5},{5,4},{6,7},{7,6},{8,9},{9,8},{10,11... | collective-permute-start | bytes 2555912 | tf_op jit(solution)/shard_map/ppermute | solution.py:467
  7.4 25.8 %all-to-all-start = ((bf16[256,8,256]{2,1,0:T(8,128)(2,1)}), bf16[256,8,256]{2,1,0:T(8,128)(2,1)S(1)}, u32[]{:S(2)}, u32[]{:S(2)}) async-start(bf16[256,8,256]{2,1,0:T(8,128)(2,1)} %get-tuple-element.60), calls=%async_computation | async-start | bytes 2097152 | tf_op jit(solution)/shard_map/all_to_all | solution.py:465
  12.9 5.9 %copy-start.1 = (bf16[3328,128]{1,0:T(8,128)(2,1)}, bf16[3328,128]{1,0:T(8,128)(2,1)S(1)}, u32[]{:S(2)}) copy-start(bf16[3328,128]{1,0:T(8,128)(2,1)S(1)} %collective-permute-done.other) | copy-start | bytes 2555908
  18.7 22.7 %copy-start = (bf16[32,8,256]{2,1,0:T(8,128)(2,1)S(1)}, bf16[32,8,256]{2,1,0:T(8,128)(2,1)}, u32[]{:S(2)}) copy-start(bf16[32,8,256]{2,1,0:T(8,128)(2,1)} %get-tuple-element.63.refs_5_) | copy-start | bytes 393220
  18.8 11.0 %collective-permute-start.2 = (bf16[32,8,256]{2,1,0:T(8,128)(2,1)}, bf16[32,8,256]{2,1,0:T(8,128)(2,1)S(1)}, u32[]{:S(2)}, u32[]{:S(2)}) collective-permute-start(bf16[32,8,256]{2,1,0:T(8,128)(2,1)} %get-tuple-element.52), channel_id=1, source_target_pairs={{0,2},{2,0},{4,6},{6,4},{8,10},{10,8},{12,14},{14,12},{1,3},{3,1},... | collective-permute-start | bytes 393224 | tf_op jit(solution)/shard_map/ppermute | solution.py:483
  20.3 11.7 %collective-permute-start.1 = (bf16[32,8,256]{2,1,0:T(8,128)(2,1)}, bf16[32,8,256]{2,1,0:T(8,128)(2,1)S(1)}, u32[]{:S(2)}, u32[]{:S(2)}) collective-permute-start(bf16[32,8,256]{2,1,0:T(8,128)(2,1)} %get-tuple-element.50), channel_id=1, source_target_pairs={{0,4},{2,6},{4,8},{6,10},{8,12},{10,14},{12,0},{14,2},{1,5},{3,7},... | collective-permute-start | bytes 393224 | tf_op jit(solution)/shard_map/ppermute | solution.py:483
  21.5 19.7 %collective-permute-start.3 = (bf16[32,8,256]{2,1,0:T(8,128)(2,1)}, bf16[32,8,256]{2,1,0:T(8,128)(2,1)S(1)}, u32[]{:S(2)}, u32[]{:S(2)}) collective-permute-start(bf16[32,8,256]{2,1,0:T(8,128)(2,1)} %get-tuple-element.66), channel_id=1, source_target_pairs={{0,6},{2,4},{4,10},{6,8},{8,14},{10,12},{12,2},{14,0},{1,7},{3,5},... | collective-permute-start | bytes 393224 | tf_op jit(solution)/shard_map/ppermute | solution.py:483
  22.7 18.5 %collective-permute-start.4 = (bf16[32,8,256]{2,1,0:T(8,128)(2,1)}, bf16[32,8,256]{2,1,0:T(8,128)(2,1)S(1)}, u32[]{:S(2)}, u32[]{:S(2)}) collective-permute-start(bf16[32,8,256]{2,1,0:T(8,128)(2,1)} %get-tuple-element.67), channel_id=1, source_target_pairs={{0,8},{2,10},{4,12},{6,14},{8,0},{10,2},{12,4},{14,6},{1,9},{3,11}... | collective-permute-start | bytes 393224 | tf_op jit(solution)/shard_map/ppermute | solution.py:483
  24.0 17.5 %collective-permute-start.5 = (bf16[32,8,256]{2,1,0:T(8,128)(2,1)}, bf16[32,8,256]{2,1,0:T(8,128)(2,1)}, u32[]{:S(2)}, u32[]{:S(2)}) collective-permute-start(bf16[32,8,256]{2,1,0:T(8,128)(2,1)} %get-tuple-element.68), channel_id=1, source_target_pairs={{0,10},{2,8},{4,14},{6,12},{8,2},{10,0},{12,6},{14,4},{1,11},{3,9}... | collective-permute-start | bytes 393224 | tf_op jit(solution)/shard_map/ppermute | solution.py:483
  32.0 9.5 %collective-permute-start.7 = (bf16[32,8,256]{2,1,0:T(8,128)(2,1)}, bf16[32,8,256]{2,1,0:T(8,128)(2,1)}, u32[]{:S(2)}, u32[]{:S(2)}) collective-permute-start(bf16[32,8,256]{2,1,0:T(8,128)(2,1)} %get-tuple-element.70), channel_id=1, source_target_pairs={{0,14},{2,12},{4,2},{6,0},{8,6},{10,4},{12,10},{14,8},{1,15},{3,13... | collective-permute-start | bytes 393224 | tf_op jit(solution)/shard_map/ppermute | solution.py:483
  32.8 8.7 %collective-permute-start.6 = (bf16[32,8,256]{2,1,0:T(8,128)(2,1)}, bf16[32,8,256]{2,1,0:T(8,128)(2,1)}, u32[]{:S(2)}, u32[]{:S(2)}) collective-permute-start(bf16[32,8,256]{2,1,0:T(8,128)(2,1)} %get-tuple-element.69), channel_id=1, source_target_pairs={{0,12},{2,14},{4,0},{6,2},{8,4},{10,6},{12,8},{14,10},{1,13},{3,15... | collective-permute-start | bytes 393224 | tf_op jit(solution)/shard_map/ppermute | solution.py:483
  50.5 2.5 %collective-permute-start.8 = (f32[64,4,128]{2,1,0:T(4,128)S(1)}, f32[64,4,128]{2,1,0:T(4,128)S(1)}, u32[]{:S(2)}, u32[]{:S(2)}) collective-permute-start(f32[64,4,128]{2,1,0:T(4,128)S(1)} %get-tuple-element.72), channel_id=1, source_target_pairs={{0,1},{1,0},{2,3},{3,2},{4,5},{5,4},{6,7},{7,6},{8,9},{9,8},{10,11... | collective-permute-start | bytes 393224 | tf_op jit(solution)/shard_map/ppermute | solution.py:486
  52.2 0.9 %copy-start.2 = (f32[128,4,128]{2,1,0:T(4,128)}, f32[128,4,128]{2,1,0:T(4,128)S(1)}, u32[]{:S(2)}) copy-start(f32[128,4,128]{2,1,0:T(4,128)S(1)} %constant_dynamic-update-slice_fusion.1) | copy-start | bytes 786436

commit v12 on v11

--- a/solution.py
+++ b/solution.py
@@ -268,8 +268,6 @@
     own_ref, other_ref, interest_ref = refs[-3:]
     step = pl.program_id(0)
     if later:
-        own_ref[:start] = refs[3][:start]
-        other_ref[:start] = refs[4][:start]
         pairs, (all_users, spots, _) = len(parts), parts[0].shape
     else:
         pairs, all_users, spots, _ = parts[0].shape
@@ -351,6 +349,9 @@
 
     @pl.when(step == steps - 1)
     def _():
+        if later:
+            own_ref[:start] = refs[3][:start]
+            other_ref[:start] = refs[4][:start]
         base = base_ref[int(later)]
         route(valid_ref, base, own_ref, other_ref, interest_ref, history, start)
 
@@ -465,7 +466,6 @@
     got = lax.all_to_all(sent, "pa", split_axis=0, concat_axis=0, tiled=True)
     got = got.reshape(pa_count, cut, spots, D)
     other = lax.ppermute(packed, "dev", swap)
-    ids, other = lax.optimization_barrier((ids, other))
     late = lookup(ids, features, item_table, cut, per_core - cut, *counts, True)
     lens, late = lax.optimization_barrier((lengths.reshape(pa_count, -1), late))
     ff = w_up.shape[1]

time: 54 us -> 54 us (level)
  local copies, waits for them, and re-layouts: 0.74 us -> 1.64 us
  waiting for transfers between devices: 4.65 us -> 3.95 us
    unnamed x6, local copies, waits for them, and re-layouts: 0.02 us -> 0.92 us
    ppermute x7, waiting for transfers between devices: 3.74 us -> 3.04 us  [body(): parts.append(lax.ppermute(block, 'pa', pairs))]
where the time goes in v12:
time: 54 us; the launch traced here: 53.8 us
  Pallas kernels  30.4 us (56%)
  starting transfers between devices  17.7 us (33%)
  waiting for transfers between devices  3.95 us (7%)
  local copies, waits for them, and re-layouts  1.64 us (3%)
    pallas_call x2, Pallas kernels, encode(): pl.pallas_call(functools.partial(encode_kernel, steps=steps, start=start,...  17 us
    pallas_call x2, Pallas kernels, lookup(): pl.pallas_call(functools.partial(lookup_kernel, start=start, per_pair=per...  11.5 us
    ppermute x7, starting transfers between devices, body(): parts.append(lax.ppermute(block, 'pa', pairs))  9.34 us
    all_to_all x1, starting transfers between devices, body(): got = lax.all_to_all(sent, 'pa', split_axis=0, concat_axis=0, tiled=True)  5.46 us
    ppermute x7, waiting for transfers between devices, body(): parts.append(lax.ppermute(block, 'pa', pairs))  3.04 us
    pallas_call x1, Pallas kernels, finish_weights(): pl.pallas_call(functools.partial(weights_kernel, cut=cut, ff=ff), out_sha...  1.96 us
    ppermute x1, starting transfers between devices, body(): other = lax.ppermute(packed, 'dev', swap)  1.5 us
    ppermute x1, starting transfers between devices, body(): came = lax.ppermute(passed, 'dev', swap)  1.4 us
  transfers between devices with their start and end apart: 10, of which 4 were waited for; matrix products, arithmetic and copies ran while one was open for 0% of the time, Pallas kernels for 29%

profile of v12, /device:TPU:1, one launch (start us, length us, event | category | flops | bytes accessed | tf_op | source)
XLA Modules:
  0.0 53.8 jit_solution(13748885564252450007)
XLA Ops:
  0.0 5.9 %lookup.3 = (bf16[256,8,256]{2,1,0:T(8,128)(2,1)}, bf16[3328,128]{1,0:T(8,128)(2,1)}) custom-call(s32[8,1024]{1,0:T(8,128)} %bitcast.4, bf16[1024,8,256]{2,1,0:T(8,128)(2,1)} %refs_1_.3, bf16[4096,256]{1,0:T(8,128)(2,1)} %refs_2_.3, bf16[3,256,128]{2,1,0:T(8,128)(2,1)} %refs_3_.1, bf16[128,256]{1,0:T(8,128)(2,1)} %refs_4_.1, bf16[256,128]{1,0:T(8,128)(2,1)} %refs_5_.1, ...), custom_call_target="tpu_custom_call" | custom-call | tf_op jit(solution)/shard_map/lookup/pallas_call | solution.py:151
  5.9 1.5 %collective-permute-start.2 = (bf16[3328,128]{1,0:T(8,128)(2,1)}, bf16[3328,128]{1,0:T(8,128)(2,1)S(1)}, u32[]{:S(2)}, u32[]{:S(2)}) collective-permute-start(bf16[3328,128]{1,0:T(8,128)(2,1)} %get-tuple-element.50.own), channel_id=1, source_target_pairs={{0,1},{1,0},{2,3},{3,2},{4,5},{5,4},{6,7},{7,6},{8,9},{9,8},{10,11... | collective-permute-start | bytes 2555912 | tf_op jit(solution)/shard_map/ppermute | solution.py:468
  7.4 5.5 %all-to-all-start = ((bf16[256,8,256]{2,1,0:T(8,128)(2,1)}), bf16[256,8,256]{2,1,0:T(8,128)(2,1)S(1)}, u32[]{:S(2)}, u32[]{:S(2)}) async-start(bf16[256,8,256]{2,1,0:T(8,128)(2,1)} %get-tuple-element.56), calls=%async_computation | async-start | bytes 2097152 | tf_op jit(solution)/shard_map/all_to_all | solution.py:466
  12.9 5.5 %lookup.2 = (bf16[32,8,256]{2,1,0:T(8,128)(2,1)}, bf16[32,8,256]{2,1,0:T(8,128)(2,1)}, bf16[32,8,256]{2,1,0:T(8,128)(2,1)}, bf16[32,8,256]{2,1,0:T(8,128)(2,1)},...) custom-call(s32[8,1024]{1,0:T(8,128)} %bitcast.5, ...), custom_call_target="tpu_custom_call" | custom-call | tf_op jit(solution)/shard_map/lookup/pallas_call | solution.py:151
  18.4 0.0 copy-start
  18.4 1.5 %collective-permute-start.1 = (bf16[32,8,256]{2,1,0:T(8,128)(2,1)}, bf16[32,8,256]{2,1,0:T(8,128)(2,1)S(1)}, u32[]{:S(2)}, u32[]{:S(2)}) collective-permute-start(bf16[32,8,256]{2,1,0:T(8,128)(2,1)} %get-tuple-element.48), channel_id=1, source_target_pairs={{0,2},{2,0},{4,6},{6,4},{8,10},{10,8},{12,14},{14,12},{1,3},{3,1},... | collective-permute-start | bytes 393224 | tf_op jit(solution)/shard_map/ppermute | solution.py:483
  20.0 1.2 %collective-permute-start = (bf16[32,8,256]{2,1,0:T(8,128)(2,1)}, bf16[32,8,256]{2,1,0:T(8,128)(2,1)S(1)}, u32[]{:S(2)}, u32[]{:S(2)}) collective-permute-start(bf16[32,8,256]{2,1,0:T(8,128)(2,1)} %get-tuple-element.46), channel_id=1, source_target_pairs={{0,4},{2,6},{4,8},{6,10},{8,12},{10,14},{12,0},{14,2},{1,5},{3,7},... | collective-permute-start | bytes 393224 | tf_op jit(solution)/shard_map/ppermute | solution.py:483
  21.2 1.2 %collective-permute-start.3 = (bf16[32,8,256]{2,1,0:T(8,128)(2,1)}, bf16[32,8,256]{2,1,0:T(8,128)(2,1)S(1)}, u32[]{:S(2)}, u32[]{:S(2)}) collective-permute-start(bf16[32,8,256]{2,1,0:T(8,128)(2,1)} %get-tuple-element.62), channel_id=1, source_target_pairs={{0,6},{2,4},{4,10},{6,8},{8,14},{10,12},{12,2},{14,0},{1,7},{3,5},... | collective-permute-start | bytes 393224 | tf_op jit(solution)/shard_map/ppermute | solution.py:483
  22.3 1.3 %collective-permute-start.4 = (bf16[32,8,256]{2,1,0:T(8,128)(2,1)}, bf16[32,8,256]{2,1,0:T(8,128)(2,1)S(1)}, u32[]{:S(2)}, u32[]{:S(2)}) collective-permute-start(bf16[32,8,256]{2,1,0:T(8,128)(2,1)} %get-tuple-element.63), channel_id=1, source_target_pairs={{0,8},{2,10},{4,12},{6,14},{8,0},{10,2},{12,4},{14,6},{1,9},{3,11}... | collective-permute-start | bytes 393224 | tf_op jit(solution)/shard_map/ppermute | solution.py:483
  23.6 0.0 collective-permute-done.2.other
  23.6 0.0 copy-start.1
  23.6 0.9 %copy-done.1 = bf16[3328,128]{1,0:T(8,128)(2,1)} copy-done((bf16[3328,128]{1,0:T(8,128)(2,1)}, bf16[3328,128]{1,0:T(8,128)(2,1)S(1)}, u32[]{:S(2)}) %copy-start.1) | copy-done | bytes 851992
  24.5 2.6 %collective-permute-start.5 = (bf16[32,8,256]{2,1,0:T(8,128)(2,1)}, bf16[32,8,256]{2,1,0:T(8,128)(2,1)}, u32[]{:S(2)}, u32[]{:S(2)}) collective-permute-start(bf16[32,8,256]{2,1,0:T(8,128)(2,1)} %get-tuple-element.64), channel_id=1, source_target_pairs={{0,10},{2,8},{4,14},{6,12},{8,2},{10,0},{12,6},{14,4},{1,11},{3,9}... | collective-permute-start | bytes 393224 | tf_op jit(solution)/shard_map/ppermute | solution.py:483
  27.1 2.0 %weights.1 = (bf16[3328,256]{1,0:T(8,128)(2,1)S(1)}, f32[64,256]{1,0:T(8,128)S(1)}, f32[2,4,256]{2,1,0:T(4,128)S(1)}) custom-call(s32[8,128]{1,0:T(8,128)} %bitcast.6, s32[4,64]{1,0:T(4,128)} %seed_ref.1, bf16[3328,128]{1,0:T(8,128)(2,1)} %get-tuple-element.50.own, bf16[3328,128]{1,0:T(8,128)(2,1)} %copy-done.1), custom_call_target="tpu_custom_call" | custom-call | tf_op jit(solution)/shard_map/weights/pallas_call | solution.py:241
  29.1 0.6 %collective-permute-done.1.refs_6_ = bf16[32,8,256]{2,1,0:T(8,128)(2,1)S(1)} collective-permute-done((bf16[32,8,256]{2,1,0:T(8,128)(2,1)}, bf16[32,8,256]{2,1,0:T(8,128)(2,1)S(1)}, u32[]{:S(2)}, u32[]{:S(2)}) %collective-permute-start.1) | collective-permute-done | bytes 131104 | tf_op jit(solution)/shard_map/ppermute | solution.py:483
  29.7 1.9 %collective-permute-done.refs_7_ = bf16[32,8,256]{2,1,0:T(8,128)(2,1)S(1)} collective-permute-done((bf16[32,8,256]{2,1,0:T(8,128)(2,1)}, bf16[32,8,256]{2,1,0:T(8,128)(2,1)S(1)}, u32[]{:S(2)}, u32[]{:S(2)}) %collective-permute-start) | collective-permute-done | bytes 131104 | tf_op jit(solution)/shard_map/ppermute | solution.py:483
  31.7 1.1 %collective-permute-start.7 = (bf16[32,8,256]{2,1,0:T(8,128)(2,1)}, bf16[32,8,256]{2,1,0:T(8,128)(2,1)}, u32[]{:S(2)}, u32[]{:S(2)}) collective-permute-start(bf16[32,8,256]{2,1,0:T(8,128)(2,1)} %get-tuple-element.66), channel_id=1, source_target_pairs={{0,14},{2,12},{4,2},{6,0},{8,6},{10,4},{12,10},{14,8},{1,15},{3,13... | collective-permute-start | bytes 393224 | tf_op jit(solution)/shard_map/ppermute | solution.py:483
  32.8 0.5 collective-permute-start.6
  33.2 0.0 all-to-all-done
  33.2 8.0 %encode.2 = (f32[64,4,128]{2,1,0:T(4,128)S(1)}, f32[64,4,128]{2,1,0:T(4,128)S(1)}) custom-call(f32[64,256]{1,0:T(8,128)S(1)} %get-tuple-element.53.refs_0_, f32[2,4,256]{2,1,0:T(4,128)S(1)} %get-tuple-element.54.refs_1_, bf16[3328,256]{1,0:T(8,128)(2,1)S(1)} %get-tuple-element.55.refs_2_, bf16[8,32,8,256]{3,2,1,0:T(8,128)(2,1)S(1)} %bitcast.3), custom_call_target="tpu_custom_call" | custom-call | tf_op jit(solution)/shard_map/encode/pallas_call | solution.py:440
  41.2 0.0 collective-permute-done.3.refs_8_
  41.2 0.0 collective-permute-done.4.refs_9_
  41.2 0.5 collective-permute-done.5.refs_10_
  41.7 0.0 collective-permute-done.7.refs_12_
  41.7 0.0 collective-permute-done.6.refs_11_
  41.7 0.0 copy-done
  41.7 9.0 %encode.3 = (f32[64,4,128]{2,1,0:T(4,128)S(1)}, f32[64,4,128]{2,1,0:T(4,128)S(1)}) custom-call(f32[64,256]{1,0:T(8,128)S(1)} %get-tuple-element.53.refs_0_, f32[2,4,256]{2,1,0:T(4,128)S(1)} %get-tuple-element.54.refs_1_, bf16[3328,256]{1,0:T(8,128)(2,1)S(1)} %get-tuple-element.55.refs_2_, f32[64,4,128]{2,1,0:T(4,128)S(1)} %get-tuple-element.57.refs_3_, ...), custom_call_target="tpu_custom_call" | custom-call | tf_op jit(solution)/shard_map/encode/pallas_call | solution.py:440
  50.7 1.4 %collective-permute-start.8 = (f32[64,4,128]{2,1,0:T(4,128)S(1)}, f32[64,4,128]{2,1,0:T(4,128)S(1)}, u32[]{:S(2)}, u32[]{:S(2)}) collective-permute-start(f32[64,4,128]{2,1,0:T(4,128)S(1)} %get-tuple-element.68), channel_id=1, source_target_pairs={{0,1},{1,0},{2,3},{3,2},{4,5},{5,4},{6,7},{7,6},{8,9},{9,8},{10,11... | collective-permute-start | bytes 393224 | tf_op jit(solution)/shard_map/ppermute | solution.py:486
  52.2 0.0 copy-start.2
  52.2 0.9 %collective-permute-done.8 = f32[64,4,128]{2,1,0:T(4,128)S(1)} collective-permute-done((f32[64,4,128]{2,1,0:T(4,128)S(1)}, f32[64,4,128]{2,1,0:T(4,128)S(1)}, u32[]{:S(2)}, u32[]{:S(2)}) %collective-permute-start.8) | collective-permute-done | bytes 131104 | tf_op jit(solution)/shard_map/ppermute | solution.py:486
  53.1 0.0 copy-done.2
  53.1 0.7 %constant_dynamic-update-slice_fusion = f32[128,4,128]{2,1,0:T(4,128)} fusion(f32[128,4,128]{2,1,0:T(4,128)} %copy-done.2, f32[64,4,128]{2,1,0:T(4,128)S(1)} %collective-permute-done.8, s32[]{:T(128)S(6)} %select_n.7), kind=kLoop, calls=%fused_computation | loop fusion | bytes 262148 | tf_op jit(solution)/shard_map/dynamic_update_slice | solution.py:489
  (2 shorter events, 0.1 us)
Async XLA Ops:
  5.9 17.7 %collective-permute-start.2 = (bf16[3328,128]{1,0:T(8,128)(2,1)}, bf16[3328,128]{1,0:T(8,128)(2,1)S(1)}, u32[]{:S(2)}, u32[]{:S(2)}) collective-permute-start(bf16[3328,128]{1,0:T(8,128)(2,1)} %get-tuple-element.50.own), channel_id=1, source_target_pairs={{0,1},{1,0},{2,3},{3,2},{4,5},{5,4},{6,7},{7,6},{8,9},{9,8},{10,11... | collective-permute-start | bytes 2555912 | tf_op jit(solution)/shard_map/ppermute | solution.py:468
  7.4 25.8 %all-to-all-start = ((bf16[256,8,256]{2,1,0:T(8,128)(2,1)}), bf16[256,8,256]{2,1,0:T(8,128)(2,1)S(1)}, u32[]{:S(2)}, u32[]{:S(2)}) async-start(bf16[256,8,256]{2,1,0:T(8,128)(2,1)} %get-tuple-element.56), calls=%async_computation | async-start | bytes 2097152 | tf_op jit(solution)/shard_map/all_to_all | solution.py:466
  18.4 23.3 %copy-start = (bf16[32,8,256]{2,1,0:T(8,128)(2,1)S(1)}, bf16[32,8,256]{2,1,0:T(8,128)(2,1)}, u32[]{:S(2)}) copy-start(bf16[32,8,256]{2,1,0:T(8,128)(2,1)} %get-tuple-element.59.refs_5_) | copy-start | bytes 393220
  18.4 11.3 %collective-permute-start.1 = (bf16[32,8,256]{2,1,0:T(8,128)(2,1)}, bf16[32,8,256]{2,1,0:T(8,128)(2,1)S(1)}, u32[]{:S(2)}, u32[]{:S(2)}) collective-permute-start(bf16[32,8,256]{2,1,0:T(8,128)(2,1)} %get-tuple-element.48), channel_id=1, source_target_pairs={{0,2},{2,0},{4,6},{6,4},{8,10},{10,8},{12,14},{14,12},{1,3},{3,1},... | collective-permute-start | bytes 393224 | tf_op jit(solution)/shard_map/ppermute | solution.py:483
  20.0 11.7 %collective-permute-start = (bf16[32,8,256]{2,1,0:T(8,128)(2,1)}, bf16[32,8,256]{2,1,0:T(8,128)(2,1)S(1)}, u32[]{:S(2)}, u32[]{:S(2)}) collective-permute-start(bf16[32,8,256]{2,1,0:T(8,128)(2,1)} %get-tuple-element.46), channel_id=1, source_target_pairs={{0,4},{2,6},{4,8},{6,10},{8,12},{10,14},{12,0},{14,2},{1,5},{3,7},... | collective-permute-start | bytes 393224 | tf_op jit(solution)/shard_map/ppermute | solution.py:483
  21.2 20.0 %collective-permute-start.3 = (bf16[32,8,256]{2,1,0:T(8,128)(2,1)}, bf16[32,8,256]{2,1,0:T(8,128)(2,1)S(1)}, u32[]{:S(2)}, u32[]{:S(2)}) collective-permute-start(bf16[32,8,256]{2,1,0:T(8,128)(2,1)} %get-tuple-element.62), channel_id=1, source_target_pairs={{0,6},{2,4},{4,10},{6,8},{8,14},{10,12},{12,2},{14,0},{1,7},{3,5},... | collective-permute-start | bytes 393224 | tf_op jit(solution)/shard_map/ppermute | solution.py:483
  22.3 18.9 %collective-permute-start.4 = (bf16[32,8,256]{2,1,0:T(8,128)(2,1)}, bf16[32,8,256]{2,1,0:T(8,128)(2,1)S(1)}, u32[]{:S(2)}, u32[]{:S(2)}) collective-permute-start(bf16[32,8,256]{2,1,0:T(8,128)(2,1)} %get-tuple-element.63), channel_id=1, source_target_pairs={{0,8},{2,10},{4,12},{6,14},{8,0},{10,2},{12,4},{14,6},{1,9},{3,11}... | collective-permute-start | bytes 393224 | tf_op jit(solution)/shard_map/ppermute | solution.py:483
  23.6 0.9 %copy-start.1 = (bf16[3328,128]{1,0:T(8,128)(2,1)}, bf16[3328,128]{1,0:T(8,128)(2,1)S(1)}, u32[]{:S(2)}) copy-start(bf16[3328,128]{1,0:T(8,128)(2,1)S(1)} %collective-permute-done.2.other) | copy-start | bytes 2555908
  24.5 17.1 %collective-permute-start.5 = (bf16[32,8,256]{2,1,0:T(8,128)(2,1)}, bf16[32,8,256]{2,1,0:T(8,128)(2,1)}, u32[]{:S(2)}, u32[]{:S(2)}) collective-permute-start(bf16[32,8,256]{2,1,0:T(8,128)(2,1)} %get-tuple-element.64), channel_id=1, source_target_pairs={{0,10},{2,8},{4,14},{6,12},{8,2},{10,0},{12,6},{14,4},{1,11},{3,9}... | collective-permute-start | bytes 393224 | tf_op jit(solution)/shard_map/ppermute | solution.py:483
  31.7 10.0 %collective-permute-start.7 = (bf16[32,8,256]{2,1,0:T(8,128)(2,1)}, bf16[32,8,256]{2,1,0:T(8,128)(2,1)}, u32[]{:S(2)}, u32[]{:S(2)}) collective-permute-start(bf16[32,8,256]{2,1,0:T(8,128)(2,1)} %get-tuple-element.66), channel_id=1, source_target_pairs={{0,14},{2,12},{4,2},{6,0},{8,6},{10,4},{12,10},{14,8},{1,15},{3,13... | collective-permute-start | bytes 393224 | tf_op jit(solution)/shard_map/ppermute | solution.py:483
  32.8 8.9 %collective-permute-start.6 = (bf16[32,8,256]{2,1,0:T(8,128)(2,1)}, bf16[32,8,256]{2,1,0:T(8,128)(2,1)}, u32[]{:S(2)}, u32[]{:S(2)}) collective-permute-start(bf16[32,8,256]{2,1,0:T(8,128)(2,1)} %get-tuple-element.65), channel_id=1, source_target_pairs={{0,12},{2,14},{4,0},{6,2},{8,4},{10,6},{12,8},{14,10},{1,13},{3,15... | collective-permute-start | bytes 393224 | tf_op jit(solution)/shard_map/ppermute | solution.py:483
  50.7 2.4 %collective-permute-start.8 = (f32[64,4,128]{2,1,0:T(4,128)S(1)}, f32[64,4,128]{2,1,0:T(4,128)S(1)}, u32[]{:S(2)}, u32[]{:S(2)}) collective-permute-start(f32[64,4,128]{2,1,0:T(4,128)S(1)} %get-tuple-element.68), channel_id=1, source_target_pairs={{0,1},{1,0},{2,3},{3,2},{4,5},{5,4},{6,7},{7,6},{8,9},{9,8},{10,11... | collective-permute-start | bytes 393224 | tf_op jit(solution)/shard_map/ppermute | solution.py:486
  52.2 0.9 %copy-start.2 = (f32[128,4,128]{2,1,0:T(4,128)}, f32[128,4,128]{2,1,0:T(4,128)S(1)}, u32[]{:S(2)}) copy-start(f32[128,4,128]{2,1,0:T(4,128)S(1)} %constant_dynamic-update-slice_fusion.1) | copy-start | bytes 786436
